TPU v7x, 32 devices: a whole 2x2x4 slice. The times are simulated.
32 devices in a mesh: dp: 16 (over z, x, core), tensor: 2 (over y).
Axes of the slice: x: 2, y: 2, z: 4, core: 2. Of those that a mesh axis runs over, the one named last changes fastest.
Arguments:
- patches: bfloat16 [96, 512, 768], P('dp'), may hold values from -6 to 6
- counts: int32 [96], P('dp'), may hold values from 51 to 256, as said below
- visible: int32 [96, 512], P('dp'), may hold values from 0 to 511, each once within a row
- gain_one: float32 [768], replicated, may hold values from 0.1 to 1.9
- shift_one: float32 [768], replicated, may hold values from -2 to 2
- qkv_weight: bfloat16 [768, 3, 768], P(None, None, 'tensor'), may hold values from -0.21875 to 0.21875
- out_weight: bfloat16 [768, 768], P('tensor'), may hold values from -2 to 2
- gain_two: float32 [768], replicated, may hold values from 0.1 to 1.9
- shift_two: float32 [768], replicated, may hold values from -2 to 2
- up_weight: bfloat16 [768, 3072], P(None, 'tensor'), may hold values from -0.21875 to 0.21875
- down_weight: bfloat16 [3072, 768], P('tensor'), may hold values from -0.109375 to 0.109375
- cotangent: bfloat16 [96, 512, 768], P('dp'), may hold values from -6 to 6
Outputs:
- output: bfloat16 [96, 512, 768], P('dp')
- input_grad: bfloat16 [96, 512, 768], P('dp')
- gain_one_grad: float32 [768], replicated
- shift_one_grad: float32 [768], replicated
- qkv_grad: float32 [768, 3, 768], P(None, None, 'tensor')
- out_grad: float32 [768, 768], P('tensor')
- gain_two_grad: float32 [768], replicated
- shift_two_grad: float32 [768], replicated
- up_grad: float32 [768, 3072], P(None, 'tensor')
- down_grad: float32 [3072, 768], P('tensor')
Inputs may be any that keep to these rules, and one draw needn't show every extreme that they name: `counts`: every sample has between 51 and 256 visible patches; some sample has exactly 256 and some exactly 51. Each row orders the 512 patches of a sample, its visible patches in the first counts places.
All inputs are finite; a program needn't handle non-finite values.
Results may differ from a plain program's by a relative error of at most 0.013.
Values sent between devices are 32-bit elements; how exact they have to be, the bound alone decides.
No kernel may reach another device: no remote copies, remote signals or barrier semaphores. Data moves between devices by JAX's collectives and lax.ppermute only.
A program may use at most 192 MiB of HBM per device.

v0:
```python
import jax
import jax.numpy as jnp
from jax import lax
from jax.sharding import PartitionSpec as P

HD = 64
VIS_HI = 256


norm_eps = 1e-06
masked_score = -1e30


def layer_norm(values, norm_gain, norm_shift):
    center = values - jnp.mean(values, axis=-1, keepdims=True)
    spread = jnp.mean(center * center, axis=-1, keepdims=True)
    return center * lax.rsqrt(spread + norm_eps) * norm_gain + norm_shift


def exact_gelu(values):
    return jax.nn.gelu(values, approximate=False)


def scores_of(query_rows, key_rows, live_keys):
    raw_scores = jnp.einsum(
        "qhd,khd->hqk", query_rows, key_rows, preferred_element_type=jnp.float32
    ) * HD ** (-0.5)
    return jnp.where(live_keys[None, None, :] > 0, raw_scores, masked_score)


def attend_forward(block_items):
    query_rows, key_rows, value_rows, live_keys = block_items
    scores = scores_of(query_rows, key_rows, live_keys)
    row_max = jnp.max(scores, axis=-1, keepdims=True)
    weights = jnp.exp(scores - row_max)
    row_total = jnp.sum(weights, axis=-1, keepdims=True)
    probabilities = (weights / row_total).astype(jnp.bfloat16)
    attended = jnp.einsum(
        "hqk,khd->qhd", probabilities, value_rows, preferred_element_type=jnp.float32
    )
    return (attended.astype(jnp.bfloat16), row_max + jnp.log(row_total))


def attend_backward(block_items):
    query_rows, key_rows, value_rows, live_keys, grad_attended, log_total = block_items
    scale = HD ** (-0.5)
    scores = scores_of(query_rows, key_rows, live_keys)
    probabilities = jnp.exp(scores - log_total)
    grad_probs = jnp.einsum(
        "qhd,khd->hqk", grad_attended, value_rows, preferred_element_type=jnp.float32
    )
    inner_sum = jnp.sum(probabilities * grad_probs, axis=-1, keepdims=True)
    grad_scores = (probabilities * (grad_probs - inner_sum)).astype(jnp.bfloat16)
    grad_query = (
        jnp.einsum("hqk,khd->qhd", grad_scores, key_rows, preferred_element_type=jnp.float32)
        * scale
    )
    grad_key = (
        jnp.einsum("hqk,qhd->khd", grad_scores, query_rows, preferred_element_type=jnp.float32)
        * scale
    )
    grad_value = jnp.einsum(
        "hqk,qhd->khd",
        probabilities.astype(jnp.bfloat16),
        grad_attended,
        preferred_element_type=jnp.float32,
    )
    return jnp.stack([grad_query, grad_key, grad_value], axis=1).astype(jnp.bfloat16)


def shards(
    patches,
    counts,
    visible,
    gain_one,
    shift_one,
    qkv_weight,
    out_weight,
    gain_two,
    shift_two,
    up_weight,
    down_weight,
    cotangent,
):
    samples, model_width = (patches.shape[0], patches.shape[2])
    slots = VIS_HI
    local_width = qkv_weight.shape[2]
    local_heads = local_width // HD
    row_count = samples * slots
    picked = visible[:, :slots]
    live_mask = (lax.broadcasted_iota(jnp.int32, (samples, slots), 1) < counts[:, None]).astype(
        jnp.float32
    )
    inverse = jnp.argsort(visible, axis=1)
    grid_live = (inverse < counts[:, None]).astype(jnp.float32)
    slot_of = jnp.minimum(inverse, slots - 1)
    packed = (
        jnp.take_along_axis(patches, picked[:, :, None], axis=1).astype(jnp.float32)
        * live_mask[:, :, None]
    )
    resid_in = packed.reshape(row_count, model_width)
    normed_one = layer_norm(resid_in, gain_one, shift_one).astype(jnp.bfloat16)
    qkv_flat = qkv_weight.reshape(model_width, 3 * local_width)
    projected = jnp.dot(normed_one, qkv_flat, preferred_element_type=jnp.float32).astype(
        jnp.bfloat16
    )
    projected = projected.reshape(samples, slots, 3, local_heads, HD)
    query_all = projected[:, :, 0]
    key_all = projected[:, :, 1]
    value_all = projected[:, :, 2]
    attended, log_total = lax.map(attend_forward, (query_all, key_all, value_all, live_mask))
    attended_rows = attended.reshape(row_count, local_width)
    attn_out = lax.psum(
        jnp.dot(attended_rows, out_weight, preferred_element_type=jnp.float32), "tensor"
    )
    resid_mid = resid_in + attn_out
    normed_two = layer_norm(resid_mid, gain_two, shift_two).astype(jnp.bfloat16)
    pre_act = jnp.dot(normed_two, up_weight, preferred_element_type=jnp.float32)
    activation, gelu_pullback = jax.vjp(exact_gelu, pre_act)
    activation_low = activation.astype(jnp.bfloat16)
    mlp_out = lax.psum(
        jnp.dot(activation_low, down_weight, preferred_element_type=jnp.float32), "tensor"
    )
    result = (resid_mid + mlp_out).reshape(samples, slots, model_width) * live_mask[:, :, None]
    output = (
        jnp.take_along_axis(result, slot_of[:, :, None], axis=1) * grid_live[:, :, None]
    ).astype(jnp.bfloat16)
    grad_rows = (
        jnp.take_along_axis(cotangent, picked[:, :, None], axis=1).astype(jnp.float32)
        * live_mask[:, :, None]
    )
    grad_rows = grad_rows.reshape(row_count, model_width)
    grad_mlp = grad_rows.astype(jnp.bfloat16)
    grad_down = jnp.dot(activation_low.T, grad_mlp, preferred_element_type=jnp.float32)
    grad_activation = jnp.dot(grad_mlp, down_weight.T, preferred_element_type=jnp.float32)
    grad_pre = gelu_pullback(grad_activation)[0].astype(jnp.bfloat16)
    grad_up = jnp.dot(normed_two.T, grad_pre, preferred_element_type=jnp.float32)
    grad_normed_two = lax.psum(
        jnp.dot(grad_pre, up_weight.T, preferred_element_type=jnp.float32), "tensor"
    )
    norm_two_pullback = jax.vjp(layer_norm, resid_mid, gain_two, shift_two)[1]
    grad_resid_part, grad_gain_two, grad_shift_two = norm_two_pullback(grad_normed_two)
    grad_resid_mid = grad_rows + grad_resid_part
    grad_attn = grad_resid_mid.astype(jnp.bfloat16)
    grad_wout = jnp.dot(attended_rows.T, grad_attn, preferred_element_type=jnp.float32)
    grad_attended = jnp.dot(grad_attn, out_weight.T, preferred_element_type=jnp.float32).astype(
        jnp.bfloat16
    )
    grad_attended = grad_attended.reshape(samples, slots, local_heads, HD)
    grad_projected = lax.map(
        attend_backward, (query_all, key_all, value_all, live_mask, grad_attended, log_total)
    )
    grad_flat = grad_projected.reshape(row_count, 3 * local_width)
    grad_qkv = jnp.dot(normed_one.T, grad_flat, preferred_element_type=jnp.float32).reshape(
        model_width, 3, local_width
    )
    grad_normed_one = lax.psum(
        jnp.dot(grad_flat, qkv_flat.T, preferred_element_type=jnp.float32), "tensor"
    )
    norm_one_pullback = jax.vjp(layer_norm, resid_in, gain_one, shift_one)[1]
    grad_in_part, grad_gain_one, grad_shift_one = norm_one_pullback(grad_normed_one)
    grad_input_rows = (grad_resid_mid + grad_in_part).reshape(
        samples, slots, model_width
    ) * live_mask[:, :, None]
    input_grad = (
        jnp.take_along_axis(grad_input_rows, slot_of[:, :, None], axis=1) * grid_live[:, :, None]
    ).astype(jnp.bfloat16)
    (
        grad_qkv,
        grad_wout,
        grad_up,
        grad_down,
        grad_gain_one,
        grad_shift_one,
        grad_gain_two,
        grad_shift_two,
    ) = lax.psum(
        (
            grad_qkv,
            grad_wout,
            grad_up,
            grad_down,
            grad_gain_one,
            grad_shift_one,
            grad_gain_two,
            grad_shift_two,
        ),
        "dp",
    )
    return (
        output,
        input_grad,
        grad_gain_one,
        grad_shift_one,
        grad_qkv,
        grad_wout,
        grad_gain_two,
        grad_shift_two,
        grad_up,
        grad_down,
    )


def solution(mesh):
    placed = (
        P("dp", None, None),
        P("dp"),
        P("dp", None),
        P(),
        P(),
        P(None, None, "tensor"),
        P("tensor", None),
        P(),
        P(),
        P(None, "tensor"),
        P("tensor", None),
        P("dp", None, None),
    )
    return jax.shard_map(
        shards,
        mesh=mesh,
        in_specs=placed,
        out_specs=(
            P("dp", None, None),
            P("dp", None, None),
            P(),
            P(),
            P(None, None, "tensor"),
            P("tensor", None),
            P(),
            P(),
            P(None, "tensor"),
            P("tensor", None),
        ),
        check_vma=False,
    )
```

profile of v0, /device:TPU:0, one launch (start us, length us, event | category | flops | bytes accessed | tf_op | source)
XLA Modules:
  0.0 1043.8 jit_solution(15206311019617002006)
XLA Ops:
  10.4 29.8 %gather_fusion = bf16[1536,768]{1,0:T(8,128)(2,1)} fusion(bf16[6,512,768]{2,1,0:T(8,128)(2,1)} %param.20, s32[1536]{0:T(1024)S(1)} %reshape.320), kind=kCustom, calls=%fused_computation.clone | custom fusion | bytes 4730880 | tf_op jit(solution)/shard_map/jit(take_along_axis)/gather | solution.py:98
  40.2 2.3 fusion.45
  42.5 29.8 %gather_fusion.2 = bf16[1536,768]{1,0:T(8,128)(2,1)} fusion(bf16[6,512,768]{2,1,0:T(8,128)(2,1)} %param.31, s32[1536]{0:T(1024)S(1)} %reshape.320), kind=kCustom, calls=%fused_computation.2.clone | custom fusion | bytes 4730880 | tf_op jit(solution)/shard_map/jit(take_along_axis)/gather | solution.py:129
  72.4 5.0 convert_multiply_fusion
  77.9 3.8 copy.35
  81.8 5.2 convert_multiply_fusion.1
  88.4 4.7 convolution_convert_fusion.2
  93.1 5.7 copy.36
  98.9 8.0 reshape.289
  106.8 2.8 slice_bitcast_fusion
  112.5 25.3 %while.22 = (s32[]{:T(128)}, bf16[6,256,6,64]{1,3,2,0:T(8,128)(2,1)}, f32[6,6,256,1]{2,1,3,0:T(8,128)}, bf16[6,256,6,64]{1,3,2,0:T(8,128)(2,1)}, f32[6,256]{1,0:...) while((s32[]{:T(128)}, ...), condition=%wide.region_5.7_spmd, body=%wide.region_2.6_spmd.sunk | while | flops 103906048 | bytes 5560665 | solution.py:111
  114.7 2.0 fusion.106
  118.9 2.0 fusion.106
  123.1 2.0 fusion.106
  127.4 2.0 fusion.106
  131.6 2.0 fusion.106
  135.8 2.0 fusion.106
  137.8 2.1 copy.40
  141.3 3.6 fusion.59
  145.4 4.0 bitcast_convert_fusion
  149.5 117.6 %all-reduce.8.cloned.1.call-done = f32[1536,768]{1,0:T(8,128)} async-done(((f32[1536,768]{1,0:T(8,128)}), f32[1536,768]{1,0:T(8,128)}) %all-reduce.8.cloned.1.call-update) | async-done | bytes 4718608 | tf_op jit(solution)/shard_map/psum | solution.py:113
  267.0 4.3 fusion.57
  272.1 25.6 %multiply_convert_fusion.1 = (bf16[1536,1536]{1,0:T(8,128)(2,1)}, f32[1536,1536]{1,0:T(8,128)}, f32[1536,1536]{1,0:T(8,128)}) fusion(bf16[768,1536]{1,0:T(8,128)(2,1)S(1)} %copy-done, f32[1536,768]{1,0:T(8,128)S(1)} %get-tuple-element.173, f32[768]{0:T(1024)S(1)} %copy-done.37, f32[768]{0:T(1024)S(1)} %copy-done.31, f32[1536]{0:T(1024)S(1)} %fusion.50, ...), kind=kOutput, calls=%fused_computation.65 | convolution fusion | flops 3783131136 | bytes 30689280 | tf_op jit(solution)/shard_map/dot_general | solution.py:118
  297.8 10.3 add_convert_fusion
  308.1 2.1 copy-done.39
  310.2 5.4 fusion.61
  316.5 9.1 fusion.60
  325.5 109.6 %all-reduce.10.cloned.1.call-done = f32[1536,768]{1,0:T(8,128)} async-done(((f32[1536,768]{1,0:T(8,128)}), f32[1536,768]{1,0:T(8,128)}) %all-reduce.10.cloned.1.call-update) | async-done | bytes 4718608 | tf_op jit(solution)/shard_map/psum | solution.py:138
  435.1 5.6 multiply_reduce_fusion.1
  440.8 3.8 fusion.55
  445.2 2.2 copy-done.3
  448.8 3.1 reshape.337
  451.9 4.2 copy.44
  456.1 46.3 %while.23 = (s32[]{:T(128)}, bf16[6,256,3,6,64]{1,4,3,2,0:T(8,128)(2,1)}, bf16[6,256,6,64]{1,3,2,0:T(8,128)(2,1)}, f32[6,256]{1,0:T(8,128)S(1)}, bf16[6,256,6,64...) while((s32[]{:T(128)}, ...), condition=%wide.region_16.19_spmd, body=%wide.region_14.18_spmd.sunk | while | flops 257456896 | bytes 14980457 | solution.py:150
  456.1 1.4 fusion.115
  458.3 1.5 multiply_reduce_fusion.8
  463.8 1.4 fusion.115
  466.0 1.5 multiply_reduce_fusion.8
  471.5 1.4 fusion.115
  473.7 1.5 multiply_reduce_fusion.8
  479.2 1.4 fusion.115
  481.4 1.5 multiply_reduce_fusion.8
  489.1 1.5 multiply_reduce_fusion.8
  496.8 1.5 multiply_reduce_fusion.8
  502.4 4.6 copy.46
  507.0 1.5 copy.57
  508.6 1.8 copy-done.8
  510.4 4.9 fusion.62
  517.0 8.4 fusion.64
  525.4 10.3 fusion.52
  535.7 4.6 fusion.46
  540.3 5.0 fusion.63
  548.3 187.9 %all-reduce.14.cloned.1.call-done = (f32[1536,768]{1,0:T(8,128)}, f32[1536,768]{1,0:T(8,128)}) async-done(((f32[1536,768]{1,0:T(8,128)}, f32[1536,768]{1,0:T(8,128)}), (f32[1536,768]{1,0:T(8,128)}, f32[1536,768]{1,0:T(8,128)})) %all-reduce.14.cloned.1.call-update) | async-done | bytes 9437200 | tf_op jit(solution)/shard_map/psum | solution.py:121
  736.2 4.7 add.120
  741.3 4.1 multiply_reduce_fusion.2
  745.5 2.5 fusion.54
  748.6 4.4 broadcast_multiply_fusion
  753.0 98.9 %gather_fusion.1 = f32[3072,768]{1,0:T(8,128)} fusion(f32[6,256,768]{2,1,0:T(8,128)} %get-tuple-element.188, s32[3072]{0:T(1024)S(1)} %reshape.324), kind=kCustom, calls=%fused_computation.1.clone | custom fusion | bytes 18898944 | tf_op jit(solution)/shard_map/jit(take_along_axis)/gather | solution.py:126
  851.9 99.1 %gather_fusion.3 = f32[3072,768]{1,0:T(8,128)} fusion(f32[6,256,768]{2,1,0:T(8,128)} %get-tuple-element.187, s32[3072]{0:T(1024)S(1)} %reshape.324), kind=kCustom, calls=%fused_computation.3.clone | custom fusion | bytes 18898944 | tf_op jit(solution)/shard_map/jit(take_along_axis)/gather | solution.py:166
  951.0 63.2 %all-reduce = (f32[768]{0:T(1024)}, f32[768]{0:T(1024)}, f32[768]{0:T(1024)}, f32[768]{0:T(1024)}) all-reduce(f32[768]{0:T(1024)S(1)} %get-tuple-element.122, f32[768]{0:T(1024)S(1)} %get-tuple-element.125, f32[768]{0:T(1024)S(1)} %copy-done.29, f32[768]{0:T(1024)S(1)} %copy-done.30), channel_id=1, replica_groups=mesh['dp'=16,'tensor'=2] {'dp'}, use_global_device_ids=true, to_apply=%region_21.24 | all-reduce | flops 3072 | bytes 24576 | tf_op jit(solution)/shard_map/psum | solution.py:177
  1014.2 11.1 %fusion.38 = (bf16[6,512,768]{2,1,0:T(8,128)(2,1)}, bf16[6,512,768]{2,1,0:T(8,128)(2,1)}) fusion(f32[6,512,768]{2,1,0:T(8,128)} %bitcast.190, f32[6,512]{1,0:T(8,128)S(1)} %compare_convert_fusion, pred[6,512]{1,0:T(8,128)(4,1)S(1)} %and_bitcast_fusion, f32[6,512,768]{2,1,0:T(8,128)} %bitcast.189), kind=kLoop, calls=%fused_computation.61 | loop fusion | flops 14155776 | bytes 28326912 | tf_op jit(solution)/shard_map/convert_element_type | solution.py:167
  1025.4 4.2 copy.86
  1030.6 2.4 copy.88
  1034.0 2.2 copy.89
  (214 shorter events, 64.6 us)
Async XLA Ops:
  8.0 264.1 %copy-start = (bf16[768,1536]{1,0:T(8,128)(2,1)S(1)}, bf16[768,1536]{1,0:T(8,128)(2,1)}, u32[]{:S(2)}) copy-start(bf16[768,1536]{1,0:T(8,128)(2,1)} %param.29) | copy-start | bytes 7077892
  8.0 259.0 %all-reduce.8.cloned.1.call-start = ((), (), s32[]{:S(2)}) async-start(), calls=%async_computation | async-start | bytes 9437184 | tf_op jit(solution)/shard_map/psum | solution.py:113
  42.5 39.3 %copy-start.19 = (f32[6,256]{1,0:T(8,128)}, f32[6,256]{1,0:T(8,128)S(1)}, u32[]{:S(2)}) copy-start(f32[6,256]{1,0:T(8,128)S(1)} %broadcast_multiply_fusion.3) | copy-start | bytes 18436
  72.4 9.4 copy-start.26
  72.4 9.4 copy-start.34
  81.8 6.7 copy-start.16
  87.0 1.4 copy-start.14
  137.8 3.4 copy-start.10
  140.3 1.0 copy-start.6
  144.9 290.2 %all-reduce.10.cloned.1.call-start = ((), (), s32[]{:S(2)}) async-start(), calls=%async_computation.1 | async-start | bytes 9437184 | tf_op jit(solution)/shard_map/psum | solution.py:138
  271.4 26.4 %copy-start.2 = (f32[1536,768]{1,0:T(8,128)}, f32[1536,768]{1,0:T(8,128)S(1)}, u32[]{:S(2)}) copy-start(f32[1536,768]{1,0:T(8,128)S(1)} %get-tuple-element.173) | copy-start | bytes 14155780
  271.4 0.7 copy-start.31
  271.4 0.7 copy-start.37
  272.1 25.7 %copy-start.21 = (f32[1536]{0:T(1024)}, f32[1536]{0:T(1024)S(1)}, u32[]{:S(2)}) copy-start(f32[1536]{0:T(1024)S(1)} %multiply_reduce_fusion.5) | copy-start | bytes 18436
  272.1 25.6 %copy-start.23 = (f32[1536]{0:T(1024)}, f32[1536]{0:T(1024)S(1)}, u32[]{:S(2)}) copy-start(f32[1536]{0:T(1024)S(1)} %fusion.50) | copy-start | bytes 18436
  272.1 25.6 %copy-start.12 = (bf16[1536,768]{1,0:T(8,128)(2,1)S(1)}, bf16[1536,768]{1,0:T(8,128)(2,1)}, u32[]{:S(2)}) copy-start(bf16[1536,768]{1,0:T(8,128)(2,1)} %bitcast_convert_fusion) | copy-start | bytes 7077892
  272.1 25.7 %copy-start.36 = (bf16[1536,768]{1,0:T(8,128)(2,1)S(1)}, bf16[1536,768]{1,0:T(8,128)(2,1)}, u32[]{:S(2)}) copy-start(bf16[1536,768]{1,0:T(8,128)(2,1)} %param.30) | copy-start | bytes 7077892
  308.1 2.1 copy-start.39
  315.7 230.4 %sort.19.cloned.1.call-start = ((), (), s32[]{:S(2)}) async-start(), calls=%async_computation.4 | async-start | bytes 98336 | tf_op jit(solution)/shard_map/jit(argsort)/sort | solution.py:94
  316.4 419.8 %all-reduce.14.cloned.1.call-start = ((), (), s32[]{:S(2)}) async-start(), calls=%async_computation.3 | async-start | bytes 18874368 | tf_op jit(solution)/shard_map/psum | solution.py:121
  316.4 118.7 %copy-start.24 = (f32[1536]{0:T(1024)S(1)}, f32[1536]{0:T(1024)}, u32[]{:S(2)}) copy-start(f32[1536]{0:T(1024)} %copy-done.23) | copy-start | bytes 18436
  316.4 118.7 %copy-start.32 = (f32[768]{0:T(1024)S(1)}, f32[768]{0:T(1024)}, u32[]{:S(2)}) copy-start(f32[768]{0:T(1024)} %param.27) | copy-start | bytes 9220
  325.5 115.2 %copy-start.22 = (f32[1536]{0:T(1024)S(1)}, f32[1536]{0:T(1024)}, u32[]{:S(2)}) copy-start(f32[1536]{0:T(1024)} %copy-done.21) | copy-start | bytes 18436
  435.1 5.6 copy-start.5
  435.1 9.5 slice-start.4
  440.7 3.9 slice-start.5
  444.6 2.7 copy-start.11
  445.2 2.2 copy-start.3
  507.0 3.3 copy-start.17
  508.6 1.8 copy-start.8
  515.3 1.7 copy-start.13
  515.3 10.1 copy-start.25
  515.4 10.1 copy-start.33
  515.4 10.1 copy-start.38
  515.4 510.0 %all-reduce.12.cloned.1.call-start = ((), (), s32[]{:S(2)}) async-start(), calls=%async_computation.2 | async-start | bytes 28311552 | tf_op jit(solution)/shard_map/psum | solution.py:177
  525.4 10.3 copy-start.7
  535.7 4.6 copy-start.9
  535.7 4.6 copy-start.15
  545.3 0.7 copy-start.20
  545.3 0.7 copy-start.28
  545.3 2.2 copy-start.35
  545.3 200.1 %slice-start = ((s8[4718592]{0:T(1024)(128)(4,1)}), s8[524288]{0:T(1024)(128)(4,1)S(1)}, s32[]{:S(2)}) async-start(s8[4718592]{0:T(1024)(128)(4,1)} %bitcast.183), calls=%async_computation.6 | async-start | bytes 1048576
  736.2 5.1 copy-start.4
  736.2 5.1 copy-start.27
  736.2 9.3 slice-start.1
  741.3 6.7 slice-start.2
  745.5 2.5 slice-start.3
  851.9 99.1 %copy-start.29 = (f32[768]{0:T(1024)S(1)}, f32[768]{0:T(1024)}, u32[]{:S(2)}) copy-start(f32[768]{0:T(1024)} %get-tuple-element.120) | copy-start | bytes 9220
  851.9 99.1 %copy-start.30 = (f32[768]{0:T(1024)S(1)}, f32[768]{0:T(1024)}, u32[]{:S(2)}) copy-start(f32[768]{0:T(1024)} %get-tuple-element.124) | copy-start | bytes 9220
  1025.4 4.2 copy-start.18
  1025.4 5.2 slice-start.8
  1025.4 5.2 slice-start.9
  1029.6 4.1 slice-start.6
  1030.6 3.5 slice-start.7
  1030.6 5.6 copy-start.1
Sparse Core Ops, SparseCore 0:
  145.0 121.9 all-reduce.7
  315.8 119.2 all-reduce.9
  515.5 220.6 all-reduce.13
  741.2 256.7 all-reduce.11
Sparse Core Ops, SparseCore 1:
  318.6 3.3 sort.21.cloned.1.call-done
  (1 shorter events, 0.0 us)
where the time goes:
time: 1060 us; the launch traced here: 1040 us
  waiting for transfers between devices  415 us (39%)
  local copies, waits for them, and re-layouts  324 us (31%)
  matrix products  148 us (14%)
  other arithmetic  76.3 us (7%)
  blocking collectives  63.2 us (6%)
  between operations  16.2 us (2%)
    psum x1, waiting for transfers between devices, shards(): lax.psum(jnp.dot(activation_low, down_weight, preferred_element_type=jnp....  188 us
    psum x1, waiting for transfers between devices, shards(): lax.psum(jnp.dot(attended_rows, out_weight, preferred_element_type=jnp.fl...  118 us
    psum x1, waiting for transfers between devices, shards(): lax.psum(jnp.dot(grad_pre, up_weight.T, preferred_element_type=jnp.float3...  110 us
    gather x1, local copies, waits for them, and re-layouts, shards(): jnp.take_along_axis(grad_input_rows, slot_of[:, :, None], axis=1)  99.1 us
    gather x2, local copies, waits for them, and re-layouts, shards(): jnp.take_along_axis(result, slot_of[:, :, None], axis=1)  98.9 us
    psum x1, blocking collectives, shards(): lax.psum((grad_qkv, grad_wout, grad_up, grad_down, grad_gain_one, grad_sh...  63.2 us
    gather x1, local copies, waits for them, and re-layouts, shards(): jnp.take_along_axis(cotangent, picked[:, :, None], axis=1)  29.8 us
    gather x2, local copies, waits for them, and re-layouts, shards(): jnp.take_along_axis(patches, picked[:, :, None], axis=1).astype(jnp.float32)  29.8 us
  transfers between devices with their start and end apart: 4, of which 3 were waited for; matrix products, arithmetic and copies ran while one was open for 26% of the time, Pallas kernels for 0%

commit v1 on v0

v1 whole, which is shorter than its diff:
```python
import jax
import jax.numpy as jnp
from jax import lax
from jax.sharding import Mesh, PartitionSpec as P
from jax.experimental import pallas as pl
from jax.experimental.pallas import tpu as pltpu

HD = 64
SLOTS = 256
TILE = 256
norm_eps = 1e-06
masked_score = -1e30
scale = HD ** (-0.5)
f32, bf16 = jnp.float32, jnp.bfloat16


def dot(x, y, dims=((1,), (0,))):
    return lax.dot_general(x, y, (dims, ((), ())), preferred_element_type=f32)


NT = ((1,), (1,))
TN = ((0,), (0,))


def rows_of(counts, samples):
    starts, total = [], 0
    for s in range(samples):
        starts.append(total)
        total = total + ((counts[s] + 15) // 16) * 16
    return starts, total


def win(start, size=SLOTS):
    if not isinstance(start, int):
        start = pl.multiple_of(start, 16)
    return pl.ds(start, size)


def start_of(counts, s):
    return lax.fori_loop(0, s, lambda i, t: t + ((counts[i] + 15) // 16) * 16, 0)


def total_of(counts, samples):
    return start_of(counts, samples)


def normed(values):
    center = values - jnp.mean(values, axis=-1, keepdims=True)
    spread = jnp.mean(center * center, axis=-1, keepdims=True)
    inv = lax.rsqrt(spread + norm_eps)
    return center * inv, inv


def norm_back(grad, hat, inv, gain):
    g = grad * gain
    return inv * (g - jnp.mean(g, axis=-1, keepdims=True) - hat * jnp.mean(g * hat, axis=-1, keepdims=True))


def lane_halves():
    lane = lax.broadcasted_iota(jnp.int32, (1, 128), 1)
    return lane < HD


def attend_rows(counts, qkv, out, lse, samples, width):
    left = lane_halves()
    row = lax.broadcasted_iota(jnp.int32, (SLOTS, 1), 0)

    def one(s, start):
        rows = win(start)
        live = row < counts[s]
        for pair in range(width // 128):
            lo = pair * 128
            q = qkv[rows, lo:lo + 128]
            k = qkv[rows, width + lo:width + lo + 128]
            v = qkv[rows, 2 * width + lo:2 * width + lo + 128]
            parts = []
            for side in range(2):
                keep = left if side == 0 else ~left
                sc = dot(jnp.where(keep, k, jnp.zeros_like(k)), q, NT) * scale
                sc = jnp.where(live, sc, masked_score)
                top = jnp.max(sc, axis=0, keepdims=True)
                w = jnp.exp(sc - top)
                tot = jnp.sum(w, axis=0, keepdims=True)
                lse[s, 2 * pair + side:2 * pair + side + 1, :] = top + jnp.log(tot)
                p = (w * (1.0 / tot)).astype(bf16)
                parts.append(dot(p, v, TN))
            out[rows, lo:lo + 128] = jnp.where(left, parts[0], parts[1]).astype(bf16)
        return start + ((counts[s] + 15) // 16) * 16

    lax.fori_loop(0, samples, one, 0)


def tiles(total):
    return (total + TILE - 1) // TILE


def fwd_own_body(samples, width):
    def body(counts, col, patches, cot, gain, shift, weight, h, dm, a, qkv, o, lse):
        s = pl.program_id(0)
        start = start_of(counts, s)
        pick = col[0, :SLOTS, :]
        row = lax.broadcasted_iota(jnp.int32, (SLOTS, 1), 0)
        pick = jnp.where(row < counts[s], pick, -1)
        hot = (lax.broadcasted_iota(jnp.int32, (SLOTS, patches.shape[1]), 1) == pick).astype(f32).astype(bf16)
        h[win(start), :] = dot(hot, patches[0]).astype(bf16)
        dm[win(start), :] = dot(hot, cot[0]).astype(bf16)

        @pl.when(s == samples - 1)
        def _():
            total = total_of(counts, samples)
            zeros = jnp.zeros((TILE, h.shape[1]), bf16)
            h[win(total), :] = zeros
            dm[win(total), :] = zeros

            def tile(i, c):
                r = win(i * TILE)
                hat, _ = normed(h[r, :].astype(f32))
                av = (hat * gain[...] + shift[...]).astype(bf16)
                a[r, :] = av
                qkv[r, :] = dot(av, weight[...]).astype(bf16)
                return c

            n = tiles(total)
            lax.fori_loop(0, n, tile, 0)
            qkv[win(n * TILE), :] = jnp.zeros((TILE, qkv.shape[1]), bf16)
            attend_rows(counts, qkv, o, lse, samples, width)
    return body


def fwd_other_body(samples, width):
    def body(counts, a, h, o, weight, out_own, out_other, gain, shift, qkv, o2, lse, r, c):
        total = total_of(counts, samples)
        n = tiles(total)

        def tile(i, x):
            rr = win(i * TILE)
            qkv[rr, :] = dot(a[rr, :], weight[...]).astype(bf16)
            return x

        lax.fori_loop(0, n, tile, 0)
        qkv[win(n * TILE), :] = jnp.zeros((TILE, qkv.shape[1]), bf16)
        attend_rows(counts, qkv, o2, lse, samples, width)

        def tail(i, x):
            rr = win(i * TILE)
            z = dot(o[rr, :], out_own[...]) + dot(o2[rr, :], out_other[...])
            rv = h[rr, :].astype(f32) + z
            r[rr, :] = rv
            hat, _ = normed(rv)
            c[rr, :] = (hat * gain[...] + shift[...]).astype(bf16)
            return x

        lax.fori_loop(0, n, tail, 0)
    return body


def gelu_both(u):
    cdf = 0.5 * (1.0 + lax.erf(u * (0.5 ** 0.5)))
    pdf = jnp.exp(-0.5 * u * u) * (0.5 / jnp.pi) ** 0.5
    return u * cdf, cdf + u * pdf


def mlp_tile(cv, dv, up, down):
    u = dot(cv, up[...])
    e, slope = gelu_both(u)
    e = e.astype(bf16)
    m = dot(e, down[...])
    de = dot(dv, down[...], NT)
    du = (de * slope).astype(bf16)
    dc = dot(du, up[...], NT)
    return e, du, m, dc


def mlp_own_body(samples):
    def body(counts, c, dm, up, down, m, dc, gup, gdown):
        n = tiles(total_of(counts, samples))
        gup[...] = jnp.zeros(gup.shape, f32)
        gdown[...] = jnp.zeros(gdown.shape, f32)

        def tile(i, x):
            r = win(i * TILE)
            cv, dv = c[r, :], dm[r, :]
            e, du, mv, dcv = mlp_tile(cv, dv, up, down)
            m[r, :] = mv
            dc[r, :] = dcv
            gdown[...] += dot(e, dv, TN)
            gup[...] += dot(cv, du, TN)
            return x

        lax.fori_loop(0, n, tile, 0)
    return body


def hot_back(counts, line, s, patches):
    live = lax.broadcasted_iota(jnp.int32, (1, SLOTS), 1) < counts[s]
    pick = jnp.where(live, line[s, :, :SLOTS], -1)
    return (lax.broadcasted_iota(jnp.int32, (patches, SLOTS), 0) == pick).astype(f32).astype(bf16)


def mlp_other_body(samples, patches):
    def body(counts, line, c, dm, up, down, m, dc, r, gain, out, dr, g2, y):
        n = tiles(total_of(counts, samples))
        g2[...] = jnp.zeros(g2.shape, f32)

        def tile(i, x):
            rr = win(i * TILE)
            cv, dv = c[rr, :], dm[rr, :]
            _, _, mv, dcv = mlp_tile(cv, dv, up, down)
            rv = r[rr, :]
            y[rr, :] = (rv + (m[rr, :] + mv)).astype(bf16)
            dct = dc[rr, :] + dcv
            hat, inv = normed(rv)
            g2[0:1, :] += jnp.sum(dct * hat, axis=0, keepdims=True)
            g2[1:2, :] += jnp.sum(dct, axis=0, keepdims=True)
            dr[rr, :] = dv.astype(f32) + norm_back(dct, hat, inv, gain[...])
            return x

        lax.fori_loop(0, n, tile, 0)
        y[win(n * TILE), :] = jnp.zeros((TILE, y.shape[1]), bf16)

        def scatter(s, start):
            out[s] = dot(hot_back(counts, line, s, patches), y[win(start), :]).astype(bf16)
            return start + ((counts[s] + 15) // 16) * 16

        lax.fori_loop(0, samples, scatter, 0)
    return body


def attend_back(counts, qkv, do, lse, dqkv, samples, width):
    left = lane_halves()
    row = lax.broadcasted_iota(jnp.int32, (SLOTS, 1), 0)

    def one(s, start):
        rows = win(start)
        live = row < counts[s]
        for pair in range(width // 128):
            lo = pair * 128
            q = qkv[rows, lo:lo + 128]
            k = qkv[rows, width + lo:width + lo + 128]
            v = qkv[rows, 2 * width + lo:2 * width + lo + 128]
            dov = do[rows, lo:lo + 128]
            dov = jnp.where(live, dov, jnp.zeros_like(dov))
            zero = jnp.zeros_like(k)
            dq, dk, dvv = [], [], []
            for side in range(2):
                keep = left if side == 0 else ~left
                sc = dot(jnp.where(keep, k, zero), q, NT) * scale
                sc = jnp.where(live, sc, masked_score)
                p = jnp.exp(sc - lse[s, 2 * pair + side:2 * pair + side + 1, :])
                dp = dot(jnp.where(keep, v, zero), dov, NT)
                t = jnp.sum(p * dp, axis=0, keepdims=True)
                ds = (p * (dp - t)).astype(bf16)
                dq.append(dot(ds, k, TN))
                dk.append(dot(ds, q))
                dvv.append(dot(p.astype(bf16), dov))
            dqkv[rows, lo:lo + 128] = (jnp.where(left, dq[0], dq[1]) * scale).astype(bf16)
            dqkv[rows, width + lo:width + lo + 128] = (jnp.where(left, dk[0], dk[1]) * scale).astype(bf16)
            dqkv[rows, 2 * width + lo:2 * width + lo + 128] = jnp.where(left, dvv[0], dvv[1]).astype(bf16)
        return start + ((counts[s] + 15) // 16) * 16

    lax.fori_loop(0, samples, one, 0)


def attn_own_body(samples, width):
    def body(counts, dr, qkv, lse, o, a, wout, wqkv, da, gout, gqkv, do, dqkv):
        total = total_of(counts, samples)
        n = tiles(total)
        gout[...] = jnp.zeros(gout.shape, f32)
        gqkv[...] = jnp.zeros(gqkv.shape, f32)

        def first(i, x):
            r = win(i * TILE)
            dz = dr[r, :].astype(bf16)
            do[r, :] = dot(dz, wout[...], NT).astype(bf16)
            gout[...] += dot(o[r, :], dz, TN)
            return x

        lax.fori_loop(0, n, first, 0)
        attend_back(counts, qkv, do, lse, dqkv, samples, width)
        dqkv[win(total), :] = jnp.zeros((TILE, dqkv.shape[1]), bf16)

        def last(i, x):
            r = win(i * TILE)
            dv = dqkv[r, :]
            da[r, :] = dot(dv, wqkv[...], NT)
            gqkv[...] += dot(a[r, :], dv, TN)
            return x

        lax.fori_loop(0, n, last, 0)
    return body


def attn_other_body(samples, width, patches):
    def body(counts, line, dr, qkv, lse, wout, wqkv, da, h, gain, out, g1, do, dqkv, dh):
        total = total_of(counts, samples)
        n = tiles(total)
        g1[...] = jnp.zeros(g1.shape, f32)

        def first(i, x):
            r = win(i * TILE)
            do[r, :] = dot(dr[r, :].astype(bf16), wout[...], NT).astype(bf16)
            return x

        lax.fori_loop(0, n, first, 0)
        attend_back(counts, qkv, do, lse, dqkv, samples, width)
        dqkv[win(total), :] = jnp.zeros((TILE, dqkv.shape[1]), bf16)

        def last(i, x):
            r = win(i * TILE)
            dat = da[r, :] + dot(dqkv[r, :], wqkv[...], NT)
            hat, inv = normed(h[r, :].astype(f32))
            g1[0:1, :] += jnp.sum(dat * hat, axis=0, keepdims=True)
            g1[1:2, :] += jnp.sum(dat, axis=0, keepdims=True)
            dh[r, :] = (dr[r, :] + norm_back(dat, hat, inv, gain[...])).astype(bf16)
            return x

        lax.fori_loop(0, n, last, 0)
        dh[win(n * TILE), :] = jnp.zeros((TILE, dh.shape[1]), bf16)

        def scatter(s, start):
            out[s] = dot(hot_back(counts, line, s, patches), dh[win(start), :]).astype(bf16)
            return start + ((counts[s] + 15) // 16) * 16

        lax.fori_loop(0, samples, scatter, 0)
    return body


def sds(shape, dtype):
    return jax.ShapeDtypeStruct(shape, dtype)


def call(body, name, counts, args, outs, scratch=(), flops=0):
    moved = sum(x.size * x.dtype.itemsize for x in list(args) + list(outs))
    return pl.pallas_call(
        body,
        name=name,
        out_shape=list(outs),
        grid_spec=pltpu.PrefetchScalarGridSpec(
            num_scalar_prefetch=1,
            grid=(1,),
            in_specs=[pl.BlockSpec(x.shape, lambda i, n, d=x.ndim: (0,) * d, pipeline_mode=pl.Buffered(1)) for x in args],
            out_specs=[pl.BlockSpec(x.shape, lambda i, n, d=len(x.shape): (0,) * d, pipeline_mode=pl.Buffered(1)) for x in outs],
            scratch_shapes=list(scratch),
        ),
        compiler_params=pltpu.CompilerParams(vmem_limit_bytes=62 << 20),
        cost_estimate=pl.CostEstimate(flops=flops, transcendentals=0, bytes_accessed=moved),
    )(counts, *args)


def fwd_own(counts, col, patches, cot, gain, shift, weight):
    S, L, D = patches.shape
    width = weight.shape[1] // 3
    TP = S * SLOTS + TILE
    whole = lambda d: (lambda s, n: (0,) * d)
    one = lambda s, n: (s, 0, 0)
    B1 = pl.Buffered(1)
    outs = [sds((TP, D), bf16), sds((TP, D), bf16), sds((TP, D), bf16), sds((TP, 3 * width), bf16), sds((TP, width), bf16), sds((S, width // HD, SLOTS), f32)]
    return pl.pallas_call(
        fwd_own_body(S, width),
        name="fwd_own",
        out_shape=outs,
        grid_spec=pltpu.PrefetchScalarGridSpec(
            num_scalar_prefetch=1,
            grid=(S,),
            in_specs=[
                pl.BlockSpec((1, L, 1), one),
                pl.BlockSpec((1, L, D), one),
                pl.BlockSpec((1, L, D), one),
                pl.BlockSpec((1, D), whole(2)),
                pl.BlockSpec((1, D), whole(2)),
                pl.BlockSpec(weight.shape, whole(2), pipeline_mode=B1),
            ],
            out_specs=[pl.BlockSpec(x.shape, whole(len(x.shape)), pipeline_mode=B1) for x in outs],
        ),
        compiler_params=pltpu.CompilerParams(vmem_limit_bytes=62 << 20),
        cost_estimate=pl.CostEstimate(flops=6 * 10**9, transcendentals=0, bytes_accessed=25 << 20),
    )(counts, col, patches, cot, gain, shift, weight)


def fwd_other(counts, a, h, o, weight, out_own, out_other, gain, shift, S):
    TP, D = a.shape
    width = weight.shape[1] // 3
    outs = [sds((TP, 3 * width), bf16), sds((TP, width), bf16), sds((S, width // HD, SLOTS), f32), sds((TP, D), f32), sds((TP, D), bf16)]
    return call(fwd_other_body(S, width), "fwd_other", counts, [a, h, o, weight, out_own, out_other, gain, shift], outs, flops=7 * 10**9)


def mlp_own(counts, c, dm, up, down, S):
    TP, D = c.shape
    outs = [sds((TP, D), f32), sds((TP, D), f32), sds(up.shape, f32), sds(down.shape, f32)]
    return call(mlp_own_body(S), "mlp_own", counts, [c, dm, up, down], outs, flops=18 * 10**9)


def mlp_other(counts, line, c, dm, up, down, m, dc, r, gain, S, L):
    TP, D = c.shape
    outs = [sds((S, L, D), bf16), sds((TP, D), f32), sds((8, D), f32)]
    return call(mlp_other_body(S, L), "mlp_other", counts, [line, c, dm, up, down, m, dc, r, gain], outs, [pltpu.VMEM((TP, D), bf16)], flops=12 * 10**9)


def attn_own(counts, dr, qkv, lse, o, a, wout, wqkv, S):
    TP, D = a.shape
    width = wout.shape[0]
    outs = [sds((TP, D), f32), sds(wout.shape, f32), sds(wqkv.shape, f32)]
    return call(attn_own_body(S, width), "attn_own", counts, [dr, qkv, lse, o, a, wout, wqkv], outs, [pltpu.VMEM((TP, width), bf16), pltpu.VMEM((TP, 3 * width), bf16)], flops=9 * 10**9)


def attn_other(counts, line, dr, qkv, lse, wout, wqkv, da, h, gain, S, L):
    TP, D = h.shape
    width = wout.shape[0]
    outs = [sds((S, L, D), bf16), sds((8, D), f32)]
    return call(attn_other_body(S, width, L), "attn_other", counts, [line, dr, qkv, lse, wout, wqkv, da, h, gain], outs, [pltpu.VMEM((TP, width), bf16), pltpu.VMEM((TP, 3 * width), bf16), pltpu.VMEM((TP, D), bf16)], flops=8 * 10**9)


def local(patches, counts, visible, g1, b1, g2, b2, cot, wq0, wo0, wu0, wd0, rest):
    S, L, D = patches.shape
    col, line = visible[:, :, None], visible[:, None, :]
    g1, b1, g2, b2 = (x[None, :] for x in (g1, b1, g2, b2))
    h, dm, a, qkv0, o0, lse0 = fwd_own(counts, col, patches, cot, g1, b1, wq0)
    wq1, wo1, wu1, wd1 = rest
    qkv1, o1, lse1, r, c = fwd_other(counts, a, h, o0, wq1, wo0, wo1, g2, b2, S)
    m, dc, gup, gdown = mlp_own(counts, c, dm, wu0, wd0, S)
    out, dr, gg2 = mlp_other(counts, line, c, dm, wu1, wd1, m, dc, r, g2, S, L)
    da, gout, gqkv = attn_own(counts, dr, qkv0, lse0, o0, a, wo0, wq0, S)
    gin, gg1 = attn_other(counts, line, dr, qkv1, lse1, wo1, wq1, da, h, g1, S, L)
    return out, gin, gg1, gqkv, gout, gg2, gup, gdown


def swap(x, axis, size, bit):
    return lax.ppermute(x, axis, [(k, k ^ bit) for k in range(size)])


def cast_pieces(order, pieces):
    rows, cols = pieces[0].shape

    def body(where, *refs):
        for i in range(4):
            refs[4][pl.ds(pl.multiple_of(where[i] * rows, 16), rows), :] = refs[i][...].astype(bf16)

    return call(body, "cast_pieces", order, pieces, [sds((4 * rows, cols), bf16)])[0]


def fetch(weight, dp):
    me = lax.axis_index("dp") % 4
    rows = weight.shape[0] // 4
    part = lax.dynamic_slice_in_dim(weight, me * rows, rows, 0).astype(f32)
    first = swap(part, "tensor", 2, 1)
    across = swap(first, "dp", dp, 2)
    order = jnp.stack([me, me ^ 2, me ^ 1, me ^ 3]).astype(jnp.int32)
    return cast_pieces(order, [first, across, swap(first, "dp", dp, 1), swap(across, "dp", dp, 1)])


def shards(dp, patches, counts, visible, g1, b1, wq, wo, g2, b2, wu, wd, cot):
    D = patches.shape[2]
    wq = wq.reshape(D, -1)
    rest = tuple(fetch(w, dp) for w in (wq, wo, wu, wd))
    out, gin, gg1, gqkv, gout, gg2, gup, gdown = local(patches, counts, visible, g1, b1, g2, b2, cot, wq, wo, wu, wd, rest)
    gup, gdown = lax.psum((gup, gdown), "dp")
    gqkv, gout, gg1, gg2 = lax.psum((gqkv, gout, gg1, gg2), "dp")
    return (out, gin, gg1[0], gg1[1], gqkv.reshape(D, 3, -1), gout, gg2[0], gg2[1], gup, gdown)


def solution(mesh):
    dp = mesh.shape["dp"]
    placed = (P("dp", None, None), P("dp"), P("dp", None), P(), P(), P(None, None, "tensor"), P("tensor", None), P(), P(), P(None, "tensor"), P("tensor", None), P("dp", None, None))
    outs = (P("dp", None, None), P("dp", None, None), P(), P(), P(None, None, "tensor"), P("tensor", None), P(), P(), P(None, "tensor"), P("tensor", None))
    return jax.shard_map(lambda *a: shards(dp, *a), mesh=mesh, in_specs=placed, out_specs=outs, check_vma=False)
```

time: 1060 us -> 610 us (0.58); the launches traced: 1040 us -> 613 us
  local copies, waits for them, and re-layouts: 324 us -> 28.1 us
  Pallas kernels: 0 us -> 213 us
  matrix products: 148 us -> 0 us
  waiting for transfers between devices: 415 us -> 276 us
  other arithmetic: 76.3 us -> 5.86 us
  starting transfers between devices: 0.84 us -> 14 us
    psum x4 -> x1, waiting for transfers between devices: 415 us -> 156 us  [shards(): gqkv, gout, gg1, gg2 = lax.psum((gqkv, gout, gg1, gg2), 'dp')]
    gather x6 -> x0, local copies, waits for them, and re-layouts: 258 us -> none  [the longest x1 99.1 us: shards(): jnp.take_along_axis(grad_input_rows, slot_of[:, :, None], axis=1)]
    pallas_call x0 -> x10, Pallas kernels: none -> 213 us  [the longest x9 187 us: call(): pl.pallas_call(body, name=name, out_shape=list(outs), grid_spec=pltpu.Pre...]
    dot_general x54 -> x0, matrix products: 148 us -> none  [the longest x1 25.6 us: shards(): pre_act = jnp.dot(normed_two, up_weight, preferred_element_type=jnp.float32)]
    ppermute x0 -> x16, waiting for transfers between devices: none -> 120 us  [swap(): return lax.ppermute(x, axis, [(k, k ^ bit) for k in range(size)])]
    reduce_sum x13 -> x0, other arithmetic: 24.6 us -> none  [the longest x4 12.9 us: layer_norm(): center = values - jnp.mean(values, axis=-1, keepdims=True)]
    mul x3 -> x0, other arithmetic: 14.6 us -> none  [the longest x1 5.24 us: shards(): jnp.take_along_axis(patches, picked[:, :, None], axis=1).astype(jnp.float32)]
    ppermute x0 -> x16, starting transfers between devices: none -> 14 us  [swap(): return lax.ppermute(x, axis, [(k, k ^ bit) for k in range(size)])]
  transfers between devices with their start and end apart: 4 -> 17, of which waited for: 3 -> 4; matrix products, arithmetic and copies ran while one was open for 26% -> 2% of each run, Pallas kernels for 0% -> 22%
where the time goes in v1:
time: 610 us; the launch traced here: 613 us
  waiting for transfers between devices  276 us (45%)
  Pallas kernels  213 us (35%)
  blocking collectives  60.9 us (10%)
  local copies, waits for them, and re-layouts  28.1 us (5%)
  between operations  14.2 us (2%)
  starting transfers between devices  14 us (2%)
    pallas_call x9, Pallas kernels, call(): pl.pallas_call(body, name=name, out_shape=list(outs), grid_spec=pltpu.Pre...  187 us
    psum x1, waiting for transfers between devices, shards(): gqkv, gout, gg1, gg2 = lax.psum((gqkv, gout, gg1, gg2), 'dp')  156 us
    ppermute x16, waiting for transfers between devices, swap(): return lax.ppermute(x, axis, [(k, k ^ bit) for k in range(size)])  120 us
    psum x1, blocking collectives, shards(): gqkv, gout, gg1, gg2 = lax.psum((gqkv, gout, gg1, gg2), 'dp')  60.9 us
    pallas_call x1, Pallas kernels, fwd_own(): pl.pallas_call(fwd_own_body(S, width), name='fwd_own', out_shape=outs, gr...  27 us
    unnamed x31, local copies, waits for them, and re-layouts  16.6 us
    ppermute x16, starting transfers between devices, swap(): return lax.ppermute(x, axis, [(k, k ^ bit) for k in range(size)])  14 us
  transfers between devices with their start and end apart: 17, of which 4 were waited for; matrix products, arithmetic and copies ran while one was open for 2% of the time, Pallas kernels for 22%

profile of v1, /device:TPU:0, one launch (start us, length us, event | category | flops | bytes accessed | tf_op | source)
XLA Modules:
  0.0 612.5 jit_solution(13125355965077044232)
XLA Ops:
  7.2 0.0 all-reduce.4.cloned.1.call-start
  7.2 2.6 copy.24
  9.9 1.0 copy.26.weight.wqkv
  10.9 0.0 copy-start.7
  11.0 0.0 copy-start.8
  11.0 0.0 copy-start.5
  11.0 1.0 dynamic-slice_convert_fusion.2
  12.0 3.0 collective-permute-start
  15.0 1.2 dynamic-slice_convert_fusion.1
  16.1 0.1 collective-permute-start.8
  16.2 2.2 dynamic-slice_convert_fusion
  18.4 2.0 collective-permute-start.12
  20.4 15.4 %collective-permute-done.refs_0_ = f32[192,1152]{1,0:T(8,128)} collective-permute-done((f32[192,1152]{1,0:T(8,128)}, f32[192,1152]{1,0:T(8,128)}, u32[]{:S(2)}, u32[]{:S(2)}) %collective-permute-start) | collective-permute-done | bytes 884768 | tf_op jit(solution)/shard_map/ppermute | solution.py:428
  35.8 2.0 collective-permute-start.1
  37.8 0.9 dynamic-slice_convert_fusion.3
  38.7 1.6 collective-permute-start.4
  40.3 51.4 %collective-permute-done.4.refs_0_ = f32[96,768]{1,0:T(8,128)S(1)} collective-permute-done((f32[96,768]{1,0:T(8,128)S(1)}, f32[96,768]{1,0:T(8,128)S(1)}, u32[]{:S(2)}, u32[]{:S(2)}) %collective-permute-start.4) | collective-permute-done | bytes 294944 | tf_op jit(solution)/shard_map/ppermute | solution.py:428
  91.7 0.0 collective-permute-start.6
  91.7 0.0 collective-permute-done.8.refs_0_
  91.7 1.8 collective-permute-start.9
  93.5 0.0 collective-permute-done.12.refs_0_
  93.5 0.3 collective-permute-start.13
  93.8 1.7 collective-permute-start.5
  95.5 0.0 collective-permute-done.6.refs_2_
  95.5 0.0 collective-permute-done.1.refs_1_
  95.5 0.5 collective-permute-start.3
  96.0 0.6 broadcast_in_dim.20.gain
  96.6 0.6 broadcast_in_dim.21.shift
  97.2 1.7 copy.25.col
  98.9 53.1 %collective-permute-done.5.refs_1_ = f32[96,768]{1,0:T(8,128)} collective-permute-done((f32[96,768]{1,0:T(8,128)S(1)}, f32[96,768]{1,0:T(8,128)}, u32[]{:S(2)}, u32[]{:S(2)}) %collective-permute-start.5) | collective-permute-done | bytes 294944 | tf_op jit(solution)/shard_map/ppermute | solution.py:428
  152.0 0.0 collective-permute-start.7
  152.0 27.0 %fwd_own.1 = (bf16[1792,768]{1,0:T(8,128)(2,1)}, bf16[1792,768]{1,0:T(8,128)(2,1)}, bf16[1792,768]{1,0:T(8,128)(2,1)}, bf16[1792,1152]{1,0:T(8,128)(2,1)}, bf16[...) custom-call(s32[6]{0:T(128)} %counts.11, s32[6,512,1]{2,1,0:T(8,128)} %copy.25.col, bf16[6,512,768]{2,1,0:T(8,128)(2,1)} %patches.1, ...), custom_call_target="tpu_custom_call" | custom-call | flops 6000000000 | bytes 26214400 | tf_op jit(solution)/shard_map/fwd_own/pallas_call | solution.py:358
  179.0 0.6 broadcast_in_dim.18.line
  179.6 0.6 broadcast_in_dim.22.gain
  180.2 0.6 broadcast_in_dim.23.shift
  180.8 0.6 pad_add_fusion.where
  181.4 2.8 cast_pieces.5.out_other.wout
  184.2 0.0 collective-permute-start.10
  184.2 0.0 collective-permute-done.2.refs_2_
  184.2 0.5 collective-permute-start.14
  184.7 0.0 collective-permute-done.9.refs_1_
  184.7 0.1 collective-permute-start.11
  184.7 0.0 collective-permute-done.13.refs_1_
  184.7 0.4 collective-permute-start.15
  185.2 0.0 collective-permute-done.3.refs_3_
  185.2 4.0 cast_pieces.4.weight.wqkv
  189.2 26.2 %fwd_other.1 = (bf16[1792,1152]{1,0:T(8,128)(2,1)}, bf16[1792,384]{1,0:T(8,128)(2,1)}, f32[6,6,256]{2,1,0:T(8,128)}, f32[1792,768]{1,0:T(8,128)}, bf16[1792,768]{1,0:T(8,128)(2,1)}) custom-call(s32[6]{0:T(128)} %counts.11, bf16[1792,768]{1,0:T(8,128)(2,1)} %get-tuple-element.32.a, bf16[1792,768]{1,0:T(8,128)(2,1)} %get-tuple-element.33.h, ...), custom_call_target="tpu_custom_call" | custom-call | flops 7000000000 | bytes 23635968 | tf_op jit(solution)/shard_map/fwd_other/pallas_call | solution.py:334
  215.4 36.0 %mlp_own.1 = (f32[1792,768]{1,0:T(8,128)}, f32[1792,768]{1,0:T(8,128)}, f32[768,1536]{1,0:T(8,128)}, f32[1536,768]{1,0:T(8,128)}) custom-call(s32[6]{0:T(128)} %counts.11, bf16[1792,768]{1,0:T(8,128)(2,1)} %get-tuple-element.35.c, bf16[1792,768]{1,0:T(8,128)(2,1)} %get-tuple-element.36.dm, bf16[768,1536]{1,0:T(8,128)(2,1)} %up.1, bf16[1536,768]{1,0:T(8,128)(2,1)} %down.1), custom_call_target="tpu_custom_call" | custom-call | flops 17999998976 | bytes 30670848 | tf_op jit(solution)/shard_map/mlp_own/pallas_call | solution.py:334
  251.4 0.0 collective-permute-done.10.refs_2_
  251.4 4.6 cast_pieces.6.up
  256.0 0.0 collective-permute-done.15.refs_3_
  256.0 4.6 cast_pieces.7.down
  260.7 35.0 %mlp_other.1 = (bf16[6,512,768]{2,1,0:T(8,128)(2,1)}, f32[1792,768]{1,0:T(8,128)}, f32[8,768]{1,0:T(8,128)}) custom-call(s32[6]{0:T(128)} %counts.11, s32[6,1,512]{2,1,0:T(1,128)} %broadcast_in_dim.18.line, bf16[1792,768]{1,0:T(8,128)(2,1)} %get-tuple-element.35.c, bf16[1792,768]{1,0:T(8,128)(2,1)} %get-tuple-element.36.dm, ...), custom_call_target="tpu_custom_call" | custom-call | flops 12000000000 | bytes 37002240 | tf_op jit(solution)/shard_map/mlp_other/pallas_call | solution.py:334
  295.6 36.4 %attn_own.1 = (f32[1792,768]{1,0:T(8,128)}, f32[384,768]{1,0:T(8,128)}, f32[768,1152]{1,0:T(8,128)}) custom-call(s32[6]{0:T(128)} %counts.11, f32[1792,768]{1,0:T(8,128)} %get-tuple-element.41.dr, bf16[1792,1152]{1,0:T(8,128)(2,1)} %get-tuple-element.44.qkv, f32[6,6,256]{2,1,0:T(8,128)} %get-tuple-element.45.lse, bf16[1792,384]{1,0:T(8,128)(2,1)} %get-tuple-element.34.o, ...), custom_call_target="tpu_custom_call" | custom-call | flops 8999999488 | bytes 26382336 | tf_op jit(solution)/shard_map/attn_own/pallas_call | solution.py:334
  332.0 5.2 copy.29
  337.2 0.0 all-reduce.4.cloned.1.call-update
  337.2 36.9 %attn_other.1 = (bf16[6,512,768]{2,1,0:T(8,128)(2,1)}, f32[8,768]{1,0:T(8,128)}) custom-call(s32[6]{0:T(128)} %counts.11, s32[6,1,512]{2,1,0:T(1,128)} %broadcast_in_dim.18.line, f32[1792,768]{1,0:T(8,128)} %get-tuple-element.41.dr, bf16[1792,1152]{1,0:T(8,128)(2,1)} %get-tuple-element.42.qkv, f32[6,6,256]{2,1,0:T(8,128)} %get-tuple-element.43.lse, ...), custom_call_target="tpu_custom_call" | custom-call | flops 8000000000 | bytes 25046016 | tf_op jit(solution)/shard_map/attn_other/pallas_call | solution.py:334
  374.2 60.9 %all-reduce = (f32[8,768]{1,0:T(8,128)S(1)}, f32[8,768]{1,0:T(8,128)S(1)}) all-reduce(f32[8,768]{1,0:T(8,128)} %get-tuple-element.48, f32[8,768]{1,0:T(8,128)S(1)} %copy-done.6), channel_id=1, replica_groups=mesh['dp'=16,'tensor'=2] {'dp'}, use_global_device_ids=true, to_apply=%region_0.1 | all-reduce | flops 12288 | bytes 98304 | tf_op jit(solution)/shard_map/psum | solution.py:457
  435.1 0.6 slice_reduce_fusion
  435.7 156.0 %all-reduce.4.cloned.1.call-done = (f32[768,3,384]{0,2,1:T(8,128)}, f32[384,768]{1,0:T(8,128)}, f32[768,1536]{1,0:T(8,128)}, f32[1536,768]{1,0:T(8,128)}) async-done(((f32[768,3,384]{0,2,1:T(8,128)}, f32[384,768]{1,0:T(8,128)}, f32[768,1536]{1,0:T(8,128)}, f32[1536,768]{1,0:T(8,128)}), (f32[768,3,384]{0,2,1:T(8,128)}, f32[384,768]{1,0:T(8,128)}, f32[768,1536]{1,0:T(8,128)}, ...) | async-done | bytes 14155792 | tf_op jit(solution)/shard_map/psum | solution.py:457
  591.7 5.2 copy.30
  597.0 1.0 copy.35
  598.0 5.5 copy.36
  603.5 2.2 copy.37
  (28 shorter events, 0.1 us)
Async XLA Ops:
  7.2 584.5 %all-reduce.4.cloned.1.call-start = ((), (), s32[]{:S(2)}) async-start(), calls=%async_computation | async-start | bytes 28311552 | tf_op jit(solution)/shard_map/psum | solution.py:457
  10.9 7.5 %copy-start = (bf16[768,1152]{1,0:T(8,128)(2,1)}, bf16[768,1152]{1,0:T(8,128)(2,1)S(1)}, u32[]{:S(2)}) copy-start(bf16[768,1152]{1,0:T(8,128)(2,1)S(1)} %copy.26.weight.wqkv) | copy-start | bytes 5308420
  10.9 85.1 %copy-start.7 = (f32[768]{0:T(1024)S(1)}, f32[768]{0:T(1024)}, u32[]{:S(2)}) copy-start(f32[768]{0:T(1024)} %param.15) | copy-start | bytes 9220
  11.0 85.7 %copy-start.8 = (f32[768]{0:T(1024)S(1)}, f32[768]{0:T(1024)}, u32[]{:S(2)}) copy-start(f32[768]{0:T(1024)} %param.16) | copy-start | bytes 9220
  11.0 86.2 %copy-start.5 = (s32[6,512]{1,0:T(8,128)S(1)}, s32[6,512]{1,0:T(8,128)}, u32[]{:S(2)}) copy-start(s32[6,512]{1,0:T(8,128)} %param.14) | copy-start | bytes 36868
  12.0 23.8 %collective-permute-start = (f32[192,1152]{1,0:T(8,128)}, f32[192,1152]{1,0:T(8,128)}, u32[]{:S(2)}, u32[]{:S(2)}) collective-permute-start(f32[192,1152]{1,0:T(8,128)} %dynamic-slice_convert_fusion.2), channel_id=1, source_target_pairs={{0,1},{1,0},{2,3},{3,2},{4,5},{5,4},{6,7},{7,6},{8,9},{9,8},{10,11... | collective-permute-start | bytes 2654216 | tf_op jit(solution)/shard_map/ppermute | solution.py:428
  16.1 75.5 %collective-permute-start.8 = (f32[192,1536]{1,0:T(8,128)S(1)}, f32[192,1536]{1,0:T(8,128)}, u32[]{:S(2)}, u32[]{:S(2)}) collective-permute-start(f32[192,1536]{1,0:T(8,128)S(1)} %dynamic-slice_convert_fusion.1), channel_id=1, source_target_pairs={{0,1},{1,0},{2,3},{3,2},{4,5},{5,4},{6,7},{7,6},{8,9},{9,8},{10,11... | collective-permute-start | bytes 3538952 | tf_op jit(solution)/shard_map/ppermute | solution.py:428
  18.4 75.1 %collective-permute-start.12 = (f32[384,768]{1,0:T(8,128)}, f32[384,768]{1,0:T(8,128)}, u32[]{:S(2)}, u32[]{:S(2)}) collective-permute-start(f32[384,768]{1,0:T(8,128)} %dynamic-slice_convert_fusion), channel_id=1, source_target_pairs={{0,1},{1,0},{2,3},{3,2},{4,5},{5,4},{6,7},{7,6},{8,9},{9,8},{10,11... | collective-permute-start | bytes 3538952 | tf_op jit(solution)/shard_map/ppermute | solution.py:428
  35.8 59.8 %collective-permute-start.1 = (f32[192,1152]{1,0:T(8,128)}, f32[192,1152]{1,0:T(8,128)}, u32[]{:S(2)}, u32[]{:S(2)}) collective-permute-start(f32[192,1152]{1,0:T(8,128)} %collective-permute-done.refs_0_), channel_id=1, source_target_pairs={{0,4},{2,6},{4,0},{6,2},{8,12},{10,14},{12,8},{14,10},{16,20},{18,... | collective-permute-start | bytes 2654216 | tf_op jit(solution)/shard_map/ppermute | solution.py:428
  38.7 53.0 %collective-permute-start.4 = (f32[96,768]{1,0:T(8,128)S(1)}, f32[96,768]{1,0:T(8,128)S(1)}, u32[]{:S(2)}, u32[]{:S(2)}) collective-permute-start(f32[96,768]{1,0:T(8,128)S(1)} %dynamic-slice_convert_fusion.3), channel_id=1, source_target_pairs={{0,1},{1,0},{2,3},{3,2},{4,5},{5,4},{6,7},{7,6},{8,9},{9,8},{10,11... | collective-permute-start | bytes 884744 | tf_op jit(solution)/shard_map/ppermute | solution.py:428
  91.7 87.3 %copy-start.3 = (f32[96,768]{1,0:T(8,128)}, f32[96,768]{1,0:T(8,128)S(1)}, u32[]{:S(2)}) copy-start(f32[96,768]{1,0:T(8,128)S(1)} %collective-permute-done.4.refs_0_) | copy-start | bytes 884740
  91.7 3.8 collective-permute-start.6
  91.7 93.0 %collective-permute-start.9 = (f32[192,1536]{1,0:T(8,128)}, f32[192,1536]{1,0:T(8,128)}, u32[]{:S(2)}, u32[]{:S(2)}) collective-permute-start(f32[192,1536]{1,0:T(8,128)} %collective-permute-done.8.refs_0_), channel_id=1, source_target_pairs={{0,4},{2,6},{4,0},{6,2},{8,12},{10,14},{12,8},{14,10},{16,20},{18,... | collective-permute-start | bytes 3538952 | tf_op jit(solution)/shard_map/ppermute | solution.py:428
  93.5 91.3 %collective-permute-start.13 = (f32[384,768]{1,0:T(8,128)}, f32[384,768]{1,0:T(8,128)S(1)}, u32[]{:S(2)}, u32[]{:S(2)}) collective-permute-start(f32[384,768]{1,0:T(8,128)} %collective-permute-done.12.refs_0_), channel_id=1, source_target_pairs={{0,4},{2,6},{4,0},{6,2},{8,12},{10,14},{12,8},{14,10},{16,20},{18,... | collective-permute-start | bytes 3538952 | tf_op jit(solution)/shard_map/ppermute | solution.py:428
  93.8 58.2 %collective-permute-start.5 = (f32[96,768]{1,0:T(8,128)S(1)}, f32[96,768]{1,0:T(8,128)}, u32[]{:S(2)}, u32[]{:S(2)}) collective-permute-start(f32[96,768]{1,0:T(8,128)S(1)} %collective-permute-done.4.refs_0_), channel_id=1, source_target_pairs={{0,4},{2,6},{4,0},{6,2},{8,12},{10,14},{12,8},{14,10},{16,20},{18,... | collective-permute-start | bytes 884744 | tf_op jit(solution)/shard_map/ppermute | solution.py:428
  95.5 83.5 %copy-start.4 = (f32[96,768]{1,0:T(8,128)}, f32[96,768]{1,0:T(8,128)S(1)}, u32[]{:S(2)}) copy-start(f32[96,768]{1,0:T(8,128)S(1)} %collective-permute-done.6.refs_2_) | copy-start | bytes 884740
  95.5 88.6 %collective-permute-start.2 = (f32[192,1152]{1,0:T(8,128)}, f32[192,1152]{1,0:T(8,128)}, u32[]{:S(2)}, u32[]{:S(2)}) collective-permute-start(f32[192,1152]{1,0:T(8,128)} %collective-permute-done.refs_0_), channel_id=1, source_target_pairs={{0,2},{2,0},{4,6},{6,4},{8,10},{10,8},{12,14},{14,12},{16,18},{18,... | collective-permute-start | bytes 2654216 | tf_op jit(solution)/shard_map/ppermute | solution.py:428
  95.5 89.7 %collective-permute-start.3 = (f32[192,1152]{1,0:T(8,128)}, f32[192,1152]{1,0:T(8,128)}, u32[]{:S(2)}, u32[]{:S(2)}) collective-permute-start(f32[192,1152]{1,0:T(8,128)} %collective-permute-done.1.refs_1_), channel_id=1, source_target_pairs={{0,2},{2,0},{4,6},{6,4},{8,10},{10,8},{12,14},{14,12},{16,18},{18,... | collective-permute-start | bytes 2654216 | tf_op jit(solution)/shard_map/ppermute | solution.py:428
  98.9 80.7 %copy-start.9 = (f32[768]{0:T(1024)S(1)}, f32[768]{0:T(1024)}, u32[]{:S(2)}) copy-start(f32[768]{0:T(1024)} %param.19) | copy-start | bytes 9220
  98.9 81.3 %copy-start.10 = (f32[768]{0:T(1024)S(1)}, f32[768]{0:T(1024)}, u32[]{:S(2)}) copy-start(f32[768]{0:T(1024)} %param.20) | copy-start | bytes 9220
  152.0 29.4 %collective-permute-start.7 = (f32[96,768]{1,0:T(8,128)}, f32[96,768]{1,0:T(8,128)}, u32[]{:S(2)}, u32[]{:S(2)}) collective-permute-start(f32[96,768]{1,0:T(8,128)} %collective-permute-done.5.refs_1_), channel_id=1, source_target_pairs={{0,2},{2,0},{4,6},{6,4},{8,10},{10,8},{12,14},{14,12},{16,18},{18,... | collective-permute-start | bytes 884744 | tf_op jit(solution)/shard_map/ppermute | solution.py:428
  184.2 67.2 %collective-permute-start.10 = (f32[192,1536]{1,0:T(8,128)}, f32[192,1536]{1,0:T(8,128)}, u32[]{:S(2)}, u32[]{:S(2)}) collective-permute-start(f32[192,1536]{1,0:T(8,128)} %collective-permute-done.8.refs_0_), channel_id=1, source_target_pairs={{0,2},{2,0},{4,6},{6,4},{8,10},{10,8},{12,14},{14,12},{16,18},{18,... | collective-permute-start | bytes 3538952 | tf_op jit(solution)/shard_map/ppermute | solution.py:428
  184.2 71.9 %collective-permute-start.14 = (f32[384,768]{1,0:T(8,128)}, f32[384,768]{1,0:T(8,128)}, u32[]{:S(2)}, u32[]{:S(2)}) collective-permute-start(f32[384,768]{1,0:T(8,128)} %collective-permute-done.12.refs_0_), channel_id=1, source_target_pairs={{0,2},{2,0},{4,6},{6,4},{8,10},{10,8},{12,14},{14,12},{16,18},{18,... | collective-permute-start | bytes 3538952 | tf_op jit(solution)/shard_map/ppermute | solution.py:428
  184.7 66.7 %collective-permute-start.11 = (f32[192,1536]{1,0:T(8,128)}, f32[192,1536]{1,0:T(8,128)}, u32[]{:S(2)}, u32[]{:S(2)}) collective-permute-start(f32[192,1536]{1,0:T(8,128)} %collective-permute-done.9.refs_1_), channel_id=1, source_target_pairs={{0,2},{2,0},{4,6},{6,4},{8,10},{10,8},{12,14},{14,12},{16,18},{18,... | collective-permute-start | bytes 3538952 | tf_op jit(solution)/shard_map/ppermute | solution.py:428
  184.7 4.5 copy-start.1
  184.7 71.3 %collective-permute-start.15 = (f32[384,768]{1,0:T(8,128)S(1)}, f32[384,768]{1,0:T(8,128)}, u32[]{:S(2)}, u32[]{:S(2)}) collective-permute-start(f32[384,768]{1,0:T(8,128)S(1)} %collective-permute-done.13.refs_1_), channel_id=1, source_target_pairs={{0,2},{2,0},{4,6},{6,4},{8,10},{10,8},{12,14},{14,12},{16,18},{18,... | collective-permute-start | bytes 3538952 | tf_op jit(solution)/shard_map/ppermute | solution.py:428
  337.2 37.0 %copy-start.6 = (f32[8,768]{1,0:T(8,128)S(1)}, f32[8,768]{1,0:T(8,128)}, u32[]{:S(2)}) copy-start(f32[8,768]{1,0:T(8,128)} %get-tuple-element.51) | copy-start | bytes 73732
  591.7 5.3 copy-start.2
  597.0 6.5 %slice-start = ((s8[4718592]{0:T(1024)(128)(4,1)}), s8[4194304]{0:T(1024)(128)(4,1)S(1)}, s32[]{:S(2)}) async-start(s8[4718592]{0:T(1024)(128)(4,1)} %bitcast.9), calls=%async_computation.1 | async-start | bytes 8388608
  598.0 5.5 slice-start.1
Sparse Core Ops, SparseCore 0:
  337.4 254.3 all-reduce.3

commit v2 on v1

--- a/solution.py
+++ b/solution.py
@@ -124,6 +124,7 @@
             lax.fori_loop(0, n, tile, 0)
             qkv[win(n * TILE), :] = jnp.zeros((TILE, qkv.shape[1]), bf16)
             attend_rows(counts, qkv, o, lse, samples, width)
+            o[win(total), :] = jnp.zeros((TILE, width), bf16)
     return body
 
 
@@ -140,6 +141,7 @@
         lax.fori_loop(0, n, tile, 0)
         qkv[win(n * TILE), :] = jnp.zeros((TILE, qkv.shape[1]), bf16)
         attend_rows(counts, qkv, o2, lse, samples, width)
+        o2[win(total), :] = jnp.zeros((TILE, width), bf16)
 
         def tail(i, x):
             rr = win(i * TILE)
@@ -283,7 +285,8 @@
             r = win(i * TILE)
             dv = dqkv[r, :]
             da[r, :] = dot(dv, wqkv[...], NT)
-            gqkv[...] += dot(a[r, :], dv, TN)
+            for j in range(3):
+                gqkv[j] += dot(a[r, :], dv[:, j * width:(j + 1) * width], TN)
             return x
 
         lax.fori_loop(0, n, last, 0)
@@ -399,7 +402,7 @@
 def attn_own(counts, dr, qkv, lse, o, a, wout, wqkv, S):
     TP, D = a.shape
     width = wout.shape[0]
-    outs = [sds((TP, D), f32), sds(wout.shape, f32), sds(wqkv.shape, f32)]
+    outs = [sds((TP, D), f32), sds(wout.shape, f32), sds((3, D, width), f32)]
     return call(attn_own_body(S, width), "attn_own", counts, [dr, qkv, lse, o, a, wout, wqkv], outs, [pltpu.VMEM((TP, width), bf16), pltpu.VMEM((TP, 3 * width), bf16)], flops=9 * 10**9)
 
 
@@ -410,22 +413,12 @@
     return call(attn_other_body(S, width, L), "attn_other", counts, [line, dr, qkv, lse, wout, wqkv, da, h, gain], outs, [pltpu.VMEM((TP, width), bf16), pltpu.VMEM((TP, 3 * width), bf16), pltpu.VMEM((TP, D), bf16)], flops=8 * 10**9)
 
 
-def local(patches, counts, visible, g1, b1, g2, b2, cot, wq0, wo0, wu0, wd0, rest):
-    S, L, D = patches.shape
-    col, line = visible[:, :, None], visible[:, None, :]
-    g1, b1, g2, b2 = (x[None, :] for x in (g1, b1, g2, b2))
-    h, dm, a, qkv0, o0, lse0 = fwd_own(counts, col, patches, cot, g1, b1, wq0)
-    wq1, wo1, wu1, wd1 = rest
-    qkv1, o1, lse1, r, c = fwd_other(counts, a, h, o0, wq1, wo0, wo1, g2, b2, S)
-    m, dc, gup, gdown = mlp_own(counts, c, dm, wu0, wd0, S)
-    out, dr, gg2 = mlp_other(counts, line, c, dm, wu1, wd1, m, dc, r, g2, S, L)
-    da, gout, gqkv = attn_own(counts, dr, qkv0, lse0, o0, a, wo0, wq0, S)
-    gin, gg1 = attn_other(counts, line, dr, qkv1, lse1, wo1, wq1, da, h, g1, S, L)
-    return out, gin, gg1, gqkv, gout, gg2, gup, gdown
-
-
 def swap(x, axis, size, bit):
     return lax.ppermute(x, axis, [(k, k ^ bit) for k in range(size)])
+
+
+def tie(*xs):
+    return lax.optimization_barrier(xs)
 
 
 def cast_pieces(order, pieces):
@@ -438,24 +431,90 @@
     return call(body, "cast_pieces", order, pieces, [sds((4 * rows, cols), bf16)])[0]
 
 
-def fetch(weight, dp):
+def side(bit):
+    return (lax.axis_index("dp") // bit) % 2
+
+
+def half(x, i):
+    n = x.shape[0] // 2
+    return lax.dynamic_slice_in_dim(x, i * n, n, 0)
+
+
+def fold(x, bit, dp):
+    i = side(bit)
+    return half(x, i) + swap(half(x, 1 - i), "dp", dp, bit)
+
+
+def spread(x, bit, dp):
+    got = swap(x, "dp", dp, bit)
+    first = side(bit) == 0
+    return jnp.concatenate([jnp.where(first, x, got), jnp.where(first, got, x)], 0)
+
+
+def folds(x, bits, dp):
+    for bit in bits:
+        x = fold(x, bit, dp)
+    return x
+
+
+def spreads(x, bits, dp):
+    for bit in reversed(bits):
+        x = spread(x, bit, dp)
+    return x
+
+
+def shards(dp, patches, counts, visible, g1, b1, wq, wo, g2, b2, wu, wd, cot):
+    S, L, D = patches.shape
+    wt = wq.transpose(1, 0, 2)
+    wq = jnp.concatenate([wt[0], wt[1], wt[2]], axis=1)
+    col, line = visible[:, :, None], visible[:, None, :]
+    g1, b1, g2, b2 = (x[None, :] for x in (g1, b1, g2, b2))
     me = lax.axis_index("dp") % 4
-    rows = weight.shape[0] // 4
-    part = lax.dynamic_slice_in_dim(weight, me * rows, rows, 0).astype(f32)
-    first = swap(part, "tensor", 2, 1)
-    across = swap(first, "dp", dp, 2)
     order = jnp.stack([me, me ^ 2, me ^ 1, me ^ 3]).astype(jnp.int32)
-    return cast_pieces(order, [first, across, swap(first, "dp", dp, 1), swap(across, "dp", dp, 1)])
-
-
-def shards(dp, patches, counts, visible, g1, b1, wq, wo, g2, b2, wu, wd, cot):
-    D = patches.shape[2]
-    wq = wq.reshape(D, -1)
-    rest = tuple(fetch(w, dp) for w in (wq, wo, wu, wd))
-    out, gin, gg1, gqkv, gout, gg2, gup, gdown = local(patches, counts, visible, g1, b1, g2, b2, cot, wq, wo, wu, wd, rest)
-    gup, gdown = lax.psum((gup, gdown), "dp")
-    gqkv, gout, gg1, gg2 = lax.psum((gqkv, gout, gg1, gg2), "dp")
-    return (out, gin, gg1[0], gg1[1], gqkv.reshape(D, 3, -1), gout, gg2[0], gg2[1], gup, gdown)
+
+    def part(w):
+        rows = w.shape[0] // 4
+        return lax.dynamic_slice_in_dim(w, me * rows, rows, 0).astype(f32)
+
+    def rest(first, across):
+        return cast_pieces(order, [first, across, swap(first, "dp", dp, 1), swap(across, "dp", dp, 1)])
+
+    every = [1 << i for i in range(dp.bit_length() - 1)]
+    along = every
+    other = [1, 4, 2] + every[3:] if len(every) > 2 else every
+
+    fq, fo = swap(part(wq), "tensor", 2, 1), swap(part(wo), "tensor", 2, 1)
+    h, dm, a, qkv0, o0, lse0 = fwd_own(counts, col, patches, cot, g1, b1, wq)
+    fq, fo, pu, pd, a = tie(fq, fo, part(wu), part(wd), a)
+    aq, ao = swap(fq, "dp", dp, 2), swap(fo, "dp", dp, 2)
+    fu, fd = swap(pu, "tensor", 2, 1), swap(pd, "tensor", 2, 1)
+    wq1, wo1 = rest(fq, aq), rest(fo, ao)
+    qkv1, o1, lse1, r, c = fwd_other(counts, a, h, o0, wq1, wo, wo1, g2, b2, S)
+    fu, fd, c = tie(fu, fd, c)
+    au, ad = swap(fu, "dp", dp, 2), swap(fd, "dp", dp, 2)
+    m, dc, gup, gdown = mlp_own(counts, c, dm, wu, wd, S)
+    au, ad, m = tie(au, ad, m)
+    wu1, wd1 = rest(fu, au), rest(fd, ad)
+    A, B = fold(gup, 1, dp), fold(gdown, 1, dp)
+    A, B, c = tie(A, B, c)
+    out, dr, gg2 = mlp_other(counts, line, c, dm, wu1, wd1, m, dc, r, g2, S, L)
+    A, B = fold(A, along[1], dp), fold(B, other[1], dp)
+    A, B, dr = tie(A, B, dr)
+    A, B = fold(A, along[2], dp), fold(B, other[2], dp)
+    da, gout, gqkv = attn_own(counts, dr, qkv0, lse0, o0, a, wo, wq, S)
+    A, B, da = tie(A, B, da)
+    A, B = folds(A, along[3:], dp), folds(B, other[3:], dp)
+    C, E = fold(gqkv.reshape(3 * D, -1), 1, dp), fold(gout, 1, dp)
+    gin, gg1 = attn_other(counts, line, dr, qkv1, lse1, wo1, wq1, da, h, g1, S, L)
+    C, E, A, B, gg1 = tie(C, E, A, B, gg1)
+    small = jnp.concatenate([gg1, gg2], 0)
+    for bit in every:
+        small = small + swap(small, "dp", dp, bit)
+    gg1, gg2 = small[:8], small[8:]
+    gup, gdown = spreads(A, along, dp), spreads(B, other, dp)
+    gqkv = spreads(folds(C, along[1:], dp), along, dp).reshape(3, D, -1)
+    gout = spreads(folds(E, other[1:], dp), other, dp)
+    return (out, gin, gg1[0], gg1[1], gqkv.transpose(1, 0, 2), gout, gg2[0], gg2[1], gup, gdown)
 
 
 def solution(mesh):

time: 610 us -> 533 us (0.87)
  waiting for transfers between devices: 276 us -> 213 us
  blocking collectives: 60.9 us -> 0 us
  other arithmetic: 5.86 us -> 47.4 us
  starting transfers between devices: 14 us -> 31.1 us
  between operations: 14.2 us -> 1.48 us
    psum x1 -> x0, waiting for transfers between devices: 156 us -> none  [shards(): gqkv, gout, gg1, gg2 = lax.psum((gqkv, gout, gg1, gg2), 'dp')]
    ppermute x16 -> x52, waiting for transfers between devices: 120 us -> 213 us  [swap(): return lax.ppermute(x, axis, [(k, k ^ bit) for k in range(size)])]
    psum x1 -> x0, blocking collectives: 60.9 us -> none  [shards(): gqkv, gout, gg1, gg2 = lax.psum((gqkv, gout, gg1, gg2), 'dp')]
    add x0 -> x20, other arithmetic: none -> 17.2 us  [the longest x16 15.7 us: fold(): return half(x, i) + swap(half(x, 1 - i), 'dp', dp, bit)]
    ppermute x16 -> x52, starting transfers between devices: 14 us -> 31.1 us  [swap(): return lax.ppermute(x, axis, [(k, k ^ bit) for k in range(size)])]
    dynamic_slice x0 -> x16, local copies, waits for them, and re-layouts: none -> 16.2 us  [half(): return lax.dynamic_slice_in_dim(x, i * n, n, 0)]
    concatenate x0 -> x17, other arithmetic: none -> 14.9 us  [the longest x16 13.7 us: spread(): jnp.concatenate([jnp.where(first, x, got), jnp.where(first, got, x)], 0)]
    unnamed x31 -> x59, local copies, waits for them, and re-layouts: 16.6 us -> 4.12 us
  transfers between devices with their start and end apart: 17 -> 52, of which waited for: 4 -> 20; matrix products, arithmetic and copies ran while one was open for 2% -> 11% of each run, Pallas kernels for 22% -> 33%
where the time goes in v2:
time: 533 us; the launch traced here: 534 us
  Pallas kernels  213 us (40%)
  waiting for transfers between devices  213 us (40%)
  other arithmetic  47.4 us (9%)
  starting transfers between devices  31.1 us (6%)
  local copies, waits for them, and re-layouts  28 us (5%)
    ppermute x52, waiting for transfers between devices, swap(): return lax.ppermute(x, axis, [(k, k ^ bit) for k in range(size)])  213 us
    pallas_call x9, Pallas kernels, call(): pl.pallas_call(body, name=name, out_shape=list(outs), grid_spec=pltpu.Pre...  186 us
    ppermute x52, starting transfers between devices, swap(): return lax.ppermute(x, axis, [(k, k ^ bit) for k in range(size)])  31.1 us
    pallas_call x1, Pallas kernels, fwd_own(): pl.pallas_call(fwd_own_body(S, width), name='fwd_own', out_shape=outs, gr...  26.9 us
    dynamic_slice x16, local copies, waits for them, and re-layouts, half(): return lax.dynamic_slice_in_dim(x, i * n, n, 0)  16.2 us
    add x16, other arithmetic, fold(): return half(x, i) + swap(half(x, 1 - i), 'dp', dp, bit)  15.7 us
    concatenate x16, other arithmetic, spread(): jnp.concatenate([jnp.where(first, x, got), jnp.where(first, got, x)], 0)  13.7 us
  transfers between devices with their start and end apart: 52, of which 20 were waited for; matrix products, arithmetic and copies ran while one was open for 11% of the time, Pallas kernels for 33%

profile of v2, /device:TPU:0, one launch (start us, length us, event | category | flops | bytes accessed | tf_op | source)
XLA Modules:
  0.0 533.7 jit_solution(1460418462162971067)
XLA Ops:
  0.7 2.4 slice_bitcast_fusion.2
  5.3 3.0 collective-permute-start
  8.3 1.6 dynamic-slice_convert_fusion.3
  10.5 1.7 copy.22.col
  12.8 26.9 %fwd_own.1 = (bf16[1792,768]{1,0:T(8,128)(2,1)}, bf16[1792,768]{1,0:T(8,128)(2,1)}, bf16[1792,768]{1,0:T(8,128)(2,1)}, bf16[1792,1152]{1,0:T(8,128)(2,1)}, bf16[...) custom-call(s32[6]{0:T(128)} %counts.11, s32[6,512,1]{2,1,0:T(8,128)} %copy.22.col, bf16[6,512,768]{2,1,0:T(8,128)(2,1)} %patches.1, ...), custom_call_target="tpu_custom_call" | custom-call | flops 6000000000 | bytes 26214400 | tf_op jit(solution)/shard_map/fwd_own/pallas_call | solution.py:361
  39.7 2.2 dynamic-slice_convert_fusion
  41.9 2.2 dynamic-slice_convert_fusion.1
  44.3 19.4 %collective-permute-done.4.refs_1_ = f32[192,1152]{1,0:T(8,128)} collective-permute-done((f32[192,1152]{1,0:T(8,128)}, f32[192,1152]{1,0:T(8,128)}, u32[]{:S(2)}, u32[]{:S(2)}) %collective-permute-start.4) | collective-permute-done | bytes 884768 | tf_op jit(solution)/shard_map/ppermute | solution.py:417
  63.7 1.7 collective-permute-start.7
  65.7 1.5 collective-permute-start.2
  67.2 6.1 %collective-permute-done.7.refs_1_ = f32[96,768]{1,0:T(8,128)S(1)} collective-permute-done((f32[96,768]{1,0:T(8,128)}, f32[96,768]{1,0:T(8,128)S(1)}, u32[]{:S(2)}, u32[]{:S(2)}) %collective-permute-start.7) | collective-permute-done | bytes 294944 | tf_op jit(solution)/shard_map/ppermute | solution.py:417
  73.4 1.5 collective-permute-start.3
  76.8 2.8 cast_pieces.5.out_other.wout
  79.6 4.0 cast_pieces.4.weight.wqkv
  83.6 26.1 %fwd_other.1 = (bf16[1792,1152]{1,0:T(8,128)(2,1)}, bf16[1792,384]{1,0:T(8,128)(2,1)}, f32[6,6,256]{2,1,0:T(8,128)}, f32[1792,768]{1,0:T(8,128)}, bf16[1792,768]{1,0:T(8,128)(2,1)}) custom-call(s32[6]{0:T(128)} %counts.11, bf16[1792,768]{1,0:T(8,128)(2,1)} %get-tuple-element.60.a, bf16[1792,768]{1,0:T(8,128)(2,1)} %get-tuple-element.61.h, ...), custom_call_target="tpu_custom_call" | custom-call | flops 7000000000 | bytes 23635968 | tf_op jit(solution)/shard_map/fwd_other/pallas_call | solution.py:337
  109.8 9.7 %collective-permute-done.3.refs_0_ = f32[384,768]{1,0:T(8,128)} collective-permute-done((f32[384,768]{1,0:T(8,128)}, f32[384,768]{1,0:T(8,128)}, u32[]{:S(2)}, u32[]{:S(2)}) %collective-permute-start.3) | collective-permute-done | bytes 1179680 | tf_op jit(solution)/shard_map/ppermute | solution.py:417
  119.4 35.9 %mlp_own.1 = (f32[1792,768]{1,0:T(8,128)}, f32[1792,768]{1,0:T(8,128)}, f32[768,1536]{1,0:T(8,128)}, f32[1536,768]{1,0:T(8,128)}) custom-call(s32[6]{0:T(128)} %counts.11, bf16[1792,768]{1,0:T(8,128)(2,1)} %get-tuple-element.70.c, bf16[1792,768]{1,0:T(8,128)(2,1)} %get-tuple-element.67.dm, bf16[768,1536]{1,0:T(8,128)(2,1)} %up.1, bf16[1536,768]{1,0:T(8,128)(2,1)} %down.1), custom_call_target="tpu_custom_call" | custom-call | flops 17999998976 | bytes 30670848 | tf_op jit(solution)/shard_map/mlp_own/pallas_call | solution.py:337
  155.4 3.2 constant_dynamic-slice_fusion.14
  158.6 3.2 constant_dynamic-slice_fusion.15
  162.3 2.0 collective-permute-start.13
  165.0 26.3 %collective-permute-done.12.refs_1_ = f32[192,1536]{1,0:T(8,128)} collective-permute-done((f32[192,1536]{1,0:T(8,128)S(1)}, f32[192,1536]{1,0:T(8,128)}, u32[]{:S(2)}, u32[]{:S(2)}) %collective-permute-start.12) | collective-permute-done | bytes 1179680 | tf_op jit(solution)/shard_map/ppermute | solution.py:417
  191.3 24.3 %collective-permute-done.13.refs_1_ = f32[384,768]{1,0:T(8,128)} collective-permute-done((f32[384,768]{1,0:T(8,128)}, f32[384,768]{1,0:T(8,128)}, u32[]{:S(2)}, u32[]{:S(2)}) %collective-permute-start.13) | collective-permute-done | bytes 1179680 | tf_op jit(solution)/shard_map/ppermute | solution.py:417
  216.1 2.2 dynamic-slice_add_fusion
  218.6 2.6 dynamic-slice_add_fusion.1
  224.9 4.6 cast_pieces.7.down
  229.5 4.6 cast_pieces.6.up
  234.2 34.9 %mlp_other.1 = (bf16[6,512,768]{2,1,0:T(8,128)(2,1)}, f32[1792,768]{1,0:T(8,128)}, f32[8,768]{1,0:T(8,128)}) custom-call(s32[6]{0:T(128)} %counts.11, s32[6,1,512]{2,1,0:T(1,128)} %broadcast_in_dim.18.line, bf16[1792,768]{1,0:T(8,128)(2,1)} %get-tuple-element.70.c, bf16[1792,768]{1,0:T(8,128)(2,1)} %get-tuple-element.67.dm, ...), custom_call_target="tpu_custom_call" | custom-call | flops 12000000000 | bytes 37002240 | tf_op jit(solution)/shard_map/mlp_other/pallas_call | solution.py:337
  269.1 1.9 dynamic-slice_add_fusion.3
  271.5 1.4 dynamic-slice_add_fusion.4
  274.8 37.0 %attn_own.1 = (f32[1792,768]{1,0:T(8,128)}, f32[384,768]{1,0:T(8,128)}, f32[3,768,384]{2,1,0:T(8,128)}) custom-call(s32[6]{0:T(128)} %counts.11, f32[1792,768]{1,0:T(8,128)} %get-tuple-element.83.dr, bf16[1792,1152]{1,0:T(8,128)(2,1)} %get-tuple-element.88.qkv, f32[6,6,256]{2,1,0:T(8,128)} %get-tuple-element.89.lse, bf16[1792,384]{1,0:T(8,128)(2,1)} %get-tuple-element.62.o, ...), custom_call_target="tpu_custom_call" | custom-call | flops 8999999488 | bytes 26382336 | tf_op jit(solution)/shard_map/attn_own/pallas_call | solution.py:337
  311.8 1.9 constant_dynamic-slice_fusion.8
  313.8 2.8 constant_dynamic-slice_fusion.9
  321.0 2.8 collective-permute-start.24
  323.8 36.2 %attn_other.1 = (bf16[6,512,768]{2,1,0:T(8,128)(2,1)}, f32[8,768]{1,0:T(8,128)}) custom-call(s32[6]{0:T(128)} %counts.11, s32[6,1,512]{2,1,0:T(1,128)} %broadcast_in_dim.18.line, f32[1792,768]{1,0:T(8,128)} %get-tuple-element.83.dr, bf16[1792,1152]{1,0:T(8,128)(2,1)} %get-tuple-element.84.qkv, f32[6,6,256]{2,1,0:T(8,128)} %get-tuple-element.85.lse, ...), custom_call_target="tpu_custom_call" | custom-call | flops 8000000000 | bytes 25046016 | tf_op jit(solution)/shard_map/attn_other/pallas_call | solution.py:337
  360.0 1.5 dynamic-slice_add_fusion.6
  363.4 1.7 dynamic-slice_add_fusion.2
  365.4 2.9 collective-permute-start.44
  368.5 6.5 %collective-permute-done.37 = f32[96,768]{1,0:T(8,128)S(1)} collective-permute-done((f32[96,768]{1,0:T(8,128)S(1)}, f32[96,768]{1,0:T(8,128)S(1)}, u32[]{:S(2)}, u32[]{:S(2)}) %collective-permute-start.37) | collective-permute-done | bytes 294944 | tf_op jit(solution)/shard_map/ppermute | solution.py:417
  375.1 13.5 %collective-permute-done.48 = f32[96,768]{1,0:T(8,128)S(1)} collective-permute-done((f32[96,768]{1,0:T(8,128)S(1)}, f32[96,768]{1,0:T(8,128)S(1)}, u32[]{:S(2)}, u32[]{:S(2)}) %collective-permute-start.48) | collective-permute-done | bytes 294944 | tf_op jit(solution)/shard_map/ppermute | solution.py:417
  388.7 1.6 collective-permute-done.38
  390.5 6.0 %collective-permute-done.39 = f32[24,768]{1,0:T(8,128)S(1)} collective-permute-done((f32[24,768]{1,0:T(8,128)S(1)}, f32[24,768]{1,0:T(8,128)S(1)}, u32[]{:S(2)}, u32[]{:S(2)}) %collective-permute-start.39) | collective-permute-done | bytes 73760 | tf_op jit(solution)/shard_map/ppermute | solution.py:417
  396.7 5.4 %collective-permute-done.40 = f32[24,768]{1,0:T(8,128)S(1)} collective-permute-done((f32[24,768]{1,0:T(8,128)S(1)}, f32[24,768]{1,0:T(8,128)S(1)}, u32[]{:S(2)}, u32[]{:S(2)}) %collective-permute-start.40) | collective-permute-done | bytes 73760 | tf_op jit(solution)/shard_map/ppermute | solution.py:417
  402.4 4.9 collective-permute-done.41
  407.6 2.1 collective-permute-start.50
  409.9 8.6 %collective-permute-done.45 = f32[96,1536]{1,0:T(8,128)S(1)} collective-permute-done((f32[96,1536]{1,0:T(8,128)S(1)}, f32[96,1536]{1,0:T(8,128)S(1)}, u32[]{:S(2)}, u32[]{:S(2)}) %collective-permute-start.45) | collective-permute-done | bytes 589856 | tf_op jit(solution)/shard_map/ppermute | solution.py:417
  418.7 37.2 %collective-permute-done.31 = f32[288,384]{1,0:T(8,128)S(1)} collective-permute-done((f32[288,384]{1,0:T(8,128)S(1)}, f32[288,384]{1,0:T(8,128)S(1)}, u32[]{:S(2)}, u32[]{:S(2)}) %collective-permute-start.31) | collective-permute-done | bytes 442400 | tf_op jit(solution)/shard_map/ppermute | solution.py:417
  456.4 1.7 collective-permute-start.46
  458.2 10.9 %collective-permute-done.32 = f32[144,384]{1,0:T(8,128)S(1)} collective-permute-done((f32[144,384]{1,0:T(8,128)S(1)}, f32[144,384]{1,0:T(8,128)S(1)}, u32[]{:S(2)}, u32[]{:S(2)}) %collective-permute-start.32) | collective-permute-done | bytes 221216 | tf_op jit(solution)/shard_map/ppermute | solution.py:417
  470.2 7.0 %collective-permute-done.33 = f32[144,384]{1,0:T(8,128)S(1)} collective-permute-done((f32[144,384]{1,0:T(8,128)S(1)}, f32[144,384]{1,0:T(8,128)S(1)}, u32[]{:S(2)}, u32[]{:S(2)}) %collective-permute-start.33) | collective-permute-done | bytes 221216 | tf_op jit(solution)/shard_map/ppermute | solution.py:417
  477.5 1.6 pad_maximum_fusion.4
  479.2 1.7 pad_maximum_fusion.3
  481.5 4.1 collective-permute-done.34
  489.2 1.8 collective-permute-start.27
  490.9 15.3 %collective-permute-done.27 = f32[16,768]{1,0:T(8,128)S(1)} collective-permute-done((f32[16,768]{1,0:T(8,128)S(1)}, f32[16,768]{1,0:T(8,128)S(1)}, u32[]{:S(2)}, u32[]{:S(2)}) %collective-permute-start.27) | collective-permute-done | bytes 49184 | tf_op jit(solution)/shard_map/ppermute | solution.py:417
  506.2 2.1 collective-permute-start.28
  508.3 2.1 collective-permute-done.28
  511.0 3.1 collective-permute-start.29
  514.1 2.4 collective-permute-done.29
  518.0 1.3 broadcast_select_fusion.17
  522.3 2.0 broadcast_select_fusion.1
  524.3 2.5 pad_maximum_fusion.1
  526.8 2.1 broadcast_select_fusion.3
  528.9 2.5 pad_maximum_fusion
  531.7 2.0 pad_maximum_fusion.2
  (192 shorter events, 33.2 us)
Async XLA Ops:
  4.3 8.5 %copy-start.13 = (bf16[768,1152]{1,0:T(8,128)(2,1)}, bf16[768,1152]{1,0:T(8,128)(2,1)S(1)}, u32[]{:S(2)}) copy-start(bf16[768,1152]{1,0:T(8,128)(2,1)S(1)} %pad_maximum_fusion.5.weight.wqkv) | copy-start | bytes 5308420
  4.3 5.7 %copy-start.25 = (f32[768]{0:T(1024)S(1)}, f32[768]{0:T(1024)}, u32[]{:S(2)}) copy-start(f32[768]{0:T(1024)} %param.15) | copy-start | bytes 9220
  4.3 6.2 %copy-start.22 = (s32[6,512]{1,0:T(8,128)S(1)}, s32[6,512]{1,0:T(8,128)}, u32[]{:S(2)}) copy-start(s32[6,512]{1,0:T(8,128)} %param.14) | copy-start | bytes 36868
  4.3 7.9 %copy-start.26 = (f32[768]{0:T(1024)S(1)}, f32[768]{0:T(1024)}, u32[]{:S(2)}) copy-start(f32[768]{0:T(1024)} %param.16) | copy-start | bytes 9220
  5.3 38.8 %collective-permute-start = (f32[192,1152]{1,0:T(8,128)}, f32[192,1152]{1,0:T(8,128)}, u32[]{:S(2)}, u32[]{:S(2)}) collective-permute-start(f32[192,1152]{1,0:T(8,128)} %dynamic-slice_convert_fusion.2), channel_id=1, source_target_pairs={{0,1},{1,0},{2,3},{3,2},{4,5},{5,4},{6,7},{7,6},{8,9},{9,8},{10,11... | collective-permute-start | bytes 2654216 | tf_op jit(solution)/shard_map/ppermute | solution.py:417
  10.0 34.2 %collective-permute-start.1 = (f32[96,768]{1,0:T(8,128)}, f32[96,768]{1,0:T(8,128)}, u32[]{:S(2)}, u32[]{:S(2)}) collective-permute-start(f32[96,768]{1,0:T(8,128)} %dynamic-slice_convert_fusion.3), channel_id=1, source_target_pairs={{0,1},{1,0},{2,3},{3,2},{4,5},{5,4},{6,7},{7,6},{8,9},{9,8},{10,11... | collective-permute-start | bytes 884744 | tf_op jit(solution)/shard_map/ppermute | solution.py:417
  39.7 35.2 %copy-start.27 = (f32[768]{0:T(1024)S(1)}, f32[768]{0:T(1024)}, u32[]{:S(2)}) copy-start(f32[768]{0:T(1024)} %param.19) | copy-start | bytes 9220
  39.7 35.9 %copy-start.28 = (f32[768]{0:T(1024)S(1)}, f32[768]{0:T(1024)}, u32[]{:S(2)}) copy-start(f32[768]{0:T(1024)} %param.20) | copy-start | bytes 9220
  44.1 19.6 %collective-permute-start.4 = (f32[192,1152]{1,0:T(8,128)}, f32[192,1152]{1,0:T(8,128)}, u32[]{:S(2)}, u32[]{:S(2)}) collective-permute-start(f32[192,1152]{1,0:T(8,128)} %collective-permute-done.refs_0_), channel_id=1, source_target_pairs={{0,4},{2,6},{4,0},{6,2},{8,12},{10,14},{12,8},{14,10},{16,20},{18,... | collective-permute-start | bytes 2654216 | tf_op jit(solution)/shard_map/ppermute | solution.py:417
  44.3 35.3 %collective-permute-start.5 = (f32[192,1152]{1,0:T(8,128)}, f32[192,1152]{1,0:T(8,128)}, u32[]{:S(2)}, u32[]{:S(2)}) collective-permute-start(f32[192,1152]{1,0:T(8,128)} %collective-permute-done.refs_0_), channel_id=1, source_target_pairs={{0,2},{2,0},{4,6},{6,4},{8,10},{10,8},{12,14},{14,12},{16,18},{18,... | collective-permute-start | bytes 2654216 | tf_op jit(solution)/shard_map/ppermute | solution.py:417
  63.7 15.9 %collective-permute-start.6 = (f32[192,1152]{1,0:T(8,128)}, f32[192,1152]{1,0:T(8,128)}, u32[]{:S(2)}, u32[]{:S(2)}) collective-permute-start(f32[192,1152]{1,0:T(8,128)} %collective-permute-done.4.refs_1_), channel_id=1, source_target_pairs={{0,2},{2,0},{4,6},{6,4},{8,10},{10,8},{12,14},{14,12},{16,18},{18,... | collective-permute-start | bytes 2654216 | tf_op jit(solution)/shard_map/ppermute | solution.py:417
  63.7 9.6 %collective-permute-start.7 = (f32[96,768]{1,0:T(8,128)}, f32[96,768]{1,0:T(8,128)S(1)}, u32[]{:S(2)}, u32[]{:S(2)}) collective-permute-start(f32[96,768]{1,0:T(8,128)} %collective-permute-done.1.refs_0_), channel_id=1, source_target_pairs={{0,4},{2,6},{4,0},{6,2},{8,12},{10,14},{12,8},{14,10},{16,20},{18,... | collective-permute-start | bytes 884744 | tf_op jit(solution)/shard_map/ppermute | solution.py:417
  65.5 9.4 %collective-permute-start.8 = (f32[96,768]{1,0:T(8,128)}, f32[96,768]{1,0:T(8,128)S(1)}, u32[]{:S(2)}, u32[]{:S(2)}) collective-permute-start(f32[96,768]{1,0:T(8,128)} %collective-permute-done.1.refs_0_), channel_id=1, source_target_pairs={{0,2},{2,0},{4,6},{6,4},{8,10},{10,8},{12,14},{14,12},{16,18},{18,... | collective-permute-start | bytes 884744 | tf_op jit(solution)/shard_map/ppermute | solution.py:417
  65.7 44.1 %collective-permute-start.2 = (f32[192,1536]{1,0:T(8,128)}, f32[192,1536]{1,0:T(8,128)S(1)}, u32[]{:S(2)}, u32[]{:S(2)}) collective-permute-start(f32[192,1536]{1,0:T(8,128)} %dynamic-slice_convert_fusion.1), channel_id=1, source_target_pairs={{0,1},{1,0},{2,3},{3,2},{4,5},{5,4},{6,7},{7,6},{8,9},{9,8},{10,11... | collective-permute-start | bytes 3538952 | tf_op jit(solution)/shard_map/ppermute | solution.py:417
  73.4 3.4 copy-start.20
  73.4 46.1 %collective-permute-start.3 = (f32[384,768]{1,0:T(8,128)}, f32[384,768]{1,0:T(8,128)}, u32[]{:S(2)}, u32[]{:S(2)}) collective-permute-start(f32[384,768]{1,0:T(8,128)} %dynamic-slice_convert_fusion), channel_id=1, source_target_pairs={{0,1},{1,0},{2,3},{3,2},{4,5},{5,4},{6,7},{7,6},{8,9},{9,8},{10,11... | collective-permute-start | bytes 3538952 | tf_op jit(solution)/shard_map/ppermute | solution.py:417
  74.9 1.9 collective-permute-start.9
  109.8 81.5 %copy-start.17 = (f32[192,1536]{1,0:T(8,128)}, f32[192,1536]{1,0:T(8,128)S(1)}, u32[]{:S(2)}) copy-start(f32[192,1536]{1,0:T(8,128)S(1)} %collective-permute-done.2.refs_0_) | copy-start | bytes 3538948
  158.6 57.0 %collective-permute-start.11 = (f32[768,768]{1,0:T(8,128)}, f32[768,768]{1,0:T(8,128)S(1)}, u32[]{:S(2)}, u32[]{:S(2)}) collective-permute-start(f32[768,768]{1,0:T(8,128)} %constant_dynamic-slice_fusion.14), channel_id=1, source_target_pairs={{0,2},{2,0},{4,6},{6,4},{8,10},{10,8},{12,14},{14,12},{16,18},{18,... | collective-permute-start | bytes 7077896 | tf_op jit(solution)/shard_map/ppermute | solution.py:417
  161.8 56.5 %collective-permute-start.10 = (f32[384,1536]{1,0:T(8,128)}, f32[384,1536]{1,0:T(8,128)}, u32[]{:S(2)}, u32[]{:S(2)}) collective-permute-start(f32[384,1536]{1,0:T(8,128)} %constant_dynamic-slice_fusion.15), channel_id=1, source_target_pairs={{0,2},{2,0},{4,6},{6,4},{8,10},{10,8},{12,14},{14,12},{16,18},{18,... | collective-permute-start | bytes 7077896 | tf_op jit(solution)/shard_map/ppermute | solution.py:417
  162.3 28.9 %collective-permute-start.12 = (f32[192,1536]{1,0:T(8,128)S(1)}, f32[192,1536]{1,0:T(8,128)}, u32[]{:S(2)}, u32[]{:S(2)}) collective-permute-start(f32[192,1536]{1,0:T(8,128)S(1)} %collective-permute-done.2.refs_0_), channel_id=1, source_target_pairs={{0,4},{2,6},{4,0},{6,2},{8,12},{10,14},{12,8},{14,10},{16,20},{18,... | collective-permute-start | bytes 3538952 | tf_op jit(solution)/shard_map/ppermute | solution.py:417
  162.3 53.3 %collective-permute-start.13 = (f32[384,768]{1,0:T(8,128)}, f32[384,768]{1,0:T(8,128)}, u32[]{:S(2)}, u32[]{:S(2)}) collective-permute-start(f32[384,768]{1,0:T(8,128)} %collective-permute-done.3.refs_0_), channel_id=1, source_target_pairs={{0,4},{2,6},{4,0},{6,2},{8,12},{10,14},{12,8},{14,10},{16,20},{18,... | collective-permute-start | bytes 3538952 | tf_op jit(solution)/shard_map/ppermute | solution.py:417
  165.0 58.6 %collective-permute-start.16 = (f32[384,768]{1,0:T(8,128)}, f32[384,768]{1,0:T(8,128)S(1)}, u32[]{:S(2)}, u32[]{:S(2)}) collective-permute-start(f32[384,768]{1,0:T(8,128)} %collective-permute-done.3.refs_0_), channel_id=1, source_target_pairs={{0,2},{2,0},{4,6},{6,4},{8,10},{10,8},{12,14},{14,12},{16,18},{18,... | collective-permute-start | bytes 3538952 | tf_op jit(solution)/shard_map/ppermute | solution.py:417
  191.3 38.3 %collective-permute-start.14 = (f32[192,1536]{1,0:T(8,128)S(1)}, f32[192,1536]{1,0:T(8,128)}, u32[]{:S(2)}, u32[]{:S(2)}) collective-permute-start(f32[192,1536]{1,0:T(8,128)S(1)} %collective-permute-done.2.refs_0_), channel_id=1, source_target_pairs={{0,2},{2,0},{4,6},{6,4},{8,10},{10,8},{12,14},{14,12},{16,18},{18,... | collective-permute-start | bytes 3538952 | tf_op jit(solution)/shard_map/ppermute | solution.py:417
  215.6 9.3 %collective-permute-start.17 = (f32[384,768]{1,0:T(8,128)}, f32[384,768]{1,0:T(8,128)}, u32[]{:S(2)}, u32[]{:S(2)}) collective-permute-start(f32[384,768]{1,0:T(8,128)} %collective-permute-done.13.refs_1_), channel_id=1, source_target_pairs={{0,2},{2,0},{4,6},{6,4},{8,10},{10,8},{12,14},{14,12},{16,18},{18,... | collective-permute-start | bytes 3538952 | tf_op jit(solution)/shard_map/ppermute | solution.py:417
  215.6 13.9 %collective-permute-start.15 = (f32[192,1536]{1,0:T(8,128)}, f32[192,1536]{1,0:T(8,128)}, u32[]{:S(2)}, u32[]{:S(2)}) collective-permute-start(f32[192,1536]{1,0:T(8,128)} %collective-permute-done.12.refs_1_), channel_id=1, source_target_pairs={{0,2},{2,0},{4,6},{6,4},{8,10},{10,8},{12,14},{14,12},{16,18},{18,... | collective-permute-start | bytes 3538952 | tf_op jit(solution)/shard_map/ppermute | solution.py:417
  222.5 46.6 %collective-permute-start.19 = (f32[384,768]{1,0:T(8,128)}, f32[384,768]{1,0:T(8,128)}, u32[]{:S(2)}, u32[]{:S(2)}) collective-permute-start(f32[384,768]{1,0:T(8,128)} %constant_dynamic-slice_fusion.12), channel_id=1, source_target_pairs={{0,8},{2,10},{4,12},{6,14},{8,0},{10,2},{12,4},{14,6},{16,24},{18,... | collective-permute-start | bytes 3538952 | tf_op jit(solution)/shard_map/ppermute | solution.py:417
  224.6 46.4 %collective-permute-start.18 = (f32[192,1536]{1,0:T(8,128)}, f32[192,1536]{1,0:T(8,128)}, u32[]{:S(2)}, u32[]{:S(2)}) collective-permute-start(f32[192,1536]{1,0:T(8,128)} %constant_dynamic-slice_fusion.13), channel_id=1, source_target_pairs={{0,4},{2,6},{4,0},{6,2},{8,12},{10,14},{12,8},{14,10},{16,20},{18,... | collective-permute-start | bytes 3538952 | tf_op jit(solution)/shard_map/ppermute | solution.py:417
  273.0 44.1 %collective-permute-start.21 = (f32[192,768]{1,0:T(8,128)S(1)}, f32[192,768]{1,0:T(8,128)}, u32[]{:S(2)}, u32[]{:S(2)}) collective-permute-start(f32[192,768]{1,0:T(8,128)S(1)} %constant_dynamic-slice_fusion.10), channel_id=1, source_target_pairs={{0,4},{2,6},{4,0},{6,2},{8,12},{10,14},{12,8},{14,10},{16,20},{18,... | collective-permute-start | bytes 1769480 | tf_op jit(solution)/shard_map/ppermute | solution.py:417
  274.8 43.4 %collective-permute-start.20 = (f32[96,1536]{1,0:T(8,128)}, f32[96,1536]{1,0:T(8,128)}, u32[]{:S(2)}, u32[]{:S(2)}) collective-permute-start(f32[96,1536]{1,0:T(8,128)} %constant_dynamic-slice_fusion.11), channel_id=1, source_target_pairs={{0,8},{2,10},{4,12},{6,14},{8,0},{10,2},{12,4},{14,6},{16,24},{18,... | collective-permute-start | bytes 1769480 | tf_op jit(solution)/shard_map/ppermute | solution.py:417
  313.8 46.3 %collective-permute-start.23 = (f32[192,768]{1,0:T(8,128)}, f32[192,768]{1,0:T(8,128)}, u32[]{:S(2)}, u32[]{:S(2)}) collective-permute-start(f32[192,768]{1,0:T(8,128)} %constant_dynamic-slice_fusion.8), channel_id=1, source_target_pairs={{0,2},{2,0},{4,6},{6,4},{8,10},{10,8},{12,14},{14,12},{16,18},{18,... | collective-permute-start | bytes 1769480 | tf_op jit(solution)/shard_map/ppermute | solution.py:417
  316.6 46.8 %collective-permute-start.22 = (f32[1152,384]{1,0:T(8,128)}, f32[1152,384]{1,0:T(8,128)}, u32[]{:S(2)}, u32[]{:S(2)}) collective-permute-start(f32[1152,384]{1,0:T(8,128)} %constant_dynamic-slice_fusion.9), channel_id=1, source_target_pairs={{0,2},{2,0},{4,6},{6,4},{8,10},{10,8},{12,14},{14,12},{16,18},{18,... | collective-permute-start | bytes 5308424 | tf_op jit(solution)/shard_map/ppermute | solution.py:417
  320.2 41.3 %collective-permute-start.25 = (f32[96,768]{1,0:T(8,128)}, f32[96,768]{1,0:T(8,128)S(1)}, u32[]{:S(2)}, u32[]{:S(2)}) collective-permute-start(f32[96,768]{1,0:T(8,128)} %constant_dynamic-slice_fusion.6), channel_id=1, source_target_pairs={{0,16},{2,18},{4,20},{6,22},{8,24},{10,26},{12,28},{14,30},{16,0},... | collective-permute-start | bytes 884744 | tf_op jit(solution)/shard_map/ppermute | solution.py:417
  321.0 41.2 %collective-permute-start.24 = (f32[48,1536]{1,0:T(8,128)}, f32[48,1536]{1,0:T(8,128)}, u32[]{:S(2)}, u32[]{:S(2)}) collective-permute-start(f32[48,1536]{1,0:T(8,128)} %constant_dynamic-slice_fusion.7), channel_id=1, source_target_pairs={{0,16},{2,18},{4,20},{6,22},{8,24},{10,26},{12,28},{14,30},{16,0},... | collective-permute-start | bytes 884744 | tf_op jit(solution)/shard_map/ppermute | solution.py:417
  365.2 9.8 %collective-permute-start.37 = (f32[96,768]{1,0:T(8,128)S(1)}, f32[96,768]{1,0:T(8,128)S(1)}, u32[]{:S(2)}, u32[]{:S(2)}) collective-permute-start(f32[96,768]{1,0:T(8,128)S(1)} %constant_dynamic-slice_fusion.2), channel_id=1, source_target_pairs={{0,8},{2,10},{4,12},{6,14},{8,0},{10,2},{12,4},{14,6},{16,24},{18,... | collective-permute-start | bytes 884744 | tf_op jit(solution)/shard_map/ppermute | solution.py:417
  365.3 23.3 %collective-permute-start.48 = (f32[96,768]{1,0:T(8,128)S(1)}, f32[96,768]{1,0:T(8,128)S(1)}, u32[]{:S(2)}, u32[]{:S(2)}) collective-permute-start(f32[96,768]{1,0:T(8,128)S(1)} %copy-done.19), channel_id=1, source_target_pairs={{0,16},{2,18},{4,20},{6,22},{8,24},{10,26},{12,28},{14,30},{16,0},... | collective-permute-start | bytes 884744 | tf_op jit(solution)/shard_map/ppermute | solution.py:417
  365.4 31.2 %collective-permute-start.44 = (f32[48,1536]{1,0:T(8,128)S(1)}, f32[48,1536]{1,0:T(8,128)S(1)}, u32[]{:S(2)}, u32[]{:S(2)}) collective-permute-start(f32[48,1536]{1,0:T(8,128)S(1)} %dynamic-slice_add_fusion.12), channel_id=1, source_target_pairs={{0,16},{2,18},{4,20},{6,22},{8,24},{10,26},{12,28},{14,30},{16,0},... | collective-permute-start | bytes 884744 | tf_op jit(solution)/shard_map/ppermute | solution.py:417
  368.4 41.3 %collective-permute-start.30 = (f32[576,384]{1,0:T(8,128)S(1)}, f32[576,384]{1,0:T(8,128)S(1)}, u32[]{:S(2)}, u32[]{:S(2)}) collective-permute-start(f32[576,384]{1,0:T(8,128)S(1)} %constant_dynamic-slice_fusion.5), channel_id=1, source_target_pairs={{0,4},{2,6},{4,0},{6,2},{8,12},{10,14},{12,8},{14,10},{16,20},{18,... | collective-permute-start | bytes 2654216 | tf_op jit(solution)/shard_map/ppermute | solution.py:417
  375.1 15.2 %collective-permute-start.38 = (f32[48,768]{1,0:T(8,128)S(1)}, f32[48,768]{1,0:T(8,128)S(1)}, u32[]{:S(2)}, u32[]{:S(2)}) collective-permute-start(f32[48,768]{1,0:T(8,128)S(1)} %constant_dynamic-slice_fusion.1), channel_id=1, source_target_pairs={{0,4},{2,6},{4,0},{6,2},{8,12},{10,14},{12,8},{14,10},{16,20},{18,... | collective-permute-start | bytes 442376 | tf_op jit(solution)/shard_map/ppermute | solution.py:417
  390.3 6.2 %collective-permute-start.39 = (f32[24,768]{1,0:T(8,128)S(1)}, f32[24,768]{1,0:T(8,128)S(1)}, u32[]{:S(2)}, u32[]{:S(2)}) collective-permute-start(f32[24,768]{1,0:T(8,128)S(1)} %constant_dynamic-slice_fusion), channel_id=1, source_target_pairs={{0,16},{2,18},{4,20},{6,22},{8,24},{10,26},{12,28},{14,30},{16,0},... | collective-permute-start | bytes 221192 | tf_op jit(solution)/shard_map/ppermute | solution.py:417
  390.4 17.0 %collective-permute-start.49 = (f32[192,768]{1,0:T(8,128)S(1)}, f32[192,768]{1,0:T(8,128)S(1)}, u32[]{:S(2)}, u32[]{:S(2)}) collective-permute-start(f32[192,768]{1,0:T(8,128)S(1)} %pad_maximum_fusion.13), channel_id=1, source_target_pairs={{0,4},{2,6},{4,0},{6,2},{8,12},{10,14},{12,8},{14,10},{16,20},{18,... | collective-permute-start | bytes 1769480 | tf_op jit(solution)/shard_map/ppermute | solution.py:417
  396.5 5.5 %collective-permute-start.40 = (f32[24,768]{1,0:T(8,128)S(1)}, f32[24,768]{1,0:T(8,128)S(1)}, u32[]{:S(2)}, u32[]{:S(2)}) collective-permute-start(f32[24,768]{1,0:T(8,128)S(1)} %dynamic-slice_add_fusion.15), channel_id=1, source_target_pairs={{0,16},{2,18},{4,20},{6,22},{8,24},{10,26},{12,28},{14,30},{16,0},... | collective-permute-start | bytes 221192 | tf_op jit(solution)/shard_map/ppermute | solution.py:417
  402.1 5.2 collective-permute-start.41
  402.3 16.3 %collective-permute-start.45 = (f32[96,1536]{1,0:T(8,128)S(1)}, f32[96,1536]{1,0:T(8,128)S(1)}, u32[]{:S(2)}, u32[]{:S(2)}) collective-permute-start(f32[96,1536]{1,0:T(8,128)S(1)} %pad_maximum_fusion.12), channel_id=1, source_target_pairs={{0,8},{2,10},{4,12},{6,14},{8,0},{10,2},{12,4},{14,6},{16,24},{18,... | collective-permute-start | bytes 1769480 | tf_op jit(solution)/shard_map/ppermute | solution.py:417
  407.4 61.8 %collective-permute-start.42 = (f32[96,768]{1,0:T(8,128)S(1)}, f32[96,768]{1,0:T(8,128)S(1)}, u32[]{:S(2)}, u32[]{:S(2)}) collective-permute-start(f32[96,768]{1,0:T(8,128)S(1)} %pad_maximum_fusion.15), channel_id=1, source_target_pairs={{0,8},{2,10},{4,12},{6,14},{8,0},{10,2},{12,4},{14,6},{16,24},{18,... | collective-permute-start | bytes 884744 | tf_op jit(solution)/shard_map/ppermute | solution.py:417
  407.6 69.7 %collective-permute-start.50 = (f32[384,768]{1,0:T(8,128)S(1)}, f32[384,768]{1,0:T(8,128)S(1)}, u32[]{:S(2)}, u32[]{:S(2)}) collective-permute-start(f32[384,768]{1,0:T(8,128)S(1)} %pad_maximum_fusion.9), channel_id=1, source_target_pairs={{0,8},{2,10},{4,12},{6,14},{8,0},{10,2},{12,4},{14,6},{16,24},{18,... | collective-permute-start | bytes 3538952 | tf_op jit(solution)/shard_map/ppermute | solution.py:417
  409.9 46.0 %collective-permute-start.31 = (f32[288,384]{1,0:T(8,128)S(1)}, f32[288,384]{1,0:T(8,128)S(1)}, u32[]{:S(2)}, u32[]{:S(2)}) collective-permute-start(f32[288,384]{1,0:T(8,128)S(1)} %constant_dynamic-slice_fusion.4), channel_id=1, source_target_pairs={{0,8},{2,10},{4,12},{6,14},{8,0},{10,2},{12,4},{14,6},{16,24},{18,... | collective-permute-start | bytes 1327112 | tf_op jit(solution)/shard_map/ppermute | solution.py:417
  456.0 13.1 %collective-permute-start.32 = (f32[144,384]{1,0:T(8,128)S(1)}, f32[144,384]{1,0:T(8,128)S(1)}, u32[]{:S(2)}, u32[]{:S(2)}) collective-permute-start(f32[144,384]{1,0:T(8,128)S(1)} %constant_dynamic-slice_fusion.3), channel_id=1, source_target_pairs={{0,16},{2,18},{4,20},{6,22},{8,24},{10,26},{12,28},{14,30},{16,0},... | collective-permute-start | bytes 663560 | tf_op jit(solution)/shard_map/ppermute | solution.py:417
  456.4 22.6 %collective-permute-start.46 = (f32[192,1536]{1,0:T(8,128)S(1)}, f32[192,1536]{1,0:T(8,128)S(1)}, u32[]{:S(2)}, u32[]{:S(2)}) collective-permute-start(f32[192,1536]{1,0:T(8,128)S(1)} %pad_maximum_fusion.8), channel_id=1, source_target_pairs={{0,4},{2,6},{4,0},{6,2},{8,12},{10,14},{12,8},{14,10},{16,20},{18,... | collective-permute-start | bytes 3538952 | tf_op jit(solution)/shard_map/ppermute | solution.py:417
  469.1 8.1 %collective-permute-start.33 = (f32[144,384]{1,0:T(8,128)S(1)}, f32[144,384]{1,0:T(8,128)S(1)}, u32[]{:S(2)}, u32[]{:S(2)}) collective-permute-start(f32[144,384]{1,0:T(8,128)S(1)} %dynamic-slice_add_fusion.13), channel_id=1, source_target_pairs={{0,16},{2,18},{4,20},{6,22},{8,24},{10,26},{12,28},{14,30},{16,0},... | collective-permute-start | bytes 663560 | tf_op jit(solution)/shard_map/ppermute | solution.py:417
  469.3 8.1 %copy-start.15 = (f32[96,768]{1,0:T(8,128)}, f32[96,768]{1,0:T(8,128)S(1)}, u32[]{:S(2)}) copy-start(f32[96,768]{1,0:T(8,128)S(1)} %get-tuple-element.136) | copy-start | bytes 884740
  469.3 8.2 %copy-start.14 = (f32[96,768]{1,0:T(8,128)}, f32[96,768]{1,0:T(8,128)S(1)}, u32[]{:S(2)}) copy-start(f32[96,768]{1,0:T(8,128)S(1)} %get-tuple-element.135) | copy-start | bytes 884740
  470.2 47.8 %collective-permute-start.43 = (f32[192,768]{1,0:T(8,128)}, f32[192,768]{1,0:T(8,128)}, u32[]{:S(2)}, u32[]{:S(2)}) collective-permute-start(f32[192,768]{1,0:T(8,128)} %pad_maximum_fusion.11), channel_id=1, source_target_pairs={{0,2},{2,0},{4,6},{6,4},{8,10},{10,8},{12,14},{14,12},{16,18},{18,... | collective-permute-start | bytes 1769480 | tf_op jit(solution)/shard_map/ppermute | solution.py:417
  477.2 8.5 %collective-permute-start.34 = (f32[288,384]{1,0:T(8,128)S(1)}, f32[288,384]{1,0:T(8,128)S(1)}, u32[]{:S(2)}, u32[]{:S(2)}) collective-permute-start(f32[288,384]{1,0:T(8,128)S(1)} %pad_maximum_fusion.14), channel_id=1, source_target_pairs={{0,8},{2,10},{4,12},{6,14},{8,0},{10,2},{12,4},{14,6},{16,24},{18,... | collective-permute-start | bytes 1327112 | tf_op jit(solution)/shard_map/ppermute | solution.py:417
  479.1 43.2 %collective-permute-start.51 = (f32[768,768]{1,0:T(8,128)}, f32[768,768]{1,0:T(8,128)}, u32[]{:S(2)}, u32[]{:S(2)}) collective-permute-start(f32[768,768]{1,0:T(8,128)} %pad_maximum_fusion.4), channel_id=1, source_target_pairs={{0,2},{2,0},{4,6},{6,4},{8,10},{10,8},{12,14},{14,12},{16,18},{18,... | collective-permute-start | bytes 7077896 | tf_op jit(solution)/shard_map/ppermute | solution.py:417
  481.0 6.8 %copy-start.24 = (f32[8,768]{1,0:T(8,128)S(1)}, f32[8,768]{1,0:T(8,128)}, u32[]{:S(2)}) copy-start(f32[8,768]{1,0:T(8,128)} %get-tuple-element.98) | copy-start | bytes 73732
  481.0 6.8 %copy-start.23 = (f32[8,768]{1,0:T(8,128)S(1)}, f32[8,768]{1,0:T(8,128)}, u32[]{:S(2)}) copy-start(f32[8,768]{1,0:T(8,128)} %get-tuple-element.99) | copy-start | bytes 73732
  481.0 45.8 %collective-permute-start.47 = (f32[384,1536]{1,0:T(8,128)}, f32[384,1536]{1,0:T(8,128)}, u32[]{:S(2)}, u32[]{:S(2)}) collective-permute-start(f32[384,1536]{1,0:T(8,128)} %pad_maximum_fusion.3), channel_id=1, source_target_pairs={{0,2},{2,0},{4,6},{6,4},{8,10},{10,8},{12,14},{14,12},{16,18},{18,... | collective-permute-start | bytes 7077896 | tf_op jit(solution)/shard_map/ppermute | solution.py:417
  487.5 32.9 %collective-permute-start.35 = (f32[576,384]{1,0:T(8,128)}, f32[576,384]{1,0:T(8,128)}, u32[]{:S(2)}, u32[]{:S(2)}) collective-permute-start(f32[576,384]{1,0:T(8,128)} %pad_maximum_fusion.10), channel_id=1, source_target_pairs={{0,4},{2,6},{4,0},{6,2},{8,12},{10,14},{12,8},{14,10},{16,20},{18,... | collective-permute-start | bytes 2654216 | tf_op jit(solution)/shard_map/ppermute | solution.py:417
  487.9 1.3 collective-permute-start.26
  489.2 17.1 %collective-permute-start.27 = (f32[16,768]{1,0:T(8,128)S(1)}, f32[16,768]{1,0:T(8,128)S(1)}, u32[]{:S(2)}, u32[]{:S(2)}) collective-permute-start(f32[16,768]{1,0:T(8,128)S(1)} %add.242), channel_id=1, source_target_pairs={{0,4},{2,6},{4,0},{6,2},{8,12},{10,14},{12,8},{14,10},{16,20},{18,... | collective-permute-start | bytes 147464 | tf_op jit(solution)/shard_map/ppermute | solution.py:417
  506.2 4.2 collective-permute-start.28
  511.0 5.5 %collective-permute-start.29 = (f32[16,768]{1,0:T(8,128)}, f32[16,768]{1,0:T(8,128)}, u32[]{:S(2)}, u32[]{:S(2)}) collective-permute-start(f32[16,768]{1,0:T(8,128)} %add.244), channel_id=1, source_target_pairs={{0,16},{2,18},{4,20},{6,22},{8,24},{10,26},{12,28},{14,30},{16,0},... | collective-permute-start | bytes 147464 | tf_op jit(solution)/shard_map/ppermute | solution.py:417
  522.2 9.2 %collective-permute-start.36 = (f32[1152,384]{1,0:T(8,128)S(1)}, f32[1152,384]{1,0:T(8,128)S(1)}, u32[]{:S(2)}, u32[]{:S(2)}) collective-permute-start(f32[1152,384]{1,0:T(8,128)S(1)} %pad_maximum_fusion.6), channel_id=1, source_target_pairs={{0,2},{2,0},{4,6},{6,4},{8,10},{10,8},{12,14},{14,12},{16,18},{18,... | collective-permute-start | bytes 5308424 | tf_op jit(solution)/shard_map/ppermute | solution.py:417
  (17 other events, 32.1 us)

commit v3 on v2

--- a/solution.py
+++ b/solution.py
@@ -1,7 +1,7 @@
 import jax
 import jax.numpy as jnp
 from jax import lax
-from jax.sharding import Mesh, PartitionSpec as P
+from jax.sharding import PartitionSpec as P
 from jax.experimental import pallas as pl
 from jax.experimental.pallas import tpu as pltpu
 
@@ -20,14 +20,6 @@
 
 NT = ((1,), (1,))
 TN = ((0,), (0,))
-
-
-def rows_of(counts, samples):
-    starts, total = [], 0
-    for s in range(samples):
-        starts.append(total)
-        total = total + ((counts[s] + 15) // 16) * 16
-    return starts, total
 
 
 def win(start, size=SLOTS):
@@ -125,6 +117,7 @@
             qkv[win(n * TILE), :] = jnp.zeros((TILE, qkv.shape[1]), bf16)
             attend_rows(counts, qkv, o, lse, samples, width)
             o[win(total), :] = jnp.zeros((TILE, width), bf16)
+
     return body
 
 
@@ -153,6 +146,7 @@
             return x
 
         lax.fori_loop(0, n, tail, 0)
+
     return body
 
 
@@ -190,6 +184,7 @@
             return x
 
         lax.fori_loop(0, n, tile, 0)
+
     return body
 
 
@@ -225,6 +220,7 @@
             return start + ((counts[s] + 15) // 16) * 16
 
         lax.fori_loop(0, samples, scatter, 0)
+
     return body
 
 
@@ -290,6 +286,7 @@
             return x
 
         lax.fori_loop(0, n, last, 0)
+
     return body
 
 
@@ -325,6 +322,7 @@
             return start + ((counts[s] + 15) // 16) * 16
 
         lax.fori_loop(0, samples, scatter, 0)
+
     return body
 
 
@@ -332,11 +330,10 @@
     return jax.ShapeDtypeStruct(shape, dtype)
 
 
-def call(body, name, counts, args, outs, scratch=(), flops=0):
+def call(body, counts, args, outs, scratch=(), flops=0):
     moved = sum(x.size * x.dtype.itemsize for x in list(args) + list(outs))
     return pl.pallas_call(
         body,
-        name=name,
         out_shape=list(outs),
         grid_spec=pltpu.PrefetchScalarGridSpec(
             num_scalar_prefetch=1,
@@ -384,33 +381,33 @@
     TP, D = a.shape
     width = weight.shape[1] // 3
     outs = [sds((TP, 3 * width), bf16), sds((TP, width), bf16), sds((S, width // HD, SLOTS), f32), sds((TP, D), f32), sds((TP, D), bf16)]
-    return call(fwd_other_body(S, width), "fwd_other", counts, [a, h, o, weight, out_own, out_other, gain, shift], outs, flops=7 * 10**9)
+    return call(fwd_other_body(S, width), counts, [a, h, o, weight, out_own, out_other, gain, shift], outs, flops=7 * 10**9)
 
 
 def mlp_own(counts, c, dm, up, down, S):
     TP, D = c.shape
     outs = [sds((TP, D), f32), sds((TP, D), f32), sds(up.shape, f32), sds(down.shape, f32)]
-    return call(mlp_own_body(S), "mlp_own", counts, [c, dm, up, down], outs, flops=18 * 10**9)
+    return call(mlp_own_body(S), counts, [c, dm, up, down], outs, flops=18 * 10**9)
 
 
 def mlp_other(counts, line, c, dm, up, down, m, dc, r, gain, S, L):
     TP, D = c.shape
     outs = [sds((S, L, D), bf16), sds((TP, D), f32), sds((8, D), f32)]
-    return call(mlp_other_body(S, L), "mlp_other", counts, [line, c, dm, up, down, m, dc, r, gain], outs, [pltpu.VMEM((TP, D), bf16)], flops=12 * 10**9)
+    return call(mlp_other_body(S, L), counts, [line, c, dm, up, down, m, dc, r, gain], outs, [pltpu.VMEM((TP, D), bf16)], flops=12 * 10**9)
 
 
 def attn_own(counts, dr, qkv, lse, o, a, wout, wqkv, S):
     TP, D = a.shape
     width = wout.shape[0]
     outs = [sds((TP, D), f32), sds(wout.shape, f32), sds((3, D, width), f32)]
-    return call(attn_own_body(S, width), "attn_own", counts, [dr, qkv, lse, o, a, wout, wqkv], outs, [pltpu.VMEM((TP, width), bf16), pltpu.VMEM((TP, 3 * width), bf16)], flops=9 * 10**9)
+    return call(attn_own_body(S, width), counts, [dr, qkv, lse, o, a, wout, wqkv], outs, [pltpu.VMEM((TP, width), bf16), pltpu.VMEM((TP, 3 * width), bf16)], flops=9 * 10**9)
 
 
 def attn_other(counts, line, dr, qkv, lse, wout, wqkv, da, h, gain, S, L):
     TP, D = h.shape
     width = wout.shape[0]
     outs = [sds((S, L, D), bf16), sds((8, D), f32)]
-    return call(attn_other_body(S, width, L), "attn_other", counts, [line, dr, qkv, lse, wout, wqkv, da, h, gain], outs, [pltpu.VMEM((TP, width), bf16), pltpu.VMEM((TP, 3 * width), bf16), pltpu.VMEM((TP, D), bf16)], flops=8 * 10**9)
+    return call(attn_other_body(S, width, L), counts, [line, dr, qkv, lse, wout, wqkv, da, h, gain], outs, [pltpu.VMEM((TP, width), bf16), pltpu.VMEM((TP, 3 * width), bf16), pltpu.VMEM((TP, D), bf16)], flops=8 * 10**9)
 
 
 def swap(x, axis, size, bit):
@@ -428,7 +425,7 @@
         for i in range(4):
             refs[4][pl.ds(pl.multiple_of(where[i] * rows, 16), rows), :] = refs[i][...].astype(bf16)
 
-    return call(body, "cast_pieces", order, pieces, [sds((4 * rows, cols), bf16)])[0]
+    return call(body, order, pieces, [sds((4 * rows, cols), bf16)])[0]
 
 
 def side(bit):
@@ -489,9 +486,10 @@
     aq, ao = swap(fq, "dp", dp, 2), swap(fo, "dp", dp, 2)
     fu, fd = swap(pu, "tensor", 2, 1), swap(pd, "tensor", 2, 1)
     wq1, wo1 = rest(fq, aq), rest(fo, ao)
-    qkv1, o1, lse1, r, c = fwd_other(counts, a, h, o0, wq1, wo, wo1, g2, b2, S)
+    qkv1, _, lse1, r, c = fwd_other(counts, a, h, o0, wq1, wo, wo1, g2, b2, S)
     fu, fd, c = tie(fu, fd, c)
-    au, ad = swap(fu, "dp", dp, 2), swap(fd, "dp", dp, 2)
+    au = swap(fu, "dp", dp, 2)
+    ad = swap(fd, "dp", dp, 2)
     m, dc, gup, gdown = mlp_own(counts, c, dm, wu, wd, S)
     au, ad, m = tie(au, ad, m)
     wu1, wd1 = rest(fu, au), rest(fd, ad)
@@ -504,15 +502,21 @@
     da, gout, gqkv = attn_own(counts, dr, qkv0, lse0, o0, a, wo, wq, S)
     A, B, da = tie(A, B, da)
     A, B = folds(A, along[3:], dp), folds(B, other[3:], dp)
-    C, E = fold(gqkv.reshape(3 * D, -1), 1, dp), fold(gout, 1, dp)
+    C = gqkv.reshape(2, (3 * D) // 2, -1)
+    C, F, E = fold(C[0], 1, dp), fold(C[1], 1, dp), fold(gout, 1, dp)
     gin, gg1 = attn_other(counts, line, dr, qkv1, lse1, wo1, wq1, da, h, g1, S, L)
-    C, E, A, B, gg1 = tie(C, E, A, B, gg1)
+    C, F, E, A, B, gg1 = tie(C, F, E, A, B, gg1)
     small = jnp.concatenate([gg1, gg2], 0)
-    for bit in every:
+    for bit, late in zip(reversed(along), reversed(other)):
+        A, B = spread(A, bit, dp), spread(B, late, dp)
         small = small + swap(small, "dp", dp, bit)
+        if bit != 1:
+            A, B, small = tie(A, B, small)
+    gup, gdown = A, B
     gg1, gg2 = small[:8], small[8:]
-    gup, gdown = spreads(A, along, dp), spreads(B, other, dp)
-    gqkv = spreads(folds(C, along[1:], dp), along, dp).reshape(3, D, -1)
+    C = spreads(folds(C, along[1:], dp), along, dp)
+    F = spreads(folds(F, other[1:], dp), other, dp)
+    gqkv = jnp.concatenate([C, F], 0).reshape(3, D, -1)
     gout = spreads(folds(E, other[1:], dp), other, dp)
     return (out, gin, gg1[0], gg1[1], gqkv.transpose(1, 0, 2), gout, gg2[0], gg2[1], gup, gdown)
 
@@ -521,4 +525,8 @@
     dp = mesh.shape["dp"]
     placed = (P("dp", None, None), P("dp"), P("dp", None), P(), P(), P(None, None, "tensor"), P("tensor", None), P(), P(), P(None, "tensor"), P("tensor", None), P("dp", None, None))
     outs = (P("dp", None, None), P("dp", None, None), P(), P(), P(None, None, "tensor"), P("tensor", None), P(), P(), P(None, "tensor"), P("tensor", None))
-    return jax.shard_map(lambda *a: shards(dp, *a), mesh=mesh, in_specs=placed, out_specs=outs, check_vma=False)
+
+    def layer(*a):
+        return shards(dp, *a)
+
+    return jax.shard_map(layer, mesh=mesh, in_specs=placed, out_specs=outs, check_vma=False)

time: 533 us -> 511 us (0.959)
  waiting for transfers between devices: 213 us -> 172 us
  starting transfers between devices: 31.1 us -> 59.4 us
  Pallas kernels: 213 us -> 200 us
    ppermute x52 -> x60, waiting for transfers between devices: 213 us -> 172 us  [swap(): return lax.ppermute(x, axis, [(k, k ^ bit) for k in range(size)])]
    ppermute x52 -> x60, starting transfers between devices: 31.1 us -> 59.4 us  [swap(): return lax.ppermute(x, axis, [(k, k ^ bit) for k in range(size)])]
    pallas_call x9, Pallas kernels: 186 us -> 174 us  [call(): pl.pallas_call(body, out_shape=list(outs), grid_spec=pltpu.PrefetchScalar...]
    concatenate x16 -> x18, other arithmetic: 13.7 us -> 11 us  [spread(): jnp.concatenate([jnp.where(first, x, got), jnp.where(first, got, x)], 0)]
    add x16 -> x20, other arithmetic: 15.7 us -> 16.9 us  [fold(): return half(x, i) + swap(half(x, 1 - i), 'dp', dp, bit)]
    dynamic_slice x16 -> x20, local copies, waits for them, and re-layouts: 16.2 us -> 16.2 us  [half(): return lax.dynamic_slice_in_dim(x, i * n, n, 0)]
  transfers between devices with their start and end apart: 52 -> 60, of which waited for: 20 -> 21; matrix products, arithmetic and copies ran while one was open for 11% -> 12% of each run, Pallas kernels for 33% -> 33%
where the time goes in v3:
time: 511 us; the launch traced here: 510 us
  Pallas kernels  200 us (39%)
  waiting for transfers between devices  172 us (34%)
  starting transfers between devices  59.4 us (12%)
  other arithmetic  47.4 us (9%)
  local copies, waits for them, and re-layouts  29.2 us (6%)
    pallas_call x9, Pallas kernels, call(): pl.pallas_call(body, out_shape=list(outs), grid_spec=pltpu.PrefetchScalar...  174 us
    ppermute x60, waiting for transfers between devices, swap(): return lax.ppermute(x, axis, [(k, k ^ bit) for k in range(size)])  172 us
    ppermute x60, starting transfers between devices, swap(): return lax.ppermute(x, axis, [(k, k ^ bit) for k in range(size)])  59.4 us
    pallas_call x1, Pallas kernels, fwd_own(): pl.pallas_call(fwd_own_body(S, width), name='fwd_own', out_shape=outs, gr...  26 us
    add x20, other arithmetic, fold(): return half(x, i) + swap(half(x, 1 - i), 'dp', dp, bit)  16.9 us
    dynamic_slice x20, local copies, waits for them, and re-layouts, half(): return lax.dynamic_slice_in_dim(x, i * n, n, 0)  16.2 us
    concatenate x18, other arithmetic, spread(): jnp.concatenate([jnp.where(first, x, got), jnp.where(first, got, x)], 0)  11 us
  transfers between devices with their start and end apart: 60, of which 21 were waited for; matrix products, arithmetic and copies ran while one was open for 12% of the time, Pallas kernels for 33%

profile of v3, /device:TPU:0, one launch (start us, length us, event | category | flops | bytes accessed | tf_op | source)
XLA Modules:
  0.0 510.0 jit_solution(9197879748566211046)
XLA Ops:
  0.7 2.4 slice_bitcast_fusion.2
  5.4 3.0 collective-permute-start
  8.4 1.7 dynamic-slice_convert_fusion.3
  10.6 1.7 copy.22.col
  12.9 26.0 %fwd_own.1 = (bf16[1792,768]{1,0:T(8,128)(2,1)}, bf16[1792,768]{1,0:T(8,128)(2,1)}, bf16[1792,768]{1,0:T(8,128)(2,1)}, bf16[1792,1152]{1,0:T(8,128)(2,1)}, bf16[...) custom-call(s32[6]{0:T(128)} %counts.11, s32[6,512,1]{2,1,0:T(8,128)} %copy.22.col, bf16[6,512,768]{2,1,0:T(8,128)(2,1)} %patches.1, ...), custom_call_target="tpu_custom_call" | custom-call | flops 6000000000 | bytes 26214400 | tf_op jit(solution)/shard_map/fwd_own/pallas_call | solution.py:358
  38.9 2.2 dynamic-slice_convert_fusion
  41.1 2.2 dynamic-slice_convert_fusion.1
  43.3 2.0 collective-permute-start.4
  45.3 19.4 %collective-permute-done.4.refs_1_ = f32[192,1152]{1,0:T(8,128)} collective-permute-done((f32[192,1152]{1,0:T(8,128)}, f32[192,1152]{1,0:T(8,128)}, u32[]{:S(2)}, u32[]{:S(2)}) %collective-permute-start.4) | collective-permute-done | bytes 884768 | tf_op jit(solution)/shard_map/ppermute | solution.py:414
  64.7 1.7 collective-permute-start.7
  66.7 1.5 collective-permute-start.2
  68.2 6.1 %collective-permute-done.7.refs_1_ = f32[96,768]{1,0:T(8,128)S(1)} collective-permute-done((f32[96,768]{1,0:T(8,128)}, f32[96,768]{1,0:T(8,128)S(1)}, u32[]{:S(2)}, u32[]{:S(2)}) %collective-permute-start.7) | collective-permute-done | bytes 294944 | tf_op jit(solution)/shard_map/ppermute | solution.py:414
  74.3 1.5 collective-permute-start.3
  77.7 2.8 shard_map.196.out_other.wout
  80.5 4.0 shard_map.195.weight.wqkv
  84.5 24.6 %shard_map.197 = (bf16[1792,1152]{1,0:T(8,128)(2,1)}, bf16[1792,384]{1,0:T(8,128)(2,1)}, f32[6,6,256]{2,1,0:T(8,128)}, f32[1792,768]{1,0:T(8,128)}, bf16[1792,768]{1,0:T(8,128)(2,1)}) custom-call(s32[6]{0:T(128)} %counts.11, bf16[1792,768]{1,0:T(8,128)(2,1)} %get-tuple-element.70.a, bf16[1792,768]{1,0:T(8,128)(2,1)} %get-tuple-element.71.h, ...), custom_call_target="tpu_custom_call" | custom-call | flops 7000000000 | bytes 23635968 | tf_op jit(solution)/shard_map/pallas_call | solution.py:335
  109.2 11.2 %collective-permute-done.3.refs_0_ = f32[384,768]{1,0:T(8,128)} collective-permute-done((f32[384,768]{1,0:T(8,128)}, f32[384,768]{1,0:T(8,128)}, u32[]{:S(2)}, u32[]{:S(2)}) %collective-permute-start.3) | collective-permute-done | bytes 1179680 | tf_op jit(solution)/shard_map/ppermute | solution.py:414
  120.4 32.0 %shard_map.198 = (f32[1792,768]{1,0:T(8,128)}, f32[1792,768]{1,0:T(8,128)}, f32[768,1536]{1,0:T(8,128)}, f32[1536,768]{1,0:T(8,128)}) custom-call(s32[6]{0:T(128)} %counts.11, bf16[1792,768]{1,0:T(8,128)(2,1)} %get-tuple-element.80.c, bf16[1792,768]{1,0:T(8,128)(2,1)} %get-tuple-element.77.dm, bf16[768,1536]{1,0:T(8,128)(2,1)} %up.1, bf16[1536,768]{1,0:T(8,128)(2,1)} %down.1), custom_call_target="tpu_custom_call" | custom-call | flops 17999998976 | bytes 30670848 | tf_op jit(solution)/shard_map/pallas_call | solution.py:335
  152.4 3.2 constant_dynamic-slice_fusion.16
  155.6 3.2 constant_dynamic-slice_fusion.17
  159.7 1.7 collective-permute-start.13
  162.0 26.3 %collective-permute-done.12.refs_1_ = f32[192,1536]{1,0:T(8,128)} collective-permute-done((f32[192,1536]{1,0:T(8,128)S(1)}, f32[192,1536]{1,0:T(8,128)}, u32[]{:S(2)}, u32[]{:S(2)}) %collective-permute-start.12) | collective-permute-done | bytes 1179680 | tf_op jit(solution)/shard_map/ppermute | solution.py:414
  188.3 24.3 %collective-permute-done.13.refs_1_ = f32[384,768]{1,0:T(8,128)} collective-permute-done((f32[384,768]{1,0:T(8,128)}, f32[384,768]{1,0:T(8,128)}, u32[]{:S(2)}, u32[]{:S(2)}) %collective-permute-start.13) | collective-permute-done | bytes 1179680 | tf_op jit(solution)/shard_map/ppermute | solution.py:414
  213.2 2.2 dynamic-slice_add_fusion
  215.7 2.6 dynamic-slice_add_fusion.1
  219.5 1.6 collective-permute-start.19
  223.4 4.6 shard_map.200.down
  228.1 4.6 shard_map.199.up
  232.7 31.7 %shard_map.201 = (bf16[6,512,768]{2,1,0:T(8,128)(2,1)}, f32[1792,768]{1,0:T(8,128)}, f32[8,768]{1,0:T(8,128)}) custom-call(s32[6]{0:T(128)} %counts.11, s32[6,1,512]{2,1,0:T(1,128)} %broadcast_in_dim.18.line, bf16[1792,768]{1,0:T(8,128)(2,1)} %get-tuple-element.80.c, bf16[1792,768]{1,0:T(8,128)(2,1)} %get-tuple-element.77.dm, ...), custom_call_target="tpu_custom_call" | custom-call | flops 12000000000 | bytes 37002240 | tf_op jit(solution)/shard_map/pallas_call | solution.py:335
  264.4 1.9 dynamic-slice_add_fusion.2
  269.2 1.7 collective-permute-start.21
  271.8 35.4 %shard_map.202 = (f32[1792,768]{1,0:T(8,128)}, f32[384,768]{1,0:T(8,128)}, f32[3,768,384]{2,1,0:T(8,128)}) custom-call(s32[6]{0:T(128)} %counts.11, f32[1792,768]{1,0:T(8,128)} %get-tuple-element.93.dr, bf16[1792,1152]{1,0:T(8,128)(2,1)} %get-tuple-element.98.qkv, f32[6,6,256]{2,1,0:T(8,128)} %get-tuple-element.99.lse, ...), custom_call_target="tpu_custom_call" | custom-call | flops 8999999488 | bytes 26382336 | tf_op jit(solution)/shard_map/pallas_call | solution.py:335
  307.2 1.9 constant_dynamic-slice_fusion.11
  309.1 2.2 fusion
  318.1 2.9 collective-permute-start.25
  320.9 34.6 %shard_map.203 = (bf16[6,512,768]{2,1,0:T(8,128)(2,1)}, f32[8,768]{1,0:T(8,128)}) custom-call(s32[6]{0:T(128)} %counts.11, s32[6,1,512]{2,1,0:T(1,128)} %broadcast_in_dim.18.line, f32[1792,768]{1,0:T(8,128)} %get-tuple-element.93.dr, bf16[1792,1152]{1,0:T(8,128)(2,1)} %get-tuple-element.94.qkv, f32[6,6,256]{2,1,0:T(8,128)} %get-tuple-element.95.lse, ...), custom_call_target="tpu_custom_call" | custom-call | flops 8000000000 | bytes 25046016 | tf_op jit(solution)/shard_map/pallas_call | solution.py:335
  362.0 2.1 collective-permute-start.51
  364.2 2.9 collective-permute-start.28
  367.2 1.6 collective-permute-start.37
  368.8 3.8 collective-permute-done.29
  373.0 3.0 collective-permute-start.52
  376.0 18.4 %collective-permute-done.27 = f32[48,1536]{1,0:T(8,128)S(1)} collective-permute-done((f32[48,1536]{1,0:T(8,128)S(1)}, f32[48,1536]{1,0:T(8,128)S(1)}, u32[]{:S(2)}, u32[]{:S(2)}) %collective-permute-start.27) | collective-permute-done | bytes 294944 | tf_op jit(solution)/shard_map/ppermute | solution.py:414
  394.7 2.1 collective-permute-start.44
  396.7 2.5 collective-permute-done.32
  401.6 8.7 %collective-permute-done.44 = f32[288,384]{1,0:T(8,128)S(1)} collective-permute-done((f32[288,384]{1,0:T(8,128)S(1)}, f32[288,384]{1,0:T(8,128)S(1)}, u32[]{:S(2)}, u32[]{:S(2)}) %collective-permute-start.44) | collective-permute-done | bytes 442400 | tf_op jit(solution)/shard_map/ppermute | solution.py:414
  410.3 11.2 %collective-permute-done.53 = f32[24,768]{1,0:T(8,128)S(1)} collective-permute-done((f32[24,768]{1,0:T(8,128)S(1)}, f32[24,768]{1,0:T(8,128)S(1)}, u32[]{:S(2)}, u32[]{:S(2)}) %collective-permute-start.53) | collective-permute-done | bytes 73760 | tf_op jit(solution)/shard_map/ppermute | solution.py:414
  421.5 3.4 collective-permute-start.54
  425.1 2.2 collective-permute-done.54
  427.5 3.2 collective-permute-start.39
  431.1 1.7 collective-permute-start.46
  435.1 2.5 collective-permute-start.40
  437.6 2.0 collective-permute-done.46
  440.3 2.2 collective-permute-start.35
  442.5 1.6 collective-permute-start.34
  445.2 2.0 collective-permute-start.33
  447.5 2.9 collective-permute-start.41
  452.9 23.6 %collective-permute-done.41 = f32[144,384]{1,0:T(8,128)S(1)} collective-permute-done((f32[144,384]{1,0:T(8,128)S(1)}, f32[144,384]{1,0:T(8,128)S(1)}, u32[]{:S(2)}, u32[]{:S(2)}) %collective-permute-start.41) | collective-permute-done | bytes 221216 | tf_op jit(solution)/shard_map/ppermute | solution.py:414
  479.5 1.6 pad_maximum_fusion.4
  481.1 6.5 %collective-permute-done.42 = f32[288,384]{1,0:T(8,128)S(1)} collective-permute-done((f32[288,384]{1,0:T(8,128)S(1)}, f32[288,384]{1,0:T(8,128)S(1)}, u32[]{:S(2)}, u32[]{:S(2)}) %collective-permute-start.42) | collective-permute-done | bytes 442400 | tf_op jit(solution)/shard_map/ppermute | solution.py:414
  493.8 2.8 collective-permute-done.36
  499.9 2.0 pad_maximum_fusion.2
  501.9 2.7 broadcast_select_fusion.1
  504.6 2.5 pad_maximum_fusion.1
  507.5 2.5 pad_maximum_fusion
  (230 shorter events, 51.7 us)
Async XLA Ops:
  5.4 37.9 %collective-permute-start = (f32[192,1152]{1,0:T(8,128)}, f32[192,1152]{1,0:T(8,128)}, u32[]{:S(2)}, u32[]{:S(2)}) collective-permute-start(f32[192,1152]{1,0:T(8,128)} %dynamic-slice_convert_fusion.2), channel_id=1, source_target_pairs={{0,1},{1,0},{2,3},{3,2},{4,5},{5,4},{6,7},{7,6},{8,9},{9,8},{10,11... | collective-permute-start | bytes 2654216 | tf_op jit(solution)/shard_map/ppermute | solution.py:414
  10.1 33.2 %collective-permute-start.1 = (f32[96,768]{1,0:T(8,128)}, f32[96,768]{1,0:T(8,128)}, u32[]{:S(2)}, u32[]{:S(2)}) collective-permute-start(f32[96,768]{1,0:T(8,128)} %dynamic-slice_convert_fusion.3), channel_id=1, source_target_pairs={{0,1},{1,0},{2,3},{3,2},{4,5},{5,4},{6,7},{7,6},{8,9},{9,8},{10,11... | collective-permute-start | bytes 884744 | tf_op jit(solution)/shard_map/ppermute | solution.py:414
  38.9 37.0 %copy-start.30 = (f32[768]{0:T(1024)S(1)}, f32[768]{0:T(1024)}, u32[]{:S(2)}) copy-start(f32[768]{0:T(1024)} %param.19) | copy-start | bytes 9220
  38.9 37.6 %copy-start.31 = (f32[768]{0:T(1024)S(1)}, f32[768]{0:T(1024)}, u32[]{:S(2)}) copy-start(f32[768]{0:T(1024)} %param.20) | copy-start | bytes 9220
  43.3 21.4 %collective-permute-start.4 = (f32[192,1152]{1,0:T(8,128)}, f32[192,1152]{1,0:T(8,128)}, u32[]{:S(2)}, u32[]{:S(2)}) collective-permute-start(f32[192,1152]{1,0:T(8,128)} %collective-permute-done.refs_0_), channel_id=1, source_target_pairs={{0,4},{2,6},{4,0},{6,2},{8,12},{10,14},{12,8},{14,10},{16,20},{18,... | collective-permute-start | bytes 2654216 | tf_op jit(solution)/shard_map/ppermute | solution.py:414
  45.3 35.2 %collective-permute-start.5 = (f32[192,1152]{1,0:T(8,128)}, f32[192,1152]{1,0:T(8,128)}, u32[]{:S(2)}, u32[]{:S(2)}) collective-permute-start(f32[192,1152]{1,0:T(8,128)} %collective-permute-done.refs_0_), channel_id=1, source_target_pairs={{0,2},{2,0},{4,6},{6,4},{8,10},{10,8},{12,14},{14,12},{16,18},{18,... | collective-permute-start | bytes 2654216 | tf_op jit(solution)/shard_map/ppermute | solution.py:414
  64.7 15.8 %collective-permute-start.6 = (f32[192,1152]{1,0:T(8,128)}, f32[192,1152]{1,0:T(8,128)}, u32[]{:S(2)}, u32[]{:S(2)}) collective-permute-start(f32[192,1152]{1,0:T(8,128)} %collective-permute-done.4.refs_1_), channel_id=1, source_target_pairs={{0,2},{2,0},{4,6},{6,4},{8,10},{10,8},{12,14},{14,12},{16,18},{18,... | collective-permute-start | bytes 2654216 | tf_op jit(solution)/shard_map/ppermute | solution.py:414
  64.7 9.6 %collective-permute-start.7 = (f32[96,768]{1,0:T(8,128)}, f32[96,768]{1,0:T(8,128)S(1)}, u32[]{:S(2)}, u32[]{:S(2)}) collective-permute-start(f32[96,768]{1,0:T(8,128)} %collective-permute-done.1.refs_0_), channel_id=1, source_target_pairs={{0,4},{2,6},{4,0},{6,2},{8,12},{10,14},{12,8},{14,10},{16,20},{18,... | collective-permute-start | bytes 884744 | tf_op jit(solution)/shard_map/ppermute | solution.py:414
  66.4 9.4 %collective-permute-start.8 = (f32[96,768]{1,0:T(8,128)}, f32[96,768]{1,0:T(8,128)S(1)}, u32[]{:S(2)}, u32[]{:S(2)}) collective-permute-start(f32[96,768]{1,0:T(8,128)} %collective-permute-done.1.refs_0_), channel_id=1, source_target_pairs={{0,2},{2,0},{4,6},{6,4},{8,10},{10,8},{12,14},{14,12},{16,18},{18,... | collective-permute-start | bytes 884744 | tf_op jit(solution)/shard_map/ppermute | solution.py:414
  66.7 42.5 %collective-permute-start.2 = (f32[192,1536]{1,0:T(8,128)}, f32[192,1536]{1,0:T(8,128)S(1)}, u32[]{:S(2)}, u32[]{:S(2)}) collective-permute-start(f32[192,1536]{1,0:T(8,128)} %dynamic-slice_convert_fusion.1), channel_id=1, source_target_pairs={{0,1},{1,0},{2,3},{3,2},{4,5},{5,4},{6,7},{7,6},{8,9},{9,8},{10,11... | collective-permute-start | bytes 3538952 | tf_op jit(solution)/shard_map/ppermute | solution.py:414
  74.3 46.1 %collective-permute-start.3 = (f32[384,768]{1,0:T(8,128)}, f32[384,768]{1,0:T(8,128)}, u32[]{:S(2)}, u32[]{:S(2)}) collective-permute-start(f32[384,768]{1,0:T(8,128)} %dynamic-slice_convert_fusion), channel_id=1, source_target_pairs={{0,1},{1,0},{2,3},{3,2},{4,5},{5,4},{6,7},{7,6},{8,9},{9,8},{10,11... | collective-permute-start | bytes 3538952 | tf_op jit(solution)/shard_map/ppermute | solution.py:414
  75.8 1.9 collective-permute-start.9
  109.2 79.2 %copy-start.20 = (f32[192,1536]{1,0:T(8,128)}, f32[192,1536]{1,0:T(8,128)S(1)}, u32[]{:S(2)}) copy-start(f32[192,1536]{1,0:T(8,128)S(1)} %collective-permute-done.2.refs_0_) | copy-start | bytes 3538948
  155.6 57.0 %collective-permute-start.11 = (f32[768,768]{1,0:T(8,128)}, f32[768,768]{1,0:T(8,128)S(1)}, u32[]{:S(2)}, u32[]{:S(2)}) collective-permute-start(f32[768,768]{1,0:T(8,128)} %constant_dynamic-slice_fusion.16), channel_id=1, source_target_pairs={{0,2},{2,0},{4,6},{6,4},{8,10},{10,8},{12,14},{14,12},{16,18},{18,... | collective-permute-start | bytes 7077896 | tf_op jit(solution)/shard_map/ppermute | solution.py:414
  158.9 56.5 %collective-permute-start.10 = (f32[384,1536]{1,0:T(8,128)}, f32[384,1536]{1,0:T(8,128)}, u32[]{:S(2)}, u32[]{:S(2)}) collective-permute-start(f32[384,1536]{1,0:T(8,128)} %constant_dynamic-slice_fusion.17), channel_id=1, source_target_pairs={{0,2},{2,0},{4,6},{6,4},{8,10},{10,8},{12,14},{14,12},{16,18},{18,... | collective-permute-start | bytes 7077896 | tf_op jit(solution)/shard_map/ppermute | solution.py:414
  159.4 28.9 %collective-permute-start.12 = (f32[192,1536]{1,0:T(8,128)S(1)}, f32[192,1536]{1,0:T(8,128)}, u32[]{:S(2)}, u32[]{:S(2)}) collective-permute-start(f32[192,1536]{1,0:T(8,128)S(1)} %collective-permute-done.2.refs_0_), channel_id=1, source_target_pairs={{0,4},{2,6},{4,0},{6,2},{8,12},{10,14},{12,8},{14,10},{16,20},{18,... | collective-permute-start | bytes 3538952 | tf_op jit(solution)/shard_map/ppermute | solution.py:414
  159.7 53.0 %collective-permute-start.13 = (f32[384,768]{1,0:T(8,128)}, f32[384,768]{1,0:T(8,128)}, u32[]{:S(2)}, u32[]{:S(2)}) collective-permute-start(f32[384,768]{1,0:T(8,128)} %collective-permute-done.3.refs_0_), channel_id=1, source_target_pairs={{0,4},{2,6},{4,0},{6,2},{8,12},{10,14},{12,8},{14,10},{16,20},{18,... | collective-permute-start | bytes 3538952 | tf_op jit(solution)/shard_map/ppermute | solution.py:414
  162.0 60.1 %collective-permute-start.16 = (f32[384,768]{1,0:T(8,128)}, f32[384,768]{1,0:T(8,128)S(1)}, u32[]{:S(2)}, u32[]{:S(2)}) collective-permute-start(f32[384,768]{1,0:T(8,128)} %collective-permute-done.3.refs_0_), channel_id=1, source_target_pairs={{0,2},{2,0},{4,6},{6,4},{8,10},{10,8},{12,14},{14,12},{16,18},{18,... | collective-permute-start | bytes 3538952 | tf_op jit(solution)/shard_map/ppermute | solution.py:414
  188.3 39.8 %collective-permute-start.14 = (f32[192,1536]{1,0:T(8,128)S(1)}, f32[192,1536]{1,0:T(8,128)}, u32[]{:S(2)}, u32[]{:S(2)}) collective-permute-start(f32[192,1536]{1,0:T(8,128)S(1)} %collective-permute-done.2.refs_0_), channel_id=1, source_target_pairs={{0,2},{2,0},{4,6},{6,4},{8,10},{10,8},{12,14},{14,12},{16,18},{18,... | collective-permute-start | bytes 3538952 | tf_op jit(solution)/shard_map/ppermute | solution.py:414
  212.6 10.8 %collective-permute-start.17 = (f32[384,768]{1,0:T(8,128)}, f32[384,768]{1,0:T(8,128)}, u32[]{:S(2)}, u32[]{:S(2)}) collective-permute-start(f32[384,768]{1,0:T(8,128)} %collective-permute-done.13.refs_1_), channel_id=1, source_target_pairs={{0,2},{2,0},{4,6},{6,4},{8,10},{10,8},{12,14},{14,12},{16,18},{18,... | collective-permute-start | bytes 3538952 | tf_op jit(solution)/shard_map/ppermute | solution.py:414
  212.7 15.4 %collective-permute-start.15 = (f32[192,1536]{1,0:T(8,128)}, f32[192,1536]{1,0:T(8,128)}, u32[]{:S(2)}, u32[]{:S(2)}) collective-permute-start(f32[192,1536]{1,0:T(8,128)} %collective-permute-done.12.refs_1_), channel_id=1, source_target_pairs={{0,2},{2,0},{4,6},{6,4},{8,10},{10,8},{12,14},{14,12},{16,18},{18,... | collective-permute-start | bytes 3538952 | tf_op jit(solution)/shard_map/ppermute | solution.py:414
  219.5 45.0 %collective-permute-start.19 = (f32[384,768]{1,0:T(8,128)}, f32[384,768]{1,0:T(8,128)}, u32[]{:S(2)}, u32[]{:S(2)}) collective-permute-start(f32[384,768]{1,0:T(8,128)} %constant_dynamic-slice_fusion.14), channel_id=1, source_target_pairs={{0,8},{2,10},{4,12},{6,14},{8,0},{10,2},{12,4},{14,6},{16,24},{18,... | collective-permute-start | bytes 3538952 | tf_op jit(solution)/shard_map/ppermute | solution.py:414
  223.2 43.2 %collective-permute-start.18 = (f32[192,1536]{1,0:T(8,128)}, f32[192,1536]{1,0:T(8,128)}, u32[]{:S(2)}, u32[]{:S(2)}) collective-permute-start(f32[192,1536]{1,0:T(8,128)} %constant_dynamic-slice_fusion.15), channel_id=1, source_target_pairs={{0,4},{2,6},{4,0},{6,2},{8,12},{10,14},{12,8},{14,10},{16,20},{18,... | collective-permute-start | bytes 3538952 | tf_op jit(solution)/shard_map/ppermute | solution.py:414
  269.2 44.7 %collective-permute-start.21 = (f32[192,768]{1,0:T(8,128)}, f32[192,768]{1,0:T(8,128)}, u32[]{:S(2)}, u32[]{:S(2)}) collective-permute-start(f32[192,768]{1,0:T(8,128)} %constant_dynamic-slice_fusion.12), channel_id=1, source_target_pairs={{0,4},{2,6},{4,0},{6,2},{8,12},{10,14},{12,8},{14,10},{16,20},{18,... | collective-permute-start | bytes 1769480 | tf_op jit(solution)/shard_map/ppermute | solution.py:414
  271.8 43.3 %collective-permute-start.20 = (f32[96,1536]{1,0:T(8,128)}, f32[96,1536]{1,0:T(8,128)}, u32[]{:S(2)}, u32[]{:S(2)}) collective-permute-start(f32[96,1536]{1,0:T(8,128)} %constant_dynamic-slice_fusion.13), channel_id=1, source_target_pairs={{0,8},{2,10},{4,12},{6,14},{8,0},{10,2},{12,4},{14,6},{16,24},{18,... | collective-permute-start | bytes 1769480 | tf_op jit(solution)/shard_map/ppermute | solution.py:414
  309.1 46.4 %collective-permute-start.24 = (f32[192,768]{1,0:T(8,128)}, f32[192,768]{1,0:T(8,128)}, u32[]{:S(2)}, u32[]{:S(2)}) collective-permute-start(f32[192,768]{1,0:T(8,128)} %constant_dynamic-slice_fusion.11), channel_id=1, source_target_pairs={{0,2},{2,0},{4,6},{6,4},{8,10},{10,8},{12,14},{14,12},{16,18},{18,... | collective-permute-start | bytes 1769480 | tf_op jit(solution)/shard_map/ppermute | solution.py:414
  312.4 44.6 %collective-permute-start.23 = (f32[576,384]{1,0:T(8,128)}, f32[576,384]{1,0:T(8,128)}, u32[]{:S(2)}, u32[]{:S(2)}) collective-permute-start(f32[576,384]{1,0:T(8,128)} %dynamic-slice_bitcast_fusion), channel_id=1, source_target_pairs={{0,2},{2,0},{4,6},{6,4},{8,10},{10,8},{12,14},{14,12},{16,18},{18,... | collective-permute-start | bytes 2654216 | tf_op jit(solution)/shard_map/ppermute | solution.py:414
  313.9 45.8 %collective-permute-start.22 = (f32[576,384]{1,0:T(8,128)}, f32[576,384]{1,0:T(8,128)}, u32[]{:S(2)}, u32[]{:S(2)}) collective-permute-start(f32[576,384]{1,0:T(8,128)} %dynamic-slice_bitcast_fusion.1), channel_id=1, source_target_pairs={{0,2},{2,0},{4,6},{6,4},{8,10},{10,8},{12,14},{14,12},{16,18},{18,... | collective-permute-start | bytes 2654216 | tf_op jit(solution)/shard_map/ppermute | solution.py:414
  317.3 41.3 %collective-permute-start.26 = (f32[96,768]{1,0:T(8,128)}, f32[96,768]{1,0:T(8,128)}, u32[]{:S(2)}, u32[]{:S(2)}) collective-permute-start(f32[96,768]{1,0:T(8,128)} %constant_dynamic-slice_fusion.9), channel_id=1, source_target_pairs={{0,16},{2,18},{4,20},{6,22},{8,24},{10,26},{12,28},{14,30},{16,0},... | collective-permute-start | bytes 884744 | tf_op jit(solution)/shard_map/ppermute | solution.py:414
  318.1 42.9 %collective-permute-start.25 = (f32[48,1536]{1,0:T(8,128)}, f32[48,1536]{1,0:T(8,128)}, u32[]{:S(2)}, u32[]{:S(2)}) collective-permute-start(f32[48,1536]{1,0:T(8,128)} %constant_dynamic-slice_fusion.10), channel_id=1, source_target_pairs={{0,16},{2,18},{4,20},{6,22},{8,24},{10,26},{12,28},{14,30},{16,0},... | collective-permute-start | bytes 884744 | tf_op jit(solution)/shard_map/ppermute | solution.py:414
  362.0 10.8 %collective-permute-start.51 = (f32[96,768]{1,0:T(8,128)S(1)}, f32[96,768]{1,0:T(8,128)S(1)}, u32[]{:S(2)}, u32[]{:S(2)}) collective-permute-start(f32[96,768]{1,0:T(8,128)S(1)} %constant_dynamic-slice_fusion.2), channel_id=1, source_target_pairs={{0,8},{2,10},{4,12},{6,14},{8,0},{10,2},{12,4},{14,6},{16,24},{18,... | collective-permute-start | bytes 884744 | tf_op jit(solution)/shard_map/ppermute | solution.py:414
  364.1 8.5 %collective-permute-start.29 = (f32[16,768]{1,0:T(8,128)S(1)}, f32[16,768]{1,0:T(8,128)S(1)}, u32[]{:S(2)}, u32[]{:S(2)}) collective-permute-start(f32[16,768]{1,0:T(8,128)S(1)} %constant_dynamic-update-slice_fusion), channel_id=1, source_target_pairs={{0,16},{2,18},{4,20},{6,22},{8,24},{10,26},{12,28},{14,30},{16,0},... | collective-permute-start | bytes 147464 | tf_op jit(solution)/shard_map/ppermute | solution.py:414
  364.2 30.2 %collective-permute-start.28 = (f32[96,768]{1,0:T(8,128)S(1)}, f32[96,768]{1,0:T(8,128)S(1)}, u32[]{:S(2)}, u32[]{:S(2)}) collective-permute-start(f32[96,768]{1,0:T(8,128)S(1)} %dynamic-slice_add_fusion.10), channel_id=1, source_target_pairs={{0,16},{2,18},{4,20},{6,22},{8,24},{10,26},{12,28},{14,30},{16,0},... | collective-permute-start | bytes 884744 | tf_op jit(solution)/shard_map/ppermute | solution.py:414
  367.1 27.2 %collective-permute-start.27 = (f32[48,1536]{1,0:T(8,128)S(1)}, f32[48,1536]{1,0:T(8,128)S(1)}, u32[]{:S(2)}, u32[]{:S(2)}) collective-permute-start(f32[48,1536]{1,0:T(8,128)S(1)} %dynamic-slice_add_fusion.11), channel_id=1, source_target_pairs={{0,16},{2,18},{4,20},{6,22},{8,24},{10,26},{12,28},{14,30},{16,0},... | collective-permute-start | bytes 884744 | tf_op jit(solution)/shard_map/ppermute | solution.py:414
  367.2 33.4 %collective-permute-start.37 = (f32[288,384]{1,0:T(8,128)S(1)}, f32[288,384]{1,0:T(8,128)S(1)}, u32[]{:S(2)}, u32[]{:S(2)}) collective-permute-start(f32[288,384]{1,0:T(8,128)S(1)} %constant_dynamic-slice_fusion.8), channel_id=1, source_target_pairs={{0,4},{2,6},{4,0},{6,2},{8,12},{10,14},{12,8},{14,10},{16,20},{18,... | collective-permute-start | bytes 1327112 | tf_op jit(solution)/shard_map/ppermute | solution.py:414
  373.0 26.3 %collective-permute-start.52 = (f32[48,768]{1,0:T(8,128)S(1)}, f32[48,768]{1,0:T(8,128)S(1)}, u32[]{:S(2)}, u32[]{:S(2)}) collective-permute-start(f32[48,768]{1,0:T(8,128)S(1)} %constant_dynamic-slice_fusion.1), channel_id=1, source_target_pairs={{0,4},{2,6},{4,0},{6,2},{8,12},{10,14},{12,8},{14,10},{16,20},{18,... | collective-permute-start | bytes 442376 | tf_op jit(solution)/shard_map/ppermute | solution.py:414
  394.6 4.7 collective-permute-start.32
  394.7 15.6 %collective-permute-start.44 = (f32[288,384]{1,0:T(8,128)S(1)}, f32[288,384]{1,0:T(8,128)S(1)}, u32[]{:S(2)}, u32[]{:S(2)}) collective-permute-start(f32[288,384]{1,0:T(8,128)S(1)} %constant_dynamic-slice_fusion.5), channel_id=1, source_target_pairs={{0,8},{2,10},{4,12},{6,14},{8,0},{10,2},{12,4},{14,6},{16,24},{18,... | collective-permute-start | bytes 1327112 | tf_op jit(solution)/shard_map/ppermute | solution.py:414
  396.7 43.4 %collective-permute-start.31 = (f32[192,768]{1,0:T(8,128)S(1)}, f32[192,768]{1,0:T(8,128)S(1)}, u32[]{:S(2)}, u32[]{:S(2)}) collective-permute-start(f32[192,768]{1,0:T(8,128)S(1)} %pad_maximum_fusion.12), channel_id=1, source_target_pairs={{0,4},{2,6},{4,0},{6,2},{8,12},{10,14},{12,8},{14,10},{16,20},{18,... | collective-permute-start | bytes 1769480 | tf_op jit(solution)/shard_map/ppermute | solution.py:414
  399.2 40.7 %collective-permute-start.30 = (f32[96,1536]{1,0:T(8,128)S(1)}, f32[96,1536]{1,0:T(8,128)S(1)}, u32[]{:S(2)}, u32[]{:S(2)}) collective-permute-start(f32[96,1536]{1,0:T(8,128)S(1)} %pad_maximum_fusion.11), channel_id=1, source_target_pairs={{0,8},{2,10},{4,12},{6,14},{8,0},{10,2},{12,4},{14,6},{16,24},{18,... | collective-permute-start | bytes 1769480 | tf_op jit(solution)/shard_map/ppermute | solution.py:414
  399.3 22.2 %collective-permute-start.53 = (f32[24,768]{1,0:T(8,128)S(1)}, f32[24,768]{1,0:T(8,128)S(1)}, u32[]{:S(2)}, u32[]{:S(2)}) collective-permute-start(f32[24,768]{1,0:T(8,128)S(1)} %constant_dynamic-slice_fusion), channel_id=1, source_target_pairs={{0,16},{2,18},{4,20},{6,22},{8,24},{10,26},{12,28},{14,30},{16,0},... | collective-permute-start | bytes 221192 | tf_op jit(solution)/shard_map/ppermute | solution.py:414
  400.7 26.8 %collective-permute-start.38 = (f32[144,384]{1,0:T(8,128)S(1)}, f32[144,384]{1,0:T(8,128)S(1)}, u32[]{:S(2)}, u32[]{:S(2)}) collective-permute-start(f32[144,384]{1,0:T(8,128)S(1)} %constant_dynamic-slice_fusion.7), channel_id=1, source_target_pairs={{0,8},{2,10},{4,12},{6,14},{8,0},{10,2},{12,4},{14,6},{16,24},{18,... | collective-permute-start | bytes 663560 | tf_op jit(solution)/shard_map/ppermute | solution.py:414
  421.5 5.8 %collective-permute-start.54 = (f32[24,768]{1,0:T(8,128)S(1)}, f32[24,768]{1,0:T(8,128)S(1)}, u32[]{:S(2)}, u32[]{:S(2)}) collective-permute-start(f32[24,768]{1,0:T(8,128)S(1)} %dynamic-slice_add_fusion.17), channel_id=1, source_target_pairs={{0,16},{2,18},{4,20},{6,22},{8,24},{10,26},{12,28},{14,30},{16,0},... | collective-permute-start | bytes 221192 | tf_op jit(solution)/shard_map/ppermute | solution.py:414
  425.0 6.0 %collective-permute-start.45 = (f32[144,384]{1,0:T(8,128)S(1)}, f32[144,384]{1,0:T(8,128)S(1)}, u32[]{:S(2)}, u32[]{:S(2)}) collective-permute-start(f32[144,384]{1,0:T(8,128)S(1)} %constant_dynamic-slice_fusion.4), channel_id=1, source_target_pairs={{0,4},{2,6},{4,0},{6,2},{8,12},{10,14},{12,8},{14,10},{16,20},{18,... | collective-permute-start | bytes 663560 | tf_op jit(solution)/shard_map/ppermute | solution.py:414
  427.4 5.4 %collective-permute-start.55 = (f32[48,768]{1,0:T(8,128)S(1)}, f32[48,768]{1,0:T(8,128)S(1)}, u32[]{:S(2)}, u32[]{:S(2)}) collective-permute-start(f32[48,768]{1,0:T(8,128)S(1)} %pad_maximum_fusion.19), channel_id=1, source_target_pairs={{0,4},{2,6},{4,0},{6,2},{8,12},{10,14},{12,8},{14,10},{16,20},{18,... | collective-permute-start | bytes 442376 | tf_op jit(solution)/shard_map/ppermute | solution.py:414
  427.5 7.6 %collective-permute-start.39 = (f32[72,384]{1,0:T(8,128)S(1)}, f32[72,384]{1,0:T(8,128)S(1)}, u32[]{:S(2)}, u32[]{:S(2)}) collective-permute-start(f32[72,384]{1,0:T(8,128)S(1)} %constant_dynamic-slice_fusion.6), channel_id=1, source_target_pairs={{0,16},{2,18},{4,20},{6,22},{8,24},{10,26},{12,28},{14,30},{16,0},... | collective-permute-start | bytes 331784 | tf_op jit(solution)/shard_map/ppermute | solution.py:414
  431.1 8.5 %collective-permute-start.46 = (f32[72,384]{1,0:T(8,128)S(1)}, f32[72,384]{1,0:T(8,128)S(1)}, u32[]{:S(2)}, u32[]{:S(2)}) collective-permute-start(f32[72,384]{1,0:T(8,128)S(1)} %constant_dynamic-slice_fusion.3), channel_id=1, source_target_pairs={{0,16},{2,18},{4,20},{6,22},{8,24},{10,26},{12,28},{14,30},{16,0},... | collective-permute-start | bytes 331784 | tf_op jit(solution)/shard_map/ppermute | solution.py:414
  432.8 19.2 %collective-permute-start.56 = (f32[96,768]{1,0:T(8,128)S(1)}, f32[96,768]{1,0:T(8,128)S(1)}, u32[]{:S(2)}, u32[]{:S(2)}) collective-permute-start(f32[96,768]{1,0:T(8,128)S(1)} %pad_maximum_fusion.16), channel_id=1, source_target_pairs={{0,8},{2,10},{4,12},{6,14},{8,0},{10,2},{12,4},{14,6},{16,24},{18,... | collective-permute-start | bytes 884744 | tf_op jit(solution)/shard_map/ppermute | solution.py:414
  435.1 10.1 %collective-permute-start.40 = (f32[72,384]{1,0:T(8,128)S(1)}, f32[72,384]{1,0:T(8,128)S(1)}, u32[]{:S(2)}, u32[]{:S(2)}) collective-permute-start(f32[72,384]{1,0:T(8,128)S(1)} %dynamic-slice_add_fusion.16), channel_id=1, source_target_pairs={{0,16},{2,18},{4,20},{6,22},{8,24},{10,26},{12,28},{14,30},{16,0},... | collective-permute-start | bytes 331784 | tf_op jit(solution)/shard_map/ppermute | solution.py:414
  439.6 8.0 %collective-permute-start.47 = (f32[72,384]{1,0:T(8,128)S(1)}, f32[72,384]{1,0:T(8,128)S(1)}, u32[]{:S(2)}, u32[]{:S(2)}) collective-permute-start(f32[72,384]{1,0:T(8,128)S(1)} %dynamic-slice_add_fusion.15), channel_id=1, source_target_pairs={{0,16},{2,18},{4,20},{6,22},{8,24},{10,26},{12,28},{14,30},{16,0},... | collective-permute-start | bytes 331784 | tf_op jit(solution)/shard_map/ppermute | solution.py:414
  440.3 10.2 %collective-permute-start.35 = (f32[16,768]{1,0:T(8,128)S(1)}, f32[16,768]{1,0:T(8,128)S(1)}, u32[]{:S(2)}, u32[]{:S(2)}) collective-permute-start(f32[16,768]{1,0:T(8,128)S(1)} %add.280), channel_id=1, source_target_pairs={{0,4},{2,6},{4,0},{6,2},{8,12},{10,14},{12,8},{14,10},{16,20},{18,... | collective-permute-start | bytes 147464 | tf_op jit(solution)/shard_map/ppermute | solution.py:414
  442.5 36.4 %collective-permute-start.34 = (f32[384,768]{1,0:T(8,128)S(1)}, f32[384,768]{1,0:T(8,128)S(1)}, u32[]{:S(2)}, u32[]{:S(2)}) collective-permute-start(f32[384,768]{1,0:T(8,128)S(1)} %pad_maximum_fusion.7), channel_id=1, source_target_pairs={{0,8},{2,10},{4,12},{6,14},{8,0},{10,2},{12,4},{14,6},{16,24},{18,... | collective-permute-start | bytes 3538952 | tf_op jit(solution)/shard_map/ppermute | solution.py:414
  445.2 33.9 %collective-permute-start.33 = (f32[192,1536]{1,0:T(8,128)S(1)}, f32[192,1536]{1,0:T(8,128)S(1)}, u32[]{:S(2)}, u32[]{:S(2)}) collective-permute-start(f32[192,1536]{1,0:T(8,128)S(1)} %pad_maximum_fusion.6), channel_id=1, source_target_pairs={{0,4},{2,6},{4,0},{6,2},{8,12},{10,14},{12,8},{14,10},{16,20},{18,... | collective-permute-start | bytes 3538952 | tf_op jit(solution)/shard_map/ppermute | solution.py:414
  447.5 29.0 %collective-permute-start.41 = (f32[144,384]{1,0:T(8,128)S(1)}, f32[144,384]{1,0:T(8,128)S(1)}, u32[]{:S(2)}, u32[]{:S(2)}) collective-permute-start(f32[144,384]{1,0:T(8,128)S(1)} %pad_maximum_fusion.17), channel_id=1, source_target_pairs={{0,8},{2,10},{4,12},{6,14},{8,0},{10,2},{12,4},{14,6},{16,24},{18,... | collective-permute-start | bytes 663560 | tf_op jit(solution)/shard_map/ppermute | solution.py:414
  450.5 27.4 %collective-permute-start.48 = (f32[144,384]{1,0:T(8,128)S(1)}, f32[144,384]{1,0:T(8,128)S(1)}, u32[]{:S(2)}, u32[]{:S(2)}) collective-permute-start(f32[144,384]{1,0:T(8,128)S(1)} %pad_maximum_fusion.18), channel_id=1, source_target_pairs={{0,4},{2,6},{4,0},{6,2},{8,12},{10,14},{12,8},{14,10},{16,20},{18,... | collective-permute-start | bytes 663560 | tf_op jit(solution)/shard_map/ppermute | solution.py:414
  452.0 26.0 %copy-start.15 = (f32[96,768]{1,0:T(8,128)}, f32[96,768]{1,0:T(8,128)S(1)}, u32[]{:S(2)}) copy-start(f32[96,768]{1,0:T(8,128)S(1)} %get-tuple-element.156) | copy-start | bytes 884740
  452.9 38.0 %collective-permute-start.57 = (f32[192,768]{1,0:T(8,128)}, f32[192,768]{1,0:T(8,128)}, u32[]{:S(2)}, u32[]{:S(2)}) collective-permute-start(f32[192,768]{1,0:T(8,128)} %pad_maximum_fusion.13), channel_id=1, source_target_pairs={{0,2},{2,0},{4,6},{6,4},{8,10},{10,8},{12,14},{14,12},{16,18},{18,... | collective-permute-start | bytes 1769480 | tf_op jit(solution)/shard_map/ppermute | solution.py:414
  476.6 10.9 %collective-permute-start.42 = (f32[288,384]{1,0:T(8,128)S(1)}, f32[288,384]{1,0:T(8,128)S(1)}, u32[]{:S(2)}, u32[]{:S(2)}) collective-permute-start(f32[288,384]{1,0:T(8,128)S(1)} %pad_maximum_fusion.14), channel_id=1, source_target_pairs={{0,4},{2,6},{4,0},{6,2},{8,12},{10,14},{12,8},{14,10},{16,20},{18,... | collective-permute-start | bytes 1327112 | tf_op jit(solution)/shard_map/ppermute | solution.py:414
  478.0 10.7 %collective-permute-start.49 = (f32[288,384]{1,0:T(8,128)S(1)}, f32[288,384]{1,0:T(8,128)S(1)}, u32[]{:S(2)}, u32[]{:S(2)}) collective-permute-start(f32[288,384]{1,0:T(8,128)S(1)} %pad_maximum_fusion.15), channel_id=1, source_target_pairs={{0,8},{2,10},{4,12},{6,14},{8,0},{10,2},{12,4},{14,6},{16,24},{18,... | collective-permute-start | bytes 1327112 | tf_op jit(solution)/shard_map/ppermute | solution.py:414
  481.1 20.8 %collective-permute-start.59 = (f32[768,768]{1,0:T(8,128)}, f32[768,768]{1,0:T(8,128)}, u32[]{:S(2)}, u32[]{:S(2)}) collective-permute-start(f32[768,768]{1,0:T(8,128)} %pad_maximum_fusion.4), channel_id=1, source_target_pairs={{0,2},{2,0},{4,6},{6,4},{8,10},{10,8},{12,14},{14,12},{16,18},{18,... | collective-permute-start | bytes 7077896 | tf_op jit(solution)/shard_map/ppermute | solution.py:414
  488.6 8.7 %collective-permute-start.43 = (f32[576,384]{1,0:T(8,128)}, f32[576,384]{1,0:T(8,128)}, u32[]{:S(2)}, u32[]{:S(2)}) collective-permute-start(f32[576,384]{1,0:T(8,128)} %pad_maximum_fusion.9), channel_id=1, source_target_pairs={{0,2},{2,0},{4,6},{6,4},{8,10},{10,8},{12,14},{14,12},{16,18},{18,... | collective-permute-start | bytes 2654216 | tf_op jit(solution)/shard_map/ppermute | solution.py:414
  490.5 8.1 %collective-permute-start.50 = (f32[576,384]{1,0:T(8,128)}, f32[576,384]{1,0:T(8,128)}, u32[]{:S(2)}, u32[]{:S(2)}) collective-permute-start(f32[576,384]{1,0:T(8,128)} %pad_maximum_fusion.10), channel_id=1, source_target_pairs={{0,2},{2,0},{4,6},{6,4},{8,10},{10,8},{12,14},{14,12},{16,18},{18,... | collective-permute-start | bytes 2654216 | tf_op jit(solution)/shard_map/ppermute | solution.py:414
  490.9 16.2 %collective-permute-start.58 = (f32[384,1536]{1,0:T(8,128)S(1)}, f32[384,1536]{1,0:T(8,128)S(1)}, u32[]{:S(2)}, u32[]{:S(2)}) collective-permute-start(f32[384,1536]{1,0:T(8,128)S(1)} %pad_maximum_fusion.3), channel_id=1, source_target_pairs={{0,2},{2,0},{4,6},{6,4},{8,10},{10,8},{12,14},{14,12},{16,18},{18,... | collective-permute-start | bytes 7077896 | tf_op jit(solution)/shard_map/ppermute | solution.py:414
  492.2 4.4 collective-permute-start.36
  (28 other events, 100.7 us)

commit v4 on v3

--- a/solution.py
+++ b/solution.py
@@ -121,8 +121,16 @@
     return body
 
 
+def join(counts, samples, pieces, full):
+    rows = pieces[0].shape[0]
+    for i in range(4):
+        full[pl.ds(pl.multiple_of(counts[samples + i] * rows, 16), rows), :] = pieces[i][...].astype(bf16)
+
+
 def fwd_other_body(samples, width):
-    def body(counts, a, h, o, weight, out_own, out_other, gain, shift, qkv, o2, lse, r, c):
+    def body(counts, a, h, o, q0, q1, q2, q3, w0, w1, w2, w3, out_own, gain, shift, qkv, o2, lse, r, c, weight, out_other):
+        join(counts, samples, (q0, q1, q2, q3), weight)
+        join(counts, samples, (w0, w1, w2, w3), out_other)
         total = total_of(counts, samples)
         n = tiles(total)
 
@@ -195,7 +203,9 @@
 
 
 def mlp_other_body(samples, patches):
-    def body(counts, line, c, dm, up, down, m, dc, r, gain, out, dr, g2, y):
+    def body(counts, line, c, dm, u0, u1, u2, u3, d0, d1, d2, d3, m, dc, r, gain, out, dr, g2, y, up, down):
+        join(counts, samples, (u0, u1, u2, u3), up)
+        join(counts, samples, (d0, d1, d2, d3), down)
         n = tiles(total_of(counts, samples))
         g2[...] = jnp.zeros(g2.shape, f32)
 
@@ -260,11 +270,10 @@
 
 
 def attn_own_body(samples, width):
-    def body(counts, dr, qkv, lse, o, a, wout, wqkv, da, gout, gqkv, do, dqkv):
+    def body(counts, dr, qkv, lse, o, wout, gout, dqkv, do):
         total = total_of(counts, samples)
         n = tiles(total)
         gout[...] = jnp.zeros(gout.shape, f32)
-        gqkv[...] = jnp.zeros(gqkv.shape, f32)
 
         def first(i, x):
             r = win(i * TILE)
@@ -276,6 +285,14 @@
         lax.fori_loop(0, n, first, 0)
         attend_back(counts, qkv, do, lse, dqkv, samples, width)
         dqkv[win(total), :] = jnp.zeros((TILE, dqkv.shape[1]), bf16)
+
+    return body
+
+
+def proj_own_body(samples, width):
+    def body(counts, dqkv, a, wqkv, da, gqkv):
+        n = tiles(total_of(counts, samples))
+        gqkv[...] = jnp.zeros(gqkv.shape, f32)
 
         def last(i, x):
             r = win(i * TILE)
@@ -290,11 +307,10 @@
     return body
 
 
-def attn_other_body(samples, width, patches):
-    def body(counts, line, dr, qkv, lse, wout, wqkv, da, h, gain, out, g1, do, dqkv, dh):
+def attn_other_body(samples, width):
+    def body(counts, dr, qkv, lse, wout, dqkv, do):
         total = total_of(counts, samples)
         n = tiles(total)
-        g1[...] = jnp.zeros(g1.shape, f32)
 
         def first(i, x):
             r = win(i * TILE)
@@ -304,6 +320,14 @@
         lax.fori_loop(0, n, first, 0)
         attend_back(counts, qkv, do, lse, dqkv, samples, width)
         dqkv[win(total), :] = jnp.zeros((TILE, dqkv.shape[1]), bf16)
+
+    return body
+
+
+def proj_other_body(samples, patches):
+    def body(counts, line, dr, dqkv, wqkv, da, h, gain, out, g1, dh):
+        n = tiles(total_of(counts, samples))
+        g1[...] = jnp.zeros(g1.shape, f32)
 
         def last(i, x):
             r = win(i * TILE)
@@ -377,11 +401,11 @@
     )(counts, col, patches, cot, gain, shift, weight)
 
 
-def fwd_other(counts, a, h, o, weight, out_own, out_other, gain, shift, S):
+def fwd_other(counts, a, h, o, wq, out_own, wo, gain, shift, S):
     TP, D = a.shape
-    width = weight.shape[1] // 3
-    outs = [sds((TP, 3 * width), bf16), sds((TP, width), bf16), sds((S, width // HD, SLOTS), f32), sds((TP, D), f32), sds((TP, D), bf16)]
-    return call(fwd_other_body(S, width), counts, [a, h, o, weight, out_own, out_other, gain, shift], outs, flops=7 * 10**9)
+    width = wq[0].shape[1] // 3
+    outs = [sds((TP, 3 * width), bf16), sds((TP, width), bf16), sds((S, width // HD, SLOTS), f32), sds((TP, D), f32), sds((TP, D), bf16), sds((D, 3 * width), bf16), sds((width, D), bf16)]
+    return call(fwd_other_body(S, width), counts, [a, h, o, *wq, *wo, out_own, gain, shift], outs, flops=7 * 10**9)
 
 
 def mlp_own(counts, c, dm, up, down, S):
@@ -393,21 +417,32 @@
 def mlp_other(counts, line, c, dm, up, down, m, dc, r, gain, S, L):
     TP, D = c.shape
     outs = [sds((S, L, D), bf16), sds((TP, D), f32), sds((8, D), f32)]
-    return call(mlp_other_body(S, L), counts, [line, c, dm, up, down, m, dc, r, gain], outs, [pltpu.VMEM((TP, D), bf16)], flops=12 * 10**9)
-
-
-def attn_own(counts, dr, qkv, lse, o, a, wout, wqkv, S):
+    return call(mlp_other_body(S, L), counts, [line, c, dm, *up, *down, m, dc, r, gain], outs, [pltpu.VMEM((TP, D), bf16), pltpu.VMEM((D, 4 * down[0].shape[0]), bf16), pltpu.VMEM((4 * down[0].shape[0], D), bf16)], flops=12 * 10**9)
+
+
+def attn_own(counts, dr, qkv, lse, o, wout, S):
+    TP, width = o.shape
+    outs = [sds(wout.shape, f32), sds((TP, 3 * width), bf16)]
+    return call(attn_own_body(S, width), counts, [dr, qkv, lse, o, wout], outs, [pltpu.VMEM((TP, width), bf16)], flops=5 * 10**9)
+
+
+def proj_own(counts, dqkv, a, wqkv, S):
     TP, D = a.shape
-    width = wout.shape[0]
-    outs = [sds((TP, D), f32), sds(wout.shape, f32), sds((3, D, width), f32)]
-    return call(attn_own_body(S, width), counts, [dr, qkv, lse, o, a, wout, wqkv], outs, [pltpu.VMEM((TP, width), bf16), pltpu.VMEM((TP, 3 * width), bf16)], flops=9 * 10**9)
-
-
-def attn_other(counts, line, dr, qkv, lse, wout, wqkv, da, h, gain, S, L):
+    width = wqkv.shape[1] // 3
+    outs = [sds((TP, D), f32), sds((3, D, width), f32)]
+    return call(proj_own_body(S, width), counts, [dqkv, a, wqkv], outs, flops=5 * 10**9)
+
+
+def attn_other(counts, dr, qkv, lse, wout, S):
+    TP, width = dr.shape[0], wout.shape[0]
+    outs = [sds((TP, 3 * width), bf16)]
+    return call(attn_other_body(S, width), counts, [dr, qkv, lse, wout], outs, [pltpu.VMEM((TP, width), bf16)], flops=4 * 10**9)[0]
+
+
+def proj_other(counts, line, dr, dqkv, wqkv, da, h, gain, S, L):
     TP, D = h.shape
-    width = wout.shape[0]
     outs = [sds((S, L, D), bf16), sds((8, D), f32)]
-    return call(attn_other_body(S, width, L), counts, [line, dr, qkv, lse, wout, wqkv, da, h, gain], outs, [pltpu.VMEM((TP, width), bf16), pltpu.VMEM((TP, 3 * width), bf16), pltpu.VMEM((TP, D), bf16)], flops=8 * 10**9)
+    return call(proj_other_body(S, L), counts, [line, dr, dqkv, wqkv, da, h, gain], outs, [pltpu.VMEM((TP, D), bf16)], flops=4 * 10**9)
 
 
 def swap(x, axis, size, bit):
@@ -416,16 +451,6 @@
 
 def tie(*xs):
     return lax.optimization_barrier(xs)
-
-
-def cast_pieces(order, pieces):
-    rows, cols = pieces[0].shape
-
-    def body(where, *refs):
-        for i in range(4):
-            refs[4][pl.ds(pl.multiple_of(where[i] * rows, 16), rows), :] = refs[i][...].astype(bf16)
-
-    return call(body, order, pieces, [sds((4 * rows, cols), bf16)])[0]
 
 
 def side(bit):
@@ -445,7 +470,7 @@
 def spread(x, bit, dp):
     got = swap(x, "dp", dp, bit)
     first = side(bit) == 0
-    return jnp.concatenate([jnp.where(first, x, got), jnp.where(first, got, x)], 0)
+    return jnp.where(first, jnp.concatenate([x, got], 0), jnp.concatenate([got, x], 0))
 
 
 def folds(x, bits, dp):
@@ -474,8 +499,9 @@
         return lax.dynamic_slice_in_dim(w, me * rows, rows, 0).astype(f32)
 
     def rest(first, across):
-        return cast_pieces(order, [first, across, swap(first, "dp", dp, 1), swap(across, "dp", dp, 1)])
-
+        return [first, across, swap(first, "dp", dp, 1), swap(across, "dp", dp, 1)]
+
+    counts = jnp.concatenate([counts, order])
     every = [1 << i for i in range(dp.bit_length() - 1)]
     along = every
     other = [1, 4, 2] + every[3:] if len(every) > 2 else every
@@ -486,7 +512,7 @@
     aq, ao = swap(fq, "dp", dp, 2), swap(fo, "dp", dp, 2)
     fu, fd = swap(pu, "tensor", 2, 1), swap(pd, "tensor", 2, 1)
     wq1, wo1 = rest(fq, aq), rest(fo, ao)
-    qkv1, _, lse1, r, c = fwd_other(counts, a, h, o0, wq1, wo, wo1, g2, b2, S)
+    qkv1, _, lse1, r, c, wq1, wo1 = fwd_other(counts, a, h, o0, wq1, wo, wo1, g2, b2, S)
     fu, fd, c = tie(fu, fd, c)
     au = swap(fu, "dp", dp, 2)
     ad = swap(fd, "dp", dp, 2)
@@ -499,25 +525,33 @@
     A, B = fold(A, along[1], dp), fold(B, other[1], dp)
     A, B, dr = tie(A, B, dr)
     A, B = fold(A, along[2], dp), fold(B, other[2], dp)
-    da, gout, gqkv = attn_own(counts, dr, qkv0, lse0, o0, a, wo, wq, S)
-    A, B, da = tie(A, B, da)
-    A, B = folds(A, along[3:], dp), folds(B, other[3:], dp)
+    gout, dq0 = attn_own(counts, dr, qkv0, lse0, o0, wo, S)
+    A, B, dq0, dr = tie(A, B, dq0, dr)
+    A, B, E = folds(A, along[3:], dp), folds(B, other[3:], dp), fold(gout, 1, dp)
+    da, gqkv = proj_own(counts, dq0, a, wq, S)
     C = gqkv.reshape(2, (3 * D) // 2, -1)
-    C, F, E = fold(C[0], 1, dp), fold(C[1], 1, dp), fold(gout, 1, dp)
-    gin, gg1 = attn_other(counts, line, dr, qkv1, lse1, wo1, wq1, da, h, g1, S, L)
+    C, F = fold(C[0], 1, dp), fold(C[1], 1, dp)
+    da, dr = tie(da, dr)
+    dq1 = attn_other(counts, dr, qkv1, lse1, wo1, S)
+    A, B, C, F, E, dq1 = tie(A, B, C, F, E, dq1)
+    A, B = spreads(A, along[3:], dp), spreads(B, other[3:], dp)
+    C, F, E = fold(C, along[1], dp), fold(F, other[1], dp), fold(E, other[1], dp)
+    gin, gg1 = proj_other(counts, line, dr, dq1, wq1, da, h, g1, S, L)
     C, F, E, A, B, gg1 = tie(C, F, E, A, B, gg1)
     small = jnp.concatenate([gg1, gg2], 0)
-    for bit, late in zip(reversed(along), reversed(other)):
+    for bit in along[3:]:
+        small = small + swap(small, "dp", dp, bit)
+    for bit, late in zip(reversed(along[:3]), reversed(other[:3])):
         A, B = spread(A, bit, dp), spread(B, late, dp)
         small = small + swap(small, "dp", dp, bit)
         if bit != 1:
             A, B, small = tie(A, B, small)
     gup, gdown = A, B
     gg1, gg2 = small[:8], small[8:]
-    C = spreads(folds(C, along[1:], dp), along, dp)
-    F = spreads(folds(F, other[1:], dp), other, dp)
+    C = spreads(folds(C, along[2:], dp), along, dp)
+    F = spreads(folds(F, other[2:], dp), other, dp)
     gqkv = jnp.concatenate([C, F], 0).reshape(3, D, -1)
-    gout = spreads(folds(E, other[1:], dp), other, dp)
+    gout = spreads(folds(E, other[2:], dp), other, dp)
     return (out, gin, gg1[0], gg1[1], gqkv.transpose(1, 0, 2), gout, gg2[0], gg2[1], gup, gdown)
 
 

time: 511 us -> 504 us (0.986)
  other arithmetic: 47.4 us -> 55.9 us
  starting transfers between devices: 59.4 us -> 50.9 us
    select_n x20, other arithmetic: 7.89 us -> 25.3 us  [spread(): jnp.where(first, jnp.concatenate([x, got], 0), jnp.concatenate([got, x], 0))]
    concatenate x18 -> x0, other arithmetic: 11 us -> none  [spread(): jnp.concatenate([jnp.where(first, x, got), jnp.where(first, got, x)], 0)]
    ppermute x60, starting transfers between devices: 59.4 us -> 50.9 us  [swap(): return lax.ppermute(x, axis, [(k, k ^ bit) for k in range(size)])]
    pallas_call x9 -> x7, Pallas kernels: 174 us -> 173 us  [call(): pl.pallas_call(body, out_shape=list(outs), grid_spec=pltpu.PrefetchScalar...]
  transfers between devices with their start and end apart: 60 -> 60, of which waited for: 21 -> 19; matrix products, arithmetic and copies ran while one was open for 12% -> 13% of each run, Pallas kernels for 33% -> 33%
where the time goes in v4:
time: 504 us; the launch traced here: 503 us
  Pallas kernels  199 us (39%)
  waiting for transfers between devices  168 us (33%)
  other arithmetic  55.9 us (11%)
  starting transfers between devices  50.9 us (10%)
  local copies, waits for them, and re-layouts  28.1 us (6%)
    pallas_call x7, Pallas kernels, call(): pl.pallas_call(body, out_shape=list(outs), grid_spec=pltpu.PrefetchScalar...  173 us
    ppermute x60, waiting for transfers between devices, swap(): return lax.ppermute(x, axis, [(k, k ^ bit) for k in range(size)])  168 us
    ppermute x60, starting transfers between devices, swap(): return lax.ppermute(x, axis, [(k, k ^ bit) for k in range(size)])  50.9 us
    pallas_call x1, Pallas kernels, fwd_own(): pl.pallas_call(fwd_own_body(S, width), name='fwd_own', out_shape=outs, gr...  26 us
    select_n x20, other arithmetic, spread(): jnp.where(first, jnp.concatenate([x, got], 0), jnp.concatenate([got, x], 0))  25.3 us
    add x20, other arithmetic, fold(): return half(x, i) + swap(half(x, 1 - i), 'dp', dp, bit)  21.3 us
    dynamic_slice x20, local copies, waits for them, and re-layouts, half(): return lax.dynamic_slice_in_dim(x, i * n, n, 0)  14.9 us
  transfers between devices with their start and end apart: 60, of which 19 were waited for; matrix products, arithmetic and copies ran while one was open for 13% of the time, Pallas kernels for 33%

profile of v4, /device:TPU:0, one launch (start us, length us, event | category | flops | bytes accessed | tf_op | source)
XLA Modules:
  0.0 502.6 jit_solution(2783187328079221272)
XLA Ops:
  0.7 2.4 slice_bitcast_fusion.2
  5.3 3.0 collective-permute-start
  8.3 1.6 dynamic-slice_convert_fusion.3
  10.6 1.7 copy.22.col
  13.5 26.0 %fwd_own.1 = (bf16[1792,768]{1,0:T(8,128)(2,1)}, bf16[1792,768]{1,0:T(8,128)(2,1)}, bf16[1792,768]{1,0:T(8,128)(2,1)}, bf16[1792,1152]{1,0:T(8,128)(2,1)}, bf16[...) custom-call(s32[10]{0:T(128)} %concatenate.132.counts, s32[6,512,1]{2,1,0:T(8,128)} %copy.22.col, ...), custom_call_target="tpu_custom_call" | custom-call | flops 6000000000 | bytes 26214400 | tf_op jit(solution)/shard_map/fwd_own/pallas_call | solution.py:382
  40.6 2.2 dynamic-slice_convert_fusion.1
  42.8 2.0 collective-permute-start.4
  44.8 19.3 %collective-permute-done.4.q1 = f32[192,1152]{1,0:T(8,128)S(1)} collective-permute-done((f32[192,1152]{1,0:T(8,128)}, f32[192,1152]{1,0:T(8,128)S(1)}, u32[]{:S(2)}, u32[]{:S(2)}) %collective-permute-start.4) | collective-permute-done | bytes 884768 | tf_op jit(solution)/shard_map/ppermute | solution.py:449
  64.1 1.7 collective-permute-start.7
  67.6 6.1 %collective-permute-done.7.w1 = f32[96,768]{1,0:T(8,128)S(1)} collective-permute-done((f32[96,768]{1,0:T(8,128)}, f32[96,768]{1,0:T(8,128)S(1)}, u32[]{:S(2)}, u32[]{:S(2)}) %collective-permute-start.7) | collective-permute-done | bytes 294944 | tf_op jit(solution)/shard_map/ppermute | solution.py:449
  77.6 26.1 %shard_map.195 = (bf16[1792,1152]{1,0:T(8,128)(2,1)}, bf16[1792,384]{1,0:T(8,128)(2,1)}, f32[6,6,256]{2,1,0:T(8,128)}, f32[1792,768]{1,0:T(8,128)}, bf16[1792,76...) custom-call(s32[10]{0:T(128)} %concatenate.132.counts, bf16[1792,768]{1,0:T(8,128)(2,1)} %get-tuple-element.79.a, ...), custom_call_target="tpu_custom_call" | custom-call | flops 7000000000 | bytes 28354560 | tf_op jit(solution)/shard_map/pallas_call | solution.py:359
  103.7 16.1 %collective-permute-done.3.d0 = f32[384,768]{1,0:T(8,128)} collective-permute-done((f32[384,768]{1,0:T(8,128)S(1)}, f32[384,768]{1,0:T(8,128)}, u32[]{:S(2)}, u32[]{:S(2)}) %collective-permute-start.3) | collective-permute-done | bytes 1179680 | tf_op jit(solution)/shard_map/ppermute | solution.py:449
  119.9 32.0 %shard_map.196 = (f32[1792,768]{1,0:T(8,128)}, f32[1792,768]{1,0:T(8,128)}, f32[768,1536]{1,0:T(8,128)}, f32[1536,768]{1,0:T(8,128)}) custom-call(s32[10]{0:T(128)} %concatenate.132.counts, bf16[1792,768]{1,0:T(8,128)(2,1)} %get-tuple-element.89.c, bf16[1792,768]{1,0:T(8,128)(2,1)} %get-tuple-element.86.dm, bf16[768,1536]{1,0:T(8,128)(2,1)} %up.1, ...), custom_call_target="tpu_custom_call" | custom-call | flops 17999998976 | bytes 30670848 | tf_op jit(solution)/shard_map/pallas_call | solution.py:359
  151.9 3.2 constant_dynamic-slice_fusion.16
  155.1 3.2 constant_dynamic-slice_fusion.17
  159.1 1.7 collective-permute-start.13
  161.5 26.5 %collective-permute-done.12.u1 = f32[192,1536]{1,0:T(8,128)} collective-permute-done((f32[192,1536]{1,0:T(8,128)}, f32[192,1536]{1,0:T(8,128)}, u32[]{:S(2)}, u32[]{:S(2)}) %collective-permute-start.12) | collective-permute-done | bytes 1179680 | tf_op jit(solution)/shard_map/ppermute | solution.py:449
  188.0 24.3 %collective-permute-done.13.d1 = f32[384,768]{1,0:T(8,128)} collective-permute-done((f32[384,768]{1,0:T(8,128)}, f32[384,768]{1,0:T(8,128)}, u32[]{:S(2)}, u32[]{:S(2)}) %collective-permute-start.13) | collective-permute-done | bytes 1179680 | tf_op jit(solution)/shard_map/ppermute | solution.py:449
  212.8 2.2 dynamic-slice_add_fusion
  215.4 2.6 dynamic-slice_add_fusion.1
  218.1 1.7 collective-permute-start.19
  222.1 33.6 %shard_map.197 = (bf16[6,512,768]{2,1,0:T(8,128)(2,1)}, f32[1792,768]{1,0:T(8,128)}, f32[8,768]{1,0:T(8,128)}) custom-call(s32[10]{0:T(128)} %concatenate.132.counts, s32[6,1,512]{2,1,0:T(1,128)} %broadcast_in_dim.18.line, bf16[1792,768]{1,0:T(8,128)(2,1)} %get-tuple-element.89.c, bf16[1792,768]{1,0:T(8,128)(2,1)} %get-tuple-element.86.dm, ...), custom_call_target="tpu_custom_call" | custom-call | flops 12000000000 | bytes 41720832 | tf_op jit(solution)/shard_map/pallas_call | solution.py:359
  255.7 1.9 dynamic-slice_add_fusion.2
  260.5 1.7 collective-permute-start.21
  262.4 24.9 %shard_map.198 = (f32[384,768]{1,0:T(8,128)}, bf16[1792,1152]{1,0:T(8,128)(2,1)}) custom-call(s32[10]{0:T(128)} %concatenate.132.counts, f32[1792,768]{1,0:T(8,128)} %get-tuple-element.111.dr, bf16[1792,1152]{1,0:T(8,128)(2,1)} %get-tuple-element.105.qkv, f32[6,6,256]{2,1,0:T(8,128)} %get-tuple-element.106.lse, bf16[1792,384]{1,0:T(8,128)(2,1)} %get-tuple-element.81.o, ...), custom_call_target="tpu_custom_call" | custom-call | flops 5000000000 | bytes 16945152 | tf_op jit(solution)/shard_map/pallas_call | solution.py:359
  287.3 2.0 constant_dynamic-slice_fusion.9
  289.3 2.0 dynamic-slice_add_fusion.5
  291.3 2.0 dynamic-slice_add_fusion.6
  293.2 14.8 %shard_map.199 = (f32[1792,768]{1,0:T(8,128)}, f32[3,768,384]{2,1,0:T(8,128)}) custom-call(s32[10]{0:T(128)} %concatenate.132.counts, bf16[1792,1152]{1,0:T(8,128)(2,1)} %get-tuple-element.108.dqkv, bf16[1792,768]{1,0:T(8,128)(2,1)} %get-tuple-element.79.a, bf16[768,1152]{1,0:T(8,128)(2,1)} %copy-done.12), custom_call_target="tpu_custom_call" | custom-call | flops 5000000000 | bytes 17694720 | tf_op jit(solution)/shard_map/pallas_call | solution.py:359
  308.1 2.2 fusion
  314.3 2.9 collective-permute-start.22
  317.2 23.8 %shard_map.200.dqkv = bf16[1792,1152]{1,0:T(8,128)(2,1)} custom-call(s32[10]{0:T(128)} %concatenate.132.counts, f32[1792,768]{1,0:T(8,128)} %get-tuple-element.111.dr, bf16[1792,1152]{1,0:T(8,128)(2,1)} %get-tuple-element.116.qkv, f32[6,6,256]{2,1,0:T(8,128)} %get-tuple-element.117.lse, bf16[384,768]{1,0:T(8,128)(2,1)} %get-tuple-element.118.wout), custom_call_target="tpu_custom_call" | custom-call | flops 4000000000 | bytes 14389248 | tf_op jit(solution)/shard_map/pallas_call | solution.py:359
  342.5 2.0 dynamic-slice_add_fusion.10
  344.5 1.7 dynamic-slice_add_fusion.11
  347.5 1.6 bitcast_add_fusion.1
  349.2 2.9 collective-permute-start.30
  352.8 2.0 collective-permute-start.29
  355.9 17.3 %shard_map.201 = (bf16[6,512,768]{2,1,0:T(8,128)(2,1)}, f32[8,768]{1,0:T(8,128)}) custom-call(s32[10]{0:T(128)} %concatenate.132.counts, s32[6,1,512]{2,1,0:T(1,128)} %broadcast_in_dim.18.line, f32[1792,768]{1,0:T(8,128)} %get-tuple-element.111.dr, bf16[1792,1152]{1,0:T(8,128)(2,1)} %shard_map.200.dqkv, bf16[768,1152]{1,0:T(8,128)(2,1)} %get-tuple-element.120.wqkv, ...), custom_call_target="tpu_custom_call" | custom-call | flops 4000000000 | bytes 24419328 | tf_op jit(solution)/shard_map/pallas_call | solution.py:359
  374.6 2.9 collective-permute-done.30
  379.8 1.5 collective-permute-done.28
  381.5 2.5 collective-permute-start.52
  384.0 1.9 collective-permute-start.33
  385.9 2.5 collective-permute-start.32
  391.8 16.1 %collective-permute-done.35 = f32[16,768]{1,0:T(8,128)S(1)} collective-permute-done((f32[16,768]{1,0:T(8,128)S(1)}, f32[16,768]{1,0:T(8,128)S(1)}, u32[]{:S(2)}, u32[]{:S(2)}) %collective-permute-start.35) | collective-permute-done | bytes 49184 | tf_op jit(solution)/shard_map/ppermute | solution.py:449
  408.3 1.8 collective-permute-start.54
  411.6 1.7 collective-permute-start.36
  413.3 2.6 collective-permute-done.46
  416.0 1.9 collective-permute-start.37
  417.9 1.6 collective-permute-done.41
  419.8 3.7 collective-permute-done.47
  423.6 23.2 %collective-permute-done.42 = f32[72,384]{1,0:T(8,128)S(1)} collective-permute-done((f32[72,384]{1,0:T(8,128)S(1)}, f32[72,384]{1,0:T(8,128)S(1)}, u32[]{:S(2)}, u32[]{:S(2)}) %collective-permute-start.42) | collective-permute-done | bytes 110624 | tf_op jit(solution)/shard_map/ppermute | solution.py:449
  446.8 2.1 collective-permute-start.43
  451.1 5.7 %collective-permute-done.38 = f32[16,768]{1,0:T(8,128)S(1)} collective-permute-done((f32[16,768]{1,0:T(8,128)S(1)}, f32[16,768]{1,0:T(8,128)S(1)}, u32[]{:S(2)}, u32[]{:S(2)}) %collective-permute-start.38) | collective-permute-done | bytes 49184 | tf_op jit(solution)/shard_map/ppermute | solution.py:449
  459.2 1.6 maximum_select_fusion.3
  460.9 1.8 collective-permute-done.49
  463.0 4.5 collective-permute-done.44
  468.1 2.6 collective-permute-done.56
  471.6 8.2 %collective-permute-done.50 = f32[288,384]{1,0:T(8,128)S(1)} collective-permute-done((f32[288,384]{1,0:T(8,128)S(1)}, f32[288,384]{1,0:T(8,128)S(1)}, u32[]{:S(2)}, u32[]{:S(2)}) %collective-permute-start.50) | collective-permute-done | bytes 442400 | tf_op jit(solution)/shard_map/ppermute | solution.py:449
  481.3 2.9 maximum_select_fusion.8
  484.8 1.6 maximum_select_fusion.4
  486.4 2.3 maximum_select_fusion.5
  488.7 2.0 pad_maximum_fusion
  490.7 6.5 %maximum_select_fusion.1 = f32[1536,768]{1,0:T(8,128)} fusion(f32[768,768]{1,0:T(8,128)} %collective-permute-done.59, f32[768,768]{1,0:T(8,128)} %maximum_select_fusion.3, pred[]{:T(512)S(6)} %eq.73), kind=kLoop, calls=%fused_computation.1 | loop fusion | flops 3538944 | bytes 9437185 | tf_op jit(solution)/shard_map/jit(_where)/select_n | solution.py:473
  497.3 5.3 %maximum_select_fusion = f32[768,1536]{1,0:T(8,128)} fusion(f32[384,1536]{1,0:T(8,128)} %collective-permute-done.58, f32[384,1536]{1,0:T(8,128)S(1)} %maximum_select_fusion.2, pred[]{:T(512)S(6)} %eq.73), kind=kLoop, calls=%fused_computation | loop fusion | flops 3538944 | bytes 9437185 | tf_op jit(solution)/shard_map/jit(_where)/select_n | solution.py:473
  (208 shorter events, 45.0 us)
Async XLA Ops:
  5.3 37.5 %collective-permute-start = (f32[192,1152]{1,0:T(8,128)}, f32[192,1152]{1,0:T(8,128)}, u32[]{:S(2)}, u32[]{:S(2)}) collective-permute-start(f32[192,1152]{1,0:T(8,128)} %dynamic-slice_convert_fusion.2), channel_id=1, source_target_pairs={{0,1},{1,0},{2,3},{3,2},{4,5},{5,4},{6,7},{7,6},{8,9},{9,8},{10,11... | collective-permute-start | bytes 2654216 | tf_op jit(solution)/shard_map/ppermute | solution.py:449
  10.0 32.9 %collective-permute-start.1 = (f32[96,768]{1,0:T(8,128)}, f32[96,768]{1,0:T(8,128)}, u32[]{:S(2)}, u32[]{:S(2)}) collective-permute-start(f32[96,768]{1,0:T(8,128)} %dynamic-slice_convert_fusion.3), channel_id=1, source_target_pairs={{0,1},{1,0},{2,3},{3,2},{4,5},{5,4},{6,7},{7,6},{8,9},{9,8},{10,11... | collective-permute-start | bytes 884744 | tf_op jit(solution)/shard_map/ppermute | solution.py:449
  39.4 35.9 %copy-start.23 = (f32[768]{0:T(1024)S(1)}, f32[768]{0:T(1024)}, u32[]{:S(2)}) copy-start(f32[768]{0:T(1024)} %param.19) | copy-start | bytes 9220
  39.4 36.5 %copy-start.24 = (f32[768]{0:T(1024)S(1)}, f32[768]{0:T(1024)}, u32[]{:S(2)}) copy-start(f32[768]{0:T(1024)} %param.20) | copy-start | bytes 9220
  42.8 21.3 %collective-permute-start.4 = (f32[192,1152]{1,0:T(8,128)}, f32[192,1152]{1,0:T(8,128)S(1)}, u32[]{:S(2)}, u32[]{:S(2)}) collective-permute-start(f32[192,1152]{1,0:T(8,128)} %collective-permute-done.q0), channel_id=1, source_target_pairs={{0,4},{2,6},{4,0},{6,2},{8,12},{10,14},{12,8},{14,10},{16,20},{18,... | collective-permute-start | bytes 2654216 | tf_op jit(solution)/shard_map/ppermute | solution.py:449
  44.8 32.0 %collective-permute-start.5 = (f32[192,1152]{1,0:T(8,128)}, f32[192,1152]{1,0:T(8,128)}, u32[]{:S(2)}, u32[]{:S(2)}) collective-permute-start(f32[192,1152]{1,0:T(8,128)} %collective-permute-done.q0), channel_id=1, source_target_pairs={{0,2},{2,0},{4,6},{6,4},{8,10},{10,8},{12,14},{14,12},{16,18},{18,... | collective-permute-start | bytes 2654216 | tf_op jit(solution)/shard_map/ppermute | solution.py:449
  64.1 12.4 %copy-start.27 = (f32[192,1152]{1,0:T(8,128)}, f32[192,1152]{1,0:T(8,128)S(1)}, u32[]{:S(2)}) copy-start(f32[192,1152]{1,0:T(8,128)S(1)} %collective-permute-done.4.q1) | copy-start | bytes 2654212
  64.1 12.8 %collective-permute-start.6 = (f32[192,1152]{1,0:T(8,128)S(1)}, f32[192,1152]{1,0:T(8,128)}, u32[]{:S(2)}, u32[]{:S(2)}) collective-permute-start(f32[192,1152]{1,0:T(8,128)S(1)} %collective-permute-done.4.q1), channel_id=1, source_target_pairs={{0,2},{2,0},{4,6},{6,4},{8,10},{10,8},{12,14},{14,12},{16,18},{18,... | collective-permute-start | bytes 2654216 | tf_op jit(solution)/shard_map/ppermute | solution.py:449
  64.1 9.6 %collective-permute-start.7 = (f32[96,768]{1,0:T(8,128)}, f32[96,768]{1,0:T(8,128)S(1)}, u32[]{:S(2)}, u32[]{:S(2)}) collective-permute-start(f32[96,768]{1,0:T(8,128)} %collective-permute-done.1.w0), channel_id=1, source_target_pairs={{0,4},{2,6},{4,0},{6,2},{8,12},{10,14},{12,8},{14,10},{16,20},{18,... | collective-permute-start | bytes 884744 | tf_op jit(solution)/shard_map/ppermute | solution.py:449
  65.9 9.4 %collective-permute-start.8 = (f32[96,768]{1,0:T(8,128)}, f32[96,768]{1,0:T(8,128)S(1)}, u32[]{:S(2)}, u32[]{:S(2)}) collective-permute-start(f32[96,768]{1,0:T(8,128)} %collective-permute-done.1.w0), channel_id=1, source_target_pairs={{0,2},{2,0},{4,6},{6,4},{8,10},{10,8},{12,14},{14,12},{16,18},{18,... | collective-permute-start | bytes 884744 | tf_op jit(solution)/shard_map/ppermute | solution.py:449
  66.1 37.6 %collective-permute-start.2 = (f32[192,1536]{1,0:T(8,128)}, f32[192,1536]{1,0:T(8,128)}, u32[]{:S(2)}, u32[]{:S(2)}) collective-permute-start(f32[192,1536]{1,0:T(8,128)} %dynamic-slice_convert_fusion.1), channel_id=1, source_target_pairs={{0,1},{1,0},{2,3},{3,2},{4,5},{5,4},{6,7},{7,6},{8,9},{9,8},{10,11... | collective-permute-start | bytes 3538952 | tf_op jit(solution)/shard_map/ppermute | solution.py:449
  73.8 46.1 %collective-permute-start.3 = (f32[384,768]{1,0:T(8,128)S(1)}, f32[384,768]{1,0:T(8,128)}, u32[]{:S(2)}, u32[]{:S(2)}) collective-permute-start(f32[384,768]{1,0:T(8,128)S(1)} %dynamic-slice_convert_fusion), channel_id=1, source_target_pairs={{0,1},{1,0},{2,3},{3,2},{4,5},{5,4},{6,7},{7,6},{8,9},{9,8},{10,11... | collective-permute-start | bytes 3538952 | tf_op jit(solution)/shard_map/ppermute | solution.py:449
  75.3 1.6 collective-permute-start.9
  155.1 57.2 %collective-permute-start.11 = (f32[768,768]{1,0:T(8,128)}, f32[768,768]{1,0:T(8,128)S(1)}, u32[]{:S(2)}, u32[]{:S(2)}) collective-permute-start(f32[768,768]{1,0:T(8,128)} %constant_dynamic-slice_fusion.16), channel_id=1, source_target_pairs={{0,2},{2,0},{4,6},{6,4},{8,10},{10,8},{12,14},{14,12},{16,18},{18,... | collective-permute-start | bytes 7077896 | tf_op jit(solution)/shard_map/ppermute | solution.py:449
  158.4 56.7 %collective-permute-start.10 = (f32[384,1536]{1,0:T(8,128)}, f32[384,1536]{1,0:T(8,128)}, u32[]{:S(2)}, u32[]{:S(2)}) collective-permute-start(f32[384,1536]{1,0:T(8,128)} %constant_dynamic-slice_fusion.17), channel_id=1, source_target_pairs={{0,2},{2,0},{4,6},{6,4},{8,10},{10,8},{12,14},{14,12},{16,18},{18,... | collective-permute-start | bytes 7077896 | tf_op jit(solution)/shard_map/ppermute | solution.py:449
  158.9 29.2 %collective-permute-start.12 = (f32[192,1536]{1,0:T(8,128)}, f32[192,1536]{1,0:T(8,128)}, u32[]{:S(2)}, u32[]{:S(2)}) collective-permute-start(f32[192,1536]{1,0:T(8,128)} %collective-permute-done.2.u0), channel_id=1, source_target_pairs={{0,4},{2,6},{4,0},{6,2},{8,12},{10,14},{12,8},{14,10},{16,20},{18,... | collective-permute-start | bytes 3538952 | tf_op jit(solution)/shard_map/ppermute | solution.py:449
  159.1 53.2 %collective-permute-start.13 = (f32[384,768]{1,0:T(8,128)}, f32[384,768]{1,0:T(8,128)}, u32[]{:S(2)}, u32[]{:S(2)}) collective-permute-start(f32[384,768]{1,0:T(8,128)} %collective-permute-done.3.d0), channel_id=1, source_target_pairs={{0,4},{2,6},{4,0},{6,2},{8,12},{10,14},{12,8},{14,10},{16,20},{18,... | collective-permute-start | bytes 3538952 | tf_op jit(solution)/shard_map/ppermute | solution.py:449
  161.5 59.4 %collective-permute-start.14 = (f32[192,1536]{1,0:T(8,128)}, f32[192,1536]{1,0:T(8,128)S(1)}, u32[]{:S(2)}, u32[]{:S(2)}) collective-permute-start(f32[192,1536]{1,0:T(8,128)} %collective-permute-done.2.u0), channel_id=1, source_target_pairs={{0,2},{2,0},{4,6},{6,4},{8,10},{10,8},{12,14},{14,12},{16,18},{18,... | collective-permute-start | bytes 3538952 | tf_op jit(solution)/shard_map/ppermute | solution.py:449
  188.0 34.1 %collective-permute-start.16 = (f32[384,768]{1,0:T(8,128)}, f32[384,768]{1,0:T(8,128)}, u32[]{:S(2)}, u32[]{:S(2)}) collective-permute-start(f32[384,768]{1,0:T(8,128)} %collective-permute-done.3.d0), channel_id=1, source_target_pairs={{0,2},{2,0},{4,6},{6,4},{8,10},{10,8},{12,14},{14,12},{16,18},{18,... | collective-permute-start | bytes 3538952 | tf_op jit(solution)/shard_map/ppermute | solution.py:449
  212.3 9.8 %collective-permute-start.15 = (f32[192,1536]{1,0:T(8,128)}, f32[192,1536]{1,0:T(8,128)}, u32[]{:S(2)}, u32[]{:S(2)}) collective-permute-start(f32[192,1536]{1,0:T(8,128)} %collective-permute-done.12.u1), channel_id=1, source_target_pairs={{0,2},{2,0},{4,6},{6,4},{8,10},{10,8},{12,14},{14,12},{16,18},{18,... | collective-permute-start | bytes 3538952 | tf_op jit(solution)/shard_map/ppermute | solution.py:449
  212.3 9.8 %collective-permute-start.17 = (f32[384,768]{1,0:T(8,128)}, f32[384,768]{1,0:T(8,128)}, u32[]{:S(2)}, u32[]{:S(2)}) collective-permute-start(f32[384,768]{1,0:T(8,128)} %collective-permute-done.13.d1), channel_id=1, source_target_pairs={{0,2},{2,0},{4,6},{6,4},{8,10},{10,8},{12,14},{14,12},{16,18},{18,... | collective-permute-start | bytes 3538952 | tf_op jit(solution)/shard_map/ppermute | solution.py:449
  218.1 37.7 %collective-permute-start.19 = (f32[384,768]{1,0:T(8,128)S(1)}, f32[384,768]{1,0:T(8,128)}, u32[]{:S(2)}, u32[]{:S(2)}) collective-permute-start(f32[384,768]{1,0:T(8,128)S(1)} %constant_dynamic-slice_fusion.14), channel_id=1, source_target_pairs={{0,8},{2,10},{4,12},{6,14},{8,0},{10,2},{12,4},{14,6},{16,24},{18,... | collective-permute-start | bytes 3538952 | tf_op jit(solution)/shard_map/ppermute | solution.py:449
  221.9 35.8 %collective-permute-start.18 = (f32[192,1536]{1,0:T(8,128)}, f32[192,1536]{1,0:T(8,128)}, u32[]{:S(2)}, u32[]{:S(2)}) collective-permute-start(f32[192,1536]{1,0:T(8,128)} %constant_dynamic-slice_fusion.15), channel_id=1, source_target_pairs={{0,4},{2,6},{4,0},{6,2},{8,12},{10,14},{12,8},{14,10},{16,20},{18,... | collective-permute-start | bytes 3538952 | tf_op jit(solution)/shard_map/ppermute | solution.py:449
  260.5 28.8 %collective-permute-start.21 = (f32[192,768]{1,0:T(8,128)}, f32[192,768]{1,0:T(8,128)}, u32[]{:S(2)}, u32[]{:S(2)}) collective-permute-start(f32[192,768]{1,0:T(8,128)} %constant_dynamic-slice_fusion.12), channel_id=1, source_target_pairs={{0,4},{2,6},{4,0},{6,2},{8,12},{10,14},{12,8},{14,10},{16,20},{18,... | collective-permute-start | bytes 1769480 | tf_op jit(solution)/shard_map/ppermute | solution.py:449
  262.3 29.0 %collective-permute-start.20 = (f32[96,1536]{1,0:T(8,128)S(1)}, f32[96,1536]{1,0:T(8,128)}, u32[]{:S(2)}, u32[]{:S(2)}) collective-permute-start(f32[96,1536]{1,0:T(8,128)S(1)} %constant_dynamic-slice_fusion.13), channel_id=1, source_target_pairs={{0,8},{2,10},{4,12},{6,14},{8,0},{10,2},{12,4},{14,6},{16,24},{18,... | collective-permute-start | bytes 1769480 | tf_op jit(solution)/shard_map/ppermute | solution.py:449
  289.3 51.7 %collective-permute-start.26 = (f32[192,768]{1,0:T(8,128)}, f32[192,768]{1,0:T(8,128)}, u32[]{:S(2)}, u32[]{:S(2)}) collective-permute-start(f32[192,768]{1,0:T(8,128)} %constant_dynamic-slice_fusion.9), channel_id=1, source_target_pairs={{0,2},{2,0},{4,6},{6,4},{8,10},{10,8},{12,14},{14,12},{16,18},{18,... | collective-permute-start | bytes 1769480 | tf_op jit(solution)/shard_map/ppermute | solution.py:449
  311.3 34.9 %collective-permute-start.25 = (f32[576,384]{1,0:T(8,128)}, f32[576,384]{1,0:T(8,128)}, u32[]{:S(2)}, u32[]{:S(2)}) collective-permute-start(f32[576,384]{1,0:T(8,128)} %dynamic-slice_bitcast_fusion), channel_id=1, source_target_pairs={{0,2},{2,0},{4,6},{6,4},{8,10},{10,8},{12,14},{14,12},{16,18},{18,... | collective-permute-start | bytes 2654216 | tf_op jit(solution)/shard_map/ppermute | solution.py:449
  312.3 35.2 %collective-permute-start.24 = (f32[576,384]{1,0:T(8,128)}, f32[576,384]{1,0:T(8,128)}, u32[]{:S(2)}, u32[]{:S(2)}) collective-permute-start(f32[576,384]{1,0:T(8,128)} %dynamic-slice_bitcast_fusion.1), channel_id=1, source_target_pairs={{0,2},{2,0},{4,6},{6,4},{8,10},{10,8},{12,14},{14,12},{16,18},{18,... | collective-permute-start | bytes 2654216 | tf_op jit(solution)/shard_map/ppermute | solution.py:449
  313.5 29.0 %collective-permute-start.23 = (f32[96,768]{1,0:T(8,128)}, f32[96,768]{1,0:T(8,128)}, u32[]{:S(2)}, u32[]{:S(2)}) collective-permute-start(f32[96,768]{1,0:T(8,128)} %constant_dynamic-slice_fusion.10), channel_id=1, source_target_pairs={{0,16},{2,18},{4,20},{6,22},{8,24},{10,26},{12,28},{14,30},{16,0},... | collective-permute-start | bytes 884744 | tf_op jit(solution)/shard_map/ppermute | solution.py:449
  314.3 30.3 %collective-permute-start.22 = (f32[48,1536]{1,0:T(8,128)}, f32[48,1536]{1,0:T(8,128)}, u32[]{:S(2)}, u32[]{:S(2)}) collective-permute-start(f32[48,1536]{1,0:T(8,128)} %constant_dynamic-slice_fusion.11), channel_id=1, source_target_pairs={{0,16},{2,18},{4,20},{6,22},{8,24},{10,26},{12,28},{14,30},{16,0},... | collective-permute-start | bytes 884744 | tf_op jit(solution)/shard_map/ppermute | solution.py:449
  342.5 9.6 %copy-start.13 = (f32[192,768]{1,0:T(8,128)}, f32[192,768]{1,0:T(8,128)S(1)}, u32[]{:S(2)}) copy-start(f32[192,768]{1,0:T(8,128)S(1)} %dynamic-slice_add_fusion.4) | copy-start | bytes 1769476
  349.1 24.0 %collective-permute-start.31 = (f32[96,768]{1,0:T(8,128)}, f32[96,768]{1,0:T(8,128)}, u32[]{:S(2)}, u32[]{:S(2)}) collective-permute-start(f32[96,768]{1,0:T(8,128)} %dynamic-slice_add_fusion.10), channel_id=1, source_target_pairs={{0,16},{2,18},{4,20},{6,22},{8,24},{10,26},{12,28},{14,30},{16,0},... | collective-permute-start | bytes 884744 | tf_op jit(solution)/shard_map/ppermute | solution.py:449
  349.2 28.2 %collective-permute-start.30 = (f32[48,1536]{1,0:T(8,128)}, f32[48,1536]{1,0:T(8,128)}, u32[]{:S(2)}, u32[]{:S(2)}) collective-permute-start(f32[48,1536]{1,0:T(8,128)} %dynamic-slice_add_fusion.11), channel_id=1, source_target_pairs={{0,16},{2,18},{4,20},{6,22},{8,24},{10,26},{12,28},{14,30},{16,0},... | collective-permute-start | bytes 884744 | tf_op jit(solution)/shard_map/ppermute | solution.py:449
  352.8 25.9 %collective-permute-start.29 = (f32[96,768]{1,0:T(8,128)}, f32[96,768]{1,0:T(8,128)}, u32[]{:S(2)}, u32[]{:S(2)}) collective-permute-start(f32[96,768]{1,0:T(8,128)} %constant_dynamic-slice_fusion.6), channel_id=1, source_target_pairs={{0,8},{2,10},{4,12},{6,14},{8,0},{10,2},{12,4},{14,6},{16,24},{18,... | collective-permute-start | bytes 884744 | tf_op jit(solution)/shard_map/ppermute | solution.py:449
  354.9 26.5 %collective-permute-start.28 = (f32[288,384]{1,0:T(8,128)S(1)}, f32[288,384]{1,0:T(8,128)S(1)}, u32[]{:S(2)}, u32[]{:S(2)}) collective-permute-start(f32[288,384]{1,0:T(8,128)S(1)} %constant_dynamic-slice_fusion.7), channel_id=1, source_target_pairs={{0,8},{2,10},{4,12},{6,14},{8,0},{10,2},{12,4},{14,6},{16,24},{18,... | collective-permute-start | bytes 1327112 | tf_op jit(solution)/shard_map/ppermute | solution.py:449
  355.0 26.4 %collective-permute-start.27 = (f32[288,384]{1,0:T(8,128)S(1)}, f32[288,384]{1,0:T(8,128)S(1)}, u32[]{:S(2)}, u32[]{:S(2)}) collective-permute-start(f32[288,384]{1,0:T(8,128)S(1)} %constant_dynamic-slice_fusion.8), channel_id=1, source_target_pairs={{0,4},{2,6},{4,0},{6,2},{8,12},{10,14},{12,8},{14,10},{16,20},{18,... | collective-permute-start | bytes 1327112 | tf_op jit(solution)/shard_map/ppermute | solution.py:449
  381.5 9.1 %collective-permute-start.52 = (f32[48,768]{1,0:T(8,128)S(1)}, f32[48,768]{1,0:T(8,128)S(1)}, u32[]{:S(2)}, u32[]{:S(2)}) collective-permute-start(f32[48,768]{1,0:T(8,128)S(1)} %constant_dynamic-slice_fusion.1), channel_id=1, source_target_pairs={{0,4},{2,6},{4,0},{6,2},{8,12},{10,14},{12,8},{14,10},{16,20},{18,... | collective-permute-start | bytes 442376 | tf_op jit(solution)/shard_map/ppermute | solution.py:449
  384.0 5.1 %collective-permute-start.34 = (f32[16,768]{1,0:T(8,128)S(1)}, f32[16,768]{1,0:T(8,128)S(1)}, u32[]{:S(2)}, u32[]{:S(2)}) collective-permute-start(f32[16,768]{1,0:T(8,128)S(1)} %constant_dynamic-update-slice_fusion), channel_id=1, source_target_pairs={{0,16},{2,18},{4,20},{6,22},{8,24},{10,26},{12,28},{14,30},{16,0},... | collective-permute-start | bytes 147464 | tf_op jit(solution)/shard_map/ppermute | solution.py:449
  384.0 27.4 %collective-permute-start.33 = (f32[192,768]{1,0:T(8,128)S(1)}, f32[192,768]{1,0:T(8,128)S(1)}, u32[]{:S(2)}, u32[]{:S(2)}) collective-permute-start(f32[192,768]{1,0:T(8,128)S(1)} %maximum_select_fusion.12), channel_id=1, source_target_pairs={{0,4},{2,6},{4,0},{6,2},{8,12},{10,14},{12,8},{14,10},{16,20},{18,... | collective-permute-start | bytes 1769480 | tf_op jit(solution)/shard_map/ppermute | solution.py:449
  385.9 25.6 %collective-permute-start.32 = (f32[96,1536]{1,0:T(8,128)S(1)}, f32[96,1536]{1,0:T(8,128)S(1)}, u32[]{:S(2)}, u32[]{:S(2)}) collective-permute-start(f32[96,1536]{1,0:T(8,128)S(1)} %maximum_select_fusion.11), channel_id=1, source_target_pairs={{0,8},{2,10},{4,12},{6,14},{8,0},{10,2},{12,4},{14,6},{16,24},{18,... | collective-permute-start | bytes 1769480 | tf_op jit(solution)/shard_map/ppermute | solution.py:449
  388.4 21.6 %collective-permute-start.40 = (f32[144,384]{1,0:T(8,128)S(1)}, f32[144,384]{1,0:T(8,128)S(1)}, u32[]{:S(2)}, u32[]{:S(2)}) collective-permute-start(f32[144,384]{1,0:T(8,128)S(1)} %constant_dynamic-slice_fusion.5), channel_id=1, source_target_pairs={{0,8},{2,10},{4,12},{6,14},{8,0},{10,2},{12,4},{14,6},{16,24},{18,... | collective-permute-start | bytes 663560 | tf_op jit(solution)/shard_map/ppermute | solution.py:449
  389.1 18.8 %collective-permute-start.35 = (f32[16,768]{1,0:T(8,128)S(1)}, f32[16,768]{1,0:T(8,128)S(1)}, u32[]{:S(2)}, u32[]{:S(2)}) collective-permute-start(f32[16,768]{1,0:T(8,128)S(1)} %add.286), channel_id=1, source_target_pairs={{0,8},{2,10},{4,12},{6,14},{8,0},{10,2},{12,4},{14,6},{16,24},{18,... | collective-permute-start | bytes 147464 | tf_op jit(solution)/shard_map/ppermute | solution.py:449
  390.7 17.6 %collective-permute-start.53 = (f32[24,768]{1,0:T(8,128)S(1)}, f32[24,768]{1,0:T(8,128)S(1)}, u32[]{:S(2)}, u32[]{:S(2)}) collective-permute-start(f32[24,768]{1,0:T(8,128)S(1)} %constant_dynamic-slice_fusion), channel_id=1, source_target_pairs={{0,16},{2,18},{4,20},{6,22},{8,24},{10,26},{12,28},{14,30},{16,0},... | collective-permute-start | bytes 221192 | tf_op jit(solution)/shard_map/ppermute | solution.py:449
  407.9 8.0 %collective-permute-start.46 = (f32[144,384]{1,0:T(8,128)S(1)}, f32[144,384]{1,0:T(8,128)S(1)}, u32[]{:S(2)}, u32[]{:S(2)}) collective-permute-start(f32[144,384]{1,0:T(8,128)S(1)} %constant_dynamic-slice_fusion.3), channel_id=1, source_target_pairs={{0,4},{2,6},{4,0},{6,2},{8,12},{10,14},{12,8},{14,10},{16,20},{18,... | collective-permute-start | bytes 663560 | tf_op jit(solution)/shard_map/ppermute | solution.py:449
  408.3 40.6 %collective-permute-start.54 = (f32[24,768]{1,0:T(8,128)S(1)}, f32[24,768]{1,0:T(8,128)S(1)}, u32[]{:S(2)}, u32[]{:S(2)}) collective-permute-start(f32[24,768]{1,0:T(8,128)S(1)} %dynamic-slice_add_fusion.17), channel_id=1, source_target_pairs={{0,16},{2,18},{4,20},{6,22},{8,24},{10,26},{12,28},{14,30},{16,0},... | collective-permute-start | bytes 221192 | tf_op jit(solution)/shard_map/ppermute | solution.py:449
  410.1 9.4 %collective-permute-start.41 = (f32[72,384]{1,0:T(8,128)S(1)}, f32[72,384]{1,0:T(8,128)S(1)}, u32[]{:S(2)}, u32[]{:S(2)}) collective-permute-start(f32[72,384]{1,0:T(8,128)S(1)} %constant_dynamic-slice_fusion.4), channel_id=1, source_target_pairs={{0,16},{2,18},{4,20},{6,22},{8,24},{10,26},{12,28},{14,30},{16,0},... | collective-permute-start | bytes 331784 | tf_op jit(solution)/shard_map/ppermute | solution.py:449
  411.6 47.3 %collective-permute-start.36 = (f32[192,1536]{1,0:T(8,128)S(1)}, f32[192,1536]{1,0:T(8,128)S(1)}, u32[]{:S(2)}, u32[]{:S(2)}) collective-permute-start(f32[192,1536]{1,0:T(8,128)S(1)} %maximum_select_fusion.6), channel_id=1, source_target_pairs={{0,4},{2,6},{4,0},{6,2},{8,12},{10,14},{12,8},{14,10},{16,20},{18,... | collective-permute-start | bytes 3538952 | tf_op jit(solution)/shard_map/ppermute | solution.py:449
  416.0 7.5 %collective-permute-start.47 = (f32[72,384]{1,0:T(8,128)S(1)}, f32[72,384]{1,0:T(8,128)S(1)}, u32[]{:S(2)}, u32[]{:S(2)}) collective-permute-start(f32[72,384]{1,0:T(8,128)S(1)} %constant_dynamic-slice_fusion.2), channel_id=1, source_target_pairs={{0,16},{2,18},{4,20},{6,22},{8,24},{10,26},{12,28},{14,30},{16,0},... | collective-permute-start | bytes 331784 | tf_op jit(solution)/shard_map/ppermute | solution.py:449
  416.0 43.1 %collective-permute-start.37 = (f32[384,768]{1,0:T(8,128)S(1)}, f32[384,768]{1,0:T(8,128)S(1)}, u32[]{:S(2)}, u32[]{:S(2)}) collective-permute-start(f32[384,768]{1,0:T(8,128)S(1)} %maximum_select_fusion.7), channel_id=1, source_target_pairs={{0,8},{2,10},{4,12},{6,14},{8,0},{10,2},{12,4},{14,6},{16,24},{18,... | collective-permute-start | bytes 3538952 | tf_op jit(solution)/shard_map/ppermute | solution.py:449
  419.6 27.2 %collective-permute-start.42 = (f32[72,384]{1,0:T(8,128)S(1)}, f32[72,384]{1,0:T(8,128)S(1)}, u32[]{:S(2)}, u32[]{:S(2)}) collective-permute-start(f32[72,384]{1,0:T(8,128)S(1)} %dynamic-slice_add_fusion.16), channel_id=1, source_target_pairs={{0,16},{2,18},{4,20},{6,22},{8,24},{10,26},{12,28},{14,30},{16,0},... | collective-permute-start | bytes 331784 | tf_op jit(solution)/shard_map/ppermute | solution.py:449
  423.5 26.4 %collective-permute-start.48 = (f32[72,384]{1,0:T(8,128)S(1)}, f32[72,384]{1,0:T(8,128)S(1)}, u32[]{:S(2)}, u32[]{:S(2)}) collective-permute-start(f32[72,384]{1,0:T(8,128)S(1)} %dynamic-slice_add_fusion.15), channel_id=1, source_target_pairs={{0,16},{2,18},{4,20},{6,22},{8,24},{10,26},{12,28},{14,30},{16,0},... | collective-permute-start | bytes 331784 | tf_op jit(solution)/shard_map/ppermute | solution.py:449
  446.8 10.9 %collective-permute-start.43 = (f32[144,384]{1,0:T(8,128)S(1)}, f32[144,384]{1,0:T(8,128)S(1)}, u32[]{:S(2)}, u32[]{:S(2)}) collective-permute-start(f32[144,384]{1,0:T(8,128)S(1)} %maximum_select_fusion.17), channel_id=1, source_target_pairs={{0,8},{2,10},{4,12},{6,14},{8,0},{10,2},{12,4},{14,6},{16,24},{18,... | collective-permute-start | bytes 663560 | tf_op jit(solution)/shard_map/ppermute | solution.py:449
  449.0 11.8 %collective-permute-start.55 = (f32[48,768]{1,0:T(8,128)S(1)}, f32[48,768]{1,0:T(8,128)S(1)}, u32[]{:S(2)}, u32[]{:S(2)}) collective-permute-start(f32[48,768]{1,0:T(8,128)S(1)} %maximum_select_fusion.19), channel_id=1, source_target_pairs={{0,4},{2,6},{4,0},{6,2},{8,12},{10,14},{12,8},{14,10},{16,20},{18,... | collective-permute-start | bytes 442376 | tf_op jit(solution)/shard_map/ppermute | solution.py:449
  449.9 6.9 %collective-permute-start.38 = (f32[16,768]{1,0:T(8,128)S(1)}, f32[16,768]{1,0:T(8,128)S(1)}, u32[]{:S(2)}, u32[]{:S(2)}) collective-permute-start(f32[16,768]{1,0:T(8,128)S(1)} %add.287), channel_id=1, source_target_pairs={{0,4},{2,6},{4,0},{6,2},{8,12},{10,14},{12,8},{14,10},{16,20},{18,... | collective-permute-start | bytes 147464 | tf_op jit(solution)/shard_map/ppermute | solution.py:449
  456.8 5.9 %collective-permute-start.49 = (f32[144,384]{1,0:T(8,128)S(1)}, f32[144,384]{1,0:T(8,128)S(1)}, u32[]{:S(2)}, u32[]{:S(2)}) collective-permute-start(f32[144,384]{1,0:T(8,128)S(1)} %maximum_select_fusion.18), channel_id=1, source_target_pairs={{0,4},{2,6},{4,0},{6,2},{8,12},{10,14},{12,8},{14,10},{16,20},{18,... | collective-permute-start | bytes 663560 | tf_op jit(solution)/shard_map/ppermute | solution.py:449
  457.7 9.7 %collective-permute-start.44 = (f32[288,384]{1,0:T(8,128)S(1)}, f32[288,384]{1,0:T(8,128)S(1)}, u32[]{:S(2)}, u32[]{:S(2)}) collective-permute-start(f32[288,384]{1,0:T(8,128)S(1)} %maximum_select_fusion.14), channel_id=1, source_target_pairs={{0,4},{2,6},{4,0},{6,2},{8,12},{10,14},{12,8},{14,10},{16,20},{18,... | collective-permute-start | bytes 1327112 | tf_op jit(solution)/shard_map/ppermute | solution.py:449
  460.8 29.9 %collective-permute-start.59 = (f32[768,768]{1,0:T(8,128)}, f32[768,768]{1,0:T(8,128)}, u32[]{:S(2)}, u32[]{:S(2)}) collective-permute-start(f32[768,768]{1,0:T(8,128)} %maximum_select_fusion.3), channel_id=1, source_target_pairs={{0,2},{2,0},{4,6},{6,4},{8,10},{10,8},{12,14},{14,12},{16,18},{18,... | collective-permute-start | bytes 7077896 | tf_op jit(solution)/shard_map/ppermute | solution.py:449
  460.8 9.9 %collective-permute-start.56 = (f32[96,768]{1,0:T(8,128)S(1)}, f32[96,768]{1,0:T(8,128)S(1)}, u32[]{:S(2)}, u32[]{:S(2)}) collective-permute-start(f32[96,768]{1,0:T(8,128)S(1)} %maximum_select_fusion.16), channel_id=1, source_target_pairs={{0,8},{2,10},{4,12},{6,14},{8,0},{10,2},{12,4},{14,6},{16,24},{18,... | collective-permute-start | bytes 884744 | tf_op jit(solution)/shard_map/ppermute | solution.py:449
  462.8 17.0 %collective-permute-start.50 = (f32[288,384]{1,0:T(8,128)S(1)}, f32[288,384]{1,0:T(8,128)S(1)}, u32[]{:S(2)}, u32[]{:S(2)}) collective-permute-start(f32[288,384]{1,0:T(8,128)S(1)} %maximum_select_fusion.15), channel_id=1, source_target_pairs={{0,8},{2,10},{4,12},{6,14},{8,0},{10,2},{12,4},{14,6},{16,24},{18,... | collective-permute-start | bytes 1327112 | tf_op jit(solution)/shard_map/ppermute | solution.py:449
  467.5 17.3 %collective-permute-start.45 = (f32[576,384]{1,0:T(8,128)S(1)}, f32[576,384]{1,0:T(8,128)}, u32[]{:S(2)}, u32[]{:S(2)}) collective-permute-start(f32[576,384]{1,0:T(8,128)S(1)} %maximum_select_fusion.9), channel_id=1, source_target_pairs={{0,2},{2,0},{4,6},{6,4},{8,10},{10,8},{12,14},{14,12},{16,18},{18,... | collective-permute-start | bytes 2654216 | tf_op jit(solution)/shard_map/ppermute | solution.py:449
  467.6 29.6 %collective-permute-start.58 = (f32[384,1536]{1,0:T(8,128)S(1)}, f32[384,1536]{1,0:T(8,128)}, u32[]{:S(2)}, u32[]{:S(2)}) collective-permute-start(f32[384,1536]{1,0:T(8,128)S(1)} %maximum_select_fusion.2), channel_id=1, source_target_pairs={{0,2},{2,0},{4,6},{6,4},{8,10},{10,8},{12,14},{14,12},{16,18},{18,... | collective-permute-start | bytes 7077896 | tf_op jit(solution)/shard_map/ppermute | solution.py:449
  471.6 9.1 %collective-permute-start.57 = (f32[192,768]{1,0:T(8,128)}, f32[192,768]{1,0:T(8,128)}, u32[]{:S(2)}, u32[]{:S(2)}) collective-permute-start(f32[192,768]{1,0:T(8,128)} %maximum_select_fusion.13), channel_id=1, source_target_pairs={{0,2},{2,0},{4,6},{6,4},{8,10},{10,8},{12,14},{14,12},{16,18},{18,... | collective-permute-start | bytes 1769480 | tf_op jit(solution)/shard_map/ppermute | solution.py:449
  480.7 5.7 %collective-permute-start.51 = (f32[576,384]{1,0:T(8,128)}, f32[576,384]{1,0:T(8,128)}, u32[]{:S(2)}, u32[]{:S(2)}) collective-permute-start(f32[576,384]{1,0:T(8,128)} %maximum_select_fusion.10), channel_id=1, source_target_pairs={{0,2},{2,0},{4,6},{6,4},{8,10},{10,8},{12,14},{14,12},{16,18},{18,... | collective-permute-start | bytes 2654216 | tf_op jit(solution)/shard_map/ppermute | solution.py:449
  480.8 3.4 collective-permute-start.39
  (27 other events, 120.7 us)

commit v5 on v4

--- a/solution.py
+++ b/solution.py
@@ -53,30 +53,52 @@
     return lane < HD
 
 
+def by_size(counts, s, run):
+    few = counts[s] <= SLOTS // 2
+
+    @pl.when(few)
+    def _():
+        run(SLOTS // 2)
+
+    @pl.when(jnp.logical_not(few))
+    def _():
+        run(SLOTS)
+
+
+def lanes(start):
+    return pl.ds(pl.multiple_of(start, 128), 128)
+
+
 def attend_rows(counts, qkv, out, lse, samples, width):
     left = lane_halves()
-    row = lax.broadcasted_iota(jnp.int32, (SLOTS, 1), 0)
 
     def one(s, start):
-        rows = win(start)
-        live = row < counts[s]
-        for pair in range(width // 128):
-            lo = pair * 128
-            q = qkv[rows, lo:lo + 128]
-            k = qkv[rows, width + lo:width + lo + 128]
-            v = qkv[rows, 2 * width + lo:2 * width + lo + 128]
-            parts = []
-            for side in range(2):
-                keep = left if side == 0 else ~left
-                sc = dot(jnp.where(keep, k, jnp.zeros_like(k)), q, NT) * scale
-                sc = jnp.where(live, sc, masked_score)
-                top = jnp.max(sc, axis=0, keepdims=True)
-                w = jnp.exp(sc - top)
-                tot = jnp.sum(w, axis=0, keepdims=True)
-                lse[s, 2 * pair + side:2 * pair + side + 1, :] = top + jnp.log(tot)
-                p = (w * (1.0 / tot)).astype(bf16)
-                parts.append(dot(p, v, TN))
-            out[rows, lo:lo + 128] = jnp.where(left, parts[0], parts[1]).astype(bf16)
+        def run(size):
+            rows = win(start, size)
+            live = lax.broadcasted_iota(jnp.int32, (size, 1), 0) < counts[s]
+
+            def pair(j, x):
+                lo = j * 128
+                q = qkv[rows, lanes(lo)]
+                k = qkv[rows, lanes(width + lo)]
+                v = qkv[rows, lanes(2 * width + lo)]
+                parts = []
+                for side in range(2):
+                    keep = left if side == 0 else ~left
+                    sc = dot(jnp.where(keep, k, jnp.zeros_like(k)), q, NT) * scale
+                    sc = jnp.where(live, sc, masked_score)
+                    top = jnp.max(sc, axis=0, keepdims=True)
+                    w = jnp.exp(sc - top)
+                    tot = jnp.sum(w, axis=0, keepdims=True)
+                    lse[s, j, side:side + 1, :size] = top + jnp.log(tot)
+                    p = (w * (1.0 / tot)).astype(bf16)
+                    parts.append(dot(p, v, TN))
+                out[rows, lanes(lo)] = jnp.where(left, parts[0], parts[1]).astype(bf16)
+                return x
+
+            lax.fori_loop(0, width // 128, pair, 0)
+
+        by_size(counts, s, run)
         return start + ((counts[s] + 15) // 16) * 16
 
     lax.fori_loop(0, samples, one, 0)
@@ -236,34 +258,40 @@
 
 def attend_back(counts, qkv, do, lse, dqkv, samples, width):
     left = lane_halves()
-    row = lax.broadcasted_iota(jnp.int32, (SLOTS, 1), 0)
 
     def one(s, start):
-        rows = win(start)
-        live = row < counts[s]
-        for pair in range(width // 128):
-            lo = pair * 128
-            q = qkv[rows, lo:lo + 128]
-            k = qkv[rows, width + lo:width + lo + 128]
-            v = qkv[rows, 2 * width + lo:2 * width + lo + 128]
-            dov = do[rows, lo:lo + 128]
-            dov = jnp.where(live, dov, jnp.zeros_like(dov))
-            zero = jnp.zeros_like(k)
-            dq, dk, dvv = [], [], []
-            for side in range(2):
-                keep = left if side == 0 else ~left
-                sc = dot(jnp.where(keep, k, zero), q, NT) * scale
-                sc = jnp.where(live, sc, masked_score)
-                p = jnp.exp(sc - lse[s, 2 * pair + side:2 * pair + side + 1, :])
-                dp = dot(jnp.where(keep, v, zero), dov, NT)
-                t = jnp.sum(p * dp, axis=0, keepdims=True)
-                ds = (p * (dp - t)).astype(bf16)
-                dq.append(dot(ds, k, TN))
-                dk.append(dot(ds, q))
-                dvv.append(dot(p.astype(bf16), dov))
-            dqkv[rows, lo:lo + 128] = (jnp.where(left, dq[0], dq[1]) * scale).astype(bf16)
-            dqkv[rows, width + lo:width + lo + 128] = (jnp.where(left, dk[0], dk[1]) * scale).astype(bf16)
-            dqkv[rows, 2 * width + lo:2 * width + lo + 128] = jnp.where(left, dvv[0], dvv[1]).astype(bf16)
+        def run(size):
+            rows = win(start, size)
+            live = lax.broadcasted_iota(jnp.int32, (size, 1), 0) < counts[s]
+
+            def pair(j, x):
+                lo = j * 128
+                q = qkv[rows, lanes(lo)]
+                k = qkv[rows, lanes(width + lo)]
+                v = qkv[rows, lanes(2 * width + lo)]
+                dov = do[rows, lanes(lo)]
+                dov = jnp.where(live, dov, jnp.zeros_like(dov))
+                zero = jnp.zeros_like(k)
+                dq, dk, dvv = [], [], []
+                for side in range(2):
+                    keep = left if side == 0 else ~left
+                    sc = dot(jnp.where(keep, k, zero), q, NT) * scale
+                    sc = jnp.where(live, sc, masked_score)
+                    p = jnp.exp(sc - lse[s, j, side:side + 1, :size])
+                    dp = dot(jnp.where(keep, v, zero), dov, NT)
+                    t = jnp.sum(p * dp, axis=0, keepdims=True)
+                    ds = (p * (dp - t)).astype(bf16)
+                    dq.append(dot(ds, k, TN))
+                    dk.append(dot(ds, q))
+                    dvv.append(dot(p.astype(bf16), dov))
+                dqkv[rows, lanes(lo)] = (jnp.where(left, dq[0], dq[1]) * scale).astype(bf16)
+                dqkv[rows, lanes(width + lo)] = (jnp.where(left, dk[0], dk[1]) * scale).astype(bf16)
+                dqkv[rows, lanes(2 * width + lo)] = jnp.where(left, dvv[0], dvv[1]).astype(bf16)
+                return x
+
+            lax.fori_loop(0, width // 128, pair, 0)
+
+        by_size(counts, s, run)
         return start + ((counts[s] + 15) // 16) * 16
 
     lax.fori_loop(0, samples, one, 0)
@@ -378,7 +406,7 @@
     whole = lambda d: (lambda s, n: (0,) * d)
     one = lambda s, n: (s, 0, 0)
     B1 = pl.Buffered(1)
-    outs = [sds((TP, D), bf16), sds((TP, D), bf16), sds((TP, D), bf16), sds((TP, 3 * width), bf16), sds((TP, width), bf16), sds((S, width // HD, SLOTS), f32)]
+    outs = [sds((TP, D), bf16), sds((TP, D), bf16), sds((TP, D), bf16), sds((TP, 3 * width), bf16), sds((TP, width), bf16), sds((S, width // 128, 2, SLOTS), f32)]
     return pl.pallas_call(
         fwd_own_body(S, width),
         name="fwd_own",
@@ -404,7 +432,7 @@
 def fwd_other(counts, a, h, o, wq, out_own, wo, gain, shift, S):
     TP, D = a.shape
     width = wq[0].shape[1] // 3
-    outs = [sds((TP, 3 * width), bf16), sds((TP, width), bf16), sds((S, width // HD, SLOTS), f32), sds((TP, D), f32), sds((TP, D), bf16), sds((D, 3 * width), bf16), sds((width, D), bf16)]
+    outs = [sds((TP, 3 * width), bf16), sds((TP, width), bf16), sds((S, width // 128, 2, SLOTS), f32), sds((TP, D), f32), sds((TP, D), bf16), sds((D, 3 * width), bf16), sds((width, D), bf16)]
     return call(fwd_other_body(S, width), counts, [a, h, o, *wq, *wo, out_own, gain, shift], outs, flops=7 * 10**9)
 
 
@@ -509,8 +537,10 @@
     fq, fo = swap(part(wq), "tensor", 2, 1), swap(part(wo), "tensor", 2, 1)
     h, dm, a, qkv0, o0, lse0 = fwd_own(counts, col, patches, cot, g1, b1, wq)
     fq, fo, pu, pd, a = tie(fq, fo, part(wu), part(wd), a)
-    aq, ao = swap(fq, "dp", dp, 2), swap(fo, "dp", dp, 2)
-    fu, fd = swap(pu, "tensor", 2, 1), swap(pd, "tensor", 2, 1)
+    aq = swap(fq, "dp", dp, 2)
+    ao = swap(fo, "dp", dp, 2)
+    fu = swap(pu, "tensor", 2, 1)
+    fd = swap(pd, "tensor", 2, 1)
     wq1, wo1 = rest(fq, aq), rest(fo, ao)
     qkv1, _, lse1, r, c, wq1, wo1 = fwd_other(counts, a, h, o0, wq1, wo, wo1, g2, b2, S)
     fu, fd, c = tie(fu, fd, c)

time: 504 us -> 517 us (1.026)
  Pallas kernels: 199 us -> 218 us
  waiting for transfers between devices: 168 us -> 156 us
  starting transfers between devices: 50.9 us -> 56.3 us
    ppermute x60, waiting for transfers between devices: 168 us -> 156 us  [swap(): return lax.ppermute(x, axis, [(k, k ^ bit) for k in range(size)])]
    pallas_call x7, Pallas kernels: 173 us -> 184 us  [call(): pl.pallas_call(body, out_shape=list(outs), grid_spec=pltpu.PrefetchScalar...]
    pallas_call x1, Pallas kernels: 26 us -> 33.9 us  [fwd_own(): pl.pallas_call(fwd_own_body(S, width), name='fwd_own', out_shape=outs, gr...]
    ppermute x60, starting transfers between devices: 50.9 us -> 56.3 us  [swap(): return lax.ppermute(x, axis, [(k, k ^ bit) for k in range(size)])]
  transfers between devices with their start and end apart: 60 -> 60, of which waited for: 19 -> 18; matrix products, arithmetic and copies ran while one was open for 13% -> 12% of each run, Pallas kernels for 33% -> 36%
where the time goes in v5:
time: 517 us; the launch traced here: 516 us
  Pallas kernels  218 us (42%)
  waiting for transfers between devices  156 us (30%)
  starting transfers between devices  56.3 us (11%)
  other arithmetic  55.9 us (11%)
  local copies, waits for them, and re-layouts  28.1 us (5%)
    pallas_call x7, Pallas kernels, call(): pl.pallas_call(body, out_shape=list(outs), grid_spec=pltpu.PrefetchScalar...  184 us
    ppermute x60, waiting for transfers between devices, swap(): return lax.ppermute(x, axis, [(k, k ^ bit) for k in range(size)])  156 us
    ppermute x60, starting transfers between devices, swap(): return lax.ppermute(x, axis, [(k, k ^ bit) for k in range(size)])  56.3 us
    pallas_call x1, Pallas kernels, fwd_own(): pl.pallas_call(fwd_own_body(S, width), name='fwd_own', out_shape=outs, gr...  33.9 us
    select_n x20, other arithmetic, spread(): jnp.where(first, jnp.concatenate([x, got], 0), jnp.concatenate([got, x], 0))  25.3 us
    add x20, other arithmetic, fold(): return half(x, i) + swap(half(x, 1 - i), 'dp', dp, bit)  21.3 us
    dynamic_slice x20, local copies, waits for them, and re-layouts, half(): return lax.dynamic_slice_in_dim(x, i * n, n, 0)  14.9 us
  transfers between devices with their start and end apart: 60, of which 18 were waited for; matrix products, arithmetic and copies ran while one was open for 12% of the time, Pallas kernels for 36%

profile of v5, /device:TPU:0, one launch (start us, length us, event | category | flops | bytes accessed | tf_op | source)
XLA Modules:
  0.0 515.6 jit_solution(8429111774811228720)
XLA Ops:
  0.7 2.4 slice_bitcast_fusion.2
  5.3 3.0 collective-permute-start
  8.3 1.6 dynamic-slice_convert_fusion.3
  10.6 1.7 copy.22.col
  13.5 33.9 %fwd_own.1 = (bf16[1792,768]{1,0:T(8,128)(2,1)}, bf16[1792,768]{1,0:T(8,128)(2,1)}, bf16[1792,768]{1,0:T(8,128)(2,1)}, bf16[1792,1152]{1,0:T(8,128)(2,1)}, bf16[...) custom-call(s32[10]{0:T(128)} %concatenate.132.counts, s32[6,512,1]{2,1,0:T(8,128)} %copy.22.col, ...), custom_call_target="tpu_custom_call" | custom-call | flops 6000000000 | bytes 26214400 | tf_op jit(solution)/shard_map/fwd_own/pallas_call | solution.py:410
  48.6 2.2 dynamic-slice_convert_fusion.1
  52.1 19.3 %collective-permute-done.4.q1 = f32[192,1152]{1,0:T(8,128)S(1)} collective-permute-done((f32[192,1152]{1,0:T(8,128)}, f32[192,1152]{1,0:T(8,128)S(1)}, u32[]{:S(2)}, u32[]{:S(2)}) %collective-permute-start.4) | collective-permute-done | bytes 884768 | tf_op jit(solution)/shard_map/ppermute | solution.py:477
  71.4 1.7 collective-permute-start.7
  74.9 6.1 %collective-permute-done.7.w1 = f32[96,768]{1,0:T(8,128)S(1)} collective-permute-done((f32[96,768]{1,0:T(8,128)}, f32[96,768]{1,0:T(8,128)S(1)}, u32[]{:S(2)}, u32[]{:S(2)}) %collective-permute-start.7) | collective-permute-done | bytes 294944 | tf_op jit(solution)/shard_map/ppermute | solution.py:477
  81.1 1.6 collective-permute-start.3
  84.9 34.1 %shard_map.195 = (bf16[1792,1152]{1,0:T(8,128)(2,1)}, bf16[1792,384]{1,0:T(8,128)(2,1)}, f32[6,3,2,256]{3,2,1,0:T(2,128)}, f32[1792,768]{1,0:T(8,128)}, bf16[179...) custom-call(s32[10]{0:T(128)} %concatenate.132.counts, ...), custom_call_target="tpu_custom_call" | custom-call | flops 7000000000 | bytes 28354560 | tf_op jit(solution)/shard_map/pallas_call | solution.py:387
  119.0 8.1 %collective-permute-done.3.d0 = f32[384,768]{1,0:T(8,128)} collective-permute-done((f32[384,768]{1,0:T(8,128)S(1)}, f32[384,768]{1,0:T(8,128)}, u32[]{:S(2)}, u32[]{:S(2)}) %collective-permute-start.3) | collective-permute-done | bytes 1179680 | tf_op jit(solution)/shard_map/ppermute | solution.py:477
  127.1 32.0 %shard_map.196 = (f32[1792,768]{1,0:T(8,128)}, f32[1792,768]{1,0:T(8,128)}, f32[768,1536]{1,0:T(8,128)}, f32[1536,768]{1,0:T(8,128)}) custom-call(s32[10]{0:T(128)} %concatenate.132.counts, bf16[1792,768]{1,0:T(8,128)(2,1)} %get-tuple-element.89.c, bf16[1792,768]{1,0:T(8,128)(2,1)} %get-tuple-element.86.dm, bf16[768,1536]{1,0:T(8,128)(2,1)} %up.1, ...), custom_call_target="tpu_custom_call" | custom-call | flops 17999998976 | bytes 30670848 | tf_op jit(solution)/shard_map/pallas_call | solution.py:387
  159.2 3.2 constant_dynamic-slice_fusion.16
  162.4 3.2 constant_dynamic-slice_fusion.17
  166.4 1.7 collective-permute-start.13
  168.8 26.5 %collective-permute-done.12.u1 = f32[192,1536]{1,0:T(8,128)} collective-permute-done((f32[192,1536]{1,0:T(8,128)}, f32[192,1536]{1,0:T(8,128)}, u32[]{:S(2)}, u32[]{:S(2)}) %collective-permute-start.12) | collective-permute-done | bytes 1179680 | tf_op jit(solution)/shard_map/ppermute | solution.py:477
  195.3 24.3 %collective-permute-done.13.d1 = f32[384,768]{1,0:T(8,128)} collective-permute-done((f32[384,768]{1,0:T(8,128)}, f32[384,768]{1,0:T(8,128)}, u32[]{:S(2)}, u32[]{:S(2)}) %collective-permute-start.13) | collective-permute-done | bytes 1179680 | tf_op jit(solution)/shard_map/ppermute | solution.py:477
  220.1 2.2 dynamic-slice_add_fusion
  222.7 2.6 dynamic-slice_add_fusion.1
  225.4 2.3 collective-permute-start.19
  230.1 33.6 %shard_map.197 = (bf16[6,512,768]{2,1,0:T(8,128)(2,1)}, f32[1792,768]{1,0:T(8,128)}, f32[8,768]{1,0:T(8,128)}) custom-call(s32[10]{0:T(128)} %concatenate.132.counts, s32[6,1,512]{2,1,0:T(1,128)} %broadcast_in_dim.18.line, bf16[1792,768]{1,0:T(8,128)(2,1)} %get-tuple-element.89.c, bf16[1792,768]{1,0:T(8,128)(2,1)} %get-tuple-element.86.dm, ...), custom_call_target="tpu_custom_call" | custom-call | flops 12000000000 | bytes 41720832 | tf_op jit(solution)/shard_map/pallas_call | solution.py:387
  263.7 1.9 dynamic-slice_add_fusion.2
  268.4 1.7 collective-permute-start.21
  270.3 26.9 %shard_map.198 = (f32[384,768]{1,0:T(8,128)}, bf16[1792,1152]{1,0:T(8,128)(2,1)}) custom-call(s32[10]{0:T(128)} %concatenate.132.counts, f32[1792,768]{1,0:T(8,128)} %get-tuple-element.111.dr, bf16[1792,1152]{1,0:T(8,128)(2,1)} %get-tuple-element.105.qkv, f32[6,3,2,256]{3,2,1,0:T(2,128)} %get-tuple-element.106.lse, bf16[1792,384]{1,0:T(8,128)(2,1)} %get-tuple-element.81.o, ...), custom_call_target="tpu_custom_call" | custom-call | flops 5000000000 | bytes 16945152 | tf_op jit(solution)/shard_map/pallas_call | solution.py:387
  297.2 2.0 constant_dynamic-slice_fusion.9
  299.3 2.0 dynamic-slice_add_fusion.5
  301.2 2.0 dynamic-slice_add_fusion.6
  303.2 14.6 %shard_map.199 = (f32[1792,768]{1,0:T(8,128)}, f32[3,768,384]{2,1,0:T(8,128)}) custom-call(s32[10]{0:T(128)} %concatenate.132.counts, bf16[1792,1152]{1,0:T(8,128)(2,1)} %get-tuple-element.108.dqkv, bf16[1792,768]{1,0:T(8,128)(2,1)} %get-tuple-element.79.a, bf16[768,1152]{1,0:T(8,128)(2,1)} %copy-done.12), custom_call_target="tpu_custom_call" | custom-call | flops 5000000000 | bytes 17694720 | tf_op jit(solution)/shard_map/pallas_call | solution.py:387
  317.8 2.2 fusion
  324.0 2.9 collective-permute-start.22
  326.9 25.7 %shard_map.200.dqkv = bf16[1792,1152]{1,0:T(8,128)(2,1)} custom-call(s32[10]{0:T(128)} %concatenate.132.counts, f32[1792,768]{1,0:T(8,128)} %get-tuple-element.111.dr, bf16[1792,1152]{1,0:T(8,128)(2,1)} %get-tuple-element.116.qkv, f32[6,3,2,256]{3,2,1,0:T(2,128)} %get-tuple-element.117.lse, bf16[384,768]{1,0:T(8,128)(2,1)} %get-tuple-element.118.wout), custom_call_target="tpu_custom_call" | custom-call | flops 4000000000 | bytes 14389248 | tf_op jit(solution)/shard_map/pallas_call | solution.py:387
  354.1 2.0 dynamic-slice_add_fusion.10
  356.1 1.7 dynamic-slice_add_fusion.11
  359.1 1.6 bitcast_add_fusion.1
  360.8 2.9 collective-permute-start.30
  364.4 2.0 collective-permute-start.29
  366.6 1.9 collective-permute-start.27
  368.5 17.3 %shard_map.201 = (bf16[6,512,768]{2,1,0:T(8,128)(2,1)}, f32[8,768]{1,0:T(8,128)}) custom-call(s32[10]{0:T(128)} %concatenate.132.counts, s32[6,1,512]{2,1,0:T(1,128)} %broadcast_in_dim.18.line, f32[1792,768]{1,0:T(8,128)} %get-tuple-element.111.dr, bf16[1792,1152]{1,0:T(8,128)(2,1)} %shard_map.200.dqkv, bf16[768,1152]{1,0:T(8,128)(2,1)} %get-tuple-element.120.wqkv, ...), custom_call_target="tpu_custom_call" | custom-call | flops 4000000000 | bytes 24419328 | tf_op jit(solution)/shard_map/pallas_call | solution.py:387
  387.2 1.8 collective-permute-done.30
  391.4 1.6 collective-permute-done.28
  393.9 2.4 collective-permute-start.34
  396.3 1.9 collective-permute-start.33
  398.2 2.5 collective-permute-start.32
  400.8 2.1 collective-permute-start.35
  404.1 16.6 %collective-permute-done.35 = f32[16,768]{1,0:T(8,128)S(1)} collective-permute-done((f32[16,768]{1,0:T(8,128)S(1)}, f32[16,768]{1,0:T(8,128)S(1)}, u32[]{:S(2)}, u32[]{:S(2)}) %collective-permute-start.35) | collective-permute-done | bytes 49184 | tf_op jit(solution)/shard_map/ppermute | solution.py:477
  421.1 2.3 collective-permute-start.54
  424.4 1.7 collective-permute-start.36
  426.2 2.0 collective-permute-done.46
  429.8 2.5 collective-permute-start.37
  432.2 2.5 collective-permute-done.41
  434.9 2.6 collective-permute-done.47
  437.9 23.1 %collective-permute-done.42 = f32[72,384]{1,0:T(8,128)S(1)} collective-permute-done((f32[72,384]{1,0:T(8,128)S(1)}, f32[72,384]{1,0:T(8,128)S(1)}, u32[]{:S(2)}, u32[]{:S(2)}) %collective-permute-start.42) | collective-permute-done | bytes 110624 | tf_op jit(solution)/shard_map/ppermute | solution.py:477
  464.1 5.7 %collective-permute-done.38 = f32[16,768]{1,0:T(8,128)S(1)} collective-permute-done((f32[16,768]{1,0:T(8,128)S(1)}, f32[16,768]{1,0:T(8,128)S(1)}, u32[]{:S(2)}, u32[]{:S(2)}) %collective-permute-start.38) | collective-permute-done | bytes 49184 | tf_op jit(solution)/shard_map/ppermute | solution.py:477
  472.2 1.6 maximum_select_fusion.3
  475.0 2.2 collective-permute-done.49
  478.3 3.6 collective-permute-done.44
  484.6 8.2 %collective-permute-done.50 = f32[288,384]{1,0:T(8,128)S(1)} collective-permute-done((f32[288,384]{1,0:T(8,128)S(1)}, f32[288,384]{1,0:T(8,128)S(1)}, u32[]{:S(2)}, u32[]{:S(2)}) %collective-permute-start.50) | collective-permute-done | bytes 442400 | tf_op jit(solution)/shard_map/ppermute | solution.py:477
  494.3 2.9 maximum_select_fusion.8
  497.8 1.6 maximum_select_fusion.4
  499.4 2.3 maximum_select_fusion.5
  501.7 2.0 pad_maximum_fusion
  503.7 6.5 %maximum_select_fusion.1 = f32[1536,768]{1,0:T(8,128)} fusion(f32[768,768]{1,0:T(8,128)} %collective-permute-done.59, f32[768,768]{1,0:T(8,128)} %maximum_select_fusion.3, pred[]{:T(512)S(6)} %eq.73), kind=kLoop, calls=%fused_computation.1 | loop fusion | flops 3538944 | bytes 9437185 | tf_op jit(solution)/shard_map/jit(_where)/select_n | solution.py:501
  510.3 5.3 %maximum_select_fusion = f32[768,1536]{1,0:T(8,128)} fusion(f32[384,1536]{1,0:T(8,128)} %collective-permute-done.58, f32[384,1536]{1,0:T(8,128)S(1)} %maximum_select_fusion.2, pred[]{:T(512)S(6)} %eq.73), kind=kLoop, calls=%fused_computation | loop fusion | flops 3538944 | bytes 9437185 | tf_op jit(solution)/shard_map/jit(_where)/select_n | solution.py:501
  (208 shorter events, 47.9 us)
Async XLA Ops:
  5.3 45.5 %collective-permute-start = (f32[192,1152]{1,0:T(8,128)}, f32[192,1152]{1,0:T(8,128)}, u32[]{:S(2)}, u32[]{:S(2)}) collective-permute-start(f32[192,1152]{1,0:T(8,128)} %dynamic-slice_convert_fusion.2), channel_id=1, source_target_pairs={{0,1},{1,0},{2,3},{3,2},{4,5},{5,4},{6,7},{7,6},{8,9},{9,8},{10,11... | collective-permute-start | bytes 2654216 | tf_op jit(solution)/shard_map/ppermute | solution.py:477
  10.0 40.8 %collective-permute-start.1 = (f32[96,768]{1,0:T(8,128)}, f32[96,768]{1,0:T(8,128)}, u32[]{:S(2)}, u32[]{:S(2)}) collective-permute-start(f32[96,768]{1,0:T(8,128)} %dynamic-slice_convert_fusion.3), channel_id=1, source_target_pairs={{0,1},{1,0},{2,3},{3,2},{4,5},{5,4},{6,7},{7,6},{8,9},{9,8},{10,11... | collective-permute-start | bytes 884744 | tf_op jit(solution)/shard_map/ppermute | solution.py:477
  47.4 35.3 %copy-start.23 = (f32[768]{0:T(1024)S(1)}, f32[768]{0:T(1024)}, u32[]{:S(2)}) copy-start(f32[768]{0:T(1024)} %param.19) | copy-start | bytes 9220
  47.4 35.9 %copy-start.24 = (f32[768]{0:T(1024)S(1)}, f32[768]{0:T(1024)}, u32[]{:S(2)}) copy-start(f32[768]{0:T(1024)} %param.20) | copy-start | bytes 9220
  50.8 20.6 %collective-permute-start.4 = (f32[192,1152]{1,0:T(8,128)}, f32[192,1152]{1,0:T(8,128)S(1)}, u32[]{:S(2)}, u32[]{:S(2)}) collective-permute-start(f32[192,1152]{1,0:T(8,128)} %collective-permute-done.q0), channel_id=1, source_target_pairs={{0,4},{2,6},{4,0},{6,2},{8,12},{10,14},{12,8},{14,10},{16,20},{18,... | collective-permute-start | bytes 2654216 | tf_op jit(solution)/shard_map/ppermute | solution.py:477
  52.1 32.1 %collective-permute-start.5 = (f32[192,1152]{1,0:T(8,128)}, f32[192,1152]{1,0:T(8,128)}, u32[]{:S(2)}, u32[]{:S(2)}) collective-permute-start(f32[192,1152]{1,0:T(8,128)} %collective-permute-done.q0), channel_id=1, source_target_pairs={{0,2},{2,0},{4,6},{6,4},{8,10},{10,8},{12,14},{14,12},{16,18},{18,... | collective-permute-start | bytes 2654216 | tf_op jit(solution)/shard_map/ppermute | solution.py:477
  71.4 12.5 %copy-start.27 = (f32[192,1152]{1,0:T(8,128)}, f32[192,1152]{1,0:T(8,128)S(1)}, u32[]{:S(2)}) copy-start(f32[192,1152]{1,0:T(8,128)S(1)} %collective-permute-done.4.q1) | copy-start | bytes 2654212
  71.4 12.8 %collective-permute-start.6 = (f32[192,1152]{1,0:T(8,128)S(1)}, f32[192,1152]{1,0:T(8,128)}, u32[]{:S(2)}, u32[]{:S(2)}) collective-permute-start(f32[192,1152]{1,0:T(8,128)S(1)} %collective-permute-done.4.q1), channel_id=1, source_target_pairs={{0,2},{2,0},{4,6},{6,4},{8,10},{10,8},{12,14},{14,12},{16,18},{18,... | collective-permute-start | bytes 2654216 | tf_op jit(solution)/shard_map/ppermute | solution.py:477
  71.4 9.6 %collective-permute-start.7 = (f32[96,768]{1,0:T(8,128)}, f32[96,768]{1,0:T(8,128)S(1)}, u32[]{:S(2)}, u32[]{:S(2)}) collective-permute-start(f32[96,768]{1,0:T(8,128)} %collective-permute-done.1.w0), channel_id=1, source_target_pairs={{0,4},{2,6},{4,0},{6,2},{8,12},{10,14},{12,8},{14,10},{16,20},{18,... | collective-permute-start | bytes 884744 | tf_op jit(solution)/shard_map/ppermute | solution.py:477
  73.2 9.5 %collective-permute-start.8 = (f32[96,768]{1,0:T(8,128)}, f32[96,768]{1,0:T(8,128)S(1)}, u32[]{:S(2)}, u32[]{:S(2)}) collective-permute-start(f32[96,768]{1,0:T(8,128)} %collective-permute-done.1.w0), channel_id=1, source_target_pairs={{0,2},{2,0},{4,6},{6,4},{8,10},{10,8},{12,14},{14,12},{16,18},{18,... | collective-permute-start | bytes 884744 | tf_op jit(solution)/shard_map/ppermute | solution.py:477
  73.4 45.6 %collective-permute-start.2 = (f32[192,1536]{1,0:T(8,128)}, f32[192,1536]{1,0:T(8,128)}, u32[]{:S(2)}, u32[]{:S(2)}) collective-permute-start(f32[192,1536]{1,0:T(8,128)} %dynamic-slice_convert_fusion.1), channel_id=1, source_target_pairs={{0,1},{1,0},{2,3},{3,2},{4,5},{5,4},{6,7},{7,6},{8,9},{9,8},{10,11... | collective-permute-start | bytes 3538952 | tf_op jit(solution)/shard_map/ppermute | solution.py:477
  81.1 46.1 %collective-permute-start.3 = (f32[384,768]{1,0:T(8,128)S(1)}, f32[384,768]{1,0:T(8,128)}, u32[]{:S(2)}, u32[]{:S(2)}) collective-permute-start(f32[384,768]{1,0:T(8,128)S(1)} %dynamic-slice_convert_fusion), channel_id=1, source_target_pairs={{0,1},{1,0},{2,3},{3,2},{4,5},{5,4},{6,7},{7,6},{8,9},{9,8},{10,11... | collective-permute-start | bytes 3538952 | tf_op jit(solution)/shard_map/ppermute | solution.py:477
  82.6 1.6 collective-permute-start.9
  162.4 57.2 %collective-permute-start.11 = (f32[768,768]{1,0:T(8,128)}, f32[768,768]{1,0:T(8,128)S(1)}, u32[]{:S(2)}, u32[]{:S(2)}) collective-permute-start(f32[768,768]{1,0:T(8,128)} %constant_dynamic-slice_fusion.16), channel_id=1, source_target_pairs={{0,2},{2,0},{4,6},{6,4},{8,10},{10,8},{12,14},{14,12},{16,18},{18,... | collective-permute-start | bytes 7077896 | tf_op jit(solution)/shard_map/ppermute | solution.py:477
  165.6 56.7 %collective-permute-start.10 = (f32[384,1536]{1,0:T(8,128)}, f32[384,1536]{1,0:T(8,128)}, u32[]{:S(2)}, u32[]{:S(2)}) collective-permute-start(f32[384,1536]{1,0:T(8,128)} %constant_dynamic-slice_fusion.17), channel_id=1, source_target_pairs={{0,2},{2,0},{4,6},{6,4},{8,10},{10,8},{12,14},{14,12},{16,18},{18,... | collective-permute-start | bytes 7077896 | tf_op jit(solution)/shard_map/ppermute | solution.py:477
  166.1 29.2 %collective-permute-start.12 = (f32[192,1536]{1,0:T(8,128)}, f32[192,1536]{1,0:T(8,128)}, u32[]{:S(2)}, u32[]{:S(2)}) collective-permute-start(f32[192,1536]{1,0:T(8,128)} %collective-permute-done.2.u0), channel_id=1, source_target_pairs={{0,4},{2,6},{4,0},{6,2},{8,12},{10,14},{12,8},{14,10},{16,20},{18,... | collective-permute-start | bytes 3538952 | tf_op jit(solution)/shard_map/ppermute | solution.py:477
  166.4 53.2 %collective-permute-start.13 = (f32[384,768]{1,0:T(8,128)}, f32[384,768]{1,0:T(8,128)}, u32[]{:S(2)}, u32[]{:S(2)}) collective-permute-start(f32[384,768]{1,0:T(8,128)} %collective-permute-done.3.d0), channel_id=1, source_target_pairs={{0,4},{2,6},{4,0},{6,2},{8,12},{10,14},{12,8},{14,10},{16,20},{18,... | collective-permute-start | bytes 3538952 | tf_op jit(solution)/shard_map/ppermute | solution.py:477
  168.8 60.0 %collective-permute-start.14 = (f32[192,1536]{1,0:T(8,128)}, f32[192,1536]{1,0:T(8,128)S(1)}, u32[]{:S(2)}, u32[]{:S(2)}) collective-permute-start(f32[192,1536]{1,0:T(8,128)} %collective-permute-done.2.u0), channel_id=1, source_target_pairs={{0,2},{2,0},{4,6},{6,4},{8,10},{10,8},{12,14},{14,12},{16,18},{18,... | collective-permute-start | bytes 3538952 | tf_op jit(solution)/shard_map/ppermute | solution.py:477
  195.3 34.8 %collective-permute-start.16 = (f32[384,768]{1,0:T(8,128)}, f32[384,768]{1,0:T(8,128)}, u32[]{:S(2)}, u32[]{:S(2)}) collective-permute-start(f32[384,768]{1,0:T(8,128)} %collective-permute-done.3.d0), channel_id=1, source_target_pairs={{0,2},{2,0},{4,6},{6,4},{8,10},{10,8},{12,14},{14,12},{16,18},{18,... | collective-permute-start | bytes 3538952 | tf_op jit(solution)/shard_map/ppermute | solution.py:477
  219.6 10.5 %collective-permute-start.15 = (f32[192,1536]{1,0:T(8,128)}, f32[192,1536]{1,0:T(8,128)}, u32[]{:S(2)}, u32[]{:S(2)}) collective-permute-start(f32[192,1536]{1,0:T(8,128)} %collective-permute-done.12.u1), channel_id=1, source_target_pairs={{0,2},{2,0},{4,6},{6,4},{8,10},{10,8},{12,14},{14,12},{16,18},{18,... | collective-permute-start | bytes 3538952 | tf_op jit(solution)/shard_map/ppermute | solution.py:477
  219.6 10.5 %collective-permute-start.17 = (f32[384,768]{1,0:T(8,128)}, f32[384,768]{1,0:T(8,128)}, u32[]{:S(2)}, u32[]{:S(2)}) collective-permute-start(f32[384,768]{1,0:T(8,128)} %collective-permute-done.13.d1), channel_id=1, source_target_pairs={{0,2},{2,0},{4,6},{6,4},{8,10},{10,8},{12,14},{14,12},{16,18},{18,... | collective-permute-start | bytes 3538952 | tf_op jit(solution)/shard_map/ppermute | solution.py:477
  225.4 38.3 %collective-permute-start.19 = (f32[384,768]{1,0:T(8,128)S(1)}, f32[384,768]{1,0:T(8,128)}, u32[]{:S(2)}, u32[]{:S(2)}) collective-permute-start(f32[384,768]{1,0:T(8,128)S(1)} %constant_dynamic-slice_fusion.14), channel_id=1, source_target_pairs={{0,8},{2,10},{4,12},{6,14},{8,0},{10,2},{12,4},{14,6},{16,24},{18,... | collective-permute-start | bytes 3538952 | tf_op jit(solution)/shard_map/ppermute | solution.py:477
  229.8 35.8 %collective-permute-start.18 = (f32[192,1536]{1,0:T(8,128)}, f32[192,1536]{1,0:T(8,128)}, u32[]{:S(2)}, u32[]{:S(2)}) collective-permute-start(f32[192,1536]{1,0:T(8,128)} %constant_dynamic-slice_fusion.15), channel_id=1, source_target_pairs={{0,4},{2,6},{4,0},{6,2},{8,12},{10,14},{12,8},{14,10},{16,20},{18,... | collective-permute-start | bytes 3538952 | tf_op jit(solution)/shard_map/ppermute | solution.py:477
  268.4 30.8 %collective-permute-start.21 = (f32[192,768]{1,0:T(8,128)}, f32[192,768]{1,0:T(8,128)}, u32[]{:S(2)}, u32[]{:S(2)}) collective-permute-start(f32[192,768]{1,0:T(8,128)} %constant_dynamic-slice_fusion.12), channel_id=1, source_target_pairs={{0,4},{2,6},{4,0},{6,2},{8,12},{10,14},{12,8},{14,10},{16,20},{18,... | collective-permute-start | bytes 1769480 | tf_op jit(solution)/shard_map/ppermute | solution.py:477
  270.2 31.0 %collective-permute-start.20 = (f32[96,1536]{1,0:T(8,128)S(1)}, f32[96,1536]{1,0:T(8,128)}, u32[]{:S(2)}, u32[]{:S(2)}) collective-permute-start(f32[96,1536]{1,0:T(8,128)S(1)} %constant_dynamic-slice_fusion.13), channel_id=1, source_target_pairs={{0,8},{2,10},{4,12},{6,14},{8,0},{10,2},{12,4},{14,6},{16,24},{18,... | collective-permute-start | bytes 1769480 | tf_op jit(solution)/shard_map/ppermute | solution.py:477
  299.3 53.3 %collective-permute-start.26 = (f32[192,768]{1,0:T(8,128)}, f32[192,768]{1,0:T(8,128)}, u32[]{:S(2)}, u32[]{:S(2)}) collective-permute-start(f32[192,768]{1,0:T(8,128)} %constant_dynamic-slice_fusion.9), channel_id=1, source_target_pairs={{0,2},{2,0},{4,6},{6,4},{8,10},{10,8},{12,14},{14,12},{16,18},{18,... | collective-permute-start | bytes 1769480 | tf_op jit(solution)/shard_map/ppermute | solution.py:477
  321.0 36.8 %collective-permute-start.25 = (f32[576,384]{1,0:T(8,128)}, f32[576,384]{1,0:T(8,128)}, u32[]{:S(2)}, u32[]{:S(2)}) collective-permute-start(f32[576,384]{1,0:T(8,128)} %dynamic-slice_bitcast_fusion), channel_id=1, source_target_pairs={{0,2},{2,0},{4,6},{6,4},{8,10},{10,8},{12,14},{14,12},{16,18},{18,... | collective-permute-start | bytes 2654216 | tf_op jit(solution)/shard_map/ppermute | solution.py:477
  322.0 37.1 %collective-permute-start.24 = (f32[576,384]{1,0:T(8,128)}, f32[576,384]{1,0:T(8,128)}, u32[]{:S(2)}, u32[]{:S(2)}) collective-permute-start(f32[576,384]{1,0:T(8,128)} %dynamic-slice_bitcast_fusion.1), channel_id=1, source_target_pairs={{0,2},{2,0},{4,6},{6,4},{8,10},{10,8},{12,14},{14,12},{16,18},{18,... | collective-permute-start | bytes 2654216 | tf_op jit(solution)/shard_map/ppermute | solution.py:477
  323.2 30.8 %collective-permute-start.23 = (f32[96,768]{1,0:T(8,128)}, f32[96,768]{1,0:T(8,128)}, u32[]{:S(2)}, u32[]{:S(2)}) collective-permute-start(f32[96,768]{1,0:T(8,128)} %constant_dynamic-slice_fusion.10), channel_id=1, source_target_pairs={{0,16},{2,18},{4,20},{6,22},{8,24},{10,26},{12,28},{14,30},{16,0},... | collective-permute-start | bytes 884744 | tf_op jit(solution)/shard_map/ppermute | solution.py:477
  324.0 32.1 %collective-permute-start.22 = (f32[48,1536]{1,0:T(8,128)}, f32[48,1536]{1,0:T(8,128)}, u32[]{:S(2)}, u32[]{:S(2)}) collective-permute-start(f32[48,1536]{1,0:T(8,128)} %constant_dynamic-slice_fusion.11), channel_id=1, source_target_pairs={{0,16},{2,18},{4,20},{6,22},{8,24},{10,26},{12,28},{14,30},{16,0},... | collective-permute-start | bytes 884744 | tf_op jit(solution)/shard_map/ppermute | solution.py:477
  354.0 9.6 %copy-start.13 = (f32[192,768]{1,0:T(8,128)}, f32[192,768]{1,0:T(8,128)S(1)}, u32[]{:S(2)}) copy-start(f32[192,768]{1,0:T(8,128)S(1)} %dynamic-slice_add_fusion.4) | copy-start | bytes 1769476
  360.7 25.1 %collective-permute-start.31 = (f32[96,768]{1,0:T(8,128)}, f32[96,768]{1,0:T(8,128)}, u32[]{:S(2)}, u32[]{:S(2)}) collective-permute-start(f32[96,768]{1,0:T(8,128)} %dynamic-slice_add_fusion.10), channel_id=1, source_target_pairs={{0,16},{2,18},{4,20},{6,22},{8,24},{10,26},{12,28},{14,30},{16,0},... | collective-permute-start | bytes 884744 | tf_op jit(solution)/shard_map/ppermute | solution.py:477
  360.8 28.2 %collective-permute-start.30 = (f32[48,1536]{1,0:T(8,128)}, f32[48,1536]{1,0:T(8,128)}, u32[]{:S(2)}, u32[]{:S(2)}) collective-permute-start(f32[48,1536]{1,0:T(8,128)} %dynamic-slice_add_fusion.11), channel_id=1, source_target_pairs={{0,16},{2,18},{4,20},{6,22},{8,24},{10,26},{12,28},{14,30},{16,0},... | collective-permute-start | bytes 884744 | tf_op jit(solution)/shard_map/ppermute | solution.py:477
  364.4 25.9 %collective-permute-start.29 = (f32[96,768]{1,0:T(8,128)}, f32[96,768]{1,0:T(8,128)}, u32[]{:S(2)}, u32[]{:S(2)}) collective-permute-start(f32[96,768]{1,0:T(8,128)} %constant_dynamic-slice_fusion.6), channel_id=1, source_target_pairs={{0,8},{2,10},{4,12},{6,14},{8,0},{10,2},{12,4},{14,6},{16,24},{18,... | collective-permute-start | bytes 884744 | tf_op jit(solution)/shard_map/ppermute | solution.py:477
  366.4 26.5 %collective-permute-start.28 = (f32[288,384]{1,0:T(8,128)S(1)}, f32[288,384]{1,0:T(8,128)S(1)}, u32[]{:S(2)}, u32[]{:S(2)}) collective-permute-start(f32[288,384]{1,0:T(8,128)S(1)} %constant_dynamic-slice_fusion.7), channel_id=1, source_target_pairs={{0,8},{2,10},{4,12},{6,14},{8,0},{10,2},{12,4},{14,6},{16,24},{18,... | collective-permute-start | bytes 1327112 | tf_op jit(solution)/shard_map/ppermute | solution.py:477
  366.6 26.4 %collective-permute-start.27 = (f32[288,384]{1,0:T(8,128)S(1)}, f32[288,384]{1,0:T(8,128)S(1)}, u32[]{:S(2)}, u32[]{:S(2)}) collective-permute-start(f32[288,384]{1,0:T(8,128)S(1)} %constant_dynamic-slice_fusion.8), channel_id=1, source_target_pairs={{0,4},{2,6},{4,0},{6,2},{8,12},{10,14},{12,8},{14,10},{16,20},{18,... | collective-permute-start | bytes 1327112 | tf_op jit(solution)/shard_map/ppermute | solution.py:477
  393.1 9.8 %collective-permute-start.52 = (f32[48,768]{1,0:T(8,128)S(1)}, f32[48,768]{1,0:T(8,128)S(1)}, u32[]{:S(2)}, u32[]{:S(2)}) collective-permute-start(f32[48,768]{1,0:T(8,128)S(1)} %constant_dynamic-slice_fusion.1), channel_id=1, source_target_pairs={{0,4},{2,6},{4,0},{6,2},{8,12},{10,14},{12,8},{14,10},{16,20},{18,... | collective-permute-start | bytes 442376 | tf_op jit(solution)/shard_map/ppermute | solution.py:477
  393.9 6.9 %collective-permute-start.34 = (f32[16,768]{1,0:T(8,128)S(1)}, f32[16,768]{1,0:T(8,128)S(1)}, u32[]{:S(2)}, u32[]{:S(2)}) collective-permute-start(f32[16,768]{1,0:T(8,128)S(1)} %constant_dynamic-update-slice_fusion), channel_id=1, source_target_pairs={{0,16},{2,18},{4,20},{6,22},{8,24},{10,26},{12,28},{14,30},{16,0},... | collective-permute-start | bytes 147464 | tf_op jit(solution)/shard_map/ppermute | solution.py:477
  396.3 27.9 %collective-permute-start.33 = (f32[192,768]{1,0:T(8,128)S(1)}, f32[192,768]{1,0:T(8,128)S(1)}, u32[]{:S(2)}, u32[]{:S(2)}) collective-permute-start(f32[192,768]{1,0:T(8,128)S(1)} %maximum_select_fusion.12), channel_id=1, source_target_pairs={{0,4},{2,6},{4,0},{6,2},{8,12},{10,14},{12,8},{14,10},{16,20},{18,... | collective-permute-start | bytes 1769480 | tf_op jit(solution)/shard_map/ppermute | solution.py:477
  398.2 26.1 %collective-permute-start.32 = (f32[96,1536]{1,0:T(8,128)S(1)}, f32[96,1536]{1,0:T(8,128)S(1)}, u32[]{:S(2)}, u32[]{:S(2)}) collective-permute-start(f32[96,1536]{1,0:T(8,128)S(1)} %maximum_select_fusion.11), channel_id=1, source_target_pairs={{0,8},{2,10},{4,12},{6,14},{8,0},{10,2},{12,4},{14,6},{16,24},{18,... | collective-permute-start | bytes 1769480 | tf_op jit(solution)/shard_map/ppermute | solution.py:477
  400.7 22.7 %collective-permute-start.40 = (f32[144,384]{1,0:T(8,128)S(1)}, f32[144,384]{1,0:T(8,128)S(1)}, u32[]{:S(2)}, u32[]{:S(2)}) collective-permute-start(f32[144,384]{1,0:T(8,128)S(1)} %constant_dynamic-slice_fusion.5), channel_id=1, source_target_pairs={{0,8},{2,10},{4,12},{6,14},{8,0},{10,2},{12,4},{14,6},{16,24},{18,... | collective-permute-start | bytes 663560 | tf_op jit(solution)/shard_map/ppermute | solution.py:477
  400.8 19.9 %collective-permute-start.35 = (f32[16,768]{1,0:T(8,128)S(1)}, f32[16,768]{1,0:T(8,128)S(1)}, u32[]{:S(2)}, u32[]{:S(2)}) collective-permute-start(f32[16,768]{1,0:T(8,128)S(1)} %add.286), channel_id=1, source_target_pairs={{0,8},{2,10},{4,12},{6,14},{8,0},{10,2},{12,4},{14,6},{16,24},{18,... | collective-permute-start | bytes 147464 | tf_op jit(solution)/shard_map/ppermute | solution.py:477
  403.0 18.1 %collective-permute-start.53 = (f32[24,768]{1,0:T(8,128)S(1)}, f32[24,768]{1,0:T(8,128)S(1)}, u32[]{:S(2)}, u32[]{:S(2)}) collective-permute-start(f32[24,768]{1,0:T(8,128)S(1)} %constant_dynamic-slice_fusion), channel_id=1, source_target_pairs={{0,16},{2,18},{4,20},{6,22},{8,24},{10,26},{12,28},{14,30},{16,0},... | collective-permute-start | bytes 221192 | tf_op jit(solution)/shard_map/ppermute | solution.py:477
  420.7 7.5 %collective-permute-start.46 = (f32[144,384]{1,0:T(8,128)S(1)}, f32[144,384]{1,0:T(8,128)S(1)}, u32[]{:S(2)}, u32[]{:S(2)}) collective-permute-start(f32[144,384]{1,0:T(8,128)S(1)} %constant_dynamic-slice_fusion.3), channel_id=1, source_target_pairs={{0,4},{2,6},{4,0},{6,2},{8,12},{10,14},{12,8},{14,10},{16,20},{18,... | collective-permute-start | bytes 663560 | tf_op jit(solution)/shard_map/ppermute | solution.py:477
  421.1 40.8 %collective-permute-start.54 = (f32[24,768]{1,0:T(8,128)S(1)}, f32[24,768]{1,0:T(8,128)S(1)}, u32[]{:S(2)}, u32[]{:S(2)}) collective-permute-start(f32[24,768]{1,0:T(8,128)S(1)} %dynamic-slice_add_fusion.17), channel_id=1, source_target_pairs={{0,16},{2,18},{4,20},{6,22},{8,24},{10,26},{12,28},{14,30},{16,0},... | collective-permute-start | bytes 221192 | tf_op jit(solution)/shard_map/ppermute | solution.py:477
  423.5 11.3 %collective-permute-start.41 = (f32[72,384]{1,0:T(8,128)S(1)}, f32[72,384]{1,0:T(8,128)S(1)}, u32[]{:S(2)}, u32[]{:S(2)}) collective-permute-start(f32[72,384]{1,0:T(8,128)S(1)} %constant_dynamic-slice_fusion.4), channel_id=1, source_target_pairs={{0,16},{2,18},{4,20},{6,22},{8,24},{10,26},{12,28},{14,30},{16,0},... | collective-permute-start | bytes 331784 | tf_op jit(solution)/shard_map/ppermute | solution.py:477
  424.4 47.5 %collective-permute-start.36 = (f32[192,1536]{1,0:T(8,128)S(1)}, f32[192,1536]{1,0:T(8,128)S(1)}, u32[]{:S(2)}, u32[]{:S(2)}) collective-permute-start(f32[192,1536]{1,0:T(8,128)S(1)} %maximum_select_fusion.6), channel_id=1, source_target_pairs={{0,4},{2,6},{4,0},{6,2},{8,12},{10,14},{12,8},{14,10},{16,20},{18,... | collective-permute-start | bytes 3538952 | tf_op jit(solution)/shard_map/ppermute | solution.py:477
  428.2 9.2 %collective-permute-start.47 = (f32[72,384]{1,0:T(8,128)S(1)}, f32[72,384]{1,0:T(8,128)S(1)}, u32[]{:S(2)}, u32[]{:S(2)}) collective-permute-start(f32[72,384]{1,0:T(8,128)S(1)} %constant_dynamic-slice_fusion.2), channel_id=1, source_target_pairs={{0,16},{2,18},{4,20},{6,22},{8,24},{10,26},{12,28},{14,30},{16,0},... | collective-permute-start | bytes 331784 | tf_op jit(solution)/shard_map/ppermute | solution.py:477
  429.8 42.4 %collective-permute-start.37 = (f32[384,768]{1,0:T(8,128)S(1)}, f32[384,768]{1,0:T(8,128)S(1)}, u32[]{:S(2)}, u32[]{:S(2)}) collective-permute-start(f32[384,768]{1,0:T(8,128)S(1)} %maximum_select_fusion.7), channel_id=1, source_target_pairs={{0,8},{2,10},{4,12},{6,14},{8,0},{10,2},{12,4},{14,6},{16,24},{18,... | collective-permute-start | bytes 3538952 | tf_op jit(solution)/shard_map/ppermute | solution.py:477
  434.8 26.2 %collective-permute-start.42 = (f32[72,384]{1,0:T(8,128)S(1)}, f32[72,384]{1,0:T(8,128)S(1)}, u32[]{:S(2)}, u32[]{:S(2)}) collective-permute-start(f32[72,384]{1,0:T(8,128)S(1)} %dynamic-slice_add_fusion.16), channel_id=1, source_target_pairs={{0,16},{2,18},{4,20},{6,22},{8,24},{10,26},{12,28},{14,30},{16,0},... | collective-permute-start | bytes 331784 | tf_op jit(solution)/shard_map/ppermute | solution.py:477
  437.4 26.1 %collective-permute-start.48 = (f32[72,384]{1,0:T(8,128)S(1)}, f32[72,384]{1,0:T(8,128)S(1)}, u32[]{:S(2)}, u32[]{:S(2)}) collective-permute-start(f32[72,384]{1,0:T(8,128)S(1)} %dynamic-slice_add_fusion.15), channel_id=1, source_target_pairs={{0,16},{2,18},{4,20},{6,22},{8,24},{10,26},{12,28},{14,30},{16,0},... | collective-permute-start | bytes 331784 | tf_op jit(solution)/shard_map/ppermute | solution.py:477
  461.0 10.2 %collective-permute-start.43 = (f32[144,384]{1,0:T(8,128)S(1)}, f32[144,384]{1,0:T(8,128)S(1)}, u32[]{:S(2)}, u32[]{:S(2)}) collective-permute-start(f32[144,384]{1,0:T(8,128)S(1)} %maximum_select_fusion.17), channel_id=1, source_target_pairs={{0,8},{2,10},{4,12},{6,14},{8,0},{10,2},{12,4},{14,6},{16,24},{18,... | collective-permute-start | bytes 663560 | tf_op jit(solution)/shard_map/ppermute | solution.py:477
  462.0 11.8 %collective-permute-start.55 = (f32[48,768]{1,0:T(8,128)S(1)}, f32[48,768]{1,0:T(8,128)S(1)}, u32[]{:S(2)}, u32[]{:S(2)}) collective-permute-start(f32[48,768]{1,0:T(8,128)S(1)} %maximum_select_fusion.19), channel_id=1, source_target_pairs={{0,4},{2,6},{4,0},{6,2},{8,12},{10,14},{12,8},{14,10},{16,20},{18,... | collective-permute-start | bytes 442376 | tf_op jit(solution)/shard_map/ppermute | solution.py:477
  463.5 6.3 %collective-permute-start.38 = (f32[16,768]{1,0:T(8,128)S(1)}, f32[16,768]{1,0:T(8,128)S(1)}, u32[]{:S(2)}, u32[]{:S(2)}) collective-permute-start(f32[16,768]{1,0:T(8,128)S(1)} %add.287), channel_id=1, source_target_pairs={{0,4},{2,6},{4,0},{6,2},{8,12},{10,14},{12,8},{14,10},{16,20},{18,... | collective-permute-start | bytes 147464 | tf_op jit(solution)/shard_map/ppermute | solution.py:477
  469.8 7.4 %collective-permute-start.49 = (f32[144,384]{1,0:T(8,128)S(1)}, f32[144,384]{1,0:T(8,128)S(1)}, u32[]{:S(2)}, u32[]{:S(2)}) collective-permute-start(f32[144,384]{1,0:T(8,128)S(1)} %maximum_select_fusion.18), channel_id=1, source_target_pairs={{0,4},{2,6},{4,0},{6,2},{8,12},{10,14},{12,8},{14,10},{16,20},{18,... | collective-permute-start | bytes 663560 | tf_op jit(solution)/shard_map/ppermute | solution.py:477
  471.2 10.8 %collective-permute-start.44 = (f32[288,384]{1,0:T(8,128)S(1)}, f32[288,384]{1,0:T(8,128)S(1)}, u32[]{:S(2)}, u32[]{:S(2)}) collective-permute-start(f32[288,384]{1,0:T(8,128)S(1)} %maximum_select_fusion.14), channel_id=1, source_target_pairs={{0,4},{2,6},{4,0},{6,2},{8,12},{10,14},{12,8},{14,10},{16,20},{18,... | collective-permute-start | bytes 1327112 | tf_op jit(solution)/shard_map/ppermute | solution.py:477
  473.8 29.9 %collective-permute-start.59 = (f32[768,768]{1,0:T(8,128)}, f32[768,768]{1,0:T(8,128)}, u32[]{:S(2)}, u32[]{:S(2)}) collective-permute-start(f32[768,768]{1,0:T(8,128)} %maximum_select_fusion.3), channel_id=1, source_target_pairs={{0,2},{2,0},{4,6},{6,4},{8,10},{10,8},{12,14},{14,12},{16,18},{18,... | collective-permute-start | bytes 7077896 | tf_op jit(solution)/shard_map/ppermute | solution.py:477
  473.8 9.9 %collective-permute-start.56 = (f32[96,768]{1,0:T(8,128)S(1)}, f32[96,768]{1,0:T(8,128)S(1)}, u32[]{:S(2)}, u32[]{:S(2)}) collective-permute-start(f32[96,768]{1,0:T(8,128)S(1)} %maximum_select_fusion.16), channel_id=1, source_target_pairs={{0,8},{2,10},{4,12},{6,14},{8,0},{10,2},{12,4},{14,6},{16,24},{18,... | collective-permute-start | bytes 884744 | tf_op jit(solution)/shard_map/ppermute | solution.py:477
  477.3 15.5 %collective-permute-start.50 = (f32[288,384]{1,0:T(8,128)S(1)}, f32[288,384]{1,0:T(8,128)S(1)}, u32[]{:S(2)}, u32[]{:S(2)}) collective-permute-start(f32[288,384]{1,0:T(8,128)S(1)} %maximum_select_fusion.15), channel_id=1, source_target_pairs={{0,8},{2,10},{4,12},{6,14},{8,0},{10,2},{12,4},{14,6},{16,24},{18,... | collective-permute-start | bytes 1327112 | tf_op jit(solution)/shard_map/ppermute | solution.py:477
  482.0 15.8 %collective-permute-start.45 = (f32[576,384]{1,0:T(8,128)S(1)}, f32[576,384]{1,0:T(8,128)}, u32[]{:S(2)}, u32[]{:S(2)}) collective-permute-start(f32[576,384]{1,0:T(8,128)S(1)} %maximum_select_fusion.9), channel_id=1, source_target_pairs={{0,2},{2,0},{4,6},{6,4},{8,10},{10,8},{12,14},{14,12},{16,18},{18,... | collective-permute-start | bytes 2654216 | tf_op jit(solution)/shard_map/ppermute | solution.py:477
  482.1 28.2 %collective-permute-start.58 = (f32[384,1536]{1,0:T(8,128)S(1)}, f32[384,1536]{1,0:T(8,128)}, u32[]{:S(2)}, u32[]{:S(2)}) collective-permute-start(f32[384,1536]{1,0:T(8,128)S(1)} %maximum_select_fusion.2), channel_id=1, source_target_pairs={{0,2},{2,0},{4,6},{6,4},{8,10},{10,8},{12,14},{14,12},{16,18},{18,... | collective-permute-start | bytes 7077896 | tf_op jit(solution)/shard_map/ppermute | solution.py:477
  484.6 9.1 %collective-permute-start.57 = (f32[192,768]{1,0:T(8,128)}, f32[192,768]{1,0:T(8,128)}, u32[]{:S(2)}, u32[]{:S(2)}) collective-permute-start(f32[192,768]{1,0:T(8,128)} %maximum_select_fusion.13), channel_id=1, source_target_pairs={{0,2},{2,0},{4,6},{6,4},{8,10},{10,8},{12,14},{14,12},{16,18},{18,... | collective-permute-start | bytes 1769480 | tf_op jit(solution)/shard_map/ppermute | solution.py:477
  493.8 5.7 %collective-permute-start.51 = (f32[576,384]{1,0:T(8,128)}, f32[576,384]{1,0:T(8,128)}, u32[]{:S(2)}, u32[]{:S(2)}) collective-permute-start(f32[576,384]{1,0:T(8,128)} %maximum_select_fusion.10), channel_id=1, source_target_pairs={{0,2},{2,0},{4,6},{6,4},{8,10},{10,8},{12,14},{14,12},{16,18},{18,... | collective-permute-start | bytes 2654216 | tf_op jit(solution)/shard_map/ppermute | solution.py:477
  493.8 3.4 collective-permute-start.39
  (27 other events, 116.8 us)

commit v6 on v5

--- a/solution.py
+++ b/solution.py
@@ -66,7 +66,7 @@
 
 
 def lanes(start):
-    return pl.ds(pl.multiple_of(start, 128), 128)
+    return slice(start, start + 128)
 
 
 def attend_rows(counts, qkv, out, lse, samples, width):
@@ -91,12 +91,15 @@
                     w = jnp.exp(sc - top)
                     tot = jnp.sum(w, axis=0, keepdims=True)
                     lse[s, j, side:side + 1, :size] = top + jnp.log(tot)
+                    if size < SLOTS:
+                        lse[s, j, side:side + 1, size:] = jnp.full((1, SLOTS - size), 1e30, f32)
                     p = (w * (1.0 / tot)).astype(bf16)
                     parts.append(dot(p, v, TN))
                 out[rows, lanes(lo)] = jnp.where(left, parts[0], parts[1]).astype(bf16)
                 return x
 
-            lax.fori_loop(0, width // 128, pair, 0)
+            for j in range(width // 128):
+                pair(j, 0)
 
         by_size(counts, s, run)
         return start + ((counts[s] + 15) // 16) * 16
@@ -289,9 +292,10 @@
                 dqkv[rows, lanes(2 * width + lo)] = jnp.where(left, dvv[0], dvv[1]).astype(bf16)
                 return x
 
-            lax.fori_loop(0, width // 128, pair, 0)
-
-        by_size(counts, s, run)
+            for j in range(width // 128):
+                pair(j, 0)
+
+        run(SLOTS)
         return start + ((counts[s] + 15) // 16) * 16
 
     lax.fori_loop(0, samples, one, 0)

time: 517 us -> 505 us (0.977)
  Pallas kernels: 218 us -> 200 us
  waiting for transfers between devices: 156 us -> 167 us
    pallas_call x7, Pallas kernels: 184 us -> 173 us  [call(): pl.pallas_call(body, out_shape=list(outs), grid_spec=pltpu.PrefetchScalar...]
    ppermute x60, waiting for transfers between devices: 156 us -> 167 us  [swap(): return lax.ppermute(x, axis, [(k, k ^ bit) for k in range(size)])]
    pallas_call x1, Pallas kernels: 33.9 us -> 26.6 us  [fwd_own(): pl.pallas_call(fwd_own_body(S, width), name='fwd_own', out_shape=outs, gr...]
  transfers between devices with their start and end apart: 60 -> 60, of which waited for: 18 -> 19; matrix products, arithmetic and copies ran while one was open for 12% -> 13% of each run, Pallas kernels for 36% -> 33%
where the time goes in v6:
time: 505 us; the launch traced here: 504 us
  Pallas kernels  200 us (40%)
  waiting for transfers between devices  167 us (33%)
  other arithmetic  55.7 us (11%)
  starting transfers between devices  51.9 us (10%)
  local copies, waits for them, and re-layouts  28.1 us (6%)
    pallas_call x7, Pallas kernels, call(): pl.pallas_call(body, out_shape=list(outs), grid_spec=pltpu.PrefetchScalar...  173 us
    ppermute x60, waiting for transfers between devices, swap(): return lax.ppermute(x, axis, [(k, k ^ bit) for k in range(size)])  167 us
    ppermute x60, starting transfers between devices, swap(): return lax.ppermute(x, axis, [(k, k ^ bit) for k in range(size)])  51.9 us
    pallas_call x1, Pallas kernels, fwd_own(): pl.pallas_call(fwd_own_body(S, width), name='fwd_own', out_shape=outs, gr...  26.6 us
    select_n x20, other arithmetic, spread(): jnp.where(first, jnp.concatenate([x, got], 0), jnp.concatenate([got, x], 0))  25.2 us
    add x20, other arithmetic, fold(): return half(x, i) + swap(half(x, 1 - i), 'dp', dp, bit)  21.3 us
    dynamic_slice x20, local copies, waits for them, and re-layouts, half(): return lax.dynamic_slice_in_dim(x, i * n, n, 0)  15 us
  transfers between devices with their start and end apart: 60, of which 19 were waited for; matrix products, arithmetic and copies ran while one was open for 13% of the time, Pallas kernels for 33%

profile of v6, /device:TPU:0, one launch (start us, length us, event | category | flops | bytes accessed | tf_op | source)
XLA Modules:
  0.0 503.6 jit_solution(8471560540524205848)
XLA Ops:
  0.7 2.4 slice_bitcast_fusion.2
  5.3 3.0 collective-permute-start
  8.3 1.6 dynamic-slice_convert_fusion.3
  10.6 1.7 copy.22.col
  13.5 26.6 %fwd_own.1 = (bf16[1792,768]{1,0:T(8,128)(2,1)}, bf16[1792,768]{1,0:T(8,128)(2,1)}, bf16[1792,768]{1,0:T(8,128)(2,1)}, bf16[1792,1152]{1,0:T(8,128)(2,1)}, bf16[...) custom-call(s32[10]{0:T(128)} %concatenate.132.counts, s32[6,512,1]{2,1,0:T(8,128)} %copy.22.col, ...), custom_call_target="tpu_custom_call" | custom-call | flops 6000000000 | bytes 26214400 | tf_op jit(solution)/shard_map/fwd_own/pallas_call | solution.py:414
  41.2 2.2 dynamic-slice_convert_fusion.1
  43.4 2.5 collective-permute-start.4
  45.9 19.3 %collective-permute-done.4.q1 = f32[192,1152]{1,0:T(8,128)S(1)} collective-permute-done((f32[192,1152]{1,0:T(8,128)}, f32[192,1152]{1,0:T(8,128)S(1)}, u32[]{:S(2)}, u32[]{:S(2)}) %collective-permute-start.4) | collective-permute-done | bytes 884768 | tf_op jit(solution)/shard_map/ppermute | solution.py:481
  65.2 1.7 collective-permute-start.7
  67.2 1.5 collective-permute-start.2
  68.7 6.1 %collective-permute-done.7.w1 = f32[96,768]{1,0:T(8,128)S(1)} collective-permute-done((f32[96,768]{1,0:T(8,128)}, f32[96,768]{1,0:T(8,128)S(1)}, u32[]{:S(2)}, u32[]{:S(2)}) %collective-permute-start.7) | collective-permute-done | bytes 294944 | tf_op jit(solution)/shard_map/ppermute | solution.py:481
  74.8 1.5 collective-permute-start.3
  78.7 26.7 %shard_map.195 = (bf16[1792,1152]{1,0:T(8,128)(2,1)}, bf16[1792,384]{1,0:T(8,128)(2,1)}, f32[6,3,2,256]{3,2,1,0:T(2,128)}, f32[1792,768]{1,0:T(8,128)}, bf16[179...) custom-call(s32[10]{0:T(128)} %concatenate.132.counts, ...), custom_call_target="tpu_custom_call" | custom-call | flops 7000000000 | bytes 28354560 | tf_op jit(solution)/shard_map/pallas_call | solution.py:391
  105.4 15.6 %collective-permute-done.3.d0 = f32[384,768]{1,0:T(8,128)} collective-permute-done((f32[384,768]{1,0:T(8,128)S(1)}, f32[384,768]{1,0:T(8,128)}, u32[]{:S(2)}, u32[]{:S(2)}) %collective-permute-start.3) | collective-permute-done | bytes 1179680 | tf_op jit(solution)/shard_map/ppermute | solution.py:481
  120.9 32.0 %shard_map.196 = (f32[1792,768]{1,0:T(8,128)}, f32[1792,768]{1,0:T(8,128)}, f32[768,1536]{1,0:T(8,128)}, f32[1536,768]{1,0:T(8,128)}) custom-call(s32[10]{0:T(128)} %concatenate.132.counts, bf16[1792,768]{1,0:T(8,128)(2,1)} %get-tuple-element.89.c, bf16[1792,768]{1,0:T(8,128)(2,1)} %get-tuple-element.86.dm, bf16[768,1536]{1,0:T(8,128)(2,1)} %up.1, ...), custom_call_target="tpu_custom_call" | custom-call | flops 17999998976 | bytes 30670848 | tf_op jit(solution)/shard_map/pallas_call | solution.py:391
  153.0 3.2 constant_dynamic-slice_fusion.16
  156.2 3.2 constant_dynamic-slice_fusion.17
  160.2 1.7 collective-permute-start.13
  162.6 26.5 %collective-permute-done.12.u1 = f32[192,1536]{1,0:T(8,128)} collective-permute-done((f32[192,1536]{1,0:T(8,128)}, f32[192,1536]{1,0:T(8,128)}, u32[]{:S(2)}, u32[]{:S(2)}) %collective-permute-start.12) | collective-permute-done | bytes 1179680 | tf_op jit(solution)/shard_map/ppermute | solution.py:481
  189.1 24.3 %collective-permute-done.13.d1 = f32[384,768]{1,0:T(8,128)} collective-permute-done((f32[384,768]{1,0:T(8,128)}, f32[384,768]{1,0:T(8,128)}, u32[]{:S(2)}, u32[]{:S(2)}) %collective-permute-start.13) | collective-permute-done | bytes 1179680 | tf_op jit(solution)/shard_map/ppermute | solution.py:481
  213.9 2.2 dynamic-slice_add_fusion
  216.4 2.6 dynamic-slice_add_fusion.1
  222.8 33.6 %shard_map.197 = (bf16[6,512,768]{2,1,0:T(8,128)(2,1)}, f32[1792,768]{1,0:T(8,128)}, f32[8,768]{1,0:T(8,128)}) custom-call(s32[10]{0:T(128)} %concatenate.132.counts, s32[6,1,512]{2,1,0:T(1,128)} %broadcast_in_dim.18.line, bf16[1792,768]{1,0:T(8,128)(2,1)} %get-tuple-element.89.c, bf16[1792,768]{1,0:T(8,128)(2,1)} %get-tuple-element.86.dm, ...), custom_call_target="tpu_custom_call" | custom-call | flops 12000000000 | bytes 41720832 | tf_op jit(solution)/shard_map/pallas_call | solution.py:391
  256.3 1.9 dynamic-slice_add_fusion.2
  261.1 1.7 collective-permute-start.21
  263.0 25.1 %shard_map.198 = (f32[384,768]{1,0:T(8,128)}, bf16[1792,1152]{1,0:T(8,128)(2,1)}) custom-call(s32[10]{0:T(128)} %concatenate.132.counts, f32[1792,768]{1,0:T(8,128)} %get-tuple-element.111.dr, bf16[1792,1152]{1,0:T(8,128)(2,1)} %get-tuple-element.105.qkv, f32[6,3,2,256]{3,2,1,0:T(2,128)} %get-tuple-element.106.lse, bf16[1792,384]{1,0:T(8,128)(2,1)} %get-tuple-element.81.o, ...), custom_call_target="tpu_custom_call" | custom-call | flops 5000000000 | bytes 16945152 | tf_op jit(solution)/shard_map/pallas_call | solution.py:391
  288.1 2.0 constant_dynamic-slice_fusion.9
  290.2 2.0 dynamic-slice_add_fusion.5
  292.1 2.0 dynamic-slice_add_fusion.6
  294.1 14.6 %shard_map.199 = (f32[1792,768]{1,0:T(8,128)}, f32[3,768,384]{2,1,0:T(8,128)}) custom-call(s32[10]{0:T(128)} %concatenate.132.counts, bf16[1792,1152]{1,0:T(8,128)(2,1)} %get-tuple-element.108.dqkv, bf16[1792,768]{1,0:T(8,128)(2,1)} %get-tuple-element.79.a, bf16[768,1152]{1,0:T(8,128)(2,1)} %copy-done.12), custom_call_target="tpu_custom_call" | custom-call | flops 5000000000 | bytes 17694720 | tf_op jit(solution)/shard_map/pallas_call | solution.py:391
  308.7 2.2 fusion
  315.0 2.8 collective-permute-start.22
  317.8 23.8 %shard_map.200.dqkv = bf16[1792,1152]{1,0:T(8,128)(2,1)} custom-call(s32[10]{0:T(128)} %concatenate.132.counts, f32[1792,768]{1,0:T(8,128)} %get-tuple-element.111.dr, bf16[1792,1152]{1,0:T(8,128)(2,1)} %get-tuple-element.116.qkv, f32[6,3,2,256]{3,2,1,0:T(2,128)} %get-tuple-element.117.lse, bf16[384,768]{1,0:T(8,128)(2,1)} %get-tuple-element.118.wout), custom_call_target="tpu_custom_call" | custom-call | flops 4000000000 | bytes 14389248 | tf_op jit(solution)/shard_map/pallas_call | solution.py:391
  343.1 2.0 dynamic-slice_add_fusion.10
  345.1 1.7 dynamic-slice_add_fusion.11
  348.1 1.6 bitcast_add_fusion.1
  349.8 2.9 collective-permute-start.30
  353.5 1.9 collective-permute-start.29
  356.8 17.5 %shard_map.201 = (bf16[6,512,768]{2,1,0:T(8,128)(2,1)}, f32[8,768]{1,0:T(8,128)}) custom-call(s32[10]{0:T(128)} %concatenate.132.counts, s32[6,1,512]{2,1,0:T(1,128)} %broadcast_in_dim.18.line, f32[1792,768]{1,0:T(8,128)} %get-tuple-element.111.dr, bf16[1792,1152]{1,0:T(8,128)(2,1)} %shard_map.200.dqkv, bf16[768,1152]{1,0:T(8,128)(2,1)} %get-tuple-element.120.wqkv, ...), custom_call_target="tpu_custom_call" | custom-call | flops 4000000000 | bytes 24419328 | tf_op jit(solution)/shard_map/pallas_call | solution.py:391
  375.8 2.3 collective-permute-done.30
  382.1 3.2 collective-permute-start.52
  385.3 1.9 collective-permute-start.33
  387.2 2.5 collective-permute-start.32
  393.1 16.1 %collective-permute-done.35 = f32[16,768]{1,0:T(8,128)S(1)} collective-permute-done((f32[16,768]{1,0:T(8,128)S(1)}, f32[16,768]{1,0:T(8,128)S(1)}, u32[]{:S(2)}, u32[]{:S(2)}) %collective-permute-start.35) | collective-permute-done | bytes 49184 | tf_op jit(solution)/shard_map/ppermute | solution.py:481
  409.6 1.8 collective-permute-start.54
  412.9 1.7 collective-permute-start.36
  414.6 2.5 collective-permute-done.46
  417.3 2.0 collective-permute-start.37
  419.3 1.6 collective-permute-done.41
  421.0 3.8 collective-permute-done.47
  424.9 23.1 %collective-permute-done.42 = f32[72,384]{1,0:T(8,128)S(1)} collective-permute-done((f32[72,384]{1,0:T(8,128)S(1)}, f32[72,384]{1,0:T(8,128)S(1)}, u32[]{:S(2)}, u32[]{:S(2)}) %collective-permute-start.42) | collective-permute-done | bytes 110624 | tf_op jit(solution)/shard_map/ppermute | solution.py:481
  448.1 2.1 collective-permute-start.43
  452.4 5.7 %collective-permute-done.38 = f32[16,768]{1,0:T(8,128)S(1)} collective-permute-done((f32[16,768]{1,0:T(8,128)S(1)}, f32[16,768]{1,0:T(8,128)S(1)}, u32[]{:S(2)}, u32[]{:S(2)}) %collective-permute-start.38) | collective-permute-done | bytes 49184 | tf_op jit(solution)/shard_map/ppermute | solution.py:481
  460.5 1.6 maximum_select_fusion.3
  462.2 1.8 collective-permute-done.49
  464.3 4.5 collective-permute-done.44
  469.4 2.6 collective-permute-done.56
  472.9 8.2 %collective-permute-done.50 = f32[288,384]{1,0:T(8,128)S(1)} collective-permute-done((f32[288,384]{1,0:T(8,128)S(1)}, f32[288,384]{1,0:T(8,128)S(1)}, u32[]{:S(2)}, u32[]{:S(2)}) %collective-permute-start.50) | collective-permute-done | bytes 442400 | tf_op jit(solution)/shard_map/ppermute | solution.py:481
  482.5 2.8 maximum_select_fusion.8
  486.0 1.6 maximum_select_fusion.4
  487.6 2.2 maximum_select_fusion.5
  489.8 2.0 pad_maximum_fusion
  491.8 6.5 %maximum_select_fusion.1 = f32[1536,768]{1,0:T(8,128)} fusion(f32[768,768]{1,0:T(8,128)} %collective-permute-done.59, f32[768,768]{1,0:T(8,128)} %maximum_select_fusion.3, pred[]{:T(512)S(6)} %eq.73), kind=kLoop, calls=%fused_computation.1 | loop fusion | flops 3538944 | bytes 9437185 | tf_op jit(solution)/shard_map/jit(_where)/select_n | solution.py:505
  498.4 5.3 %maximum_select_fusion = f32[768,1536]{1,0:T(8,128)} fusion(f32[384,1536]{1,0:T(8,128)} %collective-permute-done.58, f32[384,1536]{1,0:T(8,128)S(1)} %maximum_select_fusion.2, pred[]{:T(512)S(6)} %eq.73), kind=kLoop, calls=%fused_computation | loop fusion | flops 3538944 | bytes 9437185 | tf_op jit(solution)/shard_map/jit(_where)/select_n | solution.py:505
  (208 shorter events, 45.2 us)
Async XLA Ops:
  5.3 38.1 %collective-permute-start = (f32[192,1152]{1,0:T(8,128)}, f32[192,1152]{1,0:T(8,128)}, u32[]{:S(2)}, u32[]{:S(2)}) collective-permute-start(f32[192,1152]{1,0:T(8,128)} %dynamic-slice_convert_fusion.2), channel_id=1, source_target_pairs={{0,1},{1,0},{2,3},{3,2},{4,5},{5,4},{6,7},{7,6},{8,9},{9,8},{10,11... | collective-permute-start | bytes 2654216 | tf_op jit(solution)/shard_map/ppermute | solution.py:481
  10.0 33.5 %collective-permute-start.1 = (f32[96,768]{1,0:T(8,128)}, f32[96,768]{1,0:T(8,128)}, u32[]{:S(2)}, u32[]{:S(2)}) collective-permute-start(f32[96,768]{1,0:T(8,128)} %dynamic-slice_convert_fusion.3), channel_id=1, source_target_pairs={{0,1},{1,0},{2,3},{3,2},{4,5},{5,4},{6,7},{7,6},{8,9},{9,8},{10,11... | collective-permute-start | bytes 884744 | tf_op jit(solution)/shard_map/ppermute | solution.py:481
  40.0 36.4 %copy-start.23 = (f32[768]{0:T(1024)S(1)}, f32[768]{0:T(1024)}, u32[]{:S(2)}) copy-start(f32[768]{0:T(1024)} %param.19) | copy-start | bytes 9220
  40.0 37.0 %copy-start.24 = (f32[768]{0:T(1024)S(1)}, f32[768]{0:T(1024)}, u32[]{:S(2)}) copy-start(f32[768]{0:T(1024)} %param.20) | copy-start | bytes 9220
  43.4 21.8 %collective-permute-start.4 = (f32[192,1152]{1,0:T(8,128)}, f32[192,1152]{1,0:T(8,128)S(1)}, u32[]{:S(2)}, u32[]{:S(2)}) collective-permute-start(f32[192,1152]{1,0:T(8,128)} %collective-permute-done.q0), channel_id=1, source_target_pairs={{0,4},{2,6},{4,0},{6,2},{8,12},{10,14},{12,8},{14,10},{16,20},{18,... | collective-permute-start | bytes 2654216 | tf_op jit(solution)/shard_map/ppermute | solution.py:481
  45.9 32.0 %collective-permute-start.5 = (f32[192,1152]{1,0:T(8,128)}, f32[192,1152]{1,0:T(8,128)}, u32[]{:S(2)}, u32[]{:S(2)}) collective-permute-start(f32[192,1152]{1,0:T(8,128)} %collective-permute-done.q0), channel_id=1, source_target_pairs={{0,2},{2,0},{4,6},{6,4},{8,10},{10,8},{12,14},{14,12},{16,18},{18,... | collective-permute-start | bytes 2654216 | tf_op jit(solution)/shard_map/ppermute | solution.py:481
  65.2 12.4 %copy-start.27 = (f32[192,1152]{1,0:T(8,128)}, f32[192,1152]{1,0:T(8,128)S(1)}, u32[]{:S(2)}) copy-start(f32[192,1152]{1,0:T(8,128)S(1)} %collective-permute-done.4.q1) | copy-start | bytes 2654212
  65.2 12.8 %collective-permute-start.6 = (f32[192,1152]{1,0:T(8,128)S(1)}, f32[192,1152]{1,0:T(8,128)}, u32[]{:S(2)}, u32[]{:S(2)}) collective-permute-start(f32[192,1152]{1,0:T(8,128)S(1)} %collective-permute-done.4.q1), channel_id=1, source_target_pairs={{0,2},{2,0},{4,6},{6,4},{8,10},{10,8},{12,14},{14,12},{16,18},{18,... | collective-permute-start | bytes 2654216 | tf_op jit(solution)/shard_map/ppermute | solution.py:481
  65.2 9.6 %collective-permute-start.7 = (f32[96,768]{1,0:T(8,128)}, f32[96,768]{1,0:T(8,128)S(1)}, u32[]{:S(2)}, u32[]{:S(2)}) collective-permute-start(f32[96,768]{1,0:T(8,128)} %collective-permute-done.1.w0), channel_id=1, source_target_pairs={{0,4},{2,6},{4,0},{6,2},{8,12},{10,14},{12,8},{14,10},{16,20},{18,... | collective-permute-start | bytes 884744 | tf_op jit(solution)/shard_map/ppermute | solution.py:481
  66.9 9.4 %collective-permute-start.8 = (f32[96,768]{1,0:T(8,128)}, f32[96,768]{1,0:T(8,128)S(1)}, u32[]{:S(2)}, u32[]{:S(2)}) collective-permute-start(f32[96,768]{1,0:T(8,128)} %collective-permute-done.1.w0), channel_id=1, source_target_pairs={{0,2},{2,0},{4,6},{6,4},{8,10},{10,8},{12,14},{14,12},{16,18},{18,... | collective-permute-start | bytes 884744 | tf_op jit(solution)/shard_map/ppermute | solution.py:481
  67.2 38.2 %collective-permute-start.2 = (f32[192,1536]{1,0:T(8,128)}, f32[192,1536]{1,0:T(8,128)}, u32[]{:S(2)}, u32[]{:S(2)}) collective-permute-start(f32[192,1536]{1,0:T(8,128)} %dynamic-slice_convert_fusion.1), channel_id=1, source_target_pairs={{0,1},{1,0},{2,3},{3,2},{4,5},{5,4},{6,7},{7,6},{8,9},{9,8},{10,11... | collective-permute-start | bytes 3538952 | tf_op jit(solution)/shard_map/ppermute | solution.py:481
  74.8 46.1 %collective-permute-start.3 = (f32[384,768]{1,0:T(8,128)S(1)}, f32[384,768]{1,0:T(8,128)}, u32[]{:S(2)}, u32[]{:S(2)}) collective-permute-start(f32[384,768]{1,0:T(8,128)S(1)} %dynamic-slice_convert_fusion), channel_id=1, source_target_pairs={{0,1},{1,0},{2,3},{3,2},{4,5},{5,4},{6,7},{7,6},{8,9},{9,8},{10,11... | collective-permute-start | bytes 3538952 | tf_op jit(solution)/shard_map/ppermute | solution.py:481
  76.4 1.6 collective-permute-start.9
  156.2 57.2 %collective-permute-start.11 = (f32[768,768]{1,0:T(8,128)}, f32[768,768]{1,0:T(8,128)S(1)}, u32[]{:S(2)}, u32[]{:S(2)}) collective-permute-start(f32[768,768]{1,0:T(8,128)} %constant_dynamic-slice_fusion.16), channel_id=1, source_target_pairs={{0,2},{2,0},{4,6},{6,4},{8,10},{10,8},{12,14},{14,12},{16,18},{18,... | collective-permute-start | bytes 7077896 | tf_op jit(solution)/shard_map/ppermute | solution.py:481
  159.4 56.7 %collective-permute-start.10 = (f32[384,1536]{1,0:T(8,128)}, f32[384,1536]{1,0:T(8,128)}, u32[]{:S(2)}, u32[]{:S(2)}) collective-permute-start(f32[384,1536]{1,0:T(8,128)} %constant_dynamic-slice_fusion.17), channel_id=1, source_target_pairs={{0,2},{2,0},{4,6},{6,4},{8,10},{10,8},{12,14},{14,12},{16,18},{18,... | collective-permute-start | bytes 7077896 | tf_op jit(solution)/shard_map/ppermute | solution.py:481
  159.9 29.2 %collective-permute-start.12 = (f32[192,1536]{1,0:T(8,128)}, f32[192,1536]{1,0:T(8,128)}, u32[]{:S(2)}, u32[]{:S(2)}) collective-permute-start(f32[192,1536]{1,0:T(8,128)} %collective-permute-done.2.u0), channel_id=1, source_target_pairs={{0,4},{2,6},{4,0},{6,2},{8,12},{10,14},{12,8},{14,10},{16,20},{18,... | collective-permute-start | bytes 3538952 | tf_op jit(solution)/shard_map/ppermute | solution.py:481
  160.2 53.2 %collective-permute-start.13 = (f32[384,768]{1,0:T(8,128)}, f32[384,768]{1,0:T(8,128)}, u32[]{:S(2)}, u32[]{:S(2)}) collective-permute-start(f32[384,768]{1,0:T(8,128)} %collective-permute-done.3.d0), channel_id=1, source_target_pairs={{0,4},{2,6},{4,0},{6,2},{8,12},{10,14},{12,8},{14,10},{16,20},{18,... | collective-permute-start | bytes 3538952 | tf_op jit(solution)/shard_map/ppermute | solution.py:481
  162.6 58.9 %collective-permute-start.14 = (f32[192,1536]{1,0:T(8,128)}, f32[192,1536]{1,0:T(8,128)S(1)}, u32[]{:S(2)}, u32[]{:S(2)}) collective-permute-start(f32[192,1536]{1,0:T(8,128)} %collective-permute-done.2.u0), channel_id=1, source_target_pairs={{0,2},{2,0},{4,6},{6,4},{8,10},{10,8},{12,14},{14,12},{16,18},{18,... | collective-permute-start | bytes 3538952 | tf_op jit(solution)/shard_map/ppermute | solution.py:481
  189.1 33.7 %collective-permute-start.16 = (f32[384,768]{1,0:T(8,128)}, f32[384,768]{1,0:T(8,128)}, u32[]{:S(2)}, u32[]{:S(2)}) collective-permute-start(f32[384,768]{1,0:T(8,128)} %collective-permute-done.3.d0), channel_id=1, source_target_pairs={{0,2},{2,0},{4,6},{6,4},{8,10},{10,8},{12,14},{14,12},{16,18},{18,... | collective-permute-start | bytes 3538952 | tf_op jit(solution)/shard_map/ppermute | solution.py:481
  213.4 9.3 %collective-permute-start.15 = (f32[192,1536]{1,0:T(8,128)}, f32[192,1536]{1,0:T(8,128)}, u32[]{:S(2)}, u32[]{:S(2)}) collective-permute-start(f32[192,1536]{1,0:T(8,128)} %collective-permute-done.12.u1), channel_id=1, source_target_pairs={{0,2},{2,0},{4,6},{6,4},{8,10},{10,8},{12,14},{14,12},{16,18},{18,... | collective-permute-start | bytes 3538952 | tf_op jit(solution)/shard_map/ppermute | solution.py:481
  213.4 9.3 %collective-permute-start.17 = (f32[384,768]{1,0:T(8,128)}, f32[384,768]{1,0:T(8,128)}, u32[]{:S(2)}, u32[]{:S(2)}) collective-permute-start(f32[384,768]{1,0:T(8,128)} %collective-permute-done.13.d1), channel_id=1, source_target_pairs={{0,2},{2,0},{4,6},{6,4},{8,10},{10,8},{12,14},{14,12},{16,18},{18,... | collective-permute-start | bytes 3538952 | tf_op jit(solution)/shard_map/ppermute | solution.py:481
  219.1 37.2 %collective-permute-start.19 = (f32[384,768]{1,0:T(8,128)S(1)}, f32[384,768]{1,0:T(8,128)}, u32[]{:S(2)}, u32[]{:S(2)}) collective-permute-start(f32[384,768]{1,0:T(8,128)S(1)} %constant_dynamic-slice_fusion.14), channel_id=1, source_target_pairs={{0,8},{2,10},{4,12},{6,14},{8,0},{10,2},{12,4},{14,6},{16,24},{18,... | collective-permute-start | bytes 3538952 | tf_op jit(solution)/shard_map/ppermute | solution.py:481
  222.5 35.8 %collective-permute-start.18 = (f32[192,1536]{1,0:T(8,128)}, f32[192,1536]{1,0:T(8,128)}, u32[]{:S(2)}, u32[]{:S(2)}) collective-permute-start(f32[192,1536]{1,0:T(8,128)} %constant_dynamic-slice_fusion.15), channel_id=1, source_target_pairs={{0,4},{2,6},{4,0},{6,2},{8,12},{10,14},{12,8},{14,10},{16,20},{18,... | collective-permute-start | bytes 3538952 | tf_op jit(solution)/shard_map/ppermute | solution.py:481
  261.1 29.0 %collective-permute-start.21 = (f32[192,768]{1,0:T(8,128)}, f32[192,768]{1,0:T(8,128)}, u32[]{:S(2)}, u32[]{:S(2)}) collective-permute-start(f32[192,768]{1,0:T(8,128)} %constant_dynamic-slice_fusion.12), channel_id=1, source_target_pairs={{0,4},{2,6},{4,0},{6,2},{8,12},{10,14},{12,8},{14,10},{16,20},{18,... | collective-permute-start | bytes 1769480 | tf_op jit(solution)/shard_map/ppermute | solution.py:481
  262.9 29.2 %collective-permute-start.20 = (f32[96,1536]{1,0:T(8,128)S(1)}, f32[96,1536]{1,0:T(8,128)}, u32[]{:S(2)}, u32[]{:S(2)}) collective-permute-start(f32[96,1536]{1,0:T(8,128)S(1)} %constant_dynamic-slice_fusion.13), channel_id=1, source_target_pairs={{0,8},{2,10},{4,12},{6,14},{8,0},{10,2},{12,4},{14,6},{16,24},{18,... | collective-permute-start | bytes 1769480 | tf_op jit(solution)/shard_map/ppermute | solution.py:481
  290.2 51.5 %collective-permute-start.26 = (f32[192,768]{1,0:T(8,128)}, f32[192,768]{1,0:T(8,128)}, u32[]{:S(2)}, u32[]{:S(2)}) collective-permute-start(f32[192,768]{1,0:T(8,128)} %constant_dynamic-slice_fusion.9), channel_id=1, source_target_pairs={{0,2},{2,0},{4,6},{6,4},{8,10},{10,8},{12,14},{14,12},{16,18},{18,... | collective-permute-start | bytes 1769480 | tf_op jit(solution)/shard_map/ppermute | solution.py:481
  311.9 34.9 %collective-permute-start.25 = (f32[576,384]{1,0:T(8,128)}, f32[576,384]{1,0:T(8,128)}, u32[]{:S(2)}, u32[]{:S(2)}) collective-permute-start(f32[576,384]{1,0:T(8,128)} %dynamic-slice_bitcast_fusion), channel_id=1, source_target_pairs={{0,2},{2,0},{4,6},{6,4},{8,10},{10,8},{12,14},{14,12},{16,18},{18,... | collective-permute-start | bytes 2654216 | tf_op jit(solution)/shard_map/ppermute | solution.py:481
  312.9 35.2 %collective-permute-start.24 = (f32[576,384]{1,0:T(8,128)}, f32[576,384]{1,0:T(8,128)}, u32[]{:S(2)}, u32[]{:S(2)}) collective-permute-start(f32[576,384]{1,0:T(8,128)} %dynamic-slice_bitcast_fusion.1), channel_id=1, source_target_pairs={{0,2},{2,0},{4,6},{6,4},{8,10},{10,8},{12,14},{14,12},{16,18},{18,... | collective-permute-start | bytes 2654216 | tf_op jit(solution)/shard_map/ppermute | solution.py:481
  314.1 29.0 %collective-permute-start.23 = (f32[96,768]{1,0:T(8,128)}, f32[96,768]{1,0:T(8,128)}, u32[]{:S(2)}, u32[]{:S(2)}) collective-permute-start(f32[96,768]{1,0:T(8,128)} %constant_dynamic-slice_fusion.10), channel_id=1, source_target_pairs={{0,16},{2,18},{4,20},{6,22},{8,24},{10,26},{12,28},{14,30},{16,0},... | collective-permute-start | bytes 884744 | tf_op jit(solution)/shard_map/ppermute | solution.py:481
  315.0 30.1 %collective-permute-start.22 = (f32[48,1536]{1,0:T(8,128)}, f32[48,1536]{1,0:T(8,128)}, u32[]{:S(2)}, u32[]{:S(2)}) collective-permute-start(f32[48,1536]{1,0:T(8,128)} %constant_dynamic-slice_fusion.11), channel_id=1, source_target_pairs={{0,16},{2,18},{4,20},{6,22},{8,24},{10,26},{12,28},{14,30},{16,0},... | collective-permute-start | bytes 884744 | tf_op jit(solution)/shard_map/ppermute | solution.py:481
  343.1 9.6 %copy-start.13 = (f32[192,768]{1,0:T(8,128)}, f32[192,768]{1,0:T(8,128)S(1)}, u32[]{:S(2)}) copy-start(f32[192,768]{1,0:T(8,128)S(1)} %dynamic-slice_add_fusion.4) | copy-start | bytes 1769476
  349.7 24.6 %collective-permute-start.31 = (f32[96,768]{1,0:T(8,128)}, f32[96,768]{1,0:T(8,128)}, u32[]{:S(2)}, u32[]{:S(2)}) collective-permute-start(f32[96,768]{1,0:T(8,128)} %dynamic-slice_add_fusion.10), channel_id=1, source_target_pairs={{0,16},{2,18},{4,20},{6,22},{8,24},{10,26},{12,28},{14,30},{16,0},... | collective-permute-start | bytes 884744 | tf_op jit(solution)/shard_map/ppermute | solution.py:481
  349.8 28.2 %collective-permute-start.30 = (f32[48,1536]{1,0:T(8,128)}, f32[48,1536]{1,0:T(8,128)}, u32[]{:S(2)}, u32[]{:S(2)}) collective-permute-start(f32[48,1536]{1,0:T(8,128)} %dynamic-slice_add_fusion.11), channel_id=1, source_target_pairs={{0,16},{2,18},{4,20},{6,22},{8,24},{10,26},{12,28},{14,30},{16,0},... | collective-permute-start | bytes 884744 | tf_op jit(solution)/shard_map/ppermute | solution.py:481
  353.5 25.9 %collective-permute-start.29 = (f32[96,768]{1,0:T(8,128)}, f32[96,768]{1,0:T(8,128)}, u32[]{:S(2)}, u32[]{:S(2)}) collective-permute-start(f32[96,768]{1,0:T(8,128)} %constant_dynamic-slice_fusion.6), channel_id=1, source_target_pairs={{0,8},{2,10},{4,12},{6,14},{8,0},{10,2},{12,4},{14,6},{16,24},{18,... | collective-permute-start | bytes 884744 | tf_op jit(solution)/shard_map/ppermute | solution.py:481
  355.5 26.5 %collective-permute-start.28 = (f32[288,384]{1,0:T(8,128)S(1)}, f32[288,384]{1,0:T(8,128)S(1)}, u32[]{:S(2)}, u32[]{:S(2)}) collective-permute-start(f32[288,384]{1,0:T(8,128)S(1)} %constant_dynamic-slice_fusion.7), channel_id=1, source_target_pairs={{0,8},{2,10},{4,12},{6,14},{8,0},{10,2},{12,4},{14,6},{16,24},{18,... | collective-permute-start | bytes 1327112 | tf_op jit(solution)/shard_map/ppermute | solution.py:481
  355.6 26.3 %collective-permute-start.27 = (f32[288,384]{1,0:T(8,128)S(1)}, f32[288,384]{1,0:T(8,128)S(1)}, u32[]{:S(2)}, u32[]{:S(2)}) collective-permute-start(f32[288,384]{1,0:T(8,128)S(1)} %constant_dynamic-slice_fusion.8), channel_id=1, source_target_pairs={{0,4},{2,6},{4,0},{6,2},{8,12},{10,14},{12,8},{14,10},{16,20},{18,... | collective-permute-start | bytes 1327112 | tf_op jit(solution)/shard_map/ppermute | solution.py:481
  382.1 9.8 %collective-permute-start.52 = (f32[48,768]{1,0:T(8,128)S(1)}, f32[48,768]{1,0:T(8,128)S(1)}, u32[]{:S(2)}, u32[]{:S(2)}) collective-permute-start(f32[48,768]{1,0:T(8,128)S(1)} %constant_dynamic-slice_fusion.1), channel_id=1, source_target_pairs={{0,4},{2,6},{4,0},{6,2},{8,12},{10,14},{12,8},{14,10},{16,20},{18,... | collective-permute-start | bytes 442376 | tf_op jit(solution)/shard_map/ppermute | solution.py:481
  385.3 5.1 %collective-permute-start.34 = (f32[16,768]{1,0:T(8,128)S(1)}, f32[16,768]{1,0:T(8,128)S(1)}, u32[]{:S(2)}, u32[]{:S(2)}) collective-permute-start(f32[16,768]{1,0:T(8,128)S(1)} %constant_dynamic-update-slice_fusion), channel_id=1, source_target_pairs={{0,16},{2,18},{4,20},{6,22},{8,24},{10,26},{12,28},{14,30},{16,0},... | collective-permute-start | bytes 147464 | tf_op jit(solution)/shard_map/ppermute | solution.py:481
  385.3 27.4 %collective-permute-start.33 = (f32[192,768]{1,0:T(8,128)S(1)}, f32[192,768]{1,0:T(8,128)S(1)}, u32[]{:S(2)}, u32[]{:S(2)}) collective-permute-start(f32[192,768]{1,0:T(8,128)S(1)} %maximum_select_fusion.12), channel_id=1, source_target_pairs={{0,4},{2,6},{4,0},{6,2},{8,12},{10,14},{12,8},{14,10},{16,20},{18,... | collective-permute-start | bytes 1769480 | tf_op jit(solution)/shard_map/ppermute | solution.py:481
  387.2 25.6 %collective-permute-start.32 = (f32[96,1536]{1,0:T(8,128)S(1)}, f32[96,1536]{1,0:T(8,128)S(1)}, u32[]{:S(2)}, u32[]{:S(2)}) collective-permute-start(f32[96,1536]{1,0:T(8,128)S(1)} %maximum_select_fusion.11), channel_id=1, source_target_pairs={{0,8},{2,10},{4,12},{6,14},{8,0},{10,2},{12,4},{14,6},{16,24},{18,... | collective-permute-start | bytes 1769480 | tf_op jit(solution)/shard_map/ppermute | solution.py:481
  389.7 21.7 %collective-permute-start.40 = (f32[144,384]{1,0:T(8,128)S(1)}, f32[144,384]{1,0:T(8,128)S(1)}, u32[]{:S(2)}, u32[]{:S(2)}) collective-permute-start(f32[144,384]{1,0:T(8,128)S(1)} %constant_dynamic-slice_fusion.5), channel_id=1, source_target_pairs={{0,8},{2,10},{4,12},{6,14},{8,0},{10,2},{12,4},{14,6},{16,24},{18,... | collective-permute-start | bytes 663560 | tf_op jit(solution)/shard_map/ppermute | solution.py:481
  390.4 18.7 %collective-permute-start.35 = (f32[16,768]{1,0:T(8,128)S(1)}, f32[16,768]{1,0:T(8,128)S(1)}, u32[]{:S(2)}, u32[]{:S(2)}) collective-permute-start(f32[16,768]{1,0:T(8,128)S(1)} %add.286), channel_id=1, source_target_pairs={{0,8},{2,10},{4,12},{6,14},{8,0},{10,2},{12,4},{14,6},{16,24},{18,... | collective-permute-start | bytes 147464 | tf_op jit(solution)/shard_map/ppermute | solution.py:481
  391.9 17.6 %collective-permute-start.53 = (f32[24,768]{1,0:T(8,128)S(1)}, f32[24,768]{1,0:T(8,128)S(1)}, u32[]{:S(2)}, u32[]{:S(2)}) collective-permute-start(f32[24,768]{1,0:T(8,128)S(1)} %constant_dynamic-slice_fusion), channel_id=1, source_target_pairs={{0,16},{2,18},{4,20},{6,22},{8,24},{10,26},{12,28},{14,30},{16,0},... | collective-permute-start | bytes 221192 | tf_op jit(solution)/shard_map/ppermute | solution.py:481
  409.2 8.0 %collective-permute-start.46 = (f32[144,384]{1,0:T(8,128)S(1)}, f32[144,384]{1,0:T(8,128)S(1)}, u32[]{:S(2)}, u32[]{:S(2)}) collective-permute-start(f32[144,384]{1,0:T(8,128)S(1)} %constant_dynamic-slice_fusion.3), channel_id=1, source_target_pairs={{0,4},{2,6},{4,0},{6,2},{8,12},{10,14},{12,8},{14,10},{16,20},{18,... | collective-permute-start | bytes 663560 | tf_op jit(solution)/shard_map/ppermute | solution.py:481
  409.6 40.6 %collective-permute-start.54 = (f32[24,768]{1,0:T(8,128)S(1)}, f32[24,768]{1,0:T(8,128)S(1)}, u32[]{:S(2)}, u32[]{:S(2)}) collective-permute-start(f32[24,768]{1,0:T(8,128)S(1)} %dynamic-slice_add_fusion.17), channel_id=1, source_target_pairs={{0,16},{2,18},{4,20},{6,22},{8,24},{10,26},{12,28},{14,30},{16,0},... | collective-permute-start | bytes 221192 | tf_op jit(solution)/shard_map/ppermute | solution.py:481
  411.4 9.4 %collective-permute-start.41 = (f32[72,384]{1,0:T(8,128)S(1)}, f32[72,384]{1,0:T(8,128)S(1)}, u32[]{:S(2)}, u32[]{:S(2)}) collective-permute-start(f32[72,384]{1,0:T(8,128)S(1)} %constant_dynamic-slice_fusion.4), channel_id=1, source_target_pairs={{0,16},{2,18},{4,20},{6,22},{8,24},{10,26},{12,28},{14,30},{16,0},... | collective-permute-start | bytes 331784 | tf_op jit(solution)/shard_map/ppermute | solution.py:481
  412.9 47.3 %collective-permute-start.36 = (f32[192,1536]{1,0:T(8,128)S(1)}, f32[192,1536]{1,0:T(8,128)S(1)}, u32[]{:S(2)}, u32[]{:S(2)}) collective-permute-start(f32[192,1536]{1,0:T(8,128)S(1)} %maximum_select_fusion.6), channel_id=1, source_target_pairs={{0,4},{2,6},{4,0},{6,2},{8,12},{10,14},{12,8},{14,10},{16,20},{18,... | collective-permute-start | bytes 3538952 | tf_op jit(solution)/shard_map/ppermute | solution.py:481
  417.2 7.6 %collective-permute-start.47 = (f32[72,384]{1,0:T(8,128)S(1)}, f32[72,384]{1,0:T(8,128)S(1)}, u32[]{:S(2)}, u32[]{:S(2)}) collective-permute-start(f32[72,384]{1,0:T(8,128)S(1)} %constant_dynamic-slice_fusion.2), channel_id=1, source_target_pairs={{0,16},{2,18},{4,20},{6,22},{8,24},{10,26},{12,28},{14,30},{16,0},... | collective-permute-start | bytes 331784 | tf_op jit(solution)/shard_map/ppermute | solution.py:481
  417.3 43.1 %collective-permute-start.37 = (f32[384,768]{1,0:T(8,128)S(1)}, f32[384,768]{1,0:T(8,128)S(1)}, u32[]{:S(2)}, u32[]{:S(2)}) collective-permute-start(f32[384,768]{1,0:T(8,128)S(1)} %maximum_select_fusion.7), channel_id=1, source_target_pairs={{0,8},{2,10},{4,12},{6,14},{8,0},{10,2},{12,4},{14,6},{16,24},{18,... | collective-permute-start | bytes 3538952 | tf_op jit(solution)/shard_map/ppermute | solution.py:481
  420.9 27.2 %collective-permute-start.42 = (f32[72,384]{1,0:T(8,128)S(1)}, f32[72,384]{1,0:T(8,128)S(1)}, u32[]{:S(2)}, u32[]{:S(2)}) collective-permute-start(f32[72,384]{1,0:T(8,128)S(1)} %dynamic-slice_add_fusion.16), channel_id=1, source_target_pairs={{0,16},{2,18},{4,20},{6,22},{8,24},{10,26},{12,28},{14,30},{16,0},... | collective-permute-start | bytes 331784 | tf_op jit(solution)/shard_map/ppermute | solution.py:481
  424.9 26.3 %collective-permute-start.48 = (f32[72,384]{1,0:T(8,128)S(1)}, f32[72,384]{1,0:T(8,128)S(1)}, u32[]{:S(2)}, u32[]{:S(2)}) collective-permute-start(f32[72,384]{1,0:T(8,128)S(1)} %dynamic-slice_add_fusion.15), channel_id=1, source_target_pairs={{0,16},{2,18},{4,20},{6,22},{8,24},{10,26},{12,28},{14,30},{16,0},... | collective-permute-start | bytes 331784 | tf_op jit(solution)/shard_map/ppermute | solution.py:481
  448.1 10.9 %collective-permute-start.43 = (f32[144,384]{1,0:T(8,128)S(1)}, f32[144,384]{1,0:T(8,128)S(1)}, u32[]{:S(2)}, u32[]{:S(2)}) collective-permute-start(f32[144,384]{1,0:T(8,128)S(1)} %maximum_select_fusion.17), channel_id=1, source_target_pairs={{0,8},{2,10},{4,12},{6,14},{8,0},{10,2},{12,4},{14,6},{16,24},{18,... | collective-permute-start | bytes 663560 | tf_op jit(solution)/shard_map/ppermute | solution.py:481
  450.2 11.8 %collective-permute-start.55 = (f32[48,768]{1,0:T(8,128)S(1)}, f32[48,768]{1,0:T(8,128)S(1)}, u32[]{:S(2)}, u32[]{:S(2)}) collective-permute-start(f32[48,768]{1,0:T(8,128)S(1)} %maximum_select_fusion.19), channel_id=1, source_target_pairs={{0,4},{2,6},{4,0},{6,2},{8,12},{10,14},{12,8},{14,10},{16,20},{18,... | collective-permute-start | bytes 442376 | tf_op jit(solution)/shard_map/ppermute | solution.py:481
  451.2 6.9 %collective-permute-start.38 = (f32[16,768]{1,0:T(8,128)S(1)}, f32[16,768]{1,0:T(8,128)S(1)}, u32[]{:S(2)}, u32[]{:S(2)}) collective-permute-start(f32[16,768]{1,0:T(8,128)S(1)} %add.287), channel_id=1, source_target_pairs={{0,4},{2,6},{4,0},{6,2},{8,12},{10,14},{12,8},{14,10},{16,20},{18,... | collective-permute-start | bytes 147464 | tf_op jit(solution)/shard_map/ppermute | solution.py:481
  458.1 5.9 %collective-permute-start.49 = (f32[144,384]{1,0:T(8,128)S(1)}, f32[144,384]{1,0:T(8,128)S(1)}, u32[]{:S(2)}, u32[]{:S(2)}) collective-permute-start(f32[144,384]{1,0:T(8,128)S(1)} %maximum_select_fusion.18), channel_id=1, source_target_pairs={{0,4},{2,6},{4,0},{6,2},{8,12},{10,14},{12,8},{14,10},{16,20},{18,... | collective-permute-start | bytes 663560 | tf_op jit(solution)/shard_map/ppermute | solution.py:481
  459.0 9.7 %collective-permute-start.44 = (f32[288,384]{1,0:T(8,128)S(1)}, f32[288,384]{1,0:T(8,128)S(1)}, u32[]{:S(2)}, u32[]{:S(2)}) collective-permute-start(f32[288,384]{1,0:T(8,128)S(1)} %maximum_select_fusion.14), channel_id=1, source_target_pairs={{0,4},{2,6},{4,0},{6,2},{8,12},{10,14},{12,8},{14,10},{16,20},{18,... | collective-permute-start | bytes 1327112 | tf_op jit(solution)/shard_map/ppermute | solution.py:481
  462.0 29.8 %collective-permute-start.59 = (f32[768,768]{1,0:T(8,128)}, f32[768,768]{1,0:T(8,128)}, u32[]{:S(2)}, u32[]{:S(2)}) collective-permute-start(f32[768,768]{1,0:T(8,128)} %maximum_select_fusion.3), channel_id=1, source_target_pairs={{0,2},{2,0},{4,6},{6,4},{8,10},{10,8},{12,14},{14,12},{16,18},{18,... | collective-permute-start | bytes 7077896 | tf_op jit(solution)/shard_map/ppermute | solution.py:481
  462.1 9.9 %collective-permute-start.56 = (f32[96,768]{1,0:T(8,128)S(1)}, f32[96,768]{1,0:T(8,128)S(1)}, u32[]{:S(2)}, u32[]{:S(2)}) collective-permute-start(f32[96,768]{1,0:T(8,128)S(1)} %maximum_select_fusion.16), channel_id=1, source_target_pairs={{0,8},{2,10},{4,12},{6,14},{8,0},{10,2},{12,4},{14,6},{16,24},{18,... | collective-permute-start | bytes 884744 | tf_op jit(solution)/shard_map/ppermute | solution.py:481
  464.0 17.0 %collective-permute-start.50 = (f32[288,384]{1,0:T(8,128)S(1)}, f32[288,384]{1,0:T(8,128)S(1)}, u32[]{:S(2)}, u32[]{:S(2)}) collective-permute-start(f32[288,384]{1,0:T(8,128)S(1)} %maximum_select_fusion.15), channel_id=1, source_target_pairs={{0,8},{2,10},{4,12},{6,14},{8,0},{10,2},{12,4},{14,6},{16,24},{18,... | collective-permute-start | bytes 1327112 | tf_op jit(solution)/shard_map/ppermute | solution.py:481
  468.8 17.2 %collective-permute-start.45 = (f32[576,384]{1,0:T(8,128)S(1)}, f32[576,384]{1,0:T(8,128)}, u32[]{:S(2)}, u32[]{:S(2)}) collective-permute-start(f32[576,384]{1,0:T(8,128)S(1)} %maximum_select_fusion.9), channel_id=1, source_target_pairs={{0,2},{2,0},{4,6},{6,4},{8,10},{10,8},{12,14},{14,12},{16,18},{18,... | collective-permute-start | bytes 2654216 | tf_op jit(solution)/shard_map/ppermute | solution.py:481
  468.9 29.5 %collective-permute-start.58 = (f32[384,1536]{1,0:T(8,128)S(1)}, f32[384,1536]{1,0:T(8,128)}, u32[]{:S(2)}, u32[]{:S(2)}) collective-permute-start(f32[384,1536]{1,0:T(8,128)S(1)} %maximum_select_fusion.2), channel_id=1, source_target_pairs={{0,2},{2,0},{4,6},{6,4},{8,10},{10,8},{12,14},{14,12},{16,18},{18,... | collective-permute-start | bytes 7077896 | tf_op jit(solution)/shard_map/ppermute | solution.py:481
  472.9 9.1 %collective-permute-start.57 = (f32[192,768]{1,0:T(8,128)}, f32[192,768]{1,0:T(8,128)}, u32[]{:S(2)}, u32[]{:S(2)}) collective-permute-start(f32[192,768]{1,0:T(8,128)} %maximum_select_fusion.13), channel_id=1, source_target_pairs={{0,2},{2,0},{4,6},{6,4},{8,10},{10,8},{12,14},{14,12},{16,18},{18,... | collective-permute-start | bytes 1769480 | tf_op jit(solution)/shard_map/ppermute | solution.py:481
  482.0 5.5 %collective-permute-start.51 = (f32[576,384]{1,0:T(8,128)}, f32[576,384]{1,0:T(8,128)}, u32[]{:S(2)}, u32[]{:S(2)}) collective-permute-start(f32[576,384]{1,0:T(8,128)} %maximum_select_fusion.10), channel_id=1, source_target_pairs={{0,2},{2,0},{4,6},{6,4},{8,10},{10,8},{12,14},{14,12},{16,18},{18,... | collective-permute-start | bytes 2654216 | tf_op jit(solution)/shard_map/ppermute | solution.py:481
  482.0 3.3 collective-permute-start.39
  (27 other events, 119.3 us)

commit v7 on v6

--- a/solution.py
+++ b/solution.py
@@ -561,17 +561,19 @@
     A, B = fold(A, along[2], dp), fold(B, other[2], dp)
     gout, dq0 = attn_own(counts, dr, qkv0, lse0, o0, wo, S)
     A, B, dq0, dr = tie(A, B, dq0, dr)
-    A, B, E = folds(A, along[3:], dp), folds(B, other[3:], dp), fold(gout, 1, dp)
+    A, B = folds(A, along[3:], dp), folds(B, other[3:], dp)
     da, gqkv = proj_own(counts, dq0, a, wq, S)
-    C = gqkv.reshape(2, (3 * D) // 2, -1)
+    width = gout.shape[0]
+    flat = [gqkv.reshape(3 * D, width)] + [gout[:, j:j + width] for j in range(0, D, width)]
+    C = jnp.concatenate(flat, 0).reshape(2, -1, width)
     C, F = fold(C[0], 1, dp), fold(C[1], 1, dp)
     da, dr = tie(da, dr)
     dq1 = attn_other(counts, dr, qkv1, lse1, wo1, S)
-    A, B, C, F, E, dq1 = tie(A, B, C, F, E, dq1)
+    A, B, C, F, dq1 = tie(A, B, C, F, dq1)
     A, B = spreads(A, along[3:], dp), spreads(B, other[3:], dp)
-    C, F, E = fold(C, along[1], dp), fold(F, other[1], dp), fold(E, other[1], dp)
+    C, F = fold(C, along[1], dp), fold(F, other[1], dp)
     gin, gg1 = proj_other(counts, line, dr, dq1, wq1, da, h, g1, S, L)
-    C, F, E, A, B, gg1 = tie(C, F, E, A, B, gg1)
+    C, F, A, B, gg1 = tie(C, F, A, B, gg1)
     small = jnp.concatenate([gg1, gg2], 0)
     for bit in along[3:]:
         small = small + swap(small, "dp", dp, bit)
@@ -584,8 +586,9 @@
     gg1, gg2 = small[:8], small[8:]
     C = spreads(folds(C, along[2:], dp), along, dp)
     F = spreads(folds(F, other[2:], dp), other, dp)
-    gqkv = jnp.concatenate([C, F], 0).reshape(3, D, -1)
-    gout = spreads(folds(E, other[2:], dp), other, dp)
+    flat = jnp.concatenate([C, F], 0)
+    gqkv = flat[:3 * D].reshape(3, D, width)
+    gout = jnp.concatenate([flat[j:j + width] for j in range(3 * D, 4 * D, width)], 1)
     return (out, gin, gg1[0], gg1[1], gqkv.transpose(1, 0, 2), gout, gg2[0], gg2[1], gup, gdown)
 
 

time: 505 us -> 507 us (level)
  starting transfers between devices: 51.9 us -> 45.4 us
    ppermute x60 -> x52, starting transfers between devices: 51.9 us -> 45.4 us  [swap(): return lax.ppermute(x, axis, [(k, k ^ bit) for k in range(size)])]
    ppermute x60 -> x52, waiting for transfers between devices: 167 us -> 172 us  [swap(): return lax.ppermute(x, axis, [(k, k ^ bit) for k in range(size)])]
    select_n x20 -> x16, other arithmetic: 25.2 us -> 22.3 us  [spread(): jnp.where(first, jnp.concatenate([x, got], 0), jnp.concatenate([got, x], 0))]
    add x20 -> x16, other arithmetic: 21.3 us -> 20.3 us  [fold(): return half(x, i) + swap(half(x, 1 - i), 'dp', dp, bit)]
    dynamic_slice x20 -> x16, local copies, waits for them, and re-layouts: 15 us -> 14.2 us  [half(): return lax.dynamic_slice_in_dim(x, i * n, n, 0)]
  transfers between devices with their start and end apart: 60 -> 52, of which waited for: 19 -> 20; matrix products, arithmetic and copies ran while one was open for 13% -> 11% of each run, Pallas kernels for 33% -> 30%
where the time goes in v7:
time: 507 us; the launch traced here: 506 us
  Pallas kernels  200 us (39%)
  waiting for transfers between devices  172 us (34%)
  other arithmetic  54.5 us (11%)
  starting transfers between devices  45.4 us (9%)
  local copies, waits for them, and re-layouts  33.1 us (7%)
    pallas_call x7, Pallas kernels, call(): pl.pallas_call(body, out_shape=list(outs), grid_spec=pltpu.PrefetchScalar...  173 us
    ppermute x52, waiting for transfers between devices, swap(): return lax.ppermute(x, axis, [(k, k ^ bit) for k in range(size)])  172 us
    ppermute x52, starting transfers between devices, swap(): return lax.ppermute(x, axis, [(k, k ^ bit) for k in range(size)])  45.4 us
    pallas_call x1, Pallas kernels, fwd_own(): pl.pallas_call(fwd_own_body(S, width), name='fwd_own', out_shape=outs, gr...  26.6 us
    select_n x16, other arithmetic, spread(): jnp.where(first, jnp.concatenate([x, got], 0), jnp.concatenate([got, x], 0))  22.3 us
    add x16, other arithmetic, fold(): return half(x, i) + swap(half(x, 1 - i), 'dp', dp, bit)  20.3 us
    dynamic_slice x16, local copies, waits for them, and re-layouts, half(): return lax.dynamic_slice_in_dim(x, i * n, n, 0)  14.2 us
  transfers between devices with their start and end apart: 52, of which 20 were waited for; matrix products, arithmetic and copies ran while one was open for 11% of the time, Pallas kernels for 30%

profile of v7, /device:TPU:0, one launch (start us, length us, event | category | flops | bytes accessed | tf_op | source)
XLA Modules:
  0.0 506.2 jit_solution(13150542704950007883)
XLA Ops:
  0.7 2.4 slice_bitcast_fusion.2
  5.3 3.0 collective-permute-start
  8.3 1.6 dynamic-slice_convert_fusion.3
  10.6 1.7 copy.22.col
  13.5 26.6 %fwd_own.1 = (bf16[1792,768]{1,0:T(8,128)(2,1)}, bf16[1792,768]{1,0:T(8,128)(2,1)}, bf16[1792,768]{1,0:T(8,128)(2,1)}, bf16[1792,1152]{1,0:T(8,128)(2,1)}, bf16[...) custom-call(s32[10]{0:T(128)} %concatenate.114.counts, s32[6,512,1]{2,1,0:T(8,128)} %copy.22.col, ...), custom_call_target="tpu_custom_call" | custom-call | flops 6000000000 | bytes 26214400 | tf_op jit(solution)/shard_map/fwd_own/pallas_call | solution.py:414
  41.2 2.2 dynamic-slice_convert_fusion.1
  43.5 2.5 collective-permute-start.4
  46.0 19.3 %collective-permute-done.4.q1 = f32[192,1152]{1,0:T(8,128)S(1)} collective-permute-done((f32[192,1152]{1,0:T(8,128)}, f32[192,1152]{1,0:T(8,128)S(1)}, u32[]{:S(2)}, u32[]{:S(2)}) %collective-permute-start.4) | collective-permute-done | bytes 884768 | tf_op jit(solution)/shard_map/ppermute | solution.py:481
  65.2 1.7 collective-permute-start.7
  67.2 1.5 collective-permute-start.2
  68.7 6.1 %collective-permute-done.7.w1 = f32[96,768]{1,0:T(8,128)S(1)} collective-permute-done((f32[96,768]{1,0:T(8,128)}, f32[96,768]{1,0:T(8,128)S(1)}, u32[]{:S(2)}, u32[]{:S(2)}) %collective-permute-start.7) | collective-permute-done | bytes 294944 | tf_op jit(solution)/shard_map/ppermute | solution.py:481
  74.9 1.5 collective-permute-start.3
  78.7 26.7 %shard_map.195 = (bf16[1792,1152]{1,0:T(8,128)(2,1)}, bf16[1792,384]{1,0:T(8,128)(2,1)}, f32[6,3,2,256]{3,2,1,0:T(2,128)}, f32[1792,768]{1,0:T(8,128)}, bf16[179...) custom-call(s32[10]{0:T(128)} %concatenate.114.counts, ...), custom_call_target="tpu_custom_call" | custom-call | flops 7000000000 | bytes 28354560 | tf_op jit(solution)/shard_map/pallas_call | solution.py:391
  105.4 15.6 %collective-permute-done.3.d0 = f32[384,768]{1,0:T(8,128)} collective-permute-done((f32[384,768]{1,0:T(8,128)S(1)}, f32[384,768]{1,0:T(8,128)}, u32[]{:S(2)}, u32[]{:S(2)}) %collective-permute-start.3) | collective-permute-done | bytes 1179680 | tf_op jit(solution)/shard_map/ppermute | solution.py:481
  121.0 32.0 %shard_map.196 = (f32[1792,768]{1,0:T(8,128)}, f32[1792,768]{1,0:T(8,128)}, f32[768,1536]{1,0:T(8,128)}, f32[1536,768]{1,0:T(8,128)}) custom-call(s32[10]{0:T(128)} %concatenate.114.counts, bf16[1792,768]{1,0:T(8,128)(2,1)} %get-tuple-element.87.c, bf16[1792,768]{1,0:T(8,128)(2,1)} %get-tuple-element.84.dm, bf16[768,1536]{1,0:T(8,128)(2,1)} %up.1, ...), custom_call_target="tpu_custom_call" | custom-call | flops 17999998976 | bytes 30670848 | tf_op jit(solution)/shard_map/pallas_call | solution.py:391
  153.0 3.2 constant_dynamic-slice_fusion.14
  156.3 3.2 constant_dynamic-slice_fusion.15
  160.3 1.7 collective-permute-start.13
  162.6 26.5 %collective-permute-done.12.u1 = f32[192,1536]{1,0:T(8,128)} collective-permute-done((f32[192,1536]{1,0:T(8,128)}, f32[192,1536]{1,0:T(8,128)}, u32[]{:S(2)}, u32[]{:S(2)}) %collective-permute-start.12) | collective-permute-done | bytes 1179680 | tf_op jit(solution)/shard_map/ppermute | solution.py:481
  189.1 24.3 %collective-permute-done.13.d1 = f32[384,768]{1,0:T(8,128)} collective-permute-done((f32[384,768]{1,0:T(8,128)}, f32[384,768]{1,0:T(8,128)}, u32[]{:S(2)}, u32[]{:S(2)}) %collective-permute-start.13) | collective-permute-done | bytes 1179680 | tf_op jit(solution)/shard_map/ppermute | solution.py:481
  214.0 2.2 dynamic-slice_add_fusion
  216.5 2.6 dynamic-slice_add_fusion.1
  225.7 33.5 %shard_map.197 = (bf16[6,512,768]{2,1,0:T(8,128)(2,1)}, f32[1792,768]{1,0:T(8,128)}, f32[8,768]{1,0:T(8,128)}) custom-call(s32[10]{0:T(128)} %concatenate.114.counts, s32[6,1,512]{2,1,0:T(1,128)} %broadcast_in_dim.18.line, bf16[1792,768]{1,0:T(8,128)(2,1)} %get-tuple-element.87.c, bf16[1792,768]{1,0:T(8,128)(2,1)} %get-tuple-element.84.dm, ...), custom_call_target="tpu_custom_call" | custom-call | flops 12000000000 | bytes 41720832 | tf_op jit(solution)/shard_map/pallas_call | solution.py:391
  259.3 1.9 dynamic-slice_add_fusion.4
  261.6 1.4 dynamic-slice_add_fusion.5
  265.9 25.1 %shard_map.198 = (f32[384,768]{1,0:T(8,128)}, bf16[1792,1152]{1,0:T(8,128)(2,1)}) custom-call(s32[10]{0:T(128)} %concatenate.114.counts, f32[1792,768]{1,0:T(8,128)} %get-tuple-element.109.dr, bf16[1792,1152]{1,0:T(8,128)(2,1)} %get-tuple-element.103.qkv, f32[6,3,2,256]{3,2,1,0:T(2,128)} %get-tuple-element.104.lse, bf16[1792,384]{1,0:T(8,128)(2,1)} %get-tuple-element.79.o, ...), custom_call_target="tpu_custom_call" | custom-call | flops 5000000000 | bytes 16945152 | tf_op jit(solution)/shard_map/pallas_call | solution.py:391
  291.0 2.2 fusion.1
  293.3 1.9 dynamic-slice_add_fusion.8
  295.2 2.0 dynamic-slice_add_fusion.9
  297.2 14.6 %shard_map.199 = (f32[1792,768]{1,0:T(8,128)}, f32[3,768,384]{2,1,0:T(8,128)}) custom-call(s32[10]{0:T(128)} %concatenate.114.counts, bf16[1792,1152]{1,0:T(8,128)(2,1)} %get-tuple-element.106.dqkv, bf16[1792,768]{1,0:T(8,128)(2,1)} %get-tuple-element.77.a, bf16[768,1152]{1,0:T(8,128)(2,1)} %copy-done.12), custom_call_target="tpu_custom_call" | custom-call | flops 5000000000 | bytes 17694720 | tf_op jit(solution)/shard_map/pallas_call | solution.py:391
  311.8 2.0 slice.57
  318.4 2.9 collective-permute-start.22
  321.3 23.7 %shard_map.200.dqkv = bf16[1792,1152]{1,0:T(8,128)(2,1)} custom-call(s32[10]{0:T(128)} %concatenate.114.counts, f32[1792,768]{1,0:T(8,128)} %get-tuple-element.109.dr, bf16[1792,1152]{1,0:T(8,128)(2,1)} %get-tuple-element.114.qkv, f32[6,3,2,256]{3,2,1,0:T(2,128)} %get-tuple-element.115.lse, bf16[384,768]{1,0:T(8,128)(2,1)} %get-tuple-element.116.wout), custom_call_target="tpu_custom_call" | custom-call | flops 4000000000 | bytes 14389248 | tf_op jit(solution)/shard_map/pallas_call | solution.py:391
  345.0 1.4 collective-permute-done.22
  347.5 1.8 dynamic-slice_add_fusion.2
  349.3 1.8 dynamic-slice_add_fusion.3
  351.2 2.9 collective-permute-start.28
  356.9 17.5 %shard_map.201 = (bf16[6,512,768]{2,1,0:T(8,128)(2,1)}, f32[8,768]{1,0:T(8,128)}) custom-call(s32[10]{0:T(128)} %concatenate.114.counts, s32[6,1,512]{2,1,0:T(1,128)} %broadcast_in_dim.18.line, f32[1792,768]{1,0:T(8,128)} %get-tuple-element.109.dr, bf16[1792,1152]{1,0:T(8,128)(2,1)} %shard_map.200.dqkv, bf16[768,1152]{1,0:T(8,128)(2,1)} %get-tuple-element.118.wqkv, ...), custom_call_target="tpu_custom_call" | custom-call | flops 4000000000 | bytes 24419328 | tf_op jit(solution)/shard_map/pallas_call | solution.py:391
  375.6 3.7 collective-permute-done.28
  384.1 1.8 collective-permute-start.44
  386.6 2.5 collective-permute-start.30
  389.1 2.3 collective-permute-done.32
  391.8 1.8 collective-permute-start.38
  393.6 11.2 %collective-permute-done.33 = f32[16,768]{1,0:T(8,128)S(1)} collective-permute-done((f32[16,768]{1,0:T(8,128)S(1)}, f32[16,768]{1,0:T(8,128)S(1)}, u32[]{:S(2)}, u32[]{:S(2)}) %collective-permute-start.33) | collective-permute-done | bytes 49184 | tf_op jit(solution)/shard_map/ppermute | solution.py:481
  405.9 1.7 collective-permute-start.45
  407.7 3.9 collective-permute-done.38
  412.0 6.7 %collective-permute-done.45 = f32[96,384]{1,0:T(8,128)S(1)} collective-permute-done((f32[96,384]{1,0:T(8,128)S(1)}, f32[96,384]{1,0:T(8,128)S(1)}, u32[]{:S(2)}, u32[]{:S(2)}) %collective-permute-start.45) | collective-permute-done | bytes 147488 | tf_op jit(solution)/shard_map/ppermute | solution.py:481
  419.0 2.7 collective-permute-start.35
  421.8 4.5 collective-permute-done.46
  426.3 1.6 collective-permute-start.47
  429.0 7.3 %collective-permute-done.47 = f32[192,384]{1,0:T(8,128)S(1)} collective-permute-done((f32[192,384]{1,0:T(8,128)S(1)}, f32[192,384]{1,0:T(8,128)S(1)}, u32[]{:S(2)}, u32[]{:S(2)}) %collective-permute-start.47) | collective-permute-done | bytes 294944 | tf_op jit(solution)/shard_map/ppermute | solution.py:481
  436.4 15.1 %collective-permute-done.40 = f32[96,384]{1,0:T(8,128)S(1)} collective-permute-done((f32[96,384]{1,0:T(8,128)S(1)}, f32[96,384]{1,0:T(8,128)S(1)}, u32[]{:S(2)}, u32[]{:S(2)}) %collective-permute-start.40) | collective-permute-done | bytes 147488 | tf_op jit(solution)/shard_map/ppermute | solution.py:481
  451.5 3.2 collective-permute-start.41
  454.7 1.6 collective-permute-start.36
  456.4 3.4 collective-permute-done.36
  460.4 8.4 %collective-permute-done.41 = f32[192,384]{1,0:T(8,128)S(1)} collective-permute-done((f32[192,384]{1,0:T(8,128)S(1)}, f32[192,384]{1,0:T(8,128)S(1)}, u32[]{:S(2)}, u32[]{:S(2)}) %collective-permute-start.41) | collective-permute-done | bytes 294944 | tf_op jit(solution)/shard_map/ppermute | solution.py:481
  470.3 1.6 maximum_select_fusion.2
  472.5 8.0 %collective-permute-done.42 = f32[384,384]{1,0:T(8,128)S(1)} collective-permute-done((f32[384,384]{1,0:T(8,128)S(1)}, f32[384,384]{1,0:T(8,128)S(1)}, u32[]{:S(2)}, u32[]{:S(2)}) %collective-permute-start.42) | collective-permute-done | bytes 589856 | tf_op jit(solution)/shard_map/ppermute | solution.py:481
  482.1 2.7 collective-permute-done.37
  486.3 2.0 maximum_select_fusion.5
  489.5 2.7 maximum_select_fusion.4
  492.2 2.0 pad_maximum_fusion
  494.3 5.1 maximum_select_fusion.1
  499.3 6.9 %maximum_select_fusion = f32[768,1536]{1,0:T(8,128)} fusion(f32[384,1536]{1,0:T(8,128)} %collective-permute-done.50, f32[384,1536]{1,0:T(8,128)} %maximum_select_fusion.2, pred[]{:T(512)S(6)} %eq.61), kind=kLoop, calls=%fused_computation | loop fusion | flops 3538944 | bytes 9437185 | tf_op jit(solution)/shard_map/jit(_where)/select_n | solution.py:505
  (188 shorter events, 45.1 us)
Async XLA Ops:
  3.1 6.9 %copy-start.20 = (f32[768]{0:T(1024)S(1)}, f32[768]{0:T(1024)}, u32[]{:S(2)}) copy-start(f32[768]{0:T(1024)} %param.15) | copy-start | bytes 9220
  3.1 7.5 %copy-start.17 = (s32[6,512]{1,0:T(8,128)S(1)}, s32[6,512]{1,0:T(8,128)}, u32[]{:S(2)}) copy-start(s32[6,512]{1,0:T(8,128)} %param.14) | copy-start | bytes 36868
  4.3 9.2 %copy-start.12 = (bf16[768,1152]{1,0:T(8,128)(2,1)}, bf16[768,1152]{1,0:T(8,128)(2,1)S(1)}, u32[]{:S(2)}) copy-start(bf16[768,1152]{1,0:T(8,128)(2,1)S(1)} %pad_maximum_fusion.3.weight.wqkv) | copy-start | bytes 5308420
  4.3 7.9 %copy-start.21 = (f32[768]{0:T(1024)S(1)}, f32[768]{0:T(1024)}, u32[]{:S(2)}) copy-start(f32[768]{0:T(1024)} %param.16) | copy-start | bytes 9220
  4.3 8.5 %copy-start.24 = (s32[6]{0:T(128)S(1)}, s32[6]{0:T(128)}, u32[]{:S(2)}) copy-start(s32[6]{0:T(128)} %param.13) | copy-start | bytes 76
  5.3 38.1 %collective-permute-start = (f32[192,1152]{1,0:T(8,128)}, f32[192,1152]{1,0:T(8,128)}, u32[]{:S(2)}, u32[]{:S(2)}) collective-permute-start(f32[192,1152]{1,0:T(8,128)} %dynamic-slice_convert_fusion.2), channel_id=1, source_target_pairs={{0,1},{1,0},{2,3},{3,2},{4,5},{5,4},{6,7},{7,6},{8,9},{9,8},{10,11... | collective-permute-start | bytes 2654216 | tf_op jit(solution)/shard_map/ppermute | solution.py:481
  10.0 33.5 %collective-permute-start.1 = (f32[96,768]{1,0:T(8,128)}, f32[96,768]{1,0:T(8,128)}, u32[]{:S(2)}, u32[]{:S(2)}) collective-permute-start(f32[96,768]{1,0:T(8,128)} %dynamic-slice_convert_fusion.3), channel_id=1, source_target_pairs={{0,1},{1,0},{2,3},{3,2},{4,5},{5,4},{6,7},{7,6},{8,9},{9,8},{10,11... | collective-permute-start | bytes 884744 | tf_op jit(solution)/shard_map/ppermute | solution.py:481
  40.1 36.4 %copy-start.22 = (f32[768]{0:T(1024)S(1)}, f32[768]{0:T(1024)}, u32[]{:S(2)}) copy-start(f32[768]{0:T(1024)} %param.19) | copy-start | bytes 9220
  40.1 37.0 %copy-start.23 = (f32[768]{0:T(1024)S(1)}, f32[768]{0:T(1024)}, u32[]{:S(2)}) copy-start(f32[768]{0:T(1024)} %param.20) | copy-start | bytes 9220
  43.5 21.8 %collective-permute-start.4 = (f32[192,1152]{1,0:T(8,128)}, f32[192,1152]{1,0:T(8,128)S(1)}, u32[]{:S(2)}, u32[]{:S(2)}) collective-permute-start(f32[192,1152]{1,0:T(8,128)} %collective-permute-done.q0), channel_id=1, source_target_pairs={{0,4},{2,6},{4,0},{6,2},{8,12},{10,14},{12,8},{14,10},{16,20},{18,... | collective-permute-start | bytes 2654216 | tf_op jit(solution)/shard_map/ppermute | solution.py:481
  45.9 32.0 %collective-permute-start.5 = (f32[192,1152]{1,0:T(8,128)}, f32[192,1152]{1,0:T(8,128)}, u32[]{:S(2)}, u32[]{:S(2)}) collective-permute-start(f32[192,1152]{1,0:T(8,128)} %collective-permute-done.q0), channel_id=1, source_target_pairs={{0,2},{2,0},{4,6},{6,4},{8,10},{10,8},{12,14},{14,12},{16,18},{18,... | collective-permute-start | bytes 2654216 | tf_op jit(solution)/shard_map/ppermute | solution.py:481
  65.2 12.4 %copy-start.29 = (f32[192,1152]{1,0:T(8,128)}, f32[192,1152]{1,0:T(8,128)S(1)}, u32[]{:S(2)}) copy-start(f32[192,1152]{1,0:T(8,128)S(1)} %collective-permute-done.4.q1) | copy-start | bytes 2654212
  65.2 12.8 %collective-permute-start.6 = (f32[192,1152]{1,0:T(8,128)S(1)}, f32[192,1152]{1,0:T(8,128)}, u32[]{:S(2)}, u32[]{:S(2)}) collective-permute-start(f32[192,1152]{1,0:T(8,128)S(1)} %collective-permute-done.4.q1), channel_id=1, source_target_pairs={{0,2},{2,0},{4,6},{6,4},{8,10},{10,8},{12,14},{14,12},{16,18},{18,... | collective-permute-start | bytes 2654216 | tf_op jit(solution)/shard_map/ppermute | solution.py:481
  65.2 9.6 %collective-permute-start.7 = (f32[96,768]{1,0:T(8,128)}, f32[96,768]{1,0:T(8,128)S(1)}, u32[]{:S(2)}, u32[]{:S(2)}) collective-permute-start(f32[96,768]{1,0:T(8,128)} %collective-permute-done.1.w0), channel_id=1, source_target_pairs={{0,4},{2,6},{4,0},{6,2},{8,12},{10,14},{12,8},{14,10},{16,20},{18,... | collective-permute-start | bytes 884744 | tf_op jit(solution)/shard_map/ppermute | solution.py:481
  67.0 9.4 %collective-permute-start.8 = (f32[96,768]{1,0:T(8,128)}, f32[96,768]{1,0:T(8,128)S(1)}, u32[]{:S(2)}, u32[]{:S(2)}) collective-permute-start(f32[96,768]{1,0:T(8,128)} %collective-permute-done.1.w0), channel_id=1, source_target_pairs={{0,2},{2,0},{4,6},{6,4},{8,10},{10,8},{12,14},{14,12},{16,18},{18,... | collective-permute-start | bytes 884744 | tf_op jit(solution)/shard_map/ppermute | solution.py:481
  67.2 38.2 %collective-permute-start.2 = (f32[192,1536]{1,0:T(8,128)}, f32[192,1536]{1,0:T(8,128)}, u32[]{:S(2)}, u32[]{:S(2)}) collective-permute-start(f32[192,1536]{1,0:T(8,128)} %dynamic-slice_convert_fusion.1), channel_id=1, source_target_pairs={{0,1},{1,0},{2,3},{3,2},{4,5},{5,4},{6,7},{7,6},{8,9},{9,8},{10,11... | collective-permute-start | bytes 3538952 | tf_op jit(solution)/shard_map/ppermute | solution.py:481
  74.9 46.1 %collective-permute-start.3 = (f32[384,768]{1,0:T(8,128)S(1)}, f32[384,768]{1,0:T(8,128)}, u32[]{:S(2)}, u32[]{:S(2)}) collective-permute-start(f32[384,768]{1,0:T(8,128)S(1)} %dynamic-slice_convert_fusion), channel_id=1, source_target_pairs={{0,1},{1,0},{2,3},{3,2},{4,5},{5,4},{6,7},{7,6},{8,9},{9,8},{10,11... | collective-permute-start | bytes 3538952 | tf_op jit(solution)/shard_map/ppermute | solution.py:481
  76.4 1.6 collective-permute-start.9
  156.3 57.2 %collective-permute-start.11 = (f32[768,768]{1,0:T(8,128)}, f32[768,768]{1,0:T(8,128)S(1)}, u32[]{:S(2)}, u32[]{:S(2)}) collective-permute-start(f32[768,768]{1,0:T(8,128)} %constant_dynamic-slice_fusion.14), channel_id=1, source_target_pairs={{0,2},{2,0},{4,6},{6,4},{8,10},{10,8},{12,14},{14,12},{16,18},{18,... | collective-permute-start | bytes 7077896 | tf_op jit(solution)/shard_map/ppermute | solution.py:481
  159.5 56.7 %collective-permute-start.10 = (f32[384,1536]{1,0:T(8,128)}, f32[384,1536]{1,0:T(8,128)}, u32[]{:S(2)}, u32[]{:S(2)}) collective-permute-start(f32[384,1536]{1,0:T(8,128)} %constant_dynamic-slice_fusion.15), channel_id=1, source_target_pairs={{0,2},{2,0},{4,6},{6,4},{8,10},{10,8},{12,14},{14,12},{16,18},{18,... | collective-permute-start | bytes 7077896 | tf_op jit(solution)/shard_map/ppermute | solution.py:481
  160.0 29.2 %collective-permute-start.12 = (f32[192,1536]{1,0:T(8,128)}, f32[192,1536]{1,0:T(8,128)}, u32[]{:S(2)}, u32[]{:S(2)}) collective-permute-start(f32[192,1536]{1,0:T(8,128)} %collective-permute-done.2.u0), channel_id=1, source_target_pairs={{0,4},{2,6},{4,0},{6,2},{8,12},{10,14},{12,8},{14,10},{16,20},{18,... | collective-permute-start | bytes 3538952 | tf_op jit(solution)/shard_map/ppermute | solution.py:481
  160.3 53.2 %collective-permute-start.13 = (f32[384,768]{1,0:T(8,128)}, f32[384,768]{1,0:T(8,128)}, u32[]{:S(2)}, u32[]{:S(2)}) collective-permute-start(f32[384,768]{1,0:T(8,128)} %collective-permute-done.3.d0), channel_id=1, source_target_pairs={{0,4},{2,6},{4,0},{6,2},{8,12},{10,14},{12,8},{14,10},{16,20},{18,... | collective-permute-start | bytes 3538952 | tf_op jit(solution)/shard_map/ppermute | solution.py:481
  162.6 58.9 %collective-permute-start.14 = (f32[192,1536]{1,0:T(8,128)}, f32[192,1536]{1,0:T(8,128)S(1)}, u32[]{:S(2)}, u32[]{:S(2)}) collective-permute-start(f32[192,1536]{1,0:T(8,128)} %collective-permute-done.2.u0), channel_id=1, source_target_pairs={{0,2},{2,0},{4,6},{6,4},{8,10},{10,8},{12,14},{14,12},{16,18},{18,... | collective-permute-start | bytes 3538952 | tf_op jit(solution)/shard_map/ppermute | solution.py:481
  189.1 33.4 %collective-permute-start.16 = (f32[384,768]{1,0:T(8,128)}, f32[384,768]{1,0:T(8,128)S(1)}, u32[]{:S(2)}, u32[]{:S(2)}) collective-permute-start(f32[384,768]{1,0:T(8,128)} %collective-permute-done.3.d0), channel_id=1, source_target_pairs={{0,2},{2,0},{4,6},{6,4},{8,10},{10,8},{12,14},{14,12},{16,18},{18,... | collective-permute-start | bytes 3538952 | tf_op jit(solution)/shard_map/ppermute | solution.py:481
  213.5 10.1 %collective-permute-start.15 = (f32[192,1536]{1,0:T(8,128)}, f32[192,1536]{1,0:T(8,128)S(1)}, u32[]{:S(2)}, u32[]{:S(2)}) collective-permute-start(f32[192,1536]{1,0:T(8,128)} %collective-permute-done.12.u1), channel_id=1, source_target_pairs={{0,2},{2,0},{4,6},{6,4},{8,10},{10,8},{12,14},{14,12},{16,18},{18,... | collective-permute-start | bytes 3538952 | tf_op jit(solution)/shard_map/ppermute | solution.py:481
  213.5 11.2 %collective-permute-start.17 = (f32[384,768]{1,0:T(8,128)}, f32[384,768]{1,0:T(8,128)S(1)}, u32[]{:S(2)}, u32[]{:S(2)}) collective-permute-start(f32[384,768]{1,0:T(8,128)} %collective-permute-done.13.d1), channel_id=1, source_target_pairs={{0,2},{2,0},{4,6},{6,4},{8,10},{10,8},{12,14},{14,12},{16,18},{18,... | collective-permute-start | bytes 3538952 | tf_op jit(solution)/shard_map/ppermute | solution.py:481
  220.3 38.9 %collective-permute-start.19 = (f32[384,768]{1,0:T(8,128)}, f32[384,768]{1,0:T(8,128)}, u32[]{:S(2)}, u32[]{:S(2)}) collective-permute-start(f32[384,768]{1,0:T(8,128)} %constant_dynamic-slice_fusion.12), channel_id=1, source_target_pairs={{0,8},{2,10},{4,12},{6,14},{8,0},{10,2},{12,4},{14,6},{16,24},{18,... | collective-permute-start | bytes 3538952 | tf_op jit(solution)/shard_map/ppermute | solution.py:481
  221.5 39.7 %collective-permute-start.18 = (f32[192,1536]{1,0:T(8,128)S(1)}, f32[192,1536]{1,0:T(8,128)}, u32[]{:S(2)}, u32[]{:S(2)}) collective-permute-start(f32[192,1536]{1,0:T(8,128)S(1)} %constant_dynamic-slice_fusion.13), channel_id=1, source_target_pairs={{0,4},{2,6},{4,0},{6,2},{8,12},{10,14},{12,8},{14,10},{16,20},{18,... | collective-permute-start | bytes 3538952 | tf_op jit(solution)/shard_map/ppermute | solution.py:481
  263.9 29.3 %collective-permute-start.21 = (f32[192,768]{1,0:T(8,128)}, f32[192,768]{1,0:T(8,128)}, u32[]{:S(2)}, u32[]{:S(2)}) collective-permute-start(f32[192,768]{1,0:T(8,128)} %constant_dynamic-slice_fusion.10), channel_id=1, source_target_pairs={{0,4},{2,6},{4,0},{6,2},{8,12},{10,14},{12,8},{14,10},{16,20},{18,... | collective-permute-start | bytes 1769480 | tf_op jit(solution)/shard_map/ppermute | solution.py:481
  265.9 29.3 %collective-permute-start.20 = (f32[96,1536]{1,0:T(8,128)}, f32[96,1536]{1,0:T(8,128)}, u32[]{:S(2)}, u32[]{:S(2)}) collective-permute-start(f32[96,1536]{1,0:T(8,128)} %constant_dynamic-slice_fusion.11), channel_id=1, source_target_pairs={{0,8},{2,10},{4,12},{6,14},{8,0},{10,2},{12,4},{14,6},{16,24},{18,... | collective-permute-start | bytes 1769480 | tf_op jit(solution)/shard_map/ppermute | solution.py:481
  315.9 31.6 %collective-permute-start.25 = (f32[768,384]{1,0:T(8,128)}, f32[768,384]{1,0:T(8,128)}, u32[]{:S(2)}, u32[]{:S(2)}) collective-permute-start(f32[768,384]{1,0:T(8,128)} %constant_dynamic-slice_fusion.6), channel_id=1, source_target_pairs={{0,2},{2,0},{4,6},{6,4},{8,10},{10,8},{12,14},{14,12},{16,18},{18,... | collective-permute-start | bytes 3538952 | tf_op jit(solution)/shard_map/ppermute | solution.py:481
  317.0 32.3 %collective-permute-start.24 = (f32[768,384]{1,0:T(8,128)}, f32[768,384]{1,0:T(8,128)}, u32[]{:S(2)}, u32[]{:S(2)}) collective-permute-start(f32[768,384]{1,0:T(8,128)} %constant_dynamic-slice_fusion.7), channel_id=1, source_target_pairs={{0,2},{2,0},{4,6},{6,4},{8,10},{10,8},{12,14},{14,12},{16,18},{18,... | collective-permute-start | bytes 3538952 | tf_op jit(solution)/shard_map/ppermute | solution.py:481
  317.5 27.5 %collective-permute-start.23 = (f32[96,768]{1,0:T(8,128)S(1)}, f32[96,768]{1,0:T(8,128)S(1)}, u32[]{:S(2)}, u32[]{:S(2)}) collective-permute-start(f32[96,768]{1,0:T(8,128)S(1)} %constant_dynamic-slice_fusion.8), channel_id=1, source_target_pairs={{0,16},{2,18},{4,20},{6,22},{8,24},{10,26},{12,28},{14,30},{16,0},... | collective-permute-start | bytes 884744 | tf_op jit(solution)/shard_map/ppermute | solution.py:481
  318.4 28.1 %collective-permute-start.22 = (f32[48,1536]{1,0:T(8,128)}, f32[48,1536]{1,0:T(8,128)}, u32[]{:S(2)}, u32[]{:S(2)}) collective-permute-start(f32[48,1536]{1,0:T(8,128)} %constant_dynamic-slice_fusion.9), channel_id=1, source_target_pairs={{0,16},{2,18},{4,20},{6,22},{8,24},{10,26},{12,28},{14,30},{16,0},... | collective-permute-start | bytes 884744 | tf_op jit(solution)/shard_map/ppermute | solution.py:481
  349.2 5.7 %copy-start.8 = (f32[768,384]{1,0:T(8,128)}, f32[768,384]{1,0:T(8,128)S(1)}, u32[]{:S(2)}) copy-start(f32[768,384]{1,0:T(8,128)S(1)} %dynamic-slice_add_fusion.2) | copy-start | bytes 3538948
  351.1 23.3 %collective-permute-start.29 = (f32[96,768]{1,0:T(8,128)S(1)}, f32[96,768]{1,0:T(8,128)}, u32[]{:S(2)}, u32[]{:S(2)}) collective-permute-start(f32[96,768]{1,0:T(8,128)S(1)} %dynamic-slice_add_fusion.12), channel_id=1, source_target_pairs={{0,16},{2,18},{4,20},{6,22},{8,24},{10,26},{12,28},{14,30},{16,0},... | collective-permute-start | bytes 884744 | tf_op jit(solution)/shard_map/ppermute | solution.py:481
  351.2 28.1 %collective-permute-start.28 = (f32[48,1536]{1,0:T(8,128)S(1)}, f32[48,1536]{1,0:T(8,128)}, u32[]{:S(2)}, u32[]{:S(2)}) collective-permute-start(f32[48,1536]{1,0:T(8,128)S(1)} %dynamic-slice_add_fusion.13), channel_id=1, source_target_pairs={{0,16},{2,18},{4,20},{6,22},{8,24},{10,26},{12,28},{14,30},{16,0},... | collective-permute-start | bytes 884744 | tf_op jit(solution)/shard_map/ppermute | solution.py:481
  354.9 26.6 %collective-permute-start.27 = (f32[384,384]{1,0:T(8,128)}, f32[384,384]{1,0:T(8,128)}, u32[]{:S(2)}, u32[]{:S(2)}) collective-permute-start(f32[384,384]{1,0:T(8,128)} %constant_dynamic-slice_fusion.4), channel_id=1, source_target_pairs={{0,8},{2,10},{4,12},{6,14},{8,0},{10,2},{12,4},{14,6},{16,24},{18,... | collective-permute-start | bytes 1769480 | tf_op jit(solution)/shard_map/ppermute | solution.py:481
  356.5 26.2 %collective-permute-start.26 = (f32[384,384]{1,0:T(8,128)}, f32[384,384]{1,0:T(8,128)}, u32[]{:S(2)}, u32[]{:S(2)}) collective-permute-start(f32[384,384]{1,0:T(8,128)} %constant_dynamic-slice_fusion.5), channel_id=1, source_target_pairs={{0,4},{2,6},{4,0},{6,2},{8,12},{10,14},{12,8},{14,10},{16,20},{18,... | collective-permute-start | bytes 1769480 | tf_op jit(solution)/shard_map/ppermute | solution.py:481
  374.4 7.2 %copy-start.9 = (f32[768,384]{1,0:T(8,128)S(1)}, f32[768,384]{1,0:T(8,128)}, u32[]{:S(2)}) copy-start(f32[768,384]{1,0:T(8,128)} %copy-done.8) | copy-start | bytes 3538948
  380.4 5.6 %copy-start.19 = (f32[8,768]{1,0:T(8,128)S(1)}, f32[8,768]{1,0:T(8,128)}, u32[]{:S(2)}) copy-start(f32[8,768]{1,0:T(8,128)} %get-tuple-element.128) | copy-start | bytes 73732
  380.4 5.5 %copy-start.18 = (f32[8,768]{1,0:T(8,128)S(1)}, f32[8,768]{1,0:T(8,128)}, u32[]{:S(2)}) copy-start(f32[8,768]{1,0:T(8,128)} %get-tuple-element.129) | copy-start | bytes 73732
  384.1 20.7 %collective-permute-start.44 = (f32[192,384]{1,0:T(8,128)S(1)}, f32[192,384]{1,0:T(8,128)}, u32[]{:S(2)}, u32[]{:S(2)}) collective-permute-start(f32[192,384]{1,0:T(8,128)S(1)} %constant_dynamic-slice_fusion.1), channel_id=1, source_target_pairs={{0,4},{2,6},{4,0},{6,2},{8,12},{10,14},{12,8},{14,10},{16,20},{18,... | collective-permute-start | bytes 884744 | tf_op jit(solution)/shard_map/ppermute | solution.py:481
  386.0 5.5 %collective-permute-start.32 = (f32[16,768]{1,0:T(8,128)S(1)}, f32[16,768]{1,0:T(8,128)S(1)}, u32[]{:S(2)}, u32[]{:S(2)}) collective-permute-start(f32[16,768]{1,0:T(8,128)S(1)} %constant_dynamic-update-slice_fusion), channel_id=1, source_target_pairs={{0,16},{2,18},{4,20},{6,22},{8,24},{10,26},{12,28},{14,30},{16,0},... | collective-permute-start | bytes 147464 | tf_op jit(solution)/shard_map/ppermute | solution.py:481
  386.6 32.3 %collective-permute-start.31 = (f32[192,768]{1,0:T(8,128)S(1)}, f32[192,768]{1,0:T(8,128)S(1)}, u32[]{:S(2)}, u32[]{:S(2)}) collective-permute-start(f32[192,768]{1,0:T(8,128)S(1)} %maximum_select_fusion.11), channel_id=1, source_target_pairs={{0,4},{2,6},{4,0},{6,2},{8,12},{10,14},{12,8},{14,10},{16,20},{18,... | collective-permute-start | bytes 1769480 | tf_op jit(solution)/shard_map/ppermute | solution.py:481
  386.6 32.2 %collective-permute-start.30 = (f32[96,1536]{1,0:T(8,128)S(1)}, f32[96,1536]{1,0:T(8,128)S(1)}, u32[]{:S(2)}, u32[]{:S(2)}) collective-permute-start(f32[96,1536]{1,0:T(8,128)S(1)} %maximum_select_fusion.10), channel_id=1, source_target_pairs={{0,8},{2,10},{4,12},{6,14},{8,0},{10,2},{12,4},{14,6},{16,24},{18,... | collective-permute-start | bytes 1769480 | tf_op jit(solution)/shard_map/ppermute | solution.py:481
  391.4 13.4 %collective-permute-start.33 = (f32[16,768]{1,0:T(8,128)S(1)}, f32[16,768]{1,0:T(8,128)S(1)}, u32[]{:S(2)}, u32[]{:S(2)}) collective-permute-start(f32[16,768]{1,0:T(8,128)S(1)} %add.222), channel_id=1, source_target_pairs={{0,8},{2,10},{4,12},{6,14},{8,0},{10,2},{12,4},{14,6},{16,24},{18,... | collective-permute-start | bytes 147464 | tf_op jit(solution)/shard_map/ppermute | solution.py:481
  391.8 19.9 %collective-permute-start.38 = (f32[192,384]{1,0:T(8,128)S(1)}, f32[192,384]{1,0:T(8,128)S(1)}, u32[]{:S(2)}, u32[]{:S(2)}) collective-permute-start(f32[192,384]{1,0:T(8,128)S(1)} %constant_dynamic-slice_fusion.3), channel_id=1, source_target_pairs={{0,8},{2,10},{4,12},{6,14},{8,0},{10,2},{12,4},{14,6},{16,24},{18,... | collective-permute-start | bytes 884744 | tf_op jit(solution)/shard_map/ppermute | solution.py:481
  405.9 12.8 %collective-permute-start.45 = (f32[96,384]{1,0:T(8,128)S(1)}, f32[96,384]{1,0:T(8,128)S(1)}, u32[]{:S(2)}, u32[]{:S(2)}) collective-permute-start(f32[96,384]{1,0:T(8,128)S(1)} %constant_dynamic-slice_fusion), channel_id=1, source_target_pairs={{0,16},{2,18},{4,20},{6,22},{8,24},{10,26},{12,28},{14,30},{16,0},... | collective-permute-start | bytes 442376 | tf_op jit(solution)/shard_map/ppermute | solution.py:481
  411.7 16.7 %collective-permute-start.39 = (f32[96,384]{1,0:T(8,128)S(1)}, f32[96,384]{1,0:T(8,128)S(1)}, u32[]{:S(2)}, u32[]{:S(2)}) collective-permute-start(f32[96,384]{1,0:T(8,128)S(1)} %constant_dynamic-slice_fusion.2), channel_id=1, source_target_pairs={{0,16},{2,18},{4,20},{6,22},{8,24},{10,26},{12,28},{14,30},{16,0},... | collective-permute-start | bytes 442376 | tf_op jit(solution)/shard_map/ppermute | solution.py:481
  418.7 7.6 %collective-permute-start.46 = (f32[96,384]{1,0:T(8,128)S(1)}, f32[96,384]{1,0:T(8,128)S(1)}, u32[]{:S(2)}, u32[]{:S(2)}) collective-permute-start(f32[96,384]{1,0:T(8,128)S(1)} %dynamic-slice_add_fusion.14), channel_id=1, source_target_pairs={{0,16},{2,18},{4,20},{6,22},{8,24},{10,26},{12,28},{14,30},{16,0},... | collective-permute-start | bytes 442376 | tf_op jit(solution)/shard_map/ppermute | solution.py:481
  419.0 51.1 %collective-permute-start.35 = (f32[384,768]{1,0:T(8,128)S(1)}, f32[384,768]{1,0:T(8,128)S(1)}, u32[]{:S(2)}, u32[]{:S(2)}) collective-permute-start(f32[384,768]{1,0:T(8,128)S(1)} %maximum_select_fusion.7), channel_id=1, source_target_pairs={{0,8},{2,10},{4,12},{6,14},{8,0},{10,2},{12,4},{14,6},{16,24},{18,... | collective-permute-start | bytes 3538952 | tf_op jit(solution)/shard_map/ppermute | solution.py:481
  426.3 9.9 %collective-permute-start.47 = (f32[192,384]{1,0:T(8,128)S(1)}, f32[192,384]{1,0:T(8,128)S(1)}, u32[]{:S(2)}, u32[]{:S(2)}) collective-permute-start(f32[192,384]{1,0:T(8,128)S(1)} %maximum_select_fusion.15), channel_id=1, source_target_pairs={{0,4},{2,6},{4,0},{6,2},{8,12},{10,14},{12,8},{14,10},{16,20},{18,... | collective-permute-start | bytes 884744 | tf_op jit(solution)/shard_map/ppermute | solution.py:481
  427.9 42.4 %collective-permute-start.34 = (f32[192,1536]{1,0:T(8,128)S(1)}, f32[192,1536]{1,0:T(8,128)S(1)}, u32[]{:S(2)}, u32[]{:S(2)}) collective-permute-start(f32[192,1536]{1,0:T(8,128)S(1)} %maximum_select_fusion.6), channel_id=1, source_target_pairs={{0,4},{2,6},{4,0},{6,2},{8,12},{10,14},{12,8},{14,10},{16,20},{18,... | collective-permute-start | bytes 3538952 | tf_op jit(solution)/shard_map/ppermute | solution.py:481
  428.4 23.0 %collective-permute-start.40 = (f32[96,384]{1,0:T(8,128)S(1)}, f32[96,384]{1,0:T(8,128)S(1)}, u32[]{:S(2)}, u32[]{:S(2)}) collective-permute-start(f32[96,384]{1,0:T(8,128)S(1)} %dynamic-slice_add_fusion.15), channel_id=1, source_target_pairs={{0,16},{2,18},{4,20},{6,22},{8,24},{10,26},{12,28},{14,30},{16,0},... | collective-permute-start | bytes 442376 | tf_op jit(solution)/shard_map/ppermute | solution.py:481
  436.3 33.6 %collective-permute-start.48 = (f32[384,384]{1,0:T(8,128)S(1)}, f32[384,384]{1,0:T(8,128)S(1)}, u32[]{:S(2)}, u32[]{:S(2)}) collective-permute-start(f32[384,384]{1,0:T(8,128)S(1)} %maximum_select_fusion.13), channel_id=1, source_target_pairs={{0,8},{2,10},{4,12},{6,14},{8,0},{10,2},{12,4},{14,6},{16,24},{18,... | collective-permute-start | bytes 1769480 | tf_op jit(solution)/shard_map/ppermute | solution.py:481
  451.5 17.3 %collective-permute-start.41 = (f32[192,384]{1,0:T(8,128)S(1)}, f32[192,384]{1,0:T(8,128)S(1)}, u32[]{:S(2)}, u32[]{:S(2)}) collective-permute-start(f32[192,384]{1,0:T(8,128)S(1)} %maximum_select_fusion.14), channel_id=1, source_target_pairs={{0,8},{2,10},{4,12},{6,14},{8,0},{10,2},{12,4},{14,6},{16,24},{18,... | collective-permute-start | bytes 884744 | tf_op jit(solution)/shard_map/ppermute | solution.py:481
  454.7 5.1 collective-permute-start.36
  468.8 11.7 %collective-permute-start.42 = (f32[384,384]{1,0:T(8,128)S(1)}, f32[384,384]{1,0:T(8,128)S(1)}, u32[]{:S(2)}, u32[]{:S(2)}) collective-permute-start(f32[384,384]{1,0:T(8,128)S(1)} %maximum_select_fusion.12), channel_id=1, source_target_pairs={{0,4},{2,6},{4,0},{6,2},{8,12},{10,14},{12,8},{14,10},{16,20},{18,... | collective-permute-start | bytes 1769480 | tf_op jit(solution)/shard_map/ppermute | solution.py:481
  470.0 16.3 %collective-permute-start.49 = (f32[768,384]{1,0:T(8,128)S(1)}, f32[768,384]{1,0:T(8,128)}, u32[]{:S(2)}, u32[]{:S(2)}) collective-permute-start(f32[768,384]{1,0:T(8,128)S(1)} %maximum_select_fusion.9), channel_id=1, source_target_pairs={{0,2},{2,0},{4,6},{6,4},{8,10},{10,8},{12,14},{14,12},{16,18},{18,... | collective-permute-start | bytes 3538952 | tf_op jit(solution)/shard_map/ppermute | solution.py:481
  471.9 22.3 %collective-permute-start.51 = (f32[768,768]{1,0:T(8,128)S(1)}, f32[768,768]{1,0:T(8,128)}, u32[]{:S(2)}, u32[]{:S(2)}) collective-permute-start(f32[768,768]{1,0:T(8,128)S(1)} %maximum_select_fusion.3), channel_id=1, source_target_pairs={{0,2},{2,0},{4,6},{6,4},{8,10},{10,8},{12,14},{14,12},{16,18},{18,... | collective-permute-start | bytes 7077896 | tf_op jit(solution)/shard_map/ppermute | solution.py:481
  472.4 26.9 %collective-permute-start.50 = (f32[384,1536]{1,0:T(8,128)}, f32[384,1536]{1,0:T(8,128)}, u32[]{:S(2)}, u32[]{:S(2)}) collective-permute-start(f32[384,1536]{1,0:T(8,128)} %maximum_select_fusion.2), channel_id=1, source_target_pairs={{0,2},{2,0},{4,6},{6,4},{8,10},{10,8},{12,14},{14,12},{16,18},{18,... | collective-permute-start | bytes 7077896 | tf_op jit(solution)/shard_map/ppermute | solution.py:481
  481.6 7.9 %collective-permute-start.43 = (f32[768,384]{1,0:T(8,128)}, f32[768,384]{1,0:T(8,128)}, u32[]{:S(2)}, u32[]{:S(2)}) collective-permute-start(f32[768,384]{1,0:T(8,128)} %maximum_select_fusion.8), channel_id=1, source_target_pairs={{0,2},{2,0},{4,6},{6,4},{8,10},{10,8},{12,14},{14,12},{16,18},{18,... | collective-permute-start | bytes 3538952 | tf_op jit(solution)/shard_map/ppermute | solution.py:481
  481.6 3.3 collective-permute-start.37
  (21 other events, 47.1 us)
